TPU v7x, 256 devices: a whole 4x4x8 slice. The times are simulated.
256 devices in a mesh: section: 8 (over y, core), seq: 32 (over z, x).
Axes of the slice: x: 4, y: 4, z: 8, core: 2. Of those that a mesh axis runs over, the one named last changes fastest.
Arguments:
- inputs: bfloat16 [3, 1536, 2048], P(None, 'seq'), may hold values from -6 to 6
- norm_gain: bfloat16 [8, 2048], P('section'), may hold values from 0.25 to 1.75
- w_query: bfloat16 [8, 2048, 2048], P('section', 'seq')
- w_key: bfloat16 [8, 2048, 512], P('section', 'seq')
- w_value: bfloat16 [8, 2048, 512], P('section', 'seq'), may hold values from -0.125 to 0.125
- w_out: bfloat16 [8, 2048, 2048], P('section', 'seq'), may hold values from -0.125 to 0.125
Outputs:
- layer_outputs: bfloat16 [8, 3, 1536, 2048], P('section', None, 'seq')
All inputs are finite; a program needn't handle non-finite values.
Results may differ from a plain program's by a relative error of at most 0.04.
Values may be sent and summed in bfloat16 or wider, within the bound.
No kernel may reach another device: no remote copies, remote signals or barrier semaphores. Data moves between devices by JAX's collectives and lax.ppermute only.
A program may use at most 64 MiB of HBM per device.

v0:
```python
import jax
import jax.numpy as jnp
from jax import lax
from jax.sharding import PartitionSpec as P

HEADS = 32
KVH = 8
HD = 64


epsilon = 1e-05


def passed_along(block, axis, distance):
    devices = range(lax.axis_size(axis))
    route = [(i - distance, i) for i in devices if i - distance in devices]
    return lax.ppermute(block, axis, route)


def local(inputs, norm_gain, w_query, w_key, w_value, w_out):
    full_query, full_key, full_value, full_out = (
        lax.all_gather(w_query, "seq", axis=1, tiled=True),
        lax.all_gather(w_key, "seq", axis=1, tiled=True),
        lax.all_gather(w_value, "seq", axis=1, tiled=True),
        lax.all_gather(w_out, "seq", axis=1, tiled=True),
    )
    query_weight = full_query[0]
    key_weight = full_key[0]
    value_weight = full_value[0]
    out_weight = full_out[0]
    gain_row = norm_gain[0].astype(jnp.float32)
    micro_count, tok_rows, model_width = inputs.shape
    seq_devices = lax.axis_size("seq")
    section_count = lax.axis_size("section")
    section_index = lax.axis_index("section")
    span_rows = tok_rows * seq_devices
    heads_dev = HEADS // seq_devices
    share_count = HEADS // KVH
    key_three = key_weight.reshape(model_width, KVH, HD)
    value_three = value_weight.reshape(model_width, KVH, HD)
    score_scale = HD ** (-0.5)
    query_pos = jnp.arange(span_rows, dtype=jnp.int32)

    def project(layer_input):
        wide_input = layer_input.astype(jnp.float32)
        scale_rows = lax.rsqrt(jnp.mean(wide_input * wide_input, axis=-1, keepdims=True) + epsilon)
        normed_rows = (wide_input * scale_rows * gain_row).astype(jnp.bfloat16)
        queries = jnp.dot(normed_rows, query_weight, preferred_element_type=jnp.float32).astype(
            jnp.bfloat16
        )
        key_part = jnp.einsum(
            "td,dhe->the", normed_rows, key_three, preferred_element_type=jnp.float32
        ).astype(jnp.bfloat16)
        value_part = jnp.einsum(
            "td,dhe->the", normed_rows, value_three, preferred_element_type=jnp.float32
        ).astype(jnp.bfloat16)
        return (queries, jnp.concatenate([key_part, value_part], axis=-1))

    def blank_projection(unused_input):
        blank_queries = jnp.zeros((tok_rows, HEADS * HD), jnp.bfloat16)
        blank_pairs = jnp.zeros((tok_rows, KVH, 2 * HD), jnp.bfloat16)
        return (blank_queries, blank_pairs)

    def run_tick(tick_id, carry):
        from_prior, kv_cache, outputs = carry
        block_id = tick_id - section_index
        active_tick = (block_id >= 0) & (block_id < micro_count)
        span_slot = jnp.clip(block_id, 0, micro_count - 1)
        first_input = lax.dynamic_index_in_dim(inputs, span_slot, 0, keepdims=False)
        layer_input = jnp.where(section_index == 0, first_input, from_prior)
        queries, key_value = lax.cond(active_tick, project, blank_projection, layer_input)
        key_value_heads = jnp.repeat(key_value, share_count, axis=1)
        packed_heads = jnp.concatenate(
            [queries.reshape(tok_rows, HEADS, HD), key_value_heads], axis=-1
        )
        packed_heads = packed_heads.reshape(tok_rows, HEADS * 3 * HD)
        arrived_heads = lax.all_to_all(
            packed_heads, "seq", split_axis=1, concat_axis=0, tiled=True
        ).reshape(span_rows, heads_dev, 3 * HD)
        local_query = arrived_heads[:, :, :HD]
        local_pair = arrived_heads[:, 0, HD:]
        kv_cache = jnp.where(
            active_tick,
            lax.dynamic_update_index_in_dim(kv_cache, local_pair, span_slot, 0),
            kv_cache,
        )

        def attend(key_block_id, online_state):
            running_peak, running_total, running_sum = online_state
            pair_block = lax.dynamic_index_in_dim(kv_cache, key_block_id, 0, keepdims=False)
            key_block = pair_block[:, :HD]
            value_block = pair_block[:, HD:]
            scores = (
                jnp.einsum(
                    "qhe,ke->qhk", local_query, key_block, preferred_element_type=jnp.float32
                )
                * score_scale
            )
            visible = (query_pos[None, None, :] <= query_pos[:, None, None]) | (
                key_block_id < span_slot
            )
            scores = jnp.where(visible, scores, jnp.float32(-1e30))
            new_peak = jnp.maximum(running_peak, jnp.max(scores, axis=-1))
            rescale = jnp.exp(running_peak - new_peak)
            soft_weights = jnp.exp(scores - new_peak[..., None])
            running_total = running_total * rescale + jnp.sum(soft_weights, axis=-1)
            block_sum = jnp.einsum(
                "qhk,ke->qhe",
                soft_weights.astype(jnp.bfloat16),
                value_block,
                preferred_element_type=jnp.float32,
            )
            running_sum = running_sum * rescale[..., None] + block_sum
            return (new_peak, running_total, running_sum)

        start_state = (
            jnp.full((span_rows, heads_dev), -1e30, jnp.float32),
            jnp.zeros((span_rows, heads_dev), jnp.float32),
            jnp.zeros((span_rows, heads_dev, HD), jnp.float32),
        )
        block_count = jnp.where(active_tick, span_slot + 1, 0)
        final_peak, final_total, final_sum = lax.fori_loop(0, block_count, attend, start_state)
        safe_total = jnp.where(active_tick, final_total, 1.0)
        attended = (
            (final_sum / safe_total[..., None])
            .astype(jnp.bfloat16)
            .reshape(span_rows, heads_dev * HD)
        )
        returned = lax.all_to_all(attended, "seq", split_axis=0, concat_axis=1, tiled=True)

        def apply_output(operands):
            head_rows, residual_rows = operands
            update = jnp.dot(head_rows, out_weight, preferred_element_type=jnp.float32)
            return (residual_rows.astype(jnp.float32) + update).astype(jnp.bfloat16)

        def blank_output(operands):
            return jnp.zeros_like(operands[1])

        layer_output = lax.cond(active_tick, apply_output, blank_output, (returned, layer_input))
        outputs = jnp.where(
            active_tick,
            lax.dynamic_update_index_in_dim(outputs, layer_output, span_slot, 0),
            outputs,
        )
        from_prior = passed_along(layer_output, "section", 1)
        return (from_prior, kv_cache, outputs)

    start_carry = (
        jnp.zeros((tok_rows, model_width), jnp.bfloat16),
        jnp.zeros((micro_count, span_rows, 2 * HD), jnp.bfloat16),
        jnp.zeros((micro_count, tok_rows, model_width), jnp.bfloat16),
    )
    final_prior, final_cache, outputs = lax.fori_loop(
        0, micro_count + section_count - 1, run_tick, start_carry
    )
    return outputs[None]


def solution(mesh):
    in_specs = (
        P(None, "seq", None),
        P("section", None),
        P("section", "seq", None),
        P("section", "seq", None),
        P("section", "seq", None),
        P("section", "seq", None),
    )
    out_specs = P("section", None, "seq", None)
    return jax.shard_map(local, mesh=mesh, in_specs=in_specs, out_specs=out_specs, check_vma=False)
```

profile of v0, /device:TPU:25, one launch (start us, length us, event | category | flops | bytes accessed | tf_op | source)
XLA Modules:
  0.0 1159.9 jit_solution(6882985113320136533)
XLA Ops:
  10.0 76.6 %all-gather.5.cloned.1.call-done = bf16[1,2048,512]{2,1,0:T(8,128)(2,1)} async-done(((bf16[1,64,512]{2,1,0:T(8,128)(2,1)}), bf16[1,2048,512]{2,1,0:T(8,128)(2,1)}) %all-gather.5.cloned.1.call-update) | async-done | bytes 2097168 | tf_op jit(solution)/shard_map/all_gather | solution.py:23
  86.7 4.0 copy.26
  90.6 73.8 %all-gather.7.cloned.1.call-done = bf16[1,2048,512]{2,1,0:T(8,128)(2,1)} async-done(((bf16[1,64,512]{2,1,0:T(8,128)(2,1)}), bf16[1,2048,512]{2,1,0:T(8,128)(2,1)}) %all-gather.7.cloned.1.call-update) | async-done | bytes 2097168 | tf_op jit(solution)/shard_map/all_gather | solution.py:24
  164.4 3.9 copy.27
  168.3 97.7 %all-gather.9.cloned.1.call-done = bf16[1,2048,2048]{2,1,0:T(8,128)(2,1)} async-done(((bf16[1,64,2048]{2,1,0:T(8,128)(2,1)}), bf16[1,2048,2048]{2,1,0:T(8,128)(2,1)}) %all-gather.9.cloned.1.call-update) | async-done | bytes 8388624 | tf_op jit(solution)/shard_map/all_gather | solution.py:22
  266.0 97.9 %all-gather.11.cloned.1.call-done = bf16[1,2048,2048]{2,1,0:T(8,128)(2,1)} async-done(((bf16[1,64,2048]{2,1,0:T(8,128)(2,1)}), bf16[1,2048,2048]{2,1,0:T(8,128)(2,1)}) %all-gather.11.cloned.1.call-update) | async-done | bytes 8388624 | tf_op jit(solution)/shard_map/all_gather | solution.py:25
  364.2 788.4 %while.55 = (s32[]{:T(128)}, bf16[48,2048]{1,0:T(8,128)(2,1)S(1)}, bf16[3,1536,128]{2,1,0:T(8,128)(2,1)S(1)}, bf16[3,48,2048]{2,1,0:T(8,128)(2,1)S(1)}, s32[]{:T...) while((s32[]{:T(128)}, bf16[48,2048]{1,0:T(8,128)(2,1)S(1)}, ...), condition=%wide.region_10.11_spmd.clone, body=%wide.region_0.10_spmd.clone.sunk | while | flops 1635932160 | bytes 66375560 | solution.py:153
  366.6 5.4 all-to-all-start
  372.0 21.0 %all-to-all-done = bf16[48,32,192]{2,0,1:T(8,128)(2,1)S(1)} async-done(((bf16[48,32,192]{2,0,1:T(8,128)(2,1)}), bf16[48,32,192]{2,0,1:T(8,128)(2,1)S(1)}, u32[]{:S(2)}, u32[]{:S(2)}) %all-to-all-start) | async-done | bytes 589856 | tf_op jit(solution)/shard_map/while/body/eval_jaxpr/all_to_all | solution.py:77
  394.8 5.9 all-to-all-start.1
  400.7 9.9 all-to-all-done.1
  412.9 5.1 collective-permute-done
  420.3 3.9 all-to-all-start
  424.2 17.9 %all-to-all-done = bf16[48,32,192]{2,0,1:T(8,128)(2,1)S(1)} async-done(((bf16[48,32,192]{2,0,1:T(8,128)(2,1)}), bf16[48,32,192]{2,0,1:T(8,128)(2,1)S(1)}, u32[]{:S(2)}, u32[]{:S(2)}) %all-to-all-start) | async-done | bytes 589856 | tf_op jit(solution)/shard_map/while/body/eval_jaxpr/all_to_all | solution.py:77
  444.0 6.8 all-to-all-start.1
  450.8 9.9 all-to-all-done.1
  463.1 7.0 collective-permute-done
  472.4 3.9 all-to-all-start
  476.4 17.9 %all-to-all-done = bf16[48,32,192]{2,0,1:T(8,128)(2,1)S(1)} async-done(((bf16[48,32,192]{2,0,1:T(8,128)(2,1)}), bf16[48,32,192]{2,0,1:T(8,128)(2,1)S(1)}, u32[]{:S(2)}, u32[]{:S(2)}) %all-to-all-start) | async-done | bytes 589856 | tf_op jit(solution)/shard_map/while/body/eval_jaxpr/all_to_all | solution.py:77
  496.1 6.8 all-to-all-start.1
  503.0 9.9 all-to-all-done.1
  515.2 7.0 collective-permute-done
  528.5 17.9 %all-to-all-done = bf16[48,32,192]{2,0,1:T(8,128)(2,1)S(1)} async-done(((bf16[48,32,192]{2,0,1:T(8,128)(2,1)}), bf16[48,32,192]{2,0,1:T(8,128)(2,1)S(1)}, u32[]{:S(2)}, u32[]{:S(2)}) %all-to-all-start) | async-done | bytes 589856 | tf_op jit(solution)/shard_map/while/body/eval_jaxpr/all_to_all | solution.py:77
  548.2 6.8 all-to-all-start.1
  555.1 9.9 all-to-all-done.1
  567.3 7.0 collective-permute-done
  580.6 17.9 %all-to-all-done = bf16[48,32,192]{2,0,1:T(8,128)(2,1)S(1)} async-done(((bf16[48,32,192]{2,0,1:T(8,128)(2,1)}), bf16[48,32,192]{2,0,1:T(8,128)(2,1)S(1)}, u32[]{:S(2)}, u32[]{:S(2)}) %all-to-all-start) | async-done | bytes 589856 | tf_op jit(solution)/shard_map/while/body/eval_jaxpr/all_to_all | solution.py:77
  600.3 6.8 all-to-all-start.1
  607.2 9.9 all-to-all-done.1
  619.4 7.0 collective-permute-done
  632.7 17.9 %all-to-all-done = bf16[48,32,192]{2,0,1:T(8,128)(2,1)S(1)} async-done(((bf16[48,32,192]{2,0,1:T(8,128)(2,1)}), bf16[48,32,192]{2,0,1:T(8,128)(2,1)S(1)}, u32[]{:S(2)}, u32[]{:S(2)}) %all-to-all-start) | async-done | bytes 589856 | tf_op jit(solution)/shard_map/while/body/eval_jaxpr/all_to_all | solution.py:77
  652.5 6.8 all-to-all-start.1
  659.3 9.9 all-to-all-done.1
  671.6 7.0 collective-permute-done
  684.9 15.2 %all-to-all-done = bf16[48,32,192]{2,0,1:T(8,128)(2,1)S(1)} async-done(((bf16[48,32,192]{2,0,1:T(8,128)(2,1)}), bf16[48,32,192]{2,0,1:T(8,128)(2,1)S(1)}, u32[]{:S(2)}, u32[]{:S(2)}) %all-to-all-start) | async-done | bytes 589856 | tf_op jit(solution)/shard_map/while/body/eval_jaxpr/all_to_all | solution.py:77
  701.9 4.3 all-to-all-start.1
  706.2 9.9 all-to-all-done.1
  718.5 128.6 %collective-permute-done = bf16[48,2048]{1,0:T(8,128)(2,1)S(1)} collective-permute-done((bf16[48,2048]{1,0:T(8,128)(2,1)}, bf16[48,2048]{1,0:T(8,128)(2,1)S(1)}, u32[]{:S(2)}, u32[]{:S(2)}) %collective-permute-start) | collective-permute-done | bytes 196640 | tf_op jit(solution)/shard_map/while/body/eval_jaxpr/ppermute | solution.py:17
  848.0 11.3 conditional.6
  853.7 5.0 convolution_convert_fusion
  864.5 15.2 %all-to-all-done = bf16[48,32,192]{2,0,1:T(8,128)(2,1)S(1)} async-done(((bf16[48,32,192]{2,0,1:T(8,128)(2,1)}), bf16[48,32,192]{2,0,1:T(8,128)(2,1)S(1)}, u32[]{:S(2)}, u32[]{:S(2)}) %all-to-all-start) | async-done | bytes 589856 | tf_op jit(solution)/shard_map/while/body/eval_jaxpr/all_to_all | solution.py:77
  880.3 5.5 while.56
  887.1 4.3 all-to-all-start.1
  891.4 9.9 all-to-all-done.1
  901.5 7.1 conditional.7
  902.0 5.6 fusion.10
  910.0 50.4 %collective-permute-done = bf16[48,2048]{1,0:T(8,128)(2,1)S(1)} collective-permute-done((bf16[48,2048]{1,0:T(8,128)(2,1)}, bf16[48,2048]{1,0:T(8,128)(2,1)S(1)}, u32[]{:S(2)}, u32[]{:S(2)}) %collective-permute-start) | collective-permute-done | bytes 196640 | tf_op jit(solution)/shard_map/while/body/eval_jaxpr/ppermute | solution.py:17
  961.3 11.3 conditional.6
  967.1 5.0 convolution_convert_fusion
  977.8 15.2 %all-to-all-done = bf16[48,32,192]{2,0,1:T(8,128)(2,1)S(1)} async-done(((bf16[48,32,192]{2,0,1:T(8,128)(2,1)}), bf16[48,32,192]{2,0,1:T(8,128)(2,1)S(1)}, u32[]{:S(2)}, u32[]{:S(2)}) %all-to-all-start) | async-done | bytes 589856 | tf_op jit(solution)/shard_map/while/body/eval_jaxpr/all_to_all | solution.py:77
  993.6 11.1 while.56
  1006.0 4.3 all-to-all-start.1
  1010.3 10.0 all-to-all-done.1
  1020.5 7.1 conditional.7
  1021.0 5.6 fusion.10
  1028.9 45.6 %collective-permute-done = bf16[48,2048]{1,0:T(8,128)(2,1)S(1)} collective-permute-done((bf16[48,2048]{1,0:T(8,128)(2,1)}, bf16[48,2048]{1,0:T(8,128)(2,1)S(1)}, u32[]{:S(2)}, u32[]{:S(2)}) %collective-permute-start) | collective-permute-done | bytes 196640 | tf_op jit(solution)/shard_map/while/body/eval_jaxpr/ppermute | solution.py:17
  1075.5 11.3 conditional.6
  1081.2 5.0 convolution_convert_fusion
  1092.0 16.6 %all-to-all-done = bf16[48,32,192]{2,0,1:T(8,128)(2,1)S(1)} async-done(((bf16[48,32,192]{2,0,1:T(8,128)(2,1)}), bf16[48,32,192]{2,0,1:T(8,128)(2,1)S(1)}, u32[]{:S(2)}, u32[]{:S(2)}) %all-to-all-start) | async-done | bytes 589856 | tf_op jit(solution)/shard_map/while/body/eval_jaxpr/all_to_all | solution.py:77
  1109.2 16.6 %while.56 = (s32[]{:T(128)}, f32[1536,1]{0,1:T(1,128)S(1)}, f32[1536,1]{0,1:T(1,128)S(1)}, f32[1536,1,64]{0,2,1:T(8,128)S(1)}, s32[]{:T(128)}, /*index=5*/s32[15...) while((s32[]{:T(128)}, f32[1536,1]{0,1:T(1,128)S(1)}, ...), condition=%wide.region_7.7_spmd, body=%wide.region_4.6_spmd.sunk | while | flops 625414656 | bytes 30988460 | solution.py:122
  1127.1 4.8 all-to-all-start.1
  1131.8 9.9 all-to-all-done.1
  1142.0 7.1 conditional.7
  1142.5 5.6 fusion.10
  (313 shorter events, 157.0 us)
Async XLA Ops:
  6.5 80.1 %all-gather.5.cloned.1.call-start = ((), (), s32[]{:S(2)}) async-start(), calls=%async_computation.2 | async-start | bytes 2162688 | tf_op jit(solution)/shard_map/all_gather | solution.py:23
  7.3 157.1 %all-gather.7.cloned.1.call-start = ((), (), s32[]{:S(2)}) async-start(), calls=%async_computation.3 | async-start | bytes 2162688 | tf_op jit(solution)/shard_map/all_gather | solution.py:24
  8.0 258.0 %all-gather.9.cloned.1.call-start = ((), (), s32[]{:S(2)}) async-start(), calls=%async_computation.4 | async-start | bytes 8650752 | tf_op jit(solution)/shard_map/all_gather | solution.py:22
  8.7 355.2 %all-gather.11.cloned.1.call-start = ((), (), s32[]{:S(2)}) async-start(), calls=%async_computation.5 | async-start | bytes 8650752 | tf_op jit(solution)/shard_map/all_gather | solution.py:25
  366.6 26.4 %all-to-all-start = ((bf16[48,32,192]{2,0,1:T(8,128)(2,1)}), bf16[48,32,192]{2,0,1:T(8,128)(2,1)S(1)}, u32[]{:S(2)}, u32[]{:S(2)}) async-start(bf16[48,32,192]{2,0,1:T(8,128)(2,1)} %pad_maximum_fusion.3), calls=%async_computation | async-start | bytes 1572864 | tf_op jit(solution)/shard_map/while/body/eval_jaxpr/all_to_all | solution.py:77
  394.8 15.7 %all-to-all-start.1 = ((bf16[32,2,1536]{2,1,0:T(2,128)(2,1)}), bf16[32,2,1536]{2,1,0:T(2,128)(2,1)S(1)}, u32[]{:S(2)}, u32[]{:S(2)}) async-start(bf16[32,2,1536]{2,1,0:T(2,128)(2,1)} %reshape.103), calls=%async_computation.1 | async-start | bytes 393216 | tf_op jit(solution)/shard_map/while/body/eval_jaxpr/all_to_all | solution.py:129
  411.5 6.4 collective-permute-start
  420.3 21.8 %all-to-all-start = ((bf16[48,32,192]{2,0,1:T(8,128)(2,1)}), bf16[48,32,192]{2,0,1:T(8,128)(2,1)S(1)}, u32[]{:S(2)}, u32[]{:S(2)}) async-start(bf16[48,32,192]{2,0,1:T(8,128)(2,1)} %pad_maximum_fusion.3), calls=%async_computation | async-start | bytes 1572864 | tf_op jit(solution)/shard_map/while/body/eval_jaxpr/all_to_all | solution.py:77
  444.0 16.7 %all-to-all-start.1 = ((bf16[32,2,1536]{2,1,0:T(2,128)(2,1)}), bf16[32,2,1536]{2,1,0:T(2,128)(2,1)S(1)}, u32[]{:S(2)}, u32[]{:S(2)}) async-start(bf16[32,2,1536]{2,1,0:T(2,128)(2,1)} %reshape.103), calls=%async_computation.1 | async-start | bytes 393216 | tf_op jit(solution)/shard_map/while/body/eval_jaxpr/all_to_all | solution.py:129
  461.7 8.4 collective-permute-start
  472.4 21.8 %all-to-all-start = ((bf16[48,32,192]{2,0,1:T(8,128)(2,1)}), bf16[48,32,192]{2,0,1:T(8,128)(2,1)S(1)}, u32[]{:S(2)}, u32[]{:S(2)}) async-start(bf16[48,32,192]{2,0,1:T(8,128)(2,1)} %pad_maximum_fusion.3), calls=%async_computation | async-start | bytes 1572864 | tf_op jit(solution)/shard_map/while/body/eval_jaxpr/all_to_all | solution.py:77
  496.1 16.7 %all-to-all-start.1 = ((bf16[32,2,1536]{2,1,0:T(2,128)(2,1)}), bf16[32,2,1536]{2,1,0:T(2,128)(2,1)S(1)}, u32[]{:S(2)}, u32[]{:S(2)}) async-start(bf16[32,2,1536]{2,1,0:T(2,128)(2,1)} %reshape.103), calls=%async_computation.1 | async-start | bytes 393216 | tf_op jit(solution)/shard_map/while/body/eval_jaxpr/all_to_all | solution.py:129
  513.8 8.4 collective-permute-start
  524.6 21.8 %all-to-all-start = ((bf16[48,32,192]{2,0,1:T(8,128)(2,1)}), bf16[48,32,192]{2,0,1:T(8,128)(2,1)S(1)}, u32[]{:S(2)}, u32[]{:S(2)}) async-start(bf16[48,32,192]{2,0,1:T(8,128)(2,1)} %pad_maximum_fusion.3), calls=%async_computation | async-start | bytes 1572864 | tf_op jit(solution)/shard_map/while/body/eval_jaxpr/all_to_all | solution.py:77
  548.2 16.7 %all-to-all-start.1 = ((bf16[32,2,1536]{2,1,0:T(2,128)(2,1)}), bf16[32,2,1536]{2,1,0:T(2,128)(2,1)S(1)}, u32[]{:S(2)}, u32[]{:S(2)}) async-start(bf16[32,2,1536]{2,1,0:T(2,128)(2,1)} %reshape.103), calls=%async_computation.1 | async-start | bytes 393216 | tf_op jit(solution)/shard_map/while/body/eval_jaxpr/all_to_all | solution.py:129
  566.0 8.4 collective-permute-start
  576.7 21.8 %all-to-all-start = ((bf16[48,32,192]{2,0,1:T(8,128)(2,1)}), bf16[48,32,192]{2,0,1:T(8,128)(2,1)S(1)}, u32[]{:S(2)}, u32[]{:S(2)}) async-start(bf16[48,32,192]{2,0,1:T(8,128)(2,1)} %pad_maximum_fusion.3), calls=%async_computation | async-start | bytes 1572864 | tf_op jit(solution)/shard_map/while/body/eval_jaxpr/all_to_all | solution.py:77
  600.3 16.7 %all-to-all-start.1 = ((bf16[32,2,1536]{2,1,0:T(2,128)(2,1)}), bf16[32,2,1536]{2,1,0:T(2,128)(2,1)S(1)}, u32[]{:S(2)}, u32[]{:S(2)}) async-start(bf16[32,2,1536]{2,1,0:T(2,128)(2,1)} %reshape.103), calls=%async_computation.1 | async-start | bytes 393216 | tf_op jit(solution)/shard_map/while/body/eval_jaxpr/all_to_all | solution.py:129
  618.1 8.4 collective-permute-start
  628.8 21.8 %all-to-all-start = ((bf16[48,32,192]{2,0,1:T(8,128)(2,1)}), bf16[48,32,192]{2,0,1:T(8,128)(2,1)S(1)}, u32[]{:S(2)}, u32[]{:S(2)}) async-start(bf16[48,32,192]{2,0,1:T(8,128)(2,1)} %pad_maximum_fusion.3), calls=%async_computation | async-start | bytes 1572864 | tf_op jit(solution)/shard_map/while/body/eval_jaxpr/all_to_all | solution.py:77
  652.5 16.7 %all-to-all-start.1 = ((bf16[32,2,1536]{2,1,0:T(2,128)(2,1)}), bf16[32,2,1536]{2,1,0:T(2,128)(2,1)S(1)}, u32[]{:S(2)}, u32[]{:S(2)}) async-start(bf16[32,2,1536]{2,1,0:T(2,128)(2,1)} %reshape.103), calls=%async_computation.1 | async-start | bytes 393216 | tf_op jit(solution)/shard_map/while/body/eval_jaxpr/all_to_all | solution.py:129
  670.2 8.4 collective-permute-start
  680.9 19.2 %all-to-all-start = ((bf16[48,32,192]{2,0,1:T(8,128)(2,1)}), bf16[48,32,192]{2,0,1:T(8,128)(2,1)S(1)}, u32[]{:S(2)}, u32[]{:S(2)}) async-start(bf16[48,32,192]{2,0,1:T(8,128)(2,1)} %pad_maximum_fusion.3), calls=%async_computation | async-start | bytes 1572864 | tf_op jit(solution)/shard_map/while/body/eval_jaxpr/all_to_all | solution.py:77
  701.9 14.2 %all-to-all-start.1 = ((bf16[32,2,1536]{2,1,0:T(2,128)(2,1)}), bf16[32,2,1536]{2,1,0:T(2,128)(2,1)S(1)}, u32[]{:S(2)}, u32[]{:S(2)}) async-start(bf16[32,2,1536]{2,1,0:T(2,128)(2,1)} %reshape.103), calls=%async_computation.1 | async-start | bytes 393216 | tf_op jit(solution)/shard_map/while/body/eval_jaxpr/all_to_all | solution.py:129
  717.1 129.9 %collective-permute-start = (bf16[48,2048]{1,0:T(8,128)(2,1)}, bf16[48,2048]{1,0:T(8,128)(2,1)S(1)}, u32[]{:S(2)}, u32[]{:S(2)}) collective-permute-start(bf16[48,2048]{1,0:T(8,128)(2,1)} %get-tuple-element.622), channel_id=1, source_target_pairs={{0,32},{32,64},{64,96},{96,128},{128,160},{160,192},{192,224},{1,3... | collective-permute-start | bytes 589832 | tf_op jit(solution)/shard_map/while/body/eval_jaxpr/ppermute | solution.py:17
  860.6 19.2 %all-to-all-start = ((bf16[48,32,192]{2,0,1:T(8,128)(2,1)}), bf16[48,32,192]{2,0,1:T(8,128)(2,1)S(1)}, u32[]{:S(2)}, u32[]{:S(2)}) async-start(bf16[48,32,192]{2,0,1:T(8,128)(2,1)} %pad_maximum_fusion.3), calls=%async_computation | async-start | bytes 1572864 | tf_op jit(solution)/shard_map/while/body/eval_jaxpr/all_to_all | solution.py:77
  887.1 14.2 %all-to-all-start.1 = ((bf16[32,2,1536]{2,1,0:T(2,128)(2,1)}), bf16[32,2,1536]{2,1,0:T(2,128)(2,1)S(1)}, u32[]{:S(2)}, u32[]{:S(2)}) async-start(bf16[32,2,1536]{2,1,0:T(2,128)(2,1)} %reshape.103), calls=%async_computation.1 | async-start | bytes 393216 | tf_op jit(solution)/shard_map/while/body/eval_jaxpr/all_to_all | solution.py:129
  908.6 51.7 %collective-permute-start = (bf16[48,2048]{1,0:T(8,128)(2,1)}, bf16[48,2048]{1,0:T(8,128)(2,1)S(1)}, u32[]{:S(2)}, u32[]{:S(2)}) collective-permute-start(bf16[48,2048]{1,0:T(8,128)(2,1)} %get-tuple-element.622), channel_id=1, source_target_pairs={{0,32},{32,64},{64,96},{96,128},{128,160},{160,192},{192,224},{1,3... | collective-permute-start | bytes 589832 | tf_op jit(solution)/shard_map/while/body/eval_jaxpr/ppermute | solution.py:17
  973.9 19.2 %all-to-all-start = ((bf16[48,32,192]{2,0,1:T(8,128)(2,1)}), bf16[48,32,192]{2,0,1:T(8,128)(2,1)S(1)}, u32[]{:S(2)}, u32[]{:S(2)}) async-start(bf16[48,32,192]{2,0,1:T(8,128)(2,1)} %pad_maximum_fusion.3), calls=%async_computation | async-start | bytes 1572864 | tf_op jit(solution)/shard_map/while/body/eval_jaxpr/all_to_all | solution.py:77
  1006.0 14.3 %all-to-all-start.1 = ((bf16[32,2,1536]{2,1,0:T(2,128)(2,1)}), bf16[32,2,1536]{2,1,0:T(2,128)(2,1)S(1)}, u32[]{:S(2)}, u32[]{:S(2)}) async-start(bf16[32,2,1536]{2,1,0:T(2,128)(2,1)} %reshape.103), calls=%async_computation.1 | async-start | bytes 393216 | tf_op jit(solution)/shard_map/while/body/eval_jaxpr/all_to_all | solution.py:129
  1027.6 46.9 %collective-permute-start = (bf16[48,2048]{1,0:T(8,128)(2,1)}, bf16[48,2048]{1,0:T(8,128)(2,1)S(1)}, u32[]{:S(2)}, u32[]{:S(2)}) collective-permute-start(bf16[48,2048]{1,0:T(8,128)(2,1)} %get-tuple-element.622), channel_id=1, source_target_pairs={{0,32},{32,64},{64,96},{96,128},{128,160},{160,192},{192,224},{1,3... | collective-permute-start | bytes 589832 | tf_op jit(solution)/shard_map/while/body/eval_jaxpr/ppermute | solution.py:17
  1088.1 20.6 %all-to-all-start = ((bf16[48,32,192]{2,0,1:T(8,128)(2,1)}), bf16[48,32,192]{2,0,1:T(8,128)(2,1)S(1)}, u32[]{:S(2)}, u32[]{:S(2)}) async-start(bf16[48,32,192]{2,0,1:T(8,128)(2,1)} %pad_maximum_fusion.3), calls=%async_computation | async-start | bytes 1572864 | tf_op jit(solution)/shard_map/while/body/eval_jaxpr/all_to_all | solution.py:77
  1127.1 14.6 %all-to-all-start.1 = ((bf16[32,2,1536]{2,1,0:T(2,128)(2,1)}), bf16[32,2,1536]{2,1,0:T(2,128)(2,1)S(1)}, u32[]{:S(2)}, u32[]{:S(2)}) async-start(bf16[32,2,1536]{2,1,0:T(2,128)(2,1)} %reshape.103), calls=%async_computation.1 | async-start | bytes 393216 | tf_op jit(solution)/shard_map/while/body/eval_jaxpr/all_to_all | solution.py:129
  1149.1 3.5 collective-permute-start
  1152.6 0.8 copy-start
Sparse Core Ops, SparseCore 0:
  9.9 76.6 all-gather.4
  89.2 75.1 all-gather.6
  167.0 99.0 all-gather.8
  268.5 95.4 all-gather.10
where the time goes:
time: 1160 us
  waiting for transfers between devices  887 us (76%)
  starting transfers between devices  111 us (10%)
  matrix products  72.6 us (6%)
  local copies, waits for them, and re-layouts  37.5 us (3%)
  other arithmetic  35.7 us (3%)
  between operations  13.2 us (1%)
    ppermute x10, waiting for transfers between devices, passed_along(): return lax.ppermute(block, axis, route)  267 us
    all_to_all x10, waiting for transfers between devices, run_tick(): lax.all_to_all(packed_heads, 'seq', split_axis=1, concat_axis=0, tiled=True)  173 us
    all_to_all x10, waiting for transfers between devices, run_tick(): lax.all_to_all(attended, 'seq', split_axis=0, concat_axis=1, tiled=True)  98.8 us
    all_gather x1, waiting for transfers between devices, local(): lax.all_gather(w_out, 'seq', axis=1, tiled=True)  97.9 us
    all_gather x1, waiting for transfers between devices, local(): lax.all_gather(w_query, 'seq', axis=1, tiled=True)  97.7 us
    all_gather x1, waiting for transfers between devices, local(): lax.all_gather(w_key, 'seq', axis=1, tiled=True)  76.6 us
    all_gather x1, waiting for transfers between devices, local(): lax.all_gather(w_value, 'seq', axis=1, tiled=True)  73.8 us
    all_to_all x10, starting transfers between devices, run_tick(): lax.all_to_all(attended, 'seq', split_axis=0, concat_axis=1, tiled=True)  57.8 us
  transfers between devices with their start and end apart: 34, of which 34 were waited for; matrix products, arithmetic and copies ran while one was open for 1% of the time, Pallas kernels for 0%

commit v1 on v0

v1 whole, which is shorter than its diff:
```python
import functools

import jax
import jax.numpy as jnp
from jax import lax
from jax.experimental import pallas as pl
from jax.experimental.pallas import tpu as pltpu
from jax.sharding import PartitionSpec as P

HEADS = 32
KVH = 8
HD = 64
SHARE = HEADS // KVH
QW = SHARE * HD
EPS = 1e-05
NEG = -1e30

ZN = 8
XN = 4
SN = 8
F32 = jnp.float32
BF16 = jnp.bfloat16


def seq_pairs(mask):
    return [(i, i ^ mask) for i in range(ZN * XN)]


def section_pairs(mask):
    return [(i, i ^ mask) for i in range(SN)]


def along_z():
    return [[z * XN + x for z in range(ZN)] for x in range(XN)]


def spread(piece):
    near = [piece] + [lax.ppermute(piece, "section", section_pairs(2 * d)) for d in (1, 2, 3)]
    other = lax.ppermute(jnp.stack(near), "section", section_pairs(1))
    return near + [other]


def in_order(refs):
    out = [(2 * d, refs[d][...]) for d in range(4)]
    out += [(2 * d + 1, refs[4][d]) for d in range(4)]
    return out


def project_kernel(me_ref, gain_ref, p0, p1, p2, p3, p4, wq_ref, wkv_ref, q_ref, kv_ref):
    me = me_ref[0]
    pieces = [(mask, value.astype(F32)) for mask, value in in_order([p0, p1, p2, p3, p4])]
    rows = pieces[0][1].shape[0]
    width = sum(value.shape[1] for _, value in pieces)
    squares = functools.reduce(jnp.add, [value * value for _, value in pieces])
    scale = lax.rsqrt(jnp.sum(squares, axis=-1, keepdims=True) / width + EPS)
    q_sum = jnp.zeros((rows, QW), F32)
    kv_sum = jnp.zeros((rows, 2 * HD), F32)
    for mask, value in pieces:
        owner = jnp.bitwise_xor(me, mask)
        gain = gain_ref[pl.ds(owner, 1), 0, :].astype(F32)
        normed = (value * scale * gain).astype(BF16)
        wq = wq_ref[pl.ds(4 * owner, 4), 0].reshape(QW, QW)
        wkv = wkv_ref[pl.ds(4 * owner, 4), 0].reshape(QW, 2 * HD)
        q_sum += jnp.dot(normed, wq, preferred_element_type=F32)
        kv_sum += jnp.dot(normed, wkv, preferred_element_type=F32)
    q_ref[...] = q_sum.astype(BF16)
    pair = kv_sum.astype(BF16)
    for i in range(kv_ref.shape[0]):
        kv_ref[i] = pair


def attend_kernel(seq_ref, q_ref, k0, k1, k2, k3, o_ref, *, blocks, tok):
    seq = seq_ref[0]
    x_me = jnp.bitwise_and(seq, XN - 1)
    keys = [k0, k1, k2, k3]
    span = ZN * tok
    rows = SHARE * tok
    q_all = q_ref[...]
    row_pos = lax.broadcasted_iota(jnp.int32, (rows, span), 0)
    row_pos = seq * tok + lax.rem(row_pos, tok)
    col = lax.broadcasted_iota(jnp.int32, (rows, span), 1)
    col_pos = lax.div(col, tok) * (XN * tok) + lax.rem(col, tok)
    slack = row_pos - col_pos
    factor = HD**-0.5
    for b in range(blocks):
        q_rows = q_all[b * tok : (b + 1) * tok]
        q_heads = jnp.concatenate([q_rows[:, h * HD : (h + 1) * HD] for h in range(SHARE)], axis=0)
        q_heads = jnp.concatenate([q_heads, jnp.zeros((rows, HD), BF16)], axis=1)
        scores = []
        for kb in range(b + 1):
            for d in range(XN):
                pair = keys[d][:, kb * tok : (kb + 1) * tok, :].reshape(span, 2 * HD)
                s = lax.dot_general(q_heads, pair, (((1,), (1,)), ((), ())), preferred_element_type=F32)
                if kb == b:
                    offset = jnp.bitwise_xor(x_me, d) * tok
                    s = jnp.where(slack >= offset, s, NEG)
                scores.append((kb, d, s))
        peak = functools.reduce(jnp.maximum, [s for _, _, s in scores])
        peak = jnp.max(peak, axis=-1, keepdims=True)
        total = jnp.zeros((rows, span), F32)
        summed = jnp.zeros((rows, 2 * HD), F32)
        for kb, d, s in scores:
            probs = jnp.exp((s - peak) * factor)
            total += probs
            pair = keys[d][:, kb * tok : (kb + 1) * tok, :].reshape(span, 2 * HD)
            summed += jnp.dot(probs.astype(BF16), pair, preferred_element_type=F32)
        total = jnp.sum(total, axis=-1, keepdims=True)
        result = (summed[:, HD:] / total).astype(BF16)
        o_ref[b * tok : (b + 1) * tok, :] = jnp.concatenate(
            [result[h * tok : (h + 1) * tok] for h in range(SHARE)], axis=1
        )


def output_kernel(me_ref, a0, a1, a2, a3, a4, h_ref, w_ref, o_ref):
    me = me_ref[0]
    total = h_ref[...].astype(F32)
    update = jnp.zeros(total.shape, F32)
    for mask, value in in_order([a0, a1, a2, a3, a4]):
        owner = jnp.bitwise_xor(me, mask)
        w = w_ref[pl.ds(4 * owner, 4), 0].reshape(QW, QW)
        update += jnp.dot(value, w, preferred_element_type=F32)
    o_ref[...] = (total + update).astype(BF16)


SMEM = pl.BlockSpec(memory_space=pltpu.SMEM)


def whole(shape):
    return pl.BlockSpec(shape, lambda i: (0,) * len(shape))


def call(kernel, out_shape, in_specs, flops, bytes_accessed, exps=0):
    if isinstance(out_shape, list):
        out_specs = [whole(o.shape) for o in out_shape]
    else:
        out_specs = whole(out_shape.shape)
    return pl.pallas_call(
        kernel,
        out_shape=out_shape,
        grid=(1,),
        in_specs=in_specs,
        out_specs=out_specs,
        compiler_params=pltpu.CompilerParams(vmem_limit_bytes=48 * 1024 * 1024),
        cost_estimate=pl.CostEstimate(flops=flops, bytes_accessed=bytes_accessed, transcendentals=exps),
    )


def local(inputs, norm_gain, w_query, w_key, w_value, w_out):
    blocks, tok, width = inputs.shape
    rows = blocks * tok
    me = lax.axis_index("section")
    seq = lax.axis_index("seq")
    me_s = me.reshape(1)
    seq_s = seq.reshape(1)
    layers = lax.axis_size("section")
    shard = w_query.shape[1]

    def cut(w):
        return w[0].reshape(shard, SN, -1).transpose(1, 0, 2)

    mine = jnp.concatenate([cut(w_query), cut(w_out), cut(w_key), cut(w_value)], axis=-1)
    by_layer = lax.all_to_all(mine, "section", split_axis=0, concat_axis=0, tiled=True)
    weights = lax.all_gather(by_layer, "seq", axis=0)
    gains = lax.all_gather(norm_gain, "section", axis=0, tiled=True).reshape(layers, SN, 1, QW)

    flat = inputs.reshape(rows, width)

    def input_piece(mask):
        return lax.dynamic_slice_in_dim(flat, jnp.bitwise_xor(me, mask) * QW, QW, 1)

    pieces = [input_piece(2 * d) for d in range(4)]
    pieces.append(jnp.stack([input_piece(2 * d + 1) for d in range(4)]))

    piece_specs = [whole((rows, QW))] * 4 + [whole((4, rows, QW))]
    kv_shape = (ZN, rows, 2 * HD)
    results = []
    for layer in range(layers):

        def weight_spec(width_, index, layer=layer):
            return pl.BlockSpec((ZN * XN, 1, shard, width_), lambda i: (0, layer, 0, index))

        with jax.named_scope("project"):
            q, kv = call(
                project_kernel,
                [
                    jax.ShapeDtypeStruct((rows, QW), BF16),
                    jax.ShapeDtypeStruct(kv_shape, BF16),
                ],
                [SMEM, whole((SN, 1, QW))] + piece_specs + [weight_spec(QW, 0), weight_spec(2 * HD, 4)],
                2 * rows * width * 384,
                2 * (width * 384 + rows * width),
            )(me_s, gains[layer], *pieces, weights, weights)
        with jax.named_scope("keys"):
            kv0 = lax.all_to_all(
                kv, "seq", split_axis=0, concat_axis=0, tiled=True, axis_index_groups=along_z()
            )
            kvs = [kv0] + [lax.ppermute(kv0, "seq", seq_pairs(d)) for d in (1, 2, 3)]
        with jax.named_scope("attend"):
            attended = call(
                functools.partial(attend_kernel, blocks=blocks, tok=tok),
                jax.ShapeDtypeStruct((rows, QW), BF16),
                [SMEM, whole((rows, QW))] + [whole(kv_shape)] * 4,
                4 * SHARE * tok * (ZN * XN * tok) * 128 * 6,
                4 * 2 * ZN * rows * 128,
                SHARE * tok * (ZN * XN * tok) * 6,
            )(seq_s, q, *kvs)
            heads = spread(attended)
        with jax.named_scope("output"):
            own = call(
                output_kernel,
                jax.ShapeDtypeStruct((rows, QW), BF16),
                [SMEM] + piece_specs + [whole((rows, QW)), weight_spec(QW, 1)],
                2 * rows * width * QW,
                2 * (width * QW + rows * width),
            )(me_s, *heads, pieces[0], weights)
            pieces = spread(own)
        results.append(pieces)

    def pick(layer):
        def branch(all_pieces):
            near, other = all_pieces[layer][:4], all_pieces[layer][4]
            parts = []
            for s in range(SN):
                mask = s ^ layer
                parts.append(other[mask // 2] if mask % 2 else near[mask // 2])
            return jnp.concatenate(parts, axis=1)

        return branch

    chosen = lax.switch(me, [pick(layer) for layer in range(layers)], results)
    return chosen.reshape(1, blocks, tok, width)


def solution(mesh):
    in_specs = (
        P(None, "seq", None),
        P("section", None),
        P("section", "seq", None),
        P("section", "seq", None),
        P("section", "seq", None),
        P("section", "seq", None),
    )
    out_specs = P("section", None, "seq", None)
    return jax.shard_map(local, mesh=mesh, in_specs=in_specs, out_specs=out_specs, check_vma=False)
```

time: 1160 us -> 713 us (0.61)
  the two profiles are of different devices: /device:TPU:25 before, /device:TPU:1 now
where the time goes in v1:
time: 713 us; the launch traced here: 702 us
  waiting for transfers between devices  328 us (46%)
  blocking collectives  151 us (21%)
  starting transfers between devices  141 us (20%)
  Pallas kernels  57.3 us (8%)
  between operations  14.4 us (2%)
  local copies, waits for them, and re-layouts  9.36 us (1%)
    all_gather x1, waiting for transfers between devices, local(): weights = lax.all_gather(by_layer, 'seq', axis=0)  148 us
    all_to_all x8, blocking collectives, local(): lax.all_to_all(kv, 'seq', split_axis=0, concat_axis=0, tiled=True, axis_i...  120 us
    ppermute x24, waiting for transfers between devices, local(): kvs = [kv0] + [lax.ppermute(kv0, 'seq', seq_pairs(d)) for d in (1, 2, 3)]  106 us
    ppermute x48, starting transfers between devices, spread(): lax.ppermute(piece, 'section', section_pairs(2 * d))  62.6 us
    ppermute x48, waiting for transfers between devices, spread(): lax.ppermute(piece, 'section', section_pairs(2 * d))  53.9 us
    ppermute x16, starting transfers between devices, spread(): other = lax.ppermute(jnp.stack(near), 'section', section_pairs(1))  46.6 us
    ppermute x24, starting transfers between devices, local(): kvs = [kv0] + [lax.ppermute(kv0, 'seq', seq_pairs(d)) for d in (1, 2, 3)]  32.2 us
    pallas_call x8, Pallas kernels, local(): call(functools.partial(attend_kernel, blocks=blocks, tok=tok), jax.ShapeD...  28.3 us
  transfers between devices with their start and end apart: 89, of which 73 were waited for; matrix products, arithmetic and copies ran while one was open for 0% of the time, Pallas kernels for 0%

profile of v1, /device:TPU:1, one launch (start us, length us, event | category | flops | bytes accessed | tf_op | source)
XLA Modules:
  0.0 702.1 jit_solution(18299695928926692870)
XLA Ops:
  10.7 17.4 %all_to_all.45 = bf16[8,64,640]{2,1,0:T(8,128)(2,1)} all-to-all(bf16[8,64,640]{2,1,0:T(8,128)(2,1)S(1)} %copy.20), channel_id=1, replica_groups=mesh['section'=8,'seq'=32] {'section'}, dimensions={0} | all-to-all | bytes 1310720 | tf_op jit(solution)/shard_map/all_to_all | solution.py:162
  28.2 13.4 %all-gather.1 = bf16[8,1,2048]{2,1,0:T(2,128)(2,1)S(1)} all-gather(bf16[1,1,2048]{2,1,0:T(2,128)(2,1)S(1)} %bitcast.328), channel_id=1, replica_groups=mesh['section'=8,'seq'=32] {'section'}, dimensions={0}, use_global_device_ids=true | all-gather | bytes 36864 | tf_op jit(solution)/shard_map/all_gather | solution.py:164
  41.9 148.1 %all-gather.4.cloned.1.call-done = bf16[256,64,640]{2,1,0:T(8,128)(2,1)} async-done(((bf16[8,64,640]{2,1,0:T(8,128)(2,1)}), bf16[256,64,640]{2,1,0:T(8,128)(2,1)}) %all-gather.4.cloned.1.call-update) | async-done | bytes 20971536 | tf_op jit(solution)/shard_map/all_gather | solution.py:163
  192.0 14.4 %all_to_all.46.k0 = bf16[8,144,128]{2,1,0:T(8,128)(2,1)S(1)} all-to-all(bf16[8,144,128]{2,1,0:T(8,128)(2,1)S(1)} %get-tuple-element.152), channel_id=1, replica_groups={{0,4,8,12,16,20,24,28},{1,5,9,13,17,21,25,29},{2,6,10,14,18,22,26,30},{..., dimensions={0} | all-to-all | bytes 589824 | tf_op jit(solution)/shard_map/keys/all_to_all | solution.py:194
  212.0 6.2 collective-permute-done.1.k2
  218.2 4.4 collective-permute-done.2.k3
  222.6 3.5 attend.8.a0
  227.4 2.4 collective-permute-start.4
  234.3 4.3 collective-permute-start.6
  242.9 2.5 collective-permute-start.9
  253.3 15.1 %all_to_all.47.k0 = bf16[8,144,128]{2,1,0:T(8,128)(2,1)S(1)} all-to-all(bf16[8,144,128]{2,1,0:T(8,128)(2,1)S(1)} %get-tuple-element.154), channel_id=1, replica_groups={{0,4,8,12,16,20,24,28},{1,5,9,13,17,21,25,29},{2,6,10,14,18,22,26,30},{..., dimensions={0} | all-to-all | bytes 589824 | tf_op jit(solution)/shard_map/keys/all_to_all | solution.py:194
  268.3 3.3 collective-permute-start.12
  272.2 3.3 collective-permute-done.11.k1
  275.5 8.2 %collective-permute-done.12.k2 = bf16[8,144,128]{2,1,0:T(8,128)(2,1)S(1)} collective-permute-done((bf16[8,144,128]{2,1,0:T(8,128)(2,1)S(1)}, bf16[8,144,128]{2,1,0:T(8,128)(2,1)S(1)}, u32[]{:S(2)}, u32[]{:S(2)}) %collective-permute-start.12) | collective-permute-done | bytes 294944 | tf_op jit(solution)/shard_map/keys/ppermute | solution.py:197
  286.1 3.6 attend.9.a0
  289.8 3.5 collective-permute-start.15
  297.8 4.3 collective-permute-start.17
  306.4 2.5 collective-permute-start.20
  316.3 15.0 %all_to_all.48.k0 = bf16[8,144,128]{2,1,0:T(8,128)(2,1)S(1)} all-to-all(bf16[8,144,128]{2,1,0:T(8,128)(2,1)S(1)} %get-tuple-element.156), channel_id=1, replica_groups={{0,4,8,12,16,20,24,28},{1,5,9,13,17,21,25,29},{2,6,10,14,18,22,26,30},{..., dimensions={0} | all-to-all | bytes 589824 | tf_op jit(solution)/shard_map/keys/all_to_all | solution.py:194
  335.3 3.6 collective-permute-done.22.k1
  339.0 6.7 collective-permute-done.23.k2
  347.8 3.6 attend.10.a0
  351.6 3.5 collective-permute-start.26
  359.5 4.1 collective-permute-start.28
  368.0 2.4 collective-permute-start.31
  377.9 15.0 %all_to_all.49.k0 = bf16[8,144,128]{2,1,0:T(8,128)(2,1)S(1)} all-to-all(bf16[8,144,128]{2,1,0:T(8,128)(2,1)S(1)} %get-tuple-element.158), channel_id=1, replica_groups={{0,4,8,12,16,20,24,28},{1,5,9,13,17,21,25,29},{2,6,10,14,18,22,26,30},{..., dimensions={0} | all-to-all | bytes 589824 | tf_op jit(solution)/shard_map/keys/all_to_all | solution.py:194
  392.9 3.3 collective-permute-start.34
  396.9 3.6 collective-permute-done.33.k1
  400.6 8.2 %collective-permute-done.34.k2 = bf16[8,144,128]{2,1,0:T(8,128)(2,1)S(1)} collective-permute-done((bf16[8,144,128]{2,1,0:T(8,128)(2,1)S(1)}, bf16[8,144,128]{2,1,0:T(8,128)(2,1)S(1)}, u32[]{:S(2)}, u32[]{:S(2)}) %collective-permute-start.34) | collective-permute-done | bytes 294944 | tf_op jit(solution)/shard_map/keys/ppermute | solution.py:197
  411.0 3.6 attend.11.a0
  414.7 3.5 collective-permute-start.37
  422.7 4.1 collective-permute-start.39
  431.1 2.4 collective-permute-start.42
  441.0 15.0 %all_to_all.50.k0 = bf16[8,144,128]{2,1,0:T(8,128)(2,1)S(1)} all-to-all(bf16[8,144,128]{2,1,0:T(8,128)(2,1)S(1)} %get-tuple-element.160), channel_id=1, replica_groups={{0,4,8,12,16,20,24,28},{1,5,9,13,17,21,25,29},{2,6,10,14,18,22,26,30},{..., dimensions={0} | all-to-all | bytes 589824 | tf_op jit(solution)/shard_map/keys/all_to_all | solution.py:194
  457.8 2.5 collective-permute-start.46
  460.3 3.4 collective-permute-done.44.k1
  463.7 6.6 collective-permute-done.45.k2
  470.3 2.4 collective-permute-done.46.k3
  472.8 3.5 attend.12.a0
  476.5 3.5 collective-permute-start.48
  484.4 4.1 collective-permute-start.50
  502.8 15.0 %all_to_all.51.k0 = bf16[8,144,128]{2,1,0:T(8,128)(2,1)S(1)} all-to-all(bf16[8,144,128]{2,1,0:T(8,128)(2,1)S(1)} %get-tuple-element.162), channel_id=1, replica_groups={{0,4,8,12,16,20,24,28},{1,5,9,13,17,21,25,29},{2,6,10,14,18,22,26,30},{..., dimensions={0} | all-to-all | bytes 589824 | tf_op jit(solution)/shard_map/keys/all_to_all | solution.py:194
  517.8 3.3 collective-permute-start.56
  521.8 3.7 collective-permute-done.55.k1
  525.5 8.2 %collective-permute-done.56.k2 = bf16[8,144,128]{2,1,0:T(8,128)(2,1)S(1)} collective-permute-done((bf16[8,144,128]{2,1,0:T(8,128)(2,1)S(1)}, bf16[8,144,128]{2,1,0:T(8,128)(2,1)S(1)}, u32[]{:S(2)}, u32[]{:S(2)}) %collective-permute-start.56) | collective-permute-done | bytes 294944 | tf_op jit(solution)/shard_map/keys/ppermute | solution.py:197
  535.9 3.5 attend.13.a0
  539.6 3.5 collective-permute-start.59
  547.5 4.1 collective-permute-start.61
  565.9 15.0 %all_to_all.52.k0 = bf16[8,144,128]{2,1,0:T(8,128)(2,1)S(1)} all-to-all(bf16[8,144,128]{2,1,0:T(8,128)(2,1)S(1)} %get-tuple-element.164), channel_id=1, replica_groups={{0,4,8,12,16,20,24,28},{1,5,9,13,17,21,25,29},{2,6,10,14,18,22,26,30},{..., dimensions={0} | all-to-all | bytes 589824 | tf_op jit(solution)/shard_map/keys/all_to_all | solution.py:194
  585.0 3.6 collective-permute-done.66.k1
  588.6 6.7 collective-permute-done.67.k2
  597.5 3.5 attend.14.a0
  601.2 3.5 collective-permute-start.70
  609.1 4.1 collective-permute-start.72
  617.6 2.4 collective-permute-start.73
  627.5 15.0 %all_to_all.53.k0 = bf16[8,144,128]{2,1,0:T(8,128)(2,1)S(1)} all-to-all(bf16[8,144,128]{2,1,0:T(8,128)(2,1)S(1)} %get-tuple-element.166), channel_id=1, replica_groups={{0,4,8,12,16,20,24,28},{1,5,9,13,17,21,25,29},{2,6,10,14,18,22,26,30},{..., dimensions={0} | all-to-all | bytes 589824 | tf_op jit(solution)/shard_map/keys/all_to_all | solution.py:194
  642.5 3.3 collective-permute-start.78
  646.6 3.6 collective-permute-done.77.k1
  650.2 8.2 %collective-permute-done.78.k2 = bf16[8,144,128]{2,1,0:T(8,128)(2,1)S(1)} collective-permute-done((bf16[8,144,128]{2,1,0:T(8,128)(2,1)S(1)}, bf16[8,144,128]{2,1,0:T(8,128)(2,1)S(1)}, u32[]{:S(2)}, u32[]{:S(2)}) %collective-permute-start.78) | collective-permute-done | bytes 294944 | tf_op jit(solution)/shard_map/keys/ppermute | solution.py:197
  660.6 3.5 attend.15.a0
  664.3 3.5 collective-permute-start.81
  672.3 4.1 collective-permute-start.83
  680.7 2.4 collective-permute-start.86
  689.6 5.1 conditional.1
  (212 shorter events, 179.5 us)
Async XLA Ops:
  6.5 183.5 %all-gather.4.cloned.1.call-start = ((), (), s32[]{:S(2)}) async-start(), calls=%async_computation.9 | async-start | bytes 21626880 | tf_op jit(solution)/shard_map/all_gather | solution.py:163
  206.4 5.6 collective-permute-start
  206.4 11.8 %collective-permute-start.1 = (bf16[8,144,128]{2,1,0:T(8,128)(2,1)S(1)}, bf16[8,144,128]{2,1,0:T(8,128)(2,1)S(1)}, u32[]{:S(2)}, u32[]{:S(2)}) collective-permute-start(bf16[8,144,128]{2,1,0:T(8,128)(2,1)S(1)} %all_to_all.46.k0), channel_id=1, source_target_pairs={{0,2},{1,3},{2,0},{3,1},{4,6},{5,7},{6,4},{7,5},{8,10},{9,11},{10,... | collective-permute-start | bytes 884744 | tf_op jit(solution)/shard_map/keys/ppermute | solution.py:197
  208.2 14.4 %collective-permute-start.2 = (bf16[8,144,128]{2,1,0:T(8,128)(2,1)S(1)}, bf16[8,144,128]{2,1,0:T(8,128)(2,1)S(1)}, u32[]{:S(2)}, u32[]{:S(2)}) collective-permute-start(bf16[8,144,128]{2,1,0:T(8,128)(2,1)S(1)} %all_to_all.46.k0), channel_id=1, source_target_pairs={{0,3},{1,2},{2,1},{3,0},{4,7},{5,6},{6,5},{7,4},{8,11},{9,10},{10,... | collective-permute-start | bytes 884744 | tf_op jit(solution)/shard_map/keys/ppermute | solution.py:197
  227.4 5.0 collective-permute-start.4
  229.8 4.4 collective-permute-start.5
  234.3 5.5 collective-permute-start.6
  241.5 4.8 collective-permute-start.8
  242.9 5.0 collective-permute-start.9
  268.3 7.1 %collective-permute-start.11 = (bf16[8,144,128]{2,1,0:T(8,128)(2,1)S(1)}, bf16[8,144,128]{2,1,0:T(8,128)(2,1)S(1)}, u32[]{:S(2)}, u32[]{:S(2)}) collective-permute-start(bf16[8,144,128]{2,1,0:T(8,128)(2,1)S(1)} %all_to_all.47.k0), channel_id=1, source_target_pairs={{0,1},{1,0},{2,3},{3,2},{4,5},{5,4},{6,7},{7,6},{8,9},{9,8},{10,11... | collective-permute-start | bytes 884744 | tf_op jit(solution)/shard_map/keys/ppermute | solution.py:197
  268.3 15.3 %collective-permute-start.12 = (bf16[8,144,128]{2,1,0:T(8,128)(2,1)S(1)}, bf16[8,144,128]{2,1,0:T(8,128)(2,1)S(1)}, u32[]{:S(2)}, u32[]{:S(2)}) collective-permute-start(bf16[8,144,128]{2,1,0:T(8,128)(2,1)S(1)} %all_to_all.47.k0), channel_id=1, source_target_pairs={{0,2},{1,3},{2,0},{3,1},{4,6},{5,7},{6,4},{7,5},{8,10},{9,11},{10,... | collective-permute-start | bytes 884744 | tf_op jit(solution)/shard_map/keys/ppermute | solution.py:197
  271.6 14.4 %collective-permute-start.13 = (bf16[8,144,128]{2,1,0:T(8,128)(2,1)S(1)}, bf16[8,144,128]{2,1,0:T(8,128)(2,1)S(1)}, u32[]{:S(2)}, u32[]{:S(2)}) collective-permute-start(bf16[8,144,128]{2,1,0:T(8,128)(2,1)S(1)} %all_to_all.47.k0), channel_id=1, source_target_pairs={{0,3},{1,2},{2,1},{3,0},{4,7},{5,6},{6,5},{7,4},{8,11},{9,10},{10,... | collective-permute-start | bytes 884744 | tf_op jit(solution)/shard_map/keys/ppermute | solution.py:197
  289.8 6.0 collective-permute-start.15
  293.3 4.4 collective-permute-start.16
  297.8 5.5 collective-permute-start.17
  305.0 4.8 collective-permute-start.19
  306.4 5.0 collective-permute-start.20
  331.3 7.7 %collective-permute-start.22 = (bf16[8,144,128]{2,1,0:T(8,128)(2,1)S(1)}, bf16[8,144,128]{2,1,0:T(8,128)(2,1)S(1)}, u32[]{:S(2)}, u32[]{:S(2)}) collective-permute-start(bf16[8,144,128]{2,1,0:T(8,128)(2,1)S(1)} %all_to_all.48.k0), channel_id=1, source_target_pairs={{0,1},{1,0},{2,3},{3,2},{4,5},{5,4},{6,7},{7,6},{8,9},{9,8},{10,11... | collective-permute-start | bytes 884744 | tf_op jit(solution)/shard_map/keys/ppermute | solution.py:197
  331.3 14.3 %collective-permute-start.23 = (bf16[8,144,128]{2,1,0:T(8,128)(2,1)S(1)}, bf16[8,144,128]{2,1,0:T(8,128)(2,1)S(1)}, u32[]{:S(2)}, u32[]{:S(2)}) collective-permute-start(bf16[8,144,128]{2,1,0:T(8,128)(2,1)S(1)} %all_to_all.48.k0), channel_id=1, source_target_pairs={{0,2},{1,3},{2,0},{3,1},{4,6},{5,7},{6,4},{7,5},{8,10},{9,11},{10,... | collective-permute-start | bytes 884744 | tf_op jit(solution)/shard_map/keys/ppermute | solution.py:197
  333.2 14.6 %collective-permute-start.24 = (bf16[8,144,128]{2,1,0:T(8,128)(2,1)S(1)}, bf16[8,144,128]{2,1,0:T(8,128)(2,1)S(1)}, u32[]{:S(2)}, u32[]{:S(2)}) collective-permute-start(bf16[8,144,128]{2,1,0:T(8,128)(2,1)S(1)} %all_to_all.48.k0), channel_id=1, source_target_pairs={{0,3},{1,2},{2,1},{3,0},{4,7},{5,6},{6,5},{7,4},{8,11},{9,10},{10,... | collective-permute-start | bytes 884744 | tf_op jit(solution)/shard_map/keys/ppermute | solution.py:197
  351.6 6.0 collective-permute-start.26
  355.0 4.4 collective-permute-start.27
  359.5 5.4 collective-permute-start.28
  366.6 4.8 collective-permute-start.30
  368.0 5.0 collective-permute-start.31
  392.9 7.7 %collective-permute-start.33 = (bf16[8,144,128]{2,1,0:T(8,128)(2,1)S(1)}, bf16[8,144,128]{2,1,0:T(8,128)(2,1)S(1)}, u32[]{:S(2)}, u32[]{:S(2)}) collective-permute-start(bf16[8,144,128]{2,1,0:T(8,128)(2,1)S(1)} %all_to_all.49.k0), channel_id=1, source_target_pairs={{0,1},{1,0},{2,3},{3,2},{4,5},{5,4},{6,7},{7,6},{8,9},{9,8},{10,11... | collective-permute-start | bytes 884744 | tf_op jit(solution)/shard_map/keys/ppermute | solution.py:197
  392.9 15.9 %collective-permute-start.34 = (bf16[8,144,128]{2,1,0:T(8,128)(2,1)S(1)}, bf16[8,144,128]{2,1,0:T(8,128)(2,1)S(1)}, u32[]{:S(2)}, u32[]{:S(2)}) collective-permute-start(bf16[8,144,128]{2,1,0:T(8,128)(2,1)S(1)} %all_to_all.49.k0), channel_id=1, source_target_pairs={{0,2},{1,3},{2,0},{3,1},{4,6},{5,7},{6,4},{7,5},{8,10},{9,11},{10,... | collective-permute-start | bytes 884744 | tf_op jit(solution)/shard_map/keys/ppermute | solution.py:197
  396.2 14.8 %collective-permute-start.35 = (bf16[8,144,128]{2,1,0:T(8,128)(2,1)S(1)}, bf16[8,144,128]{2,1,0:T(8,128)(2,1)S(1)}, u32[]{:S(2)}, u32[]{:S(2)}) collective-permute-start(bf16[8,144,128]{2,1,0:T(8,128)(2,1)S(1)} %all_to_all.49.k0), channel_id=1, source_target_pairs={{0,3},{1,2},{2,1},{3,0},{4,7},{5,6},{6,5},{7,4},{8,11},{9,10},{10,... | collective-permute-start | bytes 884744 | tf_op jit(solution)/shard_map/keys/ppermute | solution.py:197
  414.7 6.0 collective-permute-start.37
  418.2 4.4 collective-permute-start.38
  422.7 5.3 collective-permute-start.39
  429.7 4.8 collective-permute-start.41
  431.1 5.0 collective-permute-start.42
  456.0 7.7 %collective-permute-start.44 = (bf16[8,144,128]{2,1,0:T(8,128)(2,1)S(1)}, bf16[8,144,128]{2,1,0:T(8,128)(2,1)S(1)}, u32[]{:S(2)}, u32[]{:S(2)}) collective-permute-start(bf16[8,144,128]{2,1,0:T(8,128)(2,1)S(1)} %all_to_all.50.k0), channel_id=1, source_target_pairs={{0,1},{1,0},{2,3},{3,2},{4,5},{5,4},{6,7},{7,6},{8,9},{9,8},{10,11... | collective-permute-start | bytes 884744 | tf_op jit(solution)/shard_map/keys/ppermute | solution.py:197
  456.0 14.3 %collective-permute-start.45 = (bf16[8,144,128]{2,1,0:T(8,128)(2,1)S(1)}, bf16[8,144,128]{2,1,0:T(8,128)(2,1)S(1)}, u32[]{:S(2)}, u32[]{:S(2)}) collective-permute-start(bf16[8,144,128]{2,1,0:T(8,128)(2,1)S(1)} %all_to_all.50.k0), channel_id=1, source_target_pairs={{0,2},{1,3},{2,0},{3,1},{4,6},{5,7},{6,4},{7,5},{8,10},{9,11},{10,... | collective-permute-start | bytes 884744 | tf_op jit(solution)/shard_map/keys/ppermute | solution.py:197
  457.8 15.0 %collective-permute-start.46 = (bf16[8,144,128]{2,1,0:T(8,128)(2,1)S(1)}, bf16[8,144,128]{2,1,0:T(8,128)(2,1)S(1)}, u32[]{:S(2)}, u32[]{:S(2)}) collective-permute-start(bf16[8,144,128]{2,1,0:T(8,128)(2,1)S(1)} %all_to_all.50.k0), channel_id=1, source_target_pairs={{0,3},{1,2},{2,1},{3,0},{4,7},{5,6},{6,5},{7,4},{8,11},{9,10},{10,... | collective-permute-start | bytes 884744 | tf_op jit(solution)/shard_map/keys/ppermute | solution.py:197
  476.5 6.0 collective-permute-start.48
  479.9 4.4 collective-permute-start.49
  484.4 5.4 collective-permute-start.50
  491.4 4.8 collective-permute-start.51
  492.9 5.0 collective-permute-start.53
  517.8 7.7 %collective-permute-start.55 = (bf16[8,144,128]{2,1,0:T(8,128)(2,1)S(1)}, bf16[8,144,128]{2,1,0:T(8,128)(2,1)S(1)}, u32[]{:S(2)}, u32[]{:S(2)}) collective-permute-start(bf16[8,144,128]{2,1,0:T(8,128)(2,1)S(1)} %all_to_all.51.k0), channel_id=1, source_target_pairs={{0,1},{1,0},{2,3},{3,2},{4,5},{5,4},{6,7},{7,6},{8,9},{9,8},{10,11... | collective-permute-start | bytes 884744 | tf_op jit(solution)/shard_map/keys/ppermute | solution.py:197
  517.8 15.8 %collective-permute-start.56 = (bf16[8,144,128]{2,1,0:T(8,128)(2,1)S(1)}, bf16[8,144,128]{2,1,0:T(8,128)(2,1)S(1)}, u32[]{:S(2)}, u32[]{:S(2)}) collective-permute-start(bf16[8,144,128]{2,1,0:T(8,128)(2,1)S(1)} %all_to_all.51.k0), channel_id=1, source_target_pairs={{0,2},{1,3},{2,0},{3,1},{4,6},{5,7},{6,4},{7,5},{8,10},{9,11},{10,... | collective-permute-start | bytes 884744 | tf_op jit(solution)/shard_map/keys/ppermute | solution.py:197
  521.1 14.8 %collective-permute-start.57 = (bf16[8,144,128]{2,1,0:T(8,128)(2,1)S(1)}, bf16[8,144,128]{2,1,0:T(8,128)(2,1)S(1)}, u32[]{:S(2)}, u32[]{:S(2)}) collective-permute-start(bf16[8,144,128]{2,1,0:T(8,128)(2,1)S(1)} %all_to_all.51.k0), channel_id=1, source_target_pairs={{0,3},{1,2},{2,1},{3,0},{4,7},{5,6},{6,5},{7,4},{8,11},{9,10},{10,... | collective-permute-start | bytes 884744 | tf_op jit(solution)/shard_map/keys/ppermute | solution.py:197
  539.6 6.0 collective-permute-start.59
  543.0 4.4 collective-permute-start.60
  547.5 5.4 collective-permute-start.61
  554.5 4.8 collective-permute-start.63
  556.0 5.0 collective-permute-start.64
  580.9 7.7 %collective-permute-start.66 = (bf16[8,144,128]{2,1,0:T(8,128)(2,1)S(1)}, bf16[8,144,128]{2,1,0:T(8,128)(2,1)S(1)}, u32[]{:S(2)}, u32[]{:S(2)}) collective-permute-start(bf16[8,144,128]{2,1,0:T(8,128)(2,1)S(1)} %all_to_all.52.k0), channel_id=1, source_target_pairs={{0,1},{1,0},{2,3},{3,2},{4,5},{5,4},{6,7},{7,6},{8,9},{9,8},{10,11... | collective-permute-start | bytes 884744 | tf_op jit(solution)/shard_map/keys/ppermute | solution.py:197
  580.9 14.3 %collective-permute-start.67 = (bf16[8,144,128]{2,1,0:T(8,128)(2,1)S(1)}, bf16[8,144,128]{2,1,0:T(8,128)(2,1)S(1)}, u32[]{:S(2)}, u32[]{:S(2)}) collective-permute-start(bf16[8,144,128]{2,1,0:T(8,128)(2,1)S(1)} %all_to_all.52.k0), channel_id=1, source_target_pairs={{0,2},{1,3},{2,0},{3,1},{4,6},{5,7},{6,4},{7,5},{8,10},{9,11},{10,... | collective-permute-start | bytes 884744 | tf_op jit(solution)/shard_map/keys/ppermute | solution.py:197
  582.7 14.8 %collective-permute-start.68 = (bf16[8,144,128]{2,1,0:T(8,128)(2,1)S(1)}, bf16[8,144,128]{2,1,0:T(8,128)(2,1)S(1)}, u32[]{:S(2)}, u32[]{:S(2)}) collective-permute-start(bf16[8,144,128]{2,1,0:T(8,128)(2,1)S(1)} %all_to_all.52.k0), channel_id=1, source_target_pairs={{0,3},{1,2},{2,1},{3,0},{4,7},{5,6},{6,5},{7,4},{8,11},{9,10},{10,... | collective-permute-start | bytes 884744 | tf_op jit(solution)/shard_map/keys/ppermute | solution.py:197
  601.2 6.0 collective-permute-start.70
  609.1 5.3 collective-permute-start.72
  616.2 4.8 collective-permute-start.75
  617.6 5.0 collective-permute-start.73
  642.5 7.7 %collective-permute-start.77 = (bf16[8,144,128]{2,1,0:T(8,128)(2,1)S(1)}, bf16[8,144,128]{2,1,0:T(8,128)(2,1)S(1)}, u32[]{:S(2)}, u32[]{:S(2)}) collective-permute-start(bf16[8,144,128]{2,1,0:T(8,128)(2,1)S(1)} %all_to_all.53.k0), channel_id=1, source_target_pairs={{0,1},{1,0},{2,3},{3,2},{4,5},{5,4},{6,7},{7,6},{8,9},{9,8},{10,11... | collective-permute-start | bytes 884744 | tf_op jit(solution)/shard_map/keys/ppermute | solution.py:197
  642.5 15.8 %collective-permute-start.78 = (bf16[8,144,128]{2,1,0:T(8,128)(2,1)S(1)}, bf16[8,144,128]{2,1,0:T(8,128)(2,1)S(1)}, u32[]{:S(2)}, u32[]{:S(2)}) collective-permute-start(bf16[8,144,128]{2,1,0:T(8,128)(2,1)S(1)} %all_to_all.53.k0), channel_id=1, source_target_pairs={{0,2},{1,3},{2,0},{3,1},{4,6},{5,7},{6,4},{7,5},{8,10},{9,11},{10,... | collective-permute-start | bytes 884744 | tf_op jit(solution)/shard_map/keys/ppermute | solution.py:197
  645.8 14.8 %collective-permute-start.79 = (bf16[8,144,128]{2,1,0:T(8,128)(2,1)S(1)}, bf16[8,144,128]{2,1,0:T(8,128)(2,1)S(1)}, u32[]{:S(2)}, u32[]{:S(2)}) collective-permute-start(bf16[8,144,128]{2,1,0:T(8,128)(2,1)S(1)} %all_to_all.53.k0), channel_id=1, source_target_pairs={{0,3},{1,2},{2,1},{3,0},{4,7},{5,6},{6,5},{7,4},{8,11},{9,10},{10,... | collective-permute-start | bytes 884744 | tf_op jit(solution)/shard_map/keys/ppermute | solution.py:197
  664.3 6.0 collective-permute-start.81
  667.8 4.4 collective-permute-start.82
  672.3 5.4 collective-permute-start.83
  679.3 4.8 collective-permute-start.85
  680.7 5.0 collective-permute-start.86
  (39 other events, 200.9 us)
Sparse Core Ops, SparseCore 0:
  28.3 161.6 all-gather.3

commit v2 on v1

v2 whole, which is shorter than its diff:
```python
import functools

import jax
import jax.numpy as jnp
from jax import lax
from jax.experimental import pallas as pl
from jax.experimental.pallas import tpu as pltpu
from jax.sharding import PartitionSpec as P

HEADS = 32
KVH = 8
HD = 64
SHARE = HEADS // KVH
QW = SHARE * HD
EPS = 1e-05
NEG = -1e30

ZN = 8
XN = 4
SN = 8
F32 = jnp.float32
BF16 = jnp.bfloat16


def seq_pairs(mask):
    return [(i, i ^ mask) for i in range(ZN * XN)]


def section_pairs(mask):
    return [(i, i ^ mask) for i in range(SN)]


def along_z():
    return [[z * XN + x for z in range(ZN)] for x in range(XN)]


def spread(piece):
    near = [piece] + [lax.ppermute(piece, "section", section_pairs(2 * d)) for d in (1, 2, 3)]
    other = lax.ppermute(jnp.stack(near), "section", section_pairs(1))
    return near + [other]


def in_order(refs):
    out = [(2 * d, refs[d][...]) for d in range(4)]
    out += [(2 * d + 1, refs[4][d]) for d in range(4)]
    return out


def project(me, gain_ref, piece_refs, w_of, q_ref, kv_ref):
    pieces = [(mask, value.astype(F32)) for mask, value in in_order(piece_refs)]
    rows = pieces[0][1].shape[0]
    width = sum(value.shape[1] for _, value in pieces)
    squares = functools.reduce(jnp.add, [value * value for _, value in pieces])
    scale = lax.rsqrt(jnp.sum(squares, axis=-1, keepdims=True) / width + EPS)
    q_sum = jnp.zeros((rows, QW), F32)
    kv_sum = jnp.zeros((rows, 2 * HD), F32)
    for mask, value in pieces:
        owner = jnp.bitwise_xor(me, mask)
        gain = gain_ref[pl.ds(owner, 1), 0, :].astype(F32)
        normed = (value * scale * gain).astype(BF16)
        wq, wkv = w_of(owner)
        q_sum += jnp.dot(normed, wq, preferred_element_type=F32)
        kv_sum += jnp.dot(normed, wkv, preferred_element_type=F32)
    q_ref[...] = q_sum.astype(BF16)
    pair = kv_sum.astype(BF16)
    for i in range(kv_ref.shape[0]):
        kv_ref[i] = pair


def project_kernel(me_ref, gain_ref, p0, p1, p2, p3, p4, wq_ref, wkv_ref, q_ref, kv_ref):
    def w_of(owner):
        wq = wq_ref[pl.ds(XN * owner, XN), 0].reshape(QW, QW)
        wkv = wkv_ref[pl.ds(XN * owner, XN), 0].reshape(QW, 2 * HD)
        return wq, wkv

    project(me_ref[0], gain_ref, [p0, p1, p2, p3, p4], w_of, q_ref, kv_ref)


def assemble(seq, parts, held):
    x_me = jnp.bitwise_and(seq, XN - 1)
    for d in range(XN):
        held[jnp.bitwise_xor(x_me, d)] = parts[d][...]


def first_project_kernel(
    me_ref, seq_ref, gain_ref, p0, p1, p2, p3, p4, w0, w1, w2, w3, q_ref, kv_ref, held
):
    assemble(seq_ref[0], [w0, w1, w2, w3], held)

    def w_of(owner):
        w = held[:, owner].reshape(QW, QW + 2 * HD)
        return w[:, :QW], w[:, QW:]

    project(me_ref[0], gain_ref, [p0, p1, p2, p3, p4], w_of, q_ref, kv_ref)


def attend_kernel(seq_ref, q0, q1, q2, q3, k_ref, o0, o1, o2, o3, q_held, o_held, *, blocks, tok):
    seq = seq_ref[0]
    x_me = jnp.bitwise_and(seq, XN - 1)
    span = ZN * tok
    rows = SHARE * tok
    for d, q_ref in enumerate([q0, q1, q2, q3]):
        q_held[d] = q_ref[...]
    row = lax.broadcasted_iota(jnp.int32, (rows, span), 0)
    col = lax.broadcasted_iota(jnp.int32, (rows, span), 1)
    slack = lax.rem(row, tok) - lax.div(col, tok) * (XN * tok) - lax.rem(col, tok)
    lane = lax.broadcasted_iota(jnp.int32, (tok, 2 * HD), 1)
    factor = HD**-0.5

    @pl.loop(0, XN)
    def _(d):
        asker = seq - x_me + jnp.bitwise_xor(x_me, d)
        visible = slack >= (x_me - asker) * tok
        for b in range(blocks):
            q_rows = q_held[d, b * tok : (b + 1) * tok]
            q_heads = jnp.concatenate([q_rows[:, h * HD : (h + 1) * HD] for h in range(SHARE)], axis=0)
            q_heads = jnp.concatenate([q_heads, jnp.zeros((rows, HD), BF16)], axis=1)
            scores = []
            pairs = []
            for kb in range(b + 1):
                pair = k_ref[:, kb * tok : (kb + 1) * tok, :].reshape(span, 2 * HD)
                s = lax.dot_general(q_heads, pair, (((1,), (1,)), ((), ())), preferred_element_type=F32)
                if kb == b:
                    s = jnp.where(visible, s, NEG)
                scores.append(s)
                pairs.append(pair)
            peak = jnp.max(functools.reduce(jnp.maximum, scores), axis=-1, keepdims=True)
            total = jnp.zeros((rows, span), F32)
            summed = jnp.zeros((rows, 2 * HD), F32)
            for s, pair in zip(scores, pairs):
                probs = jnp.exp((s - peak) * factor)
                total += probs
                summed += jnp.dot(probs.astype(BF16), pair, preferred_element_type=F32)
            total = jnp.sum(total, axis=-1, keepdims=True)
            result = (summed[:, HD:] / total).astype(BF16)
            weight = peak * factor + jnp.log(total)
            high = weight.astype(BF16).astype(F32)
            low = weight - high
            notes = jnp.zeros((tok, 2 * HD), F32)
            for h in range(SHARE):
                part = slice(h * tok, (h + 1) * tok)
                notes = jnp.where(lane == h, high[part], notes)
                notes = jnp.where(lane == SHARE + h, low[part], notes)
            o_held[d, b * tok : (b + 1) * tok, :] = jnp.concatenate(
                [result[h * tok : (h + 1) * tok] for h in range(SHARE)] + [notes.astype(BF16)], axis=1
            )

    for d, o_ref in enumerate([o0, o1, o2, o3]):
        o_ref[...] = o_held[d]


def combine_kernel(o0, o1, o2, o3, a_ref):
    parts = [o0[...], o1[...], o2[...], o3[...]]
    notes = [part[:, QW:].astype(F32) for part in parts]
    for h in range(SHARE):
        weights = [n[:, h : h + 1] + n[:, SHARE + h : SHARE + h + 1] for n in notes]
        peak = functools.reduce(jnp.maximum, weights)
        weights = [jnp.exp(w - peak) for w in weights]
        total = functools.reduce(jnp.add, weights)
        cols = slice(h * HD, (h + 1) * HD)
        mixed = functools.reduce(
            jnp.add, [w / total * part[:, cols].astype(F32) for w, part in zip(weights, parts)]
        )
        a_ref[:, cols] = mixed.astype(BF16)


def output(me, piece_refs, h_ref, w_of, o_ref):
    total = h_ref[...].astype(F32)
    update = jnp.zeros(total.shape, F32)
    for mask, value in in_order(piece_refs):
        update += jnp.dot(value, w_of(jnp.bitwise_xor(me, mask)), preferred_element_type=F32)
    o_ref[...] = (total + update).astype(BF16)


def output_kernel(me_ref, a0, a1, a2, a3, a4, h_ref, w_ref, o_ref):
    def w_of(owner):
        return w_ref[pl.ds(XN * owner, XN), 0].reshape(QW, QW)

    output(me_ref[0], [a0, a1, a2, a3, a4], h_ref, w_of, o_ref)


def first_output_kernel(me_ref, seq_ref, a0, a1, a2, a3, a4, h_ref, w0, w1, w2, w3, o_ref, held):
    assemble(seq_ref[0], [w0, w1, w2, w3], held)
    output(me_ref[0], [a0, a1, a2, a3, a4], h_ref, lambda owner: held[:, owner].reshape(QW, QW), o_ref)


SMEM = pl.BlockSpec(memory_space=pltpu.SMEM)


def whole(shape):
    return pl.BlockSpec(shape, lambda i: (0,) * len(shape))


def call(kernel, out_shape, in_specs, flops, bytes_accessed, exps=0, scratch=()):
    if isinstance(out_shape, list):
        out_specs = [whole(o.shape) for o in out_shape]
    else:
        out_specs = whole(out_shape.shape)
    return pl.pallas_call(
        kernel,
        out_shape=out_shape,
        grid=(1,),
        in_specs=in_specs,
        out_specs=out_specs,
        scratch_shapes=list(scratch),
        compiler_params=pltpu.CompilerParams(vmem_limit_bytes=48 * 1024 * 1024),
        cost_estimate=pl.CostEstimate(flops=flops, bytes_accessed=bytes_accessed, transcendentals=exps),
    )


def local(inputs, norm_gain, w_query, w_key, w_value, w_out):
    blocks, tok, width = inputs.shape
    rows = blocks * tok
    me = lax.axis_index("section")
    seq = lax.axis_index("seq")
    me_s = me.reshape(1)
    seq_s = seq.reshape(1)
    layers = lax.axis_size("section")
    shard = w_query.shape[1]
    qkv_w = QW + 2 * HD
    all_w = QW + qkv_w

    def cut(w):
        return w[0].reshape(shard, SN, -1).transpose(1, 0, 2)

    gain_rows = jnp.pad(norm_gain.reshape(4, width // 4), ((0, 12), (0, all_w - width // 4)))
    mine = jnp.concatenate([cut(w_query), cut(w_out), cut(w_key), cut(w_value)], axis=-1)
    mine = jnp.concatenate([mine, jnp.broadcast_to(gain_rows[None], (SN, 16, all_w))], axis=1)
    by_layer = lax.all_to_all(mine, "section", split_axis=0, concat_axis=0, tiled=True)
    gains = by_layer[:, shard : shard + 4, : width // 4].reshape(layers, SN, 1, QW)

    with jax.named_scope("weights"):
        early = lax.all_gather(by_layer[1:4, :shard], "seq", axis=0)
        late = lax.all_gather(by_layer[4:, :shard], "seq", axis=0)
        first = jnp.broadcast_to(by_layer[None, 0, :shard], (ZN, shard, all_w))
        first = lax.all_to_all(
            first, "seq", split_axis=0, concat_axis=0, tiled=True, axis_index_groups=along_z()
        )
        first_qkv = jnp.concatenate([first[:, :, :QW], first[:, :, 2 * QW :]], axis=-1)
        first_out = first[:, :, QW : 2 * QW]
        first_qkv = [first_qkv] + [lax.ppermute(first_qkv, "seq", seq_pairs(d)) for d in (1, 2, 3)]
        first_out = [first_out] + [lax.ppermute(first_out, "seq", seq_pairs(d)) for d in (1, 2, 3)]

    flat = inputs.reshape(rows, width)

    def input_piece(mask):
        return lax.dynamic_slice_in_dim(flat, jnp.bitwise_xor(me, mask) * QW, QW, 1)

    pieces = [input_piece(2 * d) for d in range(4)]
    pieces.append(jnp.stack([input_piece(2 * d + 1) for d in range(4)]))

    piece_shape = jax.ShapeDtypeStruct((rows, QW), BF16)
    piece_specs = [whole((rows, QW))] * 4 + [whole((4, rows, QW))]
    kv_shape = (ZN, rows, 2 * HD)
    part_shape = (rows, QW + 2 * HD)
    seq_keys = ZN * XN * tok
    results = []
    for layer in range(layers):
        group, slot = (early, layer - 1) if layer < 4 else (late, layer - 4)

        def weight_spec(width_, index, slot=slot):
            return pl.BlockSpec((ZN * XN, 1, shard, width_), lambda i: (0, slot, 0, index))

        with jax.named_scope("project"):
            outs = [piece_shape, jax.ShapeDtypeStruct(kv_shape, BF16)]
            cost = (2 * rows * width * qkv_w, 2 * (width * qkv_w + rows * width))
            if layer == 0:
                q, kv = call(
                    first_project_kernel,
                    outs,
                    [SMEM, SMEM, whole((SN, 1, QW))] + piece_specs + [whole((ZN, shard, qkv_w))] * 4,
                    *cost,
                    scratch=[pltpu.VMEM((XN, ZN, shard, qkv_w), BF16)],
                )(me_s, seq_s, gains[layer], *pieces, *first_qkv)
            else:
                q, kv = call(
                    project_kernel,
                    outs,
                    [SMEM, whole((SN, 1, QW))] + piece_specs + [weight_spec(QW, 0), weight_spec(2 * HD, 4)],
                    *cost,
                )(me_s, gains[layer], *pieces, group, group)
        with jax.named_scope("exchange"):
            qs = [q] + [lax.ppermute(q, "seq", seq_pairs(d)) for d in (1, 2, 3)]
            kv = lax.all_to_all(
                kv, "seq", split_axis=0, concat_axis=0, tiled=True, axis_index_groups=along_z()
            )
        with jax.named_scope("attend"):
            parts = call(
                functools.partial(attend_kernel, blocks=blocks, tok=tok),
                [jax.ShapeDtypeStruct(part_shape, BF16)] * XN,
                [SMEM] + [whole((rows, QW))] * XN + [whole(kv_shape)],
                4 * SHARE * tok * seq_keys * 128 * 6,
                2 * (ZN * rows * 128 + 10 * rows * QW),
                SHARE * tok * seq_keys * 6,
                scratch=[pltpu.VMEM((XN, rows, QW), BF16), pltpu.VMEM((XN,) + part_shape, BF16)],
            )(seq_s, *qs, kv)
            parts = [parts[0]] + [lax.ppermute(parts[d], "seq", seq_pairs(d)) for d in (1, 2, 3)]
            attended = call(
                combine_kernel,
                piece_shape,
                [whole(part_shape)] * XN,
                10 * rows * QW,
                10 * rows * QW,
            )(*parts)
            heads = spread(attended)
        with jax.named_scope("output"):
            cost = (2 * rows * width * QW, 2 * (width * QW + rows * width))
            if layer == 0:
                own = call(
                    first_output_kernel,
                    piece_shape,
                    [SMEM, SMEM] + piece_specs + [whole((rows, QW))] + [whole((ZN, shard, QW))] * 4,
                    *cost,
                    scratch=[pltpu.VMEM((XN, ZN, shard, QW), BF16)],
                )(me_s, seq_s, *heads, pieces[0], *first_out)
            else:
                own = call(
                    output_kernel,
                    piece_shape,
                    [SMEM] + piece_specs + [whole((rows, QW)), weight_spec(QW, 1)],
                    *cost,
                )(me_s, *heads, pieces[0], group)
            pieces = spread(own)
        results.append(pieces)

    def pick(layer):
        def branch(all_pieces):
            near, other = all_pieces[layer][:4], all_pieces[layer][4]
            parts = []
            for s in range(SN):
                mask = s ^ layer
                parts.append(other[mask // 2] if mask % 2 else near[mask // 2])
            return jnp.concatenate(parts, axis=1)

        return branch

    chosen = lax.switch(me, [pick(layer) for layer in range(layers)], results)
    return chosen.reshape(1, blocks, tok, width)


def solution(mesh):
    in_specs = (
        P(None, "seq", None),
        P("section", None),
        P("section", "seq", None),
        P("section", "seq", None),
        P("section", "seq", None),
        P("section", "seq", None),
    )
    out_specs = P("section", None, "seq", None)
    return jax.shard_map(local, mesh=mesh, in_specs=in_specs, out_specs=out_specs, check_vma=False)
```

time: 713 us -> 616 us (0.86)
  the two profiles are of different devices: /device:TPU:1 before, /device:TPU:25 now
where the time goes in v2:
time: 616 us; the launch traced here: 606 us
  waiting for transfers between devices  259 us (42%)
  starting transfers between devices  212 us (34%)
  Pallas kernels  84.2 us (14%)
  local copies, waits for them, and re-layouts  16.3 us (3%)
  blocking collectives  16.1 us (3%)
  between operations  14.7 us (2%)
    ppermute x48, starting transfers between devices, spread(): lax.ppermute(piece, 'section', section_pairs(2 * d))  63.5 us
    ppermute x48, waiting for transfers between devices, spread(): lax.ppermute(piece, 'section', section_pairs(2 * d))  56.9 us
    ppermute x24, waiting for transfers between devices, local(): lax.ppermute(parts[d], 'seq', seq_pairs(d))  54.2 us
    pallas_call x8, Pallas kernels, local(): call(functools.partial(attend_kernel, blocks=blocks, tok=tok), [jax.Shape...  46.5 us
    all_to_all x8, waiting for transfers between devices, local(): lax.all_to_all(kv, 'seq', split_axis=0, concat_axis=0, tiled=True, axis_i...  43.2 us
    ppermute x16, starting transfers between devices, spread(): other = lax.ppermute(jnp.stack(near), 'section', section_pairs(1))  41 us
    ppermute x24, waiting for transfers between devices, local(): qs = [q] + [lax.ppermute(q, 'seq', seq_pairs(d)) for d in (1, 2, 3)]  32.6 us
    ppermute x24, starting transfers between devices, local(): qs = [q] + [lax.ppermute(q, 'seq', seq_pairs(d)) for d in (1, 2, 3)]  32 us
  transfers between devices with their start and end apart: 129, of which 100 were waited for; matrix products, arithmetic and copies ran while one was open for 1% of the time, Pallas kernels for 7%

profile of v2, /device:TPU:25, one launch (start us, length us, event | category | flops | bytes accessed | tf_op | source)
XLA Modules:
  0.0 606.0 jit_solution(18042294877476297858)
XLA Ops:
  11.5 16.1 %all_to_all.50 = bf16[8,80,640]{2,1,0:T(8,128)(2,1)S(1)} all-to-all(bf16[8,80,640]{2,1,0:T(8,128)(2,1)S(1)} %copy.59), channel_id=1, replica_groups=mesh['section'=8,'seq'=32] {'section'}, dimensions={0} | all-to-all | bytes 1638400 | tf_op jit(solution)/shard_map/all_to_all | solution.py:229
  30.2 8.3 %all-to-all-start.1 = ((bf16[8,64,640]{2,1,0:T(8,128)(2,1)}), bf16[8,64,640]{2,1,0:T(8,128)(2,1)S(1)}, u32[]{:S(2)}, u32[]{:S(2)}) async-start(bf16[8,64,640]{2,1,0:T(8,128)(2,1)} %broadcast_in_dim.15), calls=%async_computation.1 | async-start | bytes 1310720 | tf_op jit(solution)/shard_map/weights/all_to_all | solution.py:236
  38.5 24.4 %all-to-all-done.1 = bf16[8,64,640]{2,1,0:T(8,128)(2,1)S(1)} async-done(((bf16[8,64,640]{2,1,0:T(8,128)(2,1)}), bf16[8,64,640]{2,1,0:T(8,128)(2,1)S(1)}, u32[]{:S(2)}, u32[]{:S(2)}) %all-to-all-start.1) | async-done | bytes 655392 | tf_op jit(solution)/shard_map/weights/all_to_all | solution.py:236
  68.9 4.2 collective-permute-done.w1
  73.1 10.8 %collective-permute-done.1.w2 = bf16[8,64,384]{2,1,0:T(8,128)(2,1)S(1)} collective-permute-done((bf16[8,64,384]{2,1,0:T(8,128)(2,1)S(1)}, bf16[8,64,384]{2,1,0:T(8,128)(2,1)S(1)}, u32[]{:S(2)}, u32[]{:S(2)}) %collective-permute-start.1) | collective-permute-done | bytes 393248 | tf_op jit(solution)/shard_map/weights/ppermute | solution.py:241
  87.3 3.4 all-to-all-start.2
  99.1 6.1 %all-to-all-done.2.k_ref = bf16[8,144,128]{2,1,0:T(8,128)(2,1)S(1)} async-done(((bf16[8,144,128]{2,1,0:T(8,128)(2,1)}), bf16[8,144,128]{2,1,0:T(8,128)(2,1)S(1)}, u32[]{:S(2)}, u32[]{:S(2)}) %all-to-all-start.2) | async-done | bytes 294944 | tf_op jit(solution)/shard_map/exchange/all_to_all | solution.py:284
  105.3 5.8 attend.16
  117.6 4.9 collective-permute-done.7.o2
  129.0 9.2 %collective-permute-start.12 = (bf16[4,144,256]{2,1,0:T(8,128)(2,1)S(1)}, bf16[4,144,256]{2,1,0:T(8,128)(2,1)S(1)}, u32[]{:S(2)}, u32[]{:S(2)}) collective-permute-start(bf16[4,144,256]{2,1,0:T(8,128)(2,1)S(1)} %pad_maximum_fusion.3), channel_id=1, source_target_pairs={{0,32},{32,0},{64,96},{96,64},{128,160},{160,128},{192,224},{224,1... | collective-permute-start | bytes 884744 | tf_op jit(solution)/shard_map/attend/ppermute | solution.py:39
  142.4 3.7 collective-permute-done.13.w1
  146.0 5.8 collective-permute-done.14.w2
  151.8 2.8 collective-permute-done.15.w3
  161.6 4.8 collective-permute-start.19
  170.4 3.4 all-to-all-start.3
  173.9 3.2 collective-permute-start.21
  182.4 4.1 all-to-all-done.3.k_ref
  186.5 5.8 attend.18
  192.4 3.6 collective-permute-start.24
  196.3 3.2 collective-permute-done.23.o1
  199.4 6.8 %collective-permute-done.24.o2 = bf16[144,384]{1,0:T(8,128)(2,1)S(1)} collective-permute-done((bf16[144,384]{1,0:T(8,128)(2,1)S(1)}, bf16[144,384]{1,0:T(8,128)(2,1)S(1)}, u32[]{:S(2)}, u32[]{:S(2)}) %collective-permute-start.24) | collective-permute-done | bytes 110624 | tf_op jit(solution)/shard_map/attend/ppermute | solution.py:297
  207.5 3.0 collective-permute-start.27
  215.3 3.9 collective-permute-start.29
  231.6 2.8 project.10
  234.4 3.4 all-to-all-start.4
  241.8 3.1 collective-permute-done.35.q2
  245.5 8.2 %all-to-all-done.4.k_ref = bf16[8,144,128]{2,1,0:T(8,128)(2,1)S(1)} async-done(((bf16[8,144,128]{2,1,0:T(8,128)(2,1)}), bf16[8,144,128]{2,1,0:T(8,128)(2,1)S(1)}, u32[]{:S(2)}, u32[]{:S(2)}) %all-to-all-start.4) | async-done | bytes 294944 | tf_op jit(solution)/shard_map/exchange/all_to_all | solution.py:284
  253.7 5.8 attend.20
  260.6 2.9 collective-permute-start.39
  263.5 2.8 collective-permute-done.38.o2
  269.2 3.6 collective-permute-start.41
  283.2 3.6 collective-permute-start.45
  296.0 3.4 all-to-all-start.5
  299.5 3.3 collective-permute-start.49
  303.4 3.0 collective-permute-done.49.q2
  308.0 4.4 all-to-all-done.5.k_ref
  312.4 5.8 attend.22
  318.3 3.3 collective-permute-start.52
  322.4 4.2 collective-permute-done.52.o2
  355.6 3.4 all-to-all-start.6
  366.2 5.7 all-to-all-done.6.k_ref
  372.0 5.8 attend.24
  399.8 3.2 collective-permute-start.72
  413.7 3.4 all-to-all-start.7
  417.2 3.3 collective-permute-start.77
  421.2 2.9 collective-permute-done.77.q2
  425.7 4.4 all-to-all-done.7.k_ref
  430.1 5.8 attend.26
  436.0 3.3 collective-permute-start.80
  440.1 4.2 collective-permute-done.80.o2
  459.5 3.2 collective-permute-start.87
  473.3 3.4 all-to-all-start.8
  483.8 5.9 all-to-all-done.8.k_ref
  489.7 5.8 attend.28
  517.7 3.2 collective-permute-start.102
  531.6 3.4 all-to-all-start.9
  535.1 3.3 collective-permute-start.105
  538.9 3.0 collective-permute-done.105.q2
  543.6 4.4 all-to-all-done.9.k_ref
  548.0 5.8 attend.30
  553.9 3.3 collective-permute-start.108
  558.0 4.2 collective-permute-done.108.o2
  577.7 3.2 collective-permute-start.115
  589.9 8.9 %conditional.1 = (bf16[1,3,48,2048]{3,2,1,0:T(8,128)(2,1)}) conditional(s32[]{:T(128)} %clamp.3, (bf16[144,256]{1,0:T(8,128)(2,1)S(1)}, bf16[4,144,256]{2,1,0:T(8,128)(2,1)S(1)}, bf16[144,256]{1,0:T(8,128)(2,1)S(1)}, bf16[144,256]{1,0:T(8,128)(2,1)S(1)}, bf16[144,256]{1,0:T(8,128)(2,1)S(1)}) %tuple.37, ...), branch_computations={%region_0.1_spmd, %region_1.2_spmd, %region_2.3_spmd, %region_3.4_... | conditional | bytes 2064420 | solution.py:337
  (343 shorter events, 282.6 us)
Async XLA Ops:
  6.5 161.0 %all-gather.5.cloned.1.call-start = ((), (), s32[]{:S(2)}) async-start(), calls=%async_computation.10 | async-start | bytes 8110080 | tf_op jit(solution)/shard_map/weights/all_gather | solution.py:233
  28.4 324.4 %all-gather.7.cloned.1.call-start = ((), (), s32[]{:S(2)}) async-start(), calls=%async_computation.11 | async-start | bytes 10813440 | tf_op jit(solution)/shard_map/weights/all_gather | solution.py:234
  30.2 32.7 %all-to-all-start.1 = ((bf16[8,64,640]{2,1,0:T(8,128)(2,1)}), bf16[8,64,640]{2,1,0:T(8,128)(2,1)S(1)}, u32[]{:S(2)}, u32[]{:S(2)}) async-start(bf16[8,64,640]{2,1,0:T(8,128)(2,1)} %broadcast_in_dim.15), calls=%async_computation.1 | async-start | bytes 1310720 | tf_op jit(solution)/shard_map/weights/all_to_all | solution.py:236
  63.0 10.0 %collective-permute-start = (bf16[8,64,384]{2,1,0:T(8,128)(2,1)S(1)}, bf16[8,64,384]{2,1,0:T(8,128)(2,1)S(1)}, u32[]{:S(2)}, u32[]{:S(2)}) collective-permute-start(bf16[8,64,384]{2,1,0:T(8,128)(2,1)S(1)} %pad_maximum_fusion.1.w0), channel_id=1, source_target_pairs={{0,1},{1,0},{2,3},{3,2},{4,5},{5,4},{6,7},{7,6},{8,9},{9,8},{10,11... | collective-permute-start | bytes 1179656 | tf_op jit(solution)/shard_map/weights/ppermute | solution.py:241
  64.5 19.3 %collective-permute-start.1 = (bf16[8,64,384]{2,1,0:T(8,128)(2,1)S(1)}, bf16[8,64,384]{2,1,0:T(8,128)(2,1)S(1)}, u32[]{:S(2)}, u32[]{:S(2)}) collective-permute-start(bf16[8,64,384]{2,1,0:T(8,128)(2,1)S(1)} %pad_maximum_fusion.1.w0), channel_id=1, source_target_pairs={{0,2},{1,3},{2,0},{3,1},{4,6},{5,7},{6,4},{7,5},{8,10},{9,11},{10,... | collective-permute-start | bytes 1179656 | tf_op jit(solution)/shard_map/weights/ppermute | solution.py:241
  67.0 18.9 %collective-permute-start.2 = (bf16[8,64,384]{2,1,0:T(8,128)(2,1)S(1)}, bf16[8,64,384]{2,1,0:T(8,128)(2,1)S(1)}, u32[]{:S(2)}, u32[]{:S(2)}) collective-permute-start(bf16[8,64,384]{2,1,0:T(8,128)(2,1)S(1)} %pad_maximum_fusion.1.w0), channel_id=1, source_target_pairs={{0,3},{1,2},{2,1},{3,0},{4,7},{5,6},{6,5},{7,4},{8,11},{9,10},{10,... | collective-permute-start | bytes 1179656 | tf_op jit(solution)/shard_map/weights/ppermute | solution.py:241
  87.3 18.0 %all-to-all-start.2 = ((bf16[8,144,128]{2,1,0:T(8,128)(2,1)}), bf16[8,144,128]{2,1,0:T(8,128)(2,1)S(1)}, u32[]{:S(2)}, u32[]{:S(2)}) async-start(bf16[8,144,128]{2,1,0:T(8,128)(2,1)} %get-tuple-element.184), calls=%async_computation.2 | async-start | bytes 589824 | tf_op jit(solution)/shard_map/exchange/all_to_all | solution.py:284
  90.8 7.6 %collective-permute-start.4 = (bf16[144,256]{1,0:T(8,128)(2,1)S(1)}, bf16[144,256]{1,0:T(8,128)(2,1)S(1)}, u32[]{:S(2)}, u32[]{:S(2)}) collective-permute-start(bf16[144,256]{1,0:T(8,128)(2,1)S(1)} %get-tuple-element.183.q0), channel_id=1, source_target_pairs={{0,2},{1,3},{2,0},{3,1},{4,6},{5,7},{6,4},{7,5},{8,10},{9,11},{10,... | collective-permute-start | bytes 221192 | tf_op jit(solution)/shard_map/exchange/ppermute | solution.py:283
  92.1 7.0 %collective-permute-start.5 = (bf16[144,256]{1,0:T(8,128)(2,1)S(1)}, bf16[144,256]{1,0:T(8,128)(2,1)S(1)}, u32[]{:S(2)}, u32[]{:S(2)}) collective-permute-start(bf16[144,256]{1,0:T(8,128)(2,1)S(1)} %get-tuple-element.183.q0), channel_id=1, source_target_pairs={{0,3},{1,2},{2,1},{3,0},{4,7},{5,6},{6,5},{7,4},{8,11},{9,10},{10,... | collective-permute-start | bytes 221192 | tf_op jit(solution)/shard_map/exchange/ppermute | solution.py:283
  111.1 6.5 %collective-permute-start.6 = (bf16[144,384]{1,0:T(8,128)(2,1)S(1)}, bf16[144,384]{1,0:T(8,128)(2,1)S(1)}, u32[]{:S(2)}, u32[]{:S(2)}) collective-permute-start(bf16[144,384]{1,0:T(8,128)(2,1)S(1)} %get-tuple-element.186), channel_id=1, source_target_pairs={{0,1},{1,0},{2,3},{3,2},{4,5},{5,4},{6,7},{7,6},{8,9},{9,8},{10,11... | collective-permute-start | bytes 331784 | tf_op jit(solution)/shard_map/attend/ppermute | solution.py:297
  111.2 11.3 %collective-permute-start.7 = (bf16[144,384]{1,0:T(8,128)(2,1)S(1)}, bf16[144,384]{1,0:T(8,128)(2,1)S(1)}, u32[]{:S(2)}, u32[]{:S(2)}) collective-permute-start(bf16[144,384]{1,0:T(8,128)(2,1)S(1)} %get-tuple-element.187), channel_id=1, source_target_pairs={{0,2},{1,3},{2,0},{3,1},{4,6},{5,7},{6,4},{7,5},{8,10},{9,11},{10,... | collective-permute-start | bytes 331784 | tf_op jit(solution)/shard_map/attend/ppermute | solution.py:297
  112.8 9.6 %collective-permute-start.8 = (bf16[144,384]{1,0:T(8,128)(2,1)S(1)}, bf16[144,384]{1,0:T(8,128)(2,1)S(1)}, u32[]{:S(2)}, u32[]{:S(2)}) collective-permute-start(bf16[144,384]{1,0:T(8,128)(2,1)S(1)} %get-tuple-element.188), channel_id=1, source_target_pairs={{0,3},{1,2},{2,1},{3,0},{4,7},{5,6},{6,5},{7,4},{8,11},{9,10},{10,... | collective-permute-start | bytes 331784 | tf_op jit(solution)/shard_map/attend/ppermute | solution.py:297
  129.0 25.7 %collective-permute-start.12 = (bf16[4,144,256]{2,1,0:T(8,128)(2,1)S(1)}, bf16[4,144,256]{2,1,0:T(8,128)(2,1)S(1)}, u32[]{:S(2)}, u32[]{:S(2)}) collective-permute-start(bf16[4,144,256]{2,1,0:T(8,128)(2,1)S(1)} %pad_maximum_fusion.3), channel_id=1, source_target_pairs={{0,32},{32,0},{64,96},{96,64},{128,160},{160,128},{192,224},{224,1... | collective-permute-start | bytes 884744 | tf_op jit(solution)/shard_map/attend/ppermute | solution.py:39
  138.2 7.9 %collective-permute-start.13 = (bf16[8,64,256]{2,1,0:T(8,128)(2,1)S(1)}, bf16[8,64,256]{2,1,0:T(8,128)(2,1)S(1)}, u32[]{:S(2)}, u32[]{:S(2)}) collective-permute-start(bf16[8,64,256]{2,1,0:T(8,128)(2,1)S(1)} %get-tuple-element.272.w0), channel_id=1, source_target_pairs={{0,1},{1,0},{2,3},{3,2},{4,5},{5,4},{6,7},{7,6},{8,9},{9,8},{10,11... | collective-permute-start | bytes 786440 | tf_op jit(solution)/shard_map/weights/ppermute | solution.py:242
  138.2 13.7 %collective-permute-start.14 = (bf16[8,64,256]{2,1,0:T(8,128)(2,1)S(1)}, bf16[8,64,256]{2,1,0:T(8,128)(2,1)S(1)}, u32[]{:S(2)}, u32[]{:S(2)}) collective-permute-start(bf16[8,64,256]{2,1,0:T(8,128)(2,1)S(1)} %get-tuple-element.272.w0), channel_id=1, source_target_pairs={{0,2},{1,3},{2,0},{3,1},{4,6},{5,7},{6,4},{7,5},{8,10},{9,11},{10,... | collective-permute-start | bytes 786440 | tf_op jit(solution)/shard_map/weights/ppermute | solution.py:242
  140.1 14.6 %collective-permute-start.15 = (bf16[8,64,256]{2,1,0:T(8,128)(2,1)S(1)}, bf16[8,64,256]{2,1,0:T(8,128)(2,1)S(1)}, u32[]{:S(2)}, u32[]{:S(2)}) collective-permute-start(bf16[8,64,256]{2,1,0:T(8,128)(2,1)S(1)} %get-tuple-element.272.w0), channel_id=1, source_target_pairs={{0,3},{1,2},{2,1},{3,0},{4,7},{5,6},{6,5},{7,4},{8,11},{9,10},{10,... | collective-permute-start | bytes 786440 | tf_op jit(solution)/shard_map/weights/ppermute | solution.py:242
  161.6 6.0 collective-permute-start.19
  170.4 16.1 %all-to-all-start.3 = ((bf16[8,144,128]{2,1,0:T(8,128)(2,1)}), bf16[8,144,128]{2,1,0:T(8,128)(2,1)S(1)}, u32[]{:S(2)}, u32[]{:S(2)}) async-start(bf16[8,144,128]{2,1,0:T(8,128)(2,1)} %get-tuple-element.190), calls=%async_computation.3 | async-start | bytes 589824 | tf_op jit(solution)/shard_map/exchange/all_to_all | solution.py:284
  173.9 6.3 %collective-permute-start.21 = (bf16[144,256]{1,0:T(8,128)(2,1)S(1)}, bf16[144,256]{1,0:T(8,128)(2,1)S(1)}, u32[]{:S(2)}, u32[]{:S(2)}) collective-permute-start(bf16[144,256]{1,0:T(8,128)(2,1)S(1)} %get-tuple-element.189.q0), channel_id=1, source_target_pairs={{0,2},{1,3},{2,0},{3,1},{4,6},{5,7},{6,4},{7,5},{8,10},{9,11},{10,... | collective-permute-start | bytes 221192 | tf_op jit(solution)/shard_map/exchange/ppermute | solution.py:283
  177.1 5.3 collective-permute-start.22
  192.3 7.1 %collective-permute-start.23 = (bf16[144,384]{1,0:T(8,128)(2,1)S(1)}, bf16[144,384]{1,0:T(8,128)(2,1)S(1)}, u32[]{:S(2)}, u32[]{:S(2)}) collective-permute-start(bf16[144,384]{1,0:T(8,128)(2,1)S(1)} %get-tuple-element.192), channel_id=1, source_target_pairs={{0,1},{1,0},{2,3},{3,2},{4,5},{5,4},{6,7},{7,6},{8,9},{9,8},{10,11... | collective-permute-start | bytes 331784 | tf_op jit(solution)/shard_map/attend/ppermute | solution.py:297
  192.4 13.8 %collective-permute-start.24 = (bf16[144,384]{1,0:T(8,128)(2,1)S(1)}, bf16[144,384]{1,0:T(8,128)(2,1)S(1)}, u32[]{:S(2)}, u32[]{:S(2)}) collective-permute-start(bf16[144,384]{1,0:T(8,128)(2,1)S(1)} %get-tuple-element.193), channel_id=1, source_target_pairs={{0,2},{1,3},{2,0},{3,1},{4,6},{5,7},{6,4},{7,5},{8,10},{9,11},{10,... | collective-permute-start | bytes 331784 | tf_op jit(solution)/shard_map/attend/ppermute | solution.py:297
  196.0 10.3 %collective-permute-start.25 = (bf16[144,384]{1,0:T(8,128)(2,1)S(1)}, bf16[144,384]{1,0:T(8,128)(2,1)S(1)}, u32[]{:S(2)}, u32[]{:S(2)}) collective-permute-start(bf16[144,384]{1,0:T(8,128)(2,1)S(1)} %get-tuple-element.194), channel_id=1, source_target_pairs={{0,3},{1,2},{2,1},{3,0},{4,7},{5,6},{6,5},{7,4},{8,11},{9,10},{10,... | collective-permute-start | bytes 331784 | tf_op jit(solution)/shard_map/attend/ppermute | solution.py:297
  207.5 5.6 collective-permute-start.27
  223.7 5.6 collective-permute-start.32
  234.4 19.3 %all-to-all-start.4 = ((bf16[8,144,128]{2,1,0:T(8,128)(2,1)}), bf16[8,144,128]{2,1,0:T(8,128)(2,1)S(1)}, u32[]{:S(2)}, u32[]{:S(2)}) async-start(bf16[8,144,128]{2,1,0:T(8,128)(2,1)} %get-tuple-element.196), calls=%async_computation.4 | async-start | bytes 589824 | tf_op jit(solution)/shard_map/exchange/all_to_all | solution.py:284
  238.0 7.0 %collective-permute-start.35 = (bf16[144,256]{1,0:T(8,128)(2,1)S(1)}, bf16[144,256]{1,0:T(8,128)(2,1)S(1)}, u32[]{:S(2)}, u32[]{:S(2)}) collective-permute-start(bf16[144,256]{1,0:T(8,128)(2,1)S(1)} %get-tuple-element.195.q0), channel_id=1, source_target_pairs={{0,2},{1,3},{2,0},{3,1},{4,6},{5,7},{6,4},{7,5},{8,10},{9,11},{10,... | collective-permute-start | bytes 221192 | tf_op jit(solution)/shard_map/exchange/ppermute | solution.py:283
  239.1 6.5 %collective-permute-start.36 = (bf16[144,256]{1,0:T(8,128)(2,1)S(1)}, bf16[144,256]{1,0:T(8,128)(2,1)S(1)}, u32[]{:S(2)}, u32[]{:S(2)}) collective-permute-start(bf16[144,256]{1,0:T(8,128)(2,1)S(1)} %get-tuple-element.195.q0), channel_id=1, source_target_pairs={{0,3},{1,2},{2,1},{3,0},{4,7},{5,6},{6,5},{7,4},{8,11},{9,10},{10,... | collective-permute-start | bytes 221192 | tf_op jit(solution)/shard_map/exchange/ppermute | solution.py:283
  259.6 6.7 %collective-permute-start.38 = (bf16[144,384]{1,0:T(8,128)(2,1)S(1)}, bf16[144,384]{1,0:T(8,128)(2,1)S(1)}, u32[]{:S(2)}, u32[]{:S(2)}) collective-permute-start(bf16[144,384]{1,0:T(8,128)(2,1)S(1)} %get-tuple-element.199), channel_id=1, source_target_pairs={{0,2},{1,3},{2,0},{3,1},{4,6},{5,7},{6,4},{7,5},{8,10},{9,11},{10,... | collective-permute-start | bytes 331784 | tf_op jit(solution)/shard_map/attend/ppermute | solution.py:297
  260.6 7.8 %collective-permute-start.39 = (bf16[144,384]{1,0:T(8,128)(2,1)S(1)}, bf16[144,384]{1,0:T(8,128)(2,1)S(1)}, u32[]{:S(2)}, u32[]{:S(2)}) collective-permute-start(bf16[144,384]{1,0:T(8,128)(2,1)S(1)} %get-tuple-element.200), channel_id=1, source_target_pairs={{0,3},{1,2},{2,1},{3,0},{4,7},{5,6},{6,5},{7,4},{8,11},{9,10},{10,... | collective-permute-start | bytes 331784 | tf_op jit(solution)/shard_map/attend/ppermute | solution.py:297
  269.2 6.1 %collective-permute-start.41 = (bf16[144,256]{1,0:T(8,128)(2,1)S(1)}, bf16[144,256]{1,0:T(8,128)(2,1)S(1)}, u32[]{:S(2)}, u32[]{:S(2)}) collective-permute-start(bf16[144,256]{1,0:T(8,128)(2,1)S(1)} %attend.21.a0), channel_id=1, source_target_pairs={{0,128},{32,160},{64,192},{96,224},{128,0},{160,32},{192,64},{224,... | collective-permute-start | bytes 221192 | tf_op jit(solution)/shard_map/attend/ppermute | solution.py:38
  283.2 6.6 %collective-permute-start.45 = (bf16[144,256]{1,0:T(8,128)(2,1)S(1)}, bf16[144,256]{1,0:T(8,128)(2,1)S(1)}, u32[]{:S(2)}, u32[]{:S(2)}) collective-permute-start(bf16[144,256]{1,0:T(8,128)(2,1)S(1)} %output.10.p0.h_ref), channel_id=1, source_target_pairs={{0,128},{32,160},{64,192},{96,224},{128,0},{160,32},{192,64},{224,... | collective-permute-start | bytes 221192 | tf_op jit(solution)/shard_map/output/ppermute | solution.py:38
  296.0 16.4 %all-to-all-start.5 = ((bf16[8,144,128]{2,1,0:T(8,128)(2,1)}), bf16[8,144,128]{2,1,0:T(8,128)(2,1)S(1)}, u32[]{:S(2)}, u32[]{:S(2)}) async-start(bf16[8,144,128]{2,1,0:T(8,128)(2,1)} %get-tuple-element.202), calls=%async_computation.5 | async-start | bytes 589824 | tf_op jit(solution)/shard_map/exchange/all_to_all | solution.py:284
  299.5 6.9 %collective-permute-start.49 = (bf16[144,256]{1,0:T(8,128)(2,1)S(1)}, bf16[144,256]{1,0:T(8,128)(2,1)S(1)}, u32[]{:S(2)}, u32[]{:S(2)}) collective-permute-start(bf16[144,256]{1,0:T(8,128)(2,1)S(1)} %get-tuple-element.201.q0), channel_id=1, source_target_pairs={{0,2},{1,3},{2,0},{3,1},{4,6},{5,7},{6,4},{7,5},{8,10},{9,11},{10,... | collective-permute-start | bytes 221192 | tf_op jit(solution)/shard_map/exchange/ppermute | solution.py:283
  318.3 8.3 %collective-permute-start.52 = (bf16[144,384]{1,0:T(8,128)(2,1)S(1)}, bf16[144,384]{1,0:T(8,128)(2,1)S(1)}, u32[]{:S(2)}, u32[]{:S(2)}) collective-permute-start(bf16[144,384]{1,0:T(8,128)(2,1)S(1)} %get-tuple-element.205), channel_id=1, source_target_pairs={{0,2},{1,3},{2,0},{3,1},{4,6},{5,7},{6,4},{7,5},{8,10},{9,11},{10,... | collective-permute-start | bytes 331784 | tf_op jit(solution)/shard_map/attend/ppermute | solution.py:297
  321.6 7.6 %collective-permute-start.53 = (bf16[144,384]{1,0:T(8,128)(2,1)S(1)}, bf16[144,384]{1,0:T(8,128)(2,1)S(1)}, u32[]{:S(2)}, u32[]{:S(2)}) collective-permute-start(bf16[144,384]{1,0:T(8,128)(2,1)S(1)} %get-tuple-element.206), channel_id=1, source_target_pairs={{0,3},{1,2},{2,1},{3,0},{4,7},{5,6},{6,5},{7,4},{8,11},{9,10},{10,... | collective-permute-start | bytes 331784 | tf_op jit(solution)/shard_map/attend/ppermute | solution.py:297
  329.9 5.6 collective-permute-start.55
  342.2 6.1 %collective-permute-start.59 = (bf16[144,256]{1,0:T(8,128)(2,1)S(1)}, bf16[144,256]{1,0:T(8,128)(2,1)S(1)}, u32[]{:S(2)}, u32[]{:S(2)}) collective-permute-start(bf16[144,256]{1,0:T(8,128)(2,1)S(1)} %output.11.p0.h_ref), channel_id=1, source_target_pairs={{0,128},{32,160},{64,192},{96,224},{128,0},{160,32},{192,64},{224,... | collective-permute-start | bytes 221192 | tf_op jit(solution)/shard_map/output/ppermute | solution.py:38
  355.6 16.4 %all-to-all-start.6 = ((bf16[8,144,128]{2,1,0:T(8,128)(2,1)}), bf16[8,144,128]{2,1,0:T(8,128)(2,1)S(1)}, u32[]{:S(2)}, u32[]{:S(2)}) async-start(bf16[8,144,128]{2,1,0:T(8,128)(2,1)} %get-tuple-element.208), calls=%async_computation.6 | async-start | bytes 589824 | tf_op jit(solution)/shard_map/exchange/all_to_all | solution.py:284
  377.9 6.8 %collective-permute-start.66 = (bf16[144,384]{1,0:T(8,128)(2,1)S(1)}, bf16[144,384]{1,0:T(8,128)(2,1)S(1)}, u32[]{:S(2)}, u32[]{:S(2)}) collective-permute-start(bf16[144,384]{1,0:T(8,128)(2,1)S(1)} %get-tuple-element.211), channel_id=1, source_target_pairs={{0,2},{1,3},{2,0},{3,1},{4,6},{5,7},{6,4},{7,5},{8,10},{9,11},{10,... | collective-permute-start | bytes 331784 | tf_op jit(solution)/shard_map/attend/ppermute | solution.py:297
  379.7 7.6 %collective-permute-start.67 = (bf16[144,384]{1,0:T(8,128)(2,1)S(1)}, bf16[144,384]{1,0:T(8,128)(2,1)S(1)}, u32[]{:S(2)}, u32[]{:S(2)}) collective-permute-start(bf16[144,384]{1,0:T(8,128)(2,1)S(1)} %get-tuple-element.212), channel_id=1, source_target_pairs={{0,3},{1,2},{2,1},{3,0},{4,7},{5,6},{6,5},{7,4},{8,11},{9,10},{10,... | collective-permute-start | bytes 331784 | tf_op jit(solution)/shard_map/attend/ppermute | solution.py:297
  388.0 5.5 collective-permute-start.69
  389.8 5.3 collective-permute-start.70
  399.8 6.5 %collective-permute-start.72 = (bf16[144,256]{1,0:T(8,128)(2,1)S(1)}, bf16[144,256]{1,0:T(8,128)(2,1)S(1)}, u32[]{:S(2)}, u32[]{:S(2)}) collective-permute-start(bf16[144,256]{1,0:T(8,128)(2,1)S(1)} %output.12.p0.h_ref), channel_id=1, source_target_pairs={{0,128},{32,160},{64,192},{96,224},{128,0},{160,32},{192,64},{224,... | collective-permute-start | bytes 221192 | tf_op jit(solution)/shard_map/output/ppermute | solution.py:38
  413.7 16.4 %all-to-all-start.7 = ((bf16[8,144,128]{2,1,0:T(8,128)(2,1)}), bf16[8,144,128]{2,1,0:T(8,128)(2,1)S(1)}, u32[]{:S(2)}, u32[]{:S(2)}) async-start(bf16[8,144,128]{2,1,0:T(8,128)(2,1)} %get-tuple-element.214), calls=%async_computation.7 | async-start | bytes 589824 | tf_op jit(solution)/shard_map/exchange/all_to_all | solution.py:284
  417.2 6.9 %collective-permute-start.77 = (bf16[144,256]{1,0:T(8,128)(2,1)S(1)}, bf16[144,256]{1,0:T(8,128)(2,1)S(1)}, u32[]{:S(2)}, u32[]{:S(2)}) collective-permute-start(bf16[144,256]{1,0:T(8,128)(2,1)S(1)} %get-tuple-element.213.q0), channel_id=1, source_target_pairs={{0,2},{1,3},{2,0},{3,1},{4,6},{5,7},{6,4},{7,5},{8,10},{9,11},{10,... | collective-permute-start | bytes 221192 | tf_op jit(solution)/shard_map/exchange/ppermute | solution.py:283
  436.0 8.3 %collective-permute-start.80 = (bf16[144,384]{1,0:T(8,128)(2,1)S(1)}, bf16[144,384]{1,0:T(8,128)(2,1)S(1)}, u32[]{:S(2)}, u32[]{:S(2)}) collective-permute-start(bf16[144,384]{1,0:T(8,128)(2,1)S(1)} %get-tuple-element.217), channel_id=1, source_target_pairs={{0,2},{1,3},{2,0},{3,1},{4,6},{5,7},{6,4},{7,5},{8,10},{9,11},{10,... | collective-permute-start | bytes 331784 | tf_op jit(solution)/shard_map/attend/ppermute | solution.py:297
  439.3 7.6 %collective-permute-start.81 = (bf16[144,384]{1,0:T(8,128)(2,1)S(1)}, bf16[144,384]{1,0:T(8,128)(2,1)S(1)}, u32[]{:S(2)}, u32[]{:S(2)}) collective-permute-start(bf16[144,384]{1,0:T(8,128)(2,1)S(1)} %get-tuple-element.218), channel_id=1, source_target_pairs={{0,3},{1,2},{2,1},{3,0},{4,7},{5,6},{6,5},{7,4},{8,11},{9,10},{10,... | collective-permute-start | bytes 331784 | tf_op jit(solution)/shard_map/attend/ppermute | solution.py:297
  447.6 5.5 collective-permute-start.83
  449.4 5.2 collective-permute-start.84
  459.5 6.5 %collective-permute-start.87 = (bf16[144,256]{1,0:T(8,128)(2,1)S(1)}, bf16[144,256]{1,0:T(8,128)(2,1)S(1)}, u32[]{:S(2)}, u32[]{:S(2)}) collective-permute-start(bf16[144,256]{1,0:T(8,128)(2,1)S(1)} %output.13.p0.h_ref), channel_id=1, source_target_pairs={{0,128},{32,160},{64,192},{96,224},{128,0},{160,32},{192,64},{224,... | collective-permute-start | bytes 221192 | tf_op jit(solution)/shard_map/output/ppermute | solution.py:38
  473.3 16.4 %all-to-all-start.8 = ((bf16[8,144,128]{2,1,0:T(8,128)(2,1)}), bf16[8,144,128]{2,1,0:T(8,128)(2,1)S(1)}, u32[]{:S(2)}, u32[]{:S(2)}) async-start(bf16[8,144,128]{2,1,0:T(8,128)(2,1)} %get-tuple-element.220), calls=%async_computation.8 | async-start | bytes 589824 | tf_op jit(solution)/shard_map/exchange/all_to_all | solution.py:284
  476.8 5.7 collective-permute-start.91
  495.8 6.8 %collective-permute-start.94 = (bf16[144,384]{1,0:T(8,128)(2,1)S(1)}, bf16[144,384]{1,0:T(8,128)(2,1)S(1)}, u32[]{:S(2)}, u32[]{:S(2)}) collective-permute-start(bf16[144,384]{1,0:T(8,128)(2,1)S(1)} %get-tuple-element.223), channel_id=1, source_target_pairs={{0,2},{1,3},{2,0},{3,1},{4,6},{5,7},{6,4},{7,5},{8,10},{9,11},{10,... | collective-permute-start | bytes 331784 | tf_op jit(solution)/shard_map/attend/ppermute | solution.py:297
  497.6 7.6 %collective-permute-start.95 = (bf16[144,384]{1,0:T(8,128)(2,1)S(1)}, bf16[144,384]{1,0:T(8,128)(2,1)S(1)}, u32[]{:S(2)}, u32[]{:S(2)}) collective-permute-start(bf16[144,384]{1,0:T(8,128)(2,1)S(1)} %get-tuple-element.224), channel_id=1, source_target_pairs={{0,3},{1,2},{2,1},{3,0},{4,7},{5,6},{6,5},{7,4},{8,11},{9,10},{10,... | collective-permute-start | bytes 331784 | tf_op jit(solution)/shard_map/attend/ppermute | solution.py:297
  505.9 5.5 collective-permute-start.97
  507.7 5.3 collective-permute-start.98
  517.7 6.5 %collective-permute-start.102 = (bf16[144,256]{1,0:T(8,128)(2,1)S(1)}, bf16[144,256]{1,0:T(8,128)(2,1)S(1)}, u32[]{:S(2)}, u32[]{:S(2)}) collective-permute-start(bf16[144,256]{1,0:T(8,128)(2,1)S(1)} %output.14.p0.h_ref), channel_id=1, source_target_pairs={{0,128},{32,160},{64,192},{96,224},{128,0},{160,32},{192,64},{224,... | collective-permute-start | bytes 221192 | tf_op jit(solution)/shard_map/output/ppermute | solution.py:38
  531.6 16.4 %all-to-all-start.9 = ((bf16[8,144,128]{2,1,0:T(8,128)(2,1)}), bf16[8,144,128]{2,1,0:T(8,128)(2,1)S(1)}, u32[]{:S(2)}, u32[]{:S(2)}) async-start(bf16[8,144,128]{2,1,0:T(8,128)(2,1)} %get-tuple-element.226), calls=%async_computation.9 | async-start | bytes 589824 | tf_op jit(solution)/shard_map/exchange/all_to_all | solution.py:284
  535.1 6.9 %collective-permute-start.105 = (bf16[144,256]{1,0:T(8,128)(2,1)S(1)}, bf16[144,256]{1,0:T(8,128)(2,1)S(1)}, u32[]{:S(2)}, u32[]{:S(2)}) collective-permute-start(bf16[144,256]{1,0:T(8,128)(2,1)S(1)} %get-tuple-element.225.q0), channel_id=1, source_target_pairs={{0,2},{1,3},{2,0},{3,1},{4,6},{5,7},{6,4},{7,5},{8,10},{9,11},{10,... | collective-permute-start | bytes 221192 | tf_op jit(solution)/shard_map/exchange/ppermute | solution.py:283
  553.9 8.3 %collective-permute-start.108 = (bf16[144,384]{1,0:T(8,128)(2,1)S(1)}, bf16[144,384]{1,0:T(8,128)(2,1)S(1)}, u32[]{:S(2)}, u32[]{:S(2)}) collective-permute-start(bf16[144,384]{1,0:T(8,128)(2,1)S(1)} %get-tuple-element.229), channel_id=1, source_target_pairs={{0,2},{1,3},{2,0},{3,1},{4,6},{5,7},{6,4},{7,5},{8,10},{9,11},{10,... | collective-permute-start | bytes 331784 | tf_op jit(solution)/shard_map/attend/ppermute | solution.py:297
  557.2 7.6 %collective-permute-start.109 = (bf16[144,384]{1,0:T(8,128)(2,1)S(1)}, bf16[144,384]{1,0:T(8,128)(2,1)S(1)}, u32[]{:S(2)}, u32[]{:S(2)}) collective-permute-start(bf16[144,384]{1,0:T(8,128)(2,1)S(1)} %get-tuple-element.230), channel_id=1, source_target_pairs={{0,3},{1,2},{2,1},{3,0},{4,7},{5,6},{6,5},{7,4},{8,11},{9,10},{10,... | collective-permute-start | bytes 331784 | tf_op jit(solution)/shard_map/attend/ppermute | solution.py:297
  565.8 5.5 collective-permute-start.111
  577.7 6.5 %collective-permute-start.115 = (bf16[144,256]{1,0:T(8,128)(2,1)S(1)}, bf16[144,256]{1,0:T(8,128)(2,1)S(1)}, u32[]{:S(2)}, u32[]{:S(2)}) collective-permute-start(bf16[144,256]{1,0:T(8,128)(2,1)S(1)} %output.15), channel_id=1, source_target_pairs={{0,128},{32,160},{64,192},{96,224},{128,0},{160,32},{192,64},{224,... | collective-permute-start | bytes 221192 | tf_op jit(solution)/shard_map/output/ppermute | solution.py:38
  (95 other events, 587.7 us)
Sparse Core Ops, SparseCore 0:
  28.5 108.3 all-gather.4
  139.5 118.2 all-gather.6

commit v3 on v2

v3 whole, which is shorter than its diff:
```python
import functools

import jax
import jax.numpy as jnp
from jax import lax
from jax.experimental import pallas as pl
from jax.experimental.pallas import tpu as pltpu
from jax.sharding import PartitionSpec as P

HEADS = 32
KVH = 8
HD = 64
SHARE = HEADS // KVH
QW = SHARE * HD
EPS = 1e-05
NEG = -1e30
LOG2E = 1.4426950408889634
LOOPED = True

ZN = 8
XN = 4
SN = 8
F32 = jnp.float32
BF16 = jnp.bfloat16


def seq_pairs(mask):
    return [(i, i ^ mask) for i in range(ZN * XN)]


def section_pairs(mask):
    return [(i, i ^ mask) for i in range(SN)]


def along_z():
    return [[z * XN + x for z in range(ZN)] for x in range(XN)]


def spread(piece):
    near = [piece] + [lax.ppermute(piece, "section", section_pairs(2 * d)) for d in (1, 2, 3)]
    other = lax.ppermute(jnp.stack(near), "section", section_pairs(1))
    return near + [other]


def in_order(refs):
    out = [(2 * d, refs[d][...]) for d in range(4)]
    out += [(2 * d + 1, refs[4][d]) for d in range(4)]
    return out


def place(me, layer, piece_refs, out_ref, sems):
    def copies():
        for i, (mask, source) in enumerate(sources(piece_refs)):
            first = pl.multiple_of(jnp.bitwise_xor(me, mask) * QW, QW)
            yield pltpu.make_async_copy(source, out_ref.at[:, pl.ds(first, QW)], sems.at[i])

    @pl.when(me == layer - 1)
    def _():
        for copy in copies():
            copy.start()
        for copy in copies():
            copy.wait()


def sources(refs):
    out = [(2 * d, refs[d]) for d in range(4)]
    return out + [(2 * d + 1, refs[4].at[d]) for d in range(4)]


def place_kernel(scal, p0, p1, p2, p3, p4, out_in, out_ref, sems):
    place(scal[0], scal[3], [p0, p1, p2, p3, p4], out_ref, sems)


def project(me, gain_ref, piece_refs, w_of, q_ref, kv_ref):
    pieces = [(mask, value.astype(F32)) for mask, value in in_order(piece_refs)]
    rows = pieces[0][1].shape[0]
    width = sum(value.shape[1] for _, value in pieces)
    squares = functools.reduce(jnp.add, [value * value for _, value in pieces])
    scale = lax.rsqrt(jnp.sum(squares, axis=-1, keepdims=True) / width + EPS)
    q_sum = jnp.zeros((rows, QW), F32)
    kv_sum = jnp.zeros((rows, 2 * HD), F32)
    for mask, value in pieces:
        owner = jnp.bitwise_xor(me, mask)
        gain = gain_ref[0, pl.ds(owner, 1), 0, :].astype(F32)
        normed = (value * scale * gain).astype(BF16)
        wq, wkv = w_of(owner)
        q_sum += jnp.dot(normed, wq, preferred_element_type=F32)
        kv_sum += jnp.dot(normed, wkv, preferred_element_type=F32)
    q_ref[...] = q_sum.astype(BF16)
    pair = kv_sum.astype(BF16)
    for i in range(kv_ref.shape[0]):
        kv_ref[i] = pair


def project_kernel(
    scal, gain_ref, p0, p1, p2, p3, p4, wq_ref, wkv_ref, out_in, q_ref, kv_ref, out_ref, sems
):
    def w_of(owner):
        wq = wq_ref[pl.ds(XN * owner, XN), 0].reshape(QW, QW)
        wkv = wkv_ref[pl.ds(XN * owner, XN), 0].reshape(QW, 2 * HD)
        return wq, wkv

    refs = [p0, p1, p2, p3, p4]
    project(scal[0], gain_ref, refs, w_of, q_ref, kv_ref)
    place(scal[0], scal[3], refs, out_ref, sems)


def assemble(seq, parts, held):
    x_me = jnp.bitwise_and(seq, XN - 1)
    for d in range(XN):
        held[jnp.bitwise_xor(x_me, d)] = parts[d][...]


def first_project_kernel(
    scal, gain_ref, p0, p1, p2, p3, p4, w0, w1, w2, w3, q_ref, kv_ref, held
):
    assemble(scal[1], [w0, w1, w2, w3], held)

    def w_of(owner):
        w = held[:, owner].reshape(QW, QW + 2 * HD)
        return w[:, :QW], w[:, QW:]

    project(scal[0], gain_ref, [p0, p1, p2, p3, p4], w_of, q_ref, kv_ref)


def attend_kernel(scal, q_ref, k_ref, o_ref, *, d, blocks, tok):
    seq = scal[1]
    x_me = jnp.bitwise_and(seq, XN - 1)
    span = ZN * tok
    rows = SHARE * tok
    row = lax.broadcasted_iota(jnp.int32, (rows, span), 0)
    col = lax.broadcasted_iota(jnp.int32, (rows, span), 1)
    slack = lax.rem(row, tok) - lax.div(col, tok) * (XN * tok) - lax.rem(col, tok)
    asker = seq - x_me + jnp.bitwise_xor(x_me, d)
    visible = slack >= (x_me - asker) * tok
    factor = HD**-0.5 * LOG2E
    q_parts = []
    for b in range(blocks):
        q_rows = q_ref[b * tok : (b + 1) * tok, :]
        q_parts += [q_rows[:, h * HD : (h + 1) * HD] for h in range(SHARE)]
    q_rows = jnp.concatenate(q_parts, axis=0)
    q_rows = jnp.concatenate([q_rows, jnp.zeros((blocks * rows, HD), BF16)], axis=1)
    pairs = []
    scores = {}
    for kb in range(blocks):
        pair = k_ref[:, kb * tok : (kb + 1) * tok, :].reshape(span, 2 * HD)
        s = lax.dot_general(
            q_rows[kb * rows :], pair, (((1,), (1,)), ((), ())), preferred_element_type=F32
        )
        pairs.append(pair)
        for b in range(kb, blocks):
            part = s[(b - kb) * rows : (b - kb + 1) * rows]
            scores[b, kb] = jnp.where(visible, part, NEG) if b == kb else part
    peaks = []
    for b in range(blocks):
        peak = functools.reduce(jnp.maximum, [scores[b, kb] for kb in range(b + 1)])
        peaks.append(jnp.max(peak, axis=-1, keepdims=True) * factor)
    totals = [jnp.zeros((rows, span), F32) for _ in range(blocks)]
    sums = [jnp.zeros((rows, 2 * HD), F32) for _ in range(blocks)]
    for kb in range(blocks):
        probs = []
        for b in range(kb, blocks):
            p = jnp.exp2(scores[b, kb] * factor - peaks[b])
            totals[b] += p
            probs.append(p.astype(BF16))
        got = jnp.dot(jnp.concatenate(probs, axis=0), pairs[kb], preferred_element_type=F32)
        for b in range(kb, blocks):
            sums[b] += got[(b - kb) * rows : (b - kb + 1) * rows]
    lane = lax.broadcasted_iota(jnp.int32, (tok, 2 * HD), 1)
    for b in range(blocks):
        total = jnp.sum(totals[b], axis=-1, keepdims=True)
        result = (sums[b][:, HD:] / total).astype(BF16)
        weight = peaks[b] + jnp.log(total) * LOG2E
        high = weight.astype(BF16).astype(F32)
        low = weight - high
        notes = jnp.zeros((tok, 2 * HD), F32)
        for h in range(SHARE):
            part = slice(h * tok, (h + 1) * tok)
            notes = jnp.where(lane == h, high[part], notes)
            notes = jnp.where(lane == SHARE + h, low[part], notes)
        o_ref[b * tok : (b + 1) * tok, :] = jnp.concatenate(
            [result[h * tok : (h + 1) * tok] for h in range(SHARE)] + [notes.astype(BF16)], axis=1
        )


def combine_kernel(scal, o0, o1, o2, o3, a_ref):
    parts = [o0[...], o1[...], o2[...], o3[...]]
    notes = [part[:, QW:].astype(F32) for part in parts]
    for h in range(SHARE):
        weights = [n[:, h : h + 1] + n[:, SHARE + h : SHARE + h + 1] for n in notes]
        peak = functools.reduce(jnp.maximum, weights)
        weights = [jnp.exp2(w - peak) for w in weights]
        total = functools.reduce(jnp.add, weights)
        cols = slice(h * HD, (h + 1) * HD)
        mixed = functools.reduce(
            jnp.add, [w / total * part[:, cols].astype(F32) for w, part in zip(weights, parts)]
        )
        a_ref[:, cols] = mixed.astype(BF16)


def output(me, piece_refs, h_ref, w_of, o_ref):
    total = h_ref[...].astype(F32)
    update = jnp.zeros(total.shape, F32)
    for mask, value in in_order(piece_refs):
        update += jnp.dot(value, w_of(jnp.bitwise_xor(me, mask)), preferred_element_type=F32)
    o_ref[...] = (total + update).astype(BF16)


def output_kernel(scal, a0, a1, a2, a3, a4, h_ref, w_ref, o_ref):
    def w_of(owner):
        return w_ref[pl.ds(XN * owner, XN), 0].reshape(QW, QW)

    output(scal[0], [a0, a1, a2, a3, a4], h_ref, w_of, o_ref)


def first_output_kernel(scal, a0, a1, a2, a3, a4, h_ref, w0, w1, w2, w3, o_ref, held):
    assemble(scal[1], [w0, w1, w2, w3], held)
    output(scal[0], [a0, a1, a2, a3, a4], h_ref, lambda owner: held[:, owner].reshape(QW, QW), o_ref)


def whole(shape):
    return pl.BlockSpec(shape, lambda i, scal: (0,) * len(shape))


def in_place():
    return pl.BlockSpec(memory_space=pl.ANY)


def call(kernel, scal, args, in_specs, out_shape, flops, bytes_accessed, exps=0, scratch=(), own=None):
    outs = out_shape if isinstance(out_shape, list) else [out_shape]
    out_specs = [whole(o.shape) for o in outs]
    aliases = {}
    if own is not None:
        out_specs[own[1]] = in_place()
        aliases = {own[0] + 1: own[1]}
    single = not isinstance(out_shape, list)
    return pl.pallas_call(
        kernel,
        out_shape=out_shape,
        grid_spec=pltpu.PrefetchScalarGridSpec(
            num_scalar_prefetch=1,
            grid=(1,),
            in_specs=in_specs,
            out_specs=out_specs[0] if single else out_specs,
            scratch_shapes=list(scratch),
        ),
        input_output_aliases=aliases,
        compiler_params=pltpu.CompilerParams(vmem_limit_bytes=48 * 1024 * 1024),
        cost_estimate=pl.CostEstimate(flops=flops, bytes_accessed=bytes_accessed, transcendentals=exps),
    )(scal, *args)


def local(inputs, norm_gain, w_query, w_key, w_value, w_out):
    blocks, tok, width = inputs.shape
    rows = blocks * tok
    me = lax.axis_index("section")
    seq = lax.axis_index("seq")
    layers = lax.axis_size("section")
    shard = w_query.shape[1]
    qkv_w = QW + 2 * HD
    all_w = QW + qkv_w

    def cut(w):
        return w[0].reshape(shard, SN, -1).transpose(1, 0, 2)

    gain_rows = jnp.pad(norm_gain.reshape(4, width // 4), ((0, 12), (0, all_w - width // 4)))
    mine = jnp.concatenate([cut(w_query), cut(w_out), cut(w_key), cut(w_value)], axis=-1)
    mine = jnp.concatenate([mine, jnp.broadcast_to(gain_rows[None], (SN, 16, all_w))], axis=1)
    by_layer = lax.all_to_all(mine, "section", split_axis=0, concat_axis=0, tiled=True)
    gains = by_layer[:, shard : shard + 4, : width // 4].reshape(layers, SN, 1, QW)

    with jax.named_scope("weights"):
        early = lax.all_gather(by_layer[1:4, :shard], "seq", axis=0)
        late = lax.all_gather(by_layer[4:, :shard], "seq", axis=0)
        first = jnp.broadcast_to(by_layer[None, 0, :shard], (ZN, shard, all_w))
        first = lax.all_to_all(
            first, "seq", split_axis=0, concat_axis=0, tiled=True, axis_index_groups=along_z()
        )
        first_qkv = jnp.concatenate([first[:, :, :QW], first[:, :, 2 * QW :]], axis=-1)
        first_out = first[:, :, QW : 2 * QW]
        first_qkv = [first_qkv] + [lax.ppermute(first_qkv, "seq", seq_pairs(d)) for d in (1, 2, 3)]
        first_out = [first_out] + [lax.ppermute(first_out, "seq", seq_pairs(d)) for d in (1, 2, 3)]

    flat = inputs.reshape(rows, width)

    def input_piece(mask):
        return lax.dynamic_slice_in_dim(flat, jnp.bitwise_xor(me, mask) * QW, QW, 1)

    pieces = [input_piece(2 * d) for d in range(4)]
    pieces.append(jnp.stack([input_piece(2 * d + 1) for d in range(4)]))

    piece_shape = jax.ShapeDtypeStruct((rows, QW), BF16)
    piece_specs = [whole((rows, QW))] * 4 + [whole((4, rows, QW))]
    kv_shape = jax.ShapeDtypeStruct((ZN, rows, 2 * HD), BF16)
    part_shape = jax.ShapeDtypeStruct((rows, QW + 2 * HD), BF16)
    out_shape = jax.ShapeDtypeStruct((rows, width), BF16)
    gain_spec = pl.BlockSpec((1, SN, 1, QW), lambda i, scal: (scal[3], 0, 0, 0))
    sems = [pltpu.SemaphoreType.DMA((SN,))]
    seq_keys = ZN * XN * tok
    project_cost = (2 * rows * width * qkv_w, 2 * (width * qkv_w + rows * width))
    output_cost = (2 * rows * width * QW, 2 * (width * QW + rows * width))

    def weight_spec(width_, index):
        return pl.BlockSpec((ZN * XN, 1, shard, width_), lambda i, scal: (0, scal[2], 0, index))

    def exchange(q, kv):
        with jax.named_scope("exchange"):
            qs = [q] + [lax.ppermute(q, "seq", seq_pairs(d)) for d in (1, 2, 3)]
            kv = lax.all_to_all(
                kv, "seq", split_axis=0, concat_axis=0, tiled=True, axis_index_groups=along_z()
            )
        return qs, kv

    def attend(scal, qs, kv):
        parts = [None] * XN
        with jax.named_scope("attend"):
            for d in (2, 1, 3, 0):
                part = call(
                    functools.partial(attend_kernel, d=d, blocks=blocks, tok=tok),
                    scal,
                    (qs[d], kv),
                    [whole((rows, QW)), whole(kv_shape.shape)],
                    part_shape,
                    SHARE * tok * seq_keys * 128 * 6,
                    2 * (ZN * rows * 128 + 3 * rows * QW),
                    SHARE * tok * seq_keys * 6 // 4,
                )
                parts[d] = lax.ppermute(part, "seq", seq_pairs(d)) if d else part
            attended = call(
                combine_kernel,
                scal,
                parts,
                [whole(part_shape.shape)] * XN,
                piece_shape,
                10 * rows * QW,
                10 * rows * QW,
            )
            return spread(attended)

    def numbers(slot, layer):
        return jnp.stack([jnp.asarray(v, jnp.int32) for v in (me, seq, slot, layer)])

    scal = numbers(0, 0)
    with jax.named_scope("project"):
        q, kv = call(
            first_project_kernel,
            scal,
            (gains, *pieces, *first_qkv),
            [gain_spec] + piece_specs + [whole((ZN, shard, qkv_w))] * XN,
            [piece_shape, kv_shape],
            *project_cost,
            scratch=[pltpu.VMEM((XN, ZN, shard, qkv_w), BF16)],
        )
    qs, kv = exchange(q, kv)
    kv, first_out = lax.optimization_barrier((kv, first_out))
    heads = attend(scal, qs, kv)
    with jax.named_scope("output"):
        own = call(
            first_output_kernel,
            scal,
            (*heads, pieces[0], *first_out),
            piece_specs + [whole((rows, QW))] + [whole((ZN, shard, QW))] * XN,
            piece_shape,
            *output_cost,
            scratch=[pltpu.VMEM((XN, ZN, shard, QW), BF16)],
        )
        pieces = spread(own)
    out = jnp.zeros((rows, width), BF16)

    def step(group, first_layer):
        def body(layer, carry):
            pieces, out = carry
            scal = numbers(layer - first_layer, layer)
            with jax.named_scope("project"):
                q, kv, out = call(
                    project_kernel,
                    scal,
                    (gains, *pieces, group, group, out),
                    [gain_spec] + piece_specs + [weight_spec(QW, 0), weight_spec(2 * HD, 4), in_place()],
                    [piece_shape, kv_shape, out_shape],
                    *project_cost,
                    scratch=sems,
                    own=(8, 2),
                )
            heads = attend(scal, *exchange(q, kv))
            with jax.named_scope("output"):
                own = call(
                    output_kernel,
                    scal,
                    (*heads, pieces[0], group),
                    piece_specs + [whole((rows, QW)), weight_spec(QW, 1)],
                    piece_shape,
                    *output_cost,
                )
                return spread(own), out

        return body

    carry = (pieces, out)
    for group, begin, end in ((early, 1, 4), (late, 4, layers)):
        if LOOPED:
            carry = lax.fori_loop(begin, end, step(group, begin), carry)
        else:
            for layer in range(begin, end):
                carry = step(group, begin)(layer, carry)
    pieces, out = carry
    out = call(
        place_kernel,
        numbers(0, layers),
        (*pieces, out),
        piece_specs + [in_place()],
        out_shape,
        0,
        4 * rows * width,
        scratch=sems,
        own=(5, 0),
    )
    return out.reshape(1, blocks, tok, width)


def solution(mesh):
    in_specs = (
        P(None, "seq", None),
        P("section", None),
        P("section", "seq", None),
        P("section", "seq", None),
        P("section", "seq", None),
        P("section", "seq", None),
    )
    out_specs = P("section", None, "seq", None)
    return jax.shard_map(local, mesh=mesh, in_specs=in_specs, out_specs=out_specs, check_vma=False)
```

time: 616 us -> 583 us (0.946)
  the two profiles are of different devices: /device:TPU:25 before, /device:TPU:1 now
where the time goes in v3:
time: 583 us; the launch traced here: 574 us
  starting transfers between devices  195 us (33%)
  waiting for transfers between devices  193 us (33%)
  Pallas kernels  102 us (17%)
  blocking collectives  50 us (9%)
  between operations  13.8 us (2%)
  loops' own time  9.52 us (2%)
  local copies, waits for them, and re-layouts  7.83 us (1%)
    pallas_call x57, Pallas kernels, call(): pl.pallas_call(kernel, out_shape=out_shape, grid_spec=pltpu.PrefetchScala...  102 us
    all_to_all x8, waiting for transfers between devices, exchange(): lax.all_to_all(kv, 'seq', split_axis=0, concat_axis=0, tiled=True, axis_i...  60 us
    ppermute x48, starting transfers between devices, spread(): lax.ppermute(piece, 'section', section_pairs(2 * d))  54.9 us
    ppermute x48, waiting for transfers between devices, spread(): lax.ppermute(piece, 'section', section_pairs(2 * d))  49.7 us
    ppermute x16, starting transfers between devices, spread(): other = lax.ppermute(jnp.stack(near), 'section', section_pairs(1))  45.5 us
    all_to_all x8, starting transfers between devices, exchange(): lax.all_to_all(kv, 'seq', split_axis=0, concat_axis=0, tiled=True, axis_i...  33.8 us
    all_to_all x1, blocking collectives, local(): lax.all_to_all(first, 'seq', split_axis=0, concat_axis=0, tiled=True, axi...  31.2 us
    ppermute x24, starting transfers between devices, attend(): parts[d] = lax.ppermute(part, 'seq', seq_pairs(d)) if d else part  29.2 us
  transfers between devices with their start and end apart: 128, of which 89 were waited for; matrix products, arithmetic and copies ran while one was open for 1% of the time, Pallas kernels for 13%

profile of v3, /device:TPU:1, one launch (start us, length us, event | category | flops | bytes accessed | tf_op | source)
XLA Modules:
  0.0 573.8 jit_solution(5271309715130947603)
XLA Ops:
  11.5 18.8 %all_to_all.27 = bf16[8,80,640]{2,1,0:T(8,128)(2,1)S(1)} all-to-all(bf16[8,80,640]{2,1,0:T(8,128)(2,1)S(1)} %copy.36), channel_id=1, replica_groups=mesh['section'=8,'seq'=32] {'section'}, dimensions={0} | all-to-all | bytes 1638400 | tf_op jit(solution)/shard_map/all_to_all | solution.py:269
  32.0 31.2 %all_to_all.28 = bf16[8,64,640]{2,1,0:T(8,128)(2,1)S(1)} all-to-all(bf16[8,64,640]{2,1,0:T(8,128)(2,1)S(1)} %broadcast_in_dim.18), channel_id=1, replica_groups={{0,4,8,12,16,20,24,28},{1,5,9,13,17,21,25,29},{2,6,10,14,18,22,26,30},{..., dimensions={0} | all-to-all | bytes 1310720 | tf_op jit(solution)/shard_map/weights/all_to_all | solution.py:276
  64.7 2.4 collective-permute-start.29
  68.7 3.6 collective-permute-done.28.w1
  72.3 10.6 %collective-permute-done.29.w2 = bf16[8,64,384]{2,1,0:T(8,128)(2,1)S(1)} collective-permute-done((bf16[8,64,384]{2,1,0:T(8,128)(2,1)S(1)}, bf16[8,64,384]{2,1,0:T(8,128)(2,1)S(1)}, u32[]{:S(2)}, u32[]{:S(2)}) %collective-permute-start.29) | collective-permute-done | bytes 393248 | tf_op jit(solution)/shard_map/weights/ppermute | solution.py:281
  84.8 4.5 all-to-all-start.4
  90.7 2.5 collective-permute-start.33
  93.8 7.9 %collective-permute-done.31.w1 = bf16[8,64,256]{2,1,0:T(8,128)(2,1)S(1)} collective-permute-done((bf16[8,64,256]{2,1,0:T(8,128)(2,1)S(1)}, bf16[8,64,256]{2,1,0:T(8,128)(2,1)S(1)}, u32[]{:S(2)}, u32[]{:S(2)}) %collective-permute-start.31) | collective-permute-done | bytes 262176 | tf_op jit(solution)/shard_map/weights/ppermute | solution.py:282
  101.8 10.9 %collective-permute-done.32.w2 = bf16[8,64,256]{2,1,0:T(8,128)(2,1)S(1)} collective-permute-done((bf16[8,64,256]{2,1,0:T(8,128)(2,1)S(1)}, bf16[8,64,256]{2,1,0:T(8,128)(2,1)S(1)}, u32[]{:S(2)}, u32[]{:S(2)}) %collective-permute-start.32) | collective-permute-done | bytes 262176 | tf_op jit(solution)/shard_map/weights/ppermute | solution.py:282
  114.3 2.5 collective-permute-start.39
  124.0 2.3 collective-permute-done.37.o2
  126.4 3.8 collective-permute-done.35.o1
  131.7 3.7 collective-permute-start.42
  137.6 7.1 %collective-permute-start.43 = (bf16[4,144,256]{2,1,0:T(8,128)(2,1)S(1)}, bf16[4,144,256]{2,1,0:T(8,128)(2,1)S(1)}, u32[]{:S(2)}, u32[]{:S(2)}) collective-permute-start(bf16[4,144,256]{2,1,0:T(8,128)(2,1)S(1)} %pad_maximum_fusion.7), channel_id=1, source_target_pairs={{0,32},{32,0},{64,96},{96,64},{128,160},{160,128},{192,224},{224,1... | collective-permute-start | bytes 884744 | tf_op jit(solution)/shard_map/attend/ppermute | solution.py:41
  147.6 3.6 collective-permute-start.45
  151.1 3.3 collective-permute-done.45
  159.0 177.0 %while.54 = (s32[]{:T(128)}, bf16[144,256]{1,0:T(8,128)(2,1)S(1)}, bf16[144,256]{1,0:T(8,128)(2,1)S(1)}, bf16[144,256]{1,0:T(8,128)(2,1)S(1)}, bf16[144,256]{1,0...) while((s32[]{:T(128)}, bf16[144,256]{1,0:T(8,128)(2,1)S(1)}, ...), condition=%wide.region_1.2_spmd, body=%wide.region_0.1_spmd.sunk | while | flops 1284710400 | bytes 14787309 | solution.py:402
  159.1 3.5 project.24
  162.6 6.7 %all-to-all-start = ((bf16[8,144,128]{2,1,0:T(8,128)(2,1)}), bf16[8,144,128]{2,1,0:T(8,128)(2,1)S(1)}, u32[]{:S(2)}, u32[]{:S(2)}) async-start(bf16[8,144,128]{2,1,0:T(8,128)(2,1)} %get-tuple-element.1001), calls=%async_computation | async-start | bytes 589824 | tf_op jit(solution)/shard_map/while/body/eval_jaxpr/exchange/all_to_all | solution.py:309
  173.7 10.1 %all-to-all-done.k_ref = bf16[8,144,128]{2,1,0:T(8,128)(2,1)S(1)} async-done(((bf16[8,144,128]{2,1,0:T(8,128)(2,1)}), bf16[8,144,128]{2,1,0:T(8,128)(2,1)S(1)}, u32[]{:S(2)}, u32[]{:S(2)}) %all-to-all-start) | async-done | bytes 294944 | tf_op jit(solution)/shard_map/while/body/eval_jaxpr/exchange/all_to_all | solution.py:309
  185.3 2.9 collective-permute-start.5
  203.3 3.8 collective-permute-start.9
  208.3 2.1 output.24
  220.5 3.6 project.24
  224.1 3.4 all-to-all-start
  230.9 4.5 collective-permute-done.4.q_ref
  235.4 8.0 %all-to-all-done.k_ref = bf16[8,144,128]{2,1,0:T(8,128)(2,1)S(1)} async-done(((bf16[8,144,128]{2,1,0:T(8,128)(2,1)}), bf16[8,144,128]{2,1,0:T(8,128)(2,1)S(1)}, u32[]{:S(2)}, u32[]{:S(2)}) %all-to-all-start) | async-done | bytes 294944 | tf_op jit(solution)/shard_map/while/body/eval_jaxpr/exchange/all_to_all | solution.py:309
  253.1 2.5 collective-permute-done.5.o3
  263.2 2.9 collective-permute-start.9
  267.3 2.1 output.24
  279.1 3.4 project.24
  282.5 5.4 all-to-all-start
  292.4 8.0 %all-to-all-done.k_ref = bf16[8,144,128]{2,1,0:T(8,128)(2,1)S(1)} async-done(((bf16[8,144,128]{2,1,0:T(8,128)(2,1)}), bf16[8,144,128]{2,1,0:T(8,128)(2,1)S(1)}, u32[]{:S(2)}, u32[]{:S(2)}) %all-to-all-start) | async-done | bytes 294944 | tf_op jit(solution)/shard_map/while/body/eval_jaxpr/exchange/all_to_all | solution.py:309
  319.9 3.1 collective-permute-start.9
  324.2 2.1 output.24
  332.7 2.1 collective-permute-start.13
  336.0 229.4 %while.55 = (s32[]{:T(128)}, bf16[144,256]{1,0:T(8,128)(2,1)S(1)}, bf16[144,256]{1,0:T(8,128)(2,1)S(1)}, bf16[144,256]{1,0:T(8,128)(2,1)S(1)}, bf16[144,256]{1,0...) while((s32[]{:T(128)}, bf16[144,256]{1,0:T(8,128)(2,1)S(1)}, ...), condition=%wide.region_3.4_spmd, body=%wide.region_2.3_spmd.sunk | while | flops 1284710400 | bytes 14787321 | solution.py:402
  345.2 3.4 project.25
  348.6 3.4 all-to-all-start.1
  352.0 2.3 collective-permute-start.18
  356.5 8.5 %all-to-all-done.1.k_ref = bf16[8,144,128]{2,1,0:T(8,128)(2,1)S(1)} async-done(((bf16[8,144,128]{2,1,0:T(8,128)(2,1)}), bf16[8,144,128]{2,1,0:T(8,128)(2,1)S(1)}, u32[]{:S(2)}, u32[]{:S(2)}) %all-to-all-start.1) | async-done | bytes 294944 | tf_op jit(solution)/shard_map/while/body/eval_jaxpr/exchange/all_to_all | solution.py:309
  366.6 2.3 collective-permute-start.19
  384.0 3.4 collective-permute-start.23
  388.6 2.1 output.25
  397.1 2.1 collective-permute-start.27
  400.5 3.4 project.25
  403.9 3.4 all-to-all-start.1
  411.8 8.5 %all-to-all-done.1.k_ref = bf16[8,144,128]{2,1,0:T(8,128)(2,1)S(1)} async-done(((bf16[8,144,128]{2,1,0:T(8,128)(2,1)}), bf16[8,144,128]{2,1,0:T(8,128)(2,1)S(1)}, u32[]{:S(2)}, u32[]{:S(2)}) %all-to-all-start.1) | async-done | bytes 294944 | tf_op jit(solution)/shard_map/while/body/eval_jaxpr/exchange/all_to_all | solution.py:309
  439.1 3.1 collective-permute-start.23
  443.5 2.1 output.25
  452.0 2.1 collective-permute-start.27
  455.3 3.4 project.25
  458.7 3.4 all-to-all-start.1
  462.2 2.3 collective-permute-start.18
  466.7 8.5 %all-to-all-done.1.k_ref = bf16[8,144,128]{2,1,0:T(8,128)(2,1)S(1)} async-done(((bf16[8,144,128]{2,1,0:T(8,128)(2,1)}), bf16[8,144,128]{2,1,0:T(8,128)(2,1)S(1)}, u32[]{:S(2)}, u32[]{:S(2)}) %all-to-all-start.1) | async-done | bytes 294944 | tf_op jit(solution)/shard_map/while/body/eval_jaxpr/exchange/all_to_all | solution.py:309
  476.7 2.3 collective-permute-start.19
  494.1 3.4 collective-permute-start.23
  498.7 2.1 output.25
  507.2 2.1 collective-permute-start.27
  510.6 3.4 project.25
  514.0 3.4 all-to-all-start.1
  521.9 8.5 %all-to-all-done.1.k_ref = bf16[8,144,128]{2,1,0:T(8,128)(2,1)S(1)} async-done(((bf16[8,144,128]{2,1,0:T(8,128)(2,1)}), bf16[8,144,128]{2,1,0:T(8,128)(2,1)S(1)}, u32[]{:S(2)}, u32[]{:S(2)}) %all-to-all-start.1) | async-done | bytes 294944 | tf_op jit(solution)/shard_map/while/body/eval_jaxpr/exchange/all_to_all | solution.py:309
  549.3 3.1 collective-permute-start.23
  553.6 2.1 output.25
  (312 shorter events, 253.4 us)
Async XLA Ops:
  6.5 152.4 %all-gather.5.cloned.1.call-start = ((), (), s32[]{:S(2)}) async-start(), calls=%async_computation.5 | async-start | bytes 8110080 | tf_op jit(solution)/shard_map/weights/all_gather | solution.py:273
  31.1 304.9 %all-gather.7.cloned.1.call-start = ((), (), s32[]{:S(2)}) async-start(), calls=%async_computation.6 | async-start | bytes 10813440 | tf_op jit(solution)/shard_map/weights/all_gather | solution.py:274
  63.4 8.9 %collective-permute-start.28 = (bf16[8,64,384]{2,1,0:T(8,128)(2,1)S(1)}, bf16[8,64,384]{2,1,0:T(8,128)(2,1)S(1)}, u32[]{:S(2)}, u32[]{:S(2)}) collective-permute-start(bf16[8,64,384]{2,1,0:T(8,128)(2,1)S(1)} %pad_maximum_fusion.5.w0), channel_id=1, source_target_pairs={{0,1},{1,0},{2,3},{3,2},{4,5},{5,4},{6,7},{7,6},{8,9},{9,8},{10,11... | collective-permute-start | bytes 1179656 | tf_op jit(solution)/shard_map/weights/ppermute | solution.py:281
  64.7 18.2 %collective-permute-start.29 = (bf16[8,64,384]{2,1,0:T(8,128)(2,1)S(1)}, bf16[8,64,384]{2,1,0:T(8,128)(2,1)S(1)}, u32[]{:S(2)}, u32[]{:S(2)}) collective-permute-start(bf16[8,64,384]{2,1,0:T(8,128)(2,1)S(1)} %pad_maximum_fusion.5.w0), channel_id=1, source_target_pairs={{0,2},{1,3},{2,0},{3,1},{4,6},{5,7},{6,4},{7,5},{8,10},{9,11},{10,... | collective-permute-start | bytes 1179656 | tf_op jit(solution)/shard_map/weights/ppermute | solution.py:281
  67.1 15.7 %collective-permute-start.30 = (bf16[8,64,384]{2,1,0:T(8,128)(2,1)S(1)}, bf16[8,64,384]{2,1,0:T(8,128)(2,1)S(1)}, u32[]{:S(2)}, u32[]{:S(2)}) collective-permute-start(bf16[8,64,384]{2,1,0:T(8,128)(2,1)S(1)} %pad_maximum_fusion.5.w0), channel_id=1, source_target_pairs={{0,3},{1,2},{2,1},{3,0},{4,7},{5,6},{6,5},{7,4},{8,11},{9,10},{10,... | collective-permute-start | bytes 1179656 | tf_op jit(solution)/shard_map/weights/ppermute | solution.py:281
  84.8 27.9 %all-to-all-start.4 = ((bf16[8,144,128]{2,1,0:T(8,128)(2,1)}), bf16[8,144,128]{2,1,0:T(8,128)(2,1)S(1)}, u32[]{:S(2)}, u32[]{:S(2)}) async-start(bf16[8,144,128]{2,1,0:T(8,128)(2,1)} %get-tuple-element.689), calls=%async_computation.4 | async-start | bytes 589824 | tf_op jit(solution)/shard_map/exchange/all_to_all | solution.py:309
  89.3 12.4 %collective-permute-start.31 = (bf16[8,64,256]{2,1,0:T(8,128)(2,1)S(1)}, bf16[8,64,256]{2,1,0:T(8,128)(2,1)S(1)}, u32[]{:S(2)}, u32[]{:S(2)}) collective-permute-start(bf16[8,64,256]{2,1,0:T(8,128)(2,1)S(1)} %get-tuple-element.691.w0), channel_id=1, source_target_pairs={{0,1},{1,0},{2,3},{3,2},{4,5},{5,4},{6,7},{7,6},{8,9},{9,8},{10,11... | collective-permute-start | bytes 786440 | tf_op jit(solution)/shard_map/weights/ppermute | solution.py:282
  89.3 23.4 %collective-permute-start.32 = (bf16[8,64,256]{2,1,0:T(8,128)(2,1)S(1)}, bf16[8,64,256]{2,1,0:T(8,128)(2,1)S(1)}, u32[]{:S(2)}, u32[]{:S(2)}) collective-permute-start(bf16[8,64,256]{2,1,0:T(8,128)(2,1)S(1)} %get-tuple-element.691.w0), channel_id=1, source_target_pairs={{0,2},{1,3},{2,0},{3,1},{4,6},{5,7},{6,4},{7,5},{8,10},{9,11},{10,... | collective-permute-start | bytes 786440 | tf_op jit(solution)/shard_map/weights/ppermute | solution.py:282
  90.7 22.0 %collective-permute-start.33 = (bf16[8,64,256]{2,1,0:T(8,128)(2,1)S(1)}, bf16[8,64,256]{2,1,0:T(8,128)(2,1)S(1)}, u32[]{:S(2)}, u32[]{:S(2)}) collective-permute-start(bf16[8,64,256]{2,1,0:T(8,128)(2,1)S(1)} %get-tuple-element.691.w0), channel_id=1, source_target_pairs={{0,3},{1,2},{2,1},{3,0},{4,7},{5,6},{6,5},{7,4},{8,11},{9,10},{10,... | collective-permute-start | bytes 786440 | tf_op jit(solution)/shard_map/weights/ppermute | solution.py:282
  93.2 19.6 %collective-permute-start.38 = (bf16[144,256]{1,0:T(8,128)(2,1)S(1)}, bf16[144,256]{1,0:T(8,128)(2,1)S(1)}, u32[]{:S(2)}, u32[]{:S(2)}) collective-permute-start(bf16[144,256]{1,0:T(8,128)(2,1)S(1)} %get-tuple-element.688.q_ref), channel_id=1, source_target_pairs={{0,3},{1,2},{2,1},{3,0},{4,7},{5,6},{6,5},{7,4},{8,11},{9,10},{10,... | collective-permute-start | bytes 221192 | tf_op jit(solution)/shard_map/exchange/ppermute | solution.py:308
  93.4 23.5 %collective-permute-start.36 = (bf16[144,256]{1,0:T(8,128)(2,1)S(1)}, bf16[144,256]{1,0:T(8,128)(2,1)S(1)}, u32[]{:S(2)}, u32[]{:S(2)}) collective-permute-start(bf16[144,256]{1,0:T(8,128)(2,1)S(1)} %get-tuple-element.688.q_ref), channel_id=1, source_target_pairs={{0,2},{1,3},{2,0},{3,1},{4,6},{5,7},{6,4},{7,5},{8,10},{9,11},{10,... | collective-permute-start | bytes 221192 | tf_op jit(solution)/shard_map/exchange/ppermute | solution.py:308
  101.7 17.6 %collective-permute-start.34 = (bf16[144,256]{1,0:T(8,128)(2,1)S(1)}, bf16[144,256]{1,0:T(8,128)(2,1)S(1)}, u32[]{:S(2)}, u32[]{:S(2)}) collective-permute-start(bf16[144,256]{1,0:T(8,128)(2,1)S(1)} %get-tuple-element.688.q_ref), channel_id=1, source_target_pairs={{0,1},{1,0},{2,3},{3,2},{4,5},{5,4},{6,7},{7,6},{8,9},{9,8},{10,11... | collective-permute-start | bytes 221192 | tf_op jit(solution)/shard_map/exchange/ppermute | solution.py:308
  114.3 9.7 %collective-permute-start.39 = (bf16[144,384]{1,0:T(8,128)(2,1)S(1)}, bf16[144,384]{1,0:T(8,128)(2,1)S(1)}, u32[]{:S(2)}, u32[]{:S(2)}) collective-permute-start(bf16[144,384]{1,0:T(8,128)(2,1)S(1)} %attend.78), channel_id=1, source_target_pairs={{0,3},{1,2},{2,1},{3,0},{4,7},{5,6},{6,5},{7,4},{8,11},{9,10},{10,... | collective-permute-start | bytes 331784 | tf_op jit(solution)/shard_map/attend/ppermute | solution.py:328
  118.4 7.9 %collective-permute-start.37 = (bf16[144,384]{1,0:T(8,128)(2,1)S(1)}, bf16[144,384]{1,0:T(8,128)(2,1)S(1)}, u32[]{:S(2)}, u32[]{:S(2)}) collective-permute-start(bf16[144,384]{1,0:T(8,128)(2,1)S(1)} %attend.77), channel_id=1, source_target_pairs={{0,2},{1,3},{2,0},{3,1},{4,6},{5,7},{6,4},{7,5},{8,10},{9,11},{10,... | collective-permute-start | bytes 331784 | tf_op jit(solution)/shard_map/attend/ppermute | solution.py:328
  120.9 9.3 %collective-permute-start.35 = (bf16[144,384]{1,0:T(8,128)(2,1)S(1)}, bf16[144,384]{1,0:T(8,128)(2,1)S(1)}, u32[]{:S(2)}, u32[]{:S(2)}) collective-permute-start(bf16[144,384]{1,0:T(8,128)(2,1)S(1)} %attend.76), channel_id=1, source_target_pairs={{0,1},{1,0},{2,3},{3,2},{4,5},{5,4},{6,7},{7,6},{8,9},{9,8},{10,11... | collective-permute-start | bytes 331784 | tf_op jit(solution)/shard_map/attend/ppermute | solution.py:328
  131.7 5.9 %collective-permute-start.42 = (bf16[144,256]{1,0:T(8,128)(2,1)S(1)}, bf16[144,256]{1,0:T(8,128)(2,1)S(1)}, u32[]{:S(2)}, u32[]{:S(2)}) collective-permute-start(bf16[144,256]{1,0:T(8,128)(2,1)S(1)} %attend.79.a0), channel_id=1, source_target_pairs={{0,192},{32,224},{64,128},{96,160},{128,64},{160,96},{192,0},{224,... | collective-permute-start | bytes 221192 | tf_op jit(solution)/shard_map/attend/ppermute | solution.py:40
  137.6 8.4 %collective-permute-start.43 = (bf16[4,144,256]{2,1,0:T(8,128)(2,1)S(1)}, bf16[4,144,256]{2,1,0:T(8,128)(2,1)S(1)}, u32[]{:S(2)}, u32[]{:S(2)}) collective-permute-start(bf16[4,144,256]{2,1,0:T(8,128)(2,1)S(1)} %pad_maximum_fusion.7), channel_id=1, source_target_pairs={{0,32},{32,0},{64,96},{96,64},{128,160},{160,128},{192,224},{224,1... | collective-permute-start | bytes 884744 | tf_op jit(solution)/shard_map/attend/ppermute | solution.py:41
  147.6 6.9 %collective-permute-start.45 = (bf16[144,256]{1,0:T(8,128)(2,1)S(1)}, bf16[144,256]{1,0:T(8,128)(2,1)S(1)}, u32[]{:S(2)}, u32[]{:S(2)}) collective-permute-start(bf16[144,256]{1,0:T(8,128)(2,1)S(1)} %output.23), channel_id=1, source_target_pairs={{0,128},{32,160},{64,192},{96,224},{128,0},{160,32},{192,64},{224,... | collective-permute-start | bytes 221192 | tf_op jit(solution)/shard_map/output/ppermute | solution.py:40
  151.1 4.9 collective-permute-start.46
  162.6 21.2 %all-to-all-start = ((bf16[8,144,128]{2,1,0:T(8,128)(2,1)}), bf16[8,144,128]{2,1,0:T(8,128)(2,1)S(1)}, u32[]{:S(2)}, u32[]{:S(2)}) async-start(bf16[8,144,128]{2,1,0:T(8,128)(2,1)} %get-tuple-element.1001), calls=%async_computation | async-start | bytes 589824 | tf_op jit(solution)/shard_map/while/body/eval_jaxpr/exchange/all_to_all | solution.py:309
  171.0 17.2 %collective-permute-start.2 = (bf16[144,256]{1,0:T(8,128)(2,1)S(1)}, bf16[144,256]{1,0:T(8,128)(2,1)S(1)}, u32[]{:S(2)}, u32[]{:S(2)}) collective-permute-start(bf16[144,256]{1,0:T(8,128)(2,1)S(1)} %get-tuple-element.1000.q_ref), channel_id=1, source_target_pairs={{0,2},{1,3},{2,0},{3,1},{4,6},{5,7},{6,4},{7,5},{8,10},{9,11},{10,... | collective-permute-start | bytes 221192 | tf_op jit(solution)/shard_map/while/body/eval_jaxpr/exchange/ppermute | solution.py:308
  171.1 18.8 %collective-permute-start = (bf16[144,256]{1,0:T(8,128)(2,1)S(1)}, bf16[144,256]{1,0:T(8,128)(2,1)S(1)}, u32[]{:S(2)}, u32[]{:S(2)}) collective-permute-start(bf16[144,256]{1,0:T(8,128)(2,1)S(1)} %get-tuple-element.1000.q_ref), channel_id=1, source_target_pairs={{0,1},{1,0},{2,3},{3,2},{4,5},{5,4},{6,7},{7,6},{8,9},{9,8},{10,11... | collective-permute-start | bytes 221192 | tf_op jit(solution)/shard_map/while/body/eval_jaxpr/exchange/ppermute | solution.py:308
  185.3 8.3 %collective-permute-start.5 = (bf16[144,384]{1,0:T(8,128)(2,1)S(1)}, bf16[144,384]{1,0:T(8,128)(2,1)S(1)}, u32[]{:S(2)}, u32[]{:S(2)}) collective-permute-start(bf16[144,384]{1,0:T(8,128)(2,1)S(1)} %attend.83), channel_id=1, source_target_pairs={{0,3},{1,2},{2,1},{3,0},{4,7},{5,6},{6,5},{7,4},{8,11},{9,10},{10,... | collective-permute-start | bytes 331784 | tf_op jit(solution)/shard_map/while/body/eval_jaxpr/attend/ppermute | solution.py:328
  189.8 5.2 collective-permute-start.3
  203.3 5.0 collective-permute-start.9
  210.5 4.9 collective-permute-start.12
  224.1 19.3 %all-to-all-start = ((bf16[8,144,128]{2,1,0:T(8,128)(2,1)}), bf16[8,144,128]{2,1,0:T(8,128)(2,1)S(1)}, u32[]{:S(2)}, u32[]{:S(2)}) async-start(bf16[8,144,128]{2,1,0:T(8,128)(2,1)} %get-tuple-element.1001), calls=%async_computation | async-start | bytes 589824 | tf_op jit(solution)/shard_map/while/body/eval_jaxpr/exchange/all_to_all | solution.py:309
  227.6 7.8 %collective-permute-start.4 = (bf16[144,256]{1,0:T(8,128)(2,1)S(1)}, bf16[144,256]{1,0:T(8,128)(2,1)S(1)}, u32[]{:S(2)}, u32[]{:S(2)}) collective-permute-start(bf16[144,256]{1,0:T(8,128)(2,1)S(1)} %get-tuple-element.1000.q_ref), channel_id=1, source_target_pairs={{0,3},{1,2},{2,1},{3,0},{4,7},{5,6},{6,5},{7,4},{8,11},{9,10},{10,... | collective-permute-start | bytes 221192 | tf_op jit(solution)/shard_map/while/body/eval_jaxpr/exchange/ppermute | solution.py:308
  229.0 17.4 %collective-permute-start.2 = (bf16[144,256]{1,0:T(8,128)(2,1)S(1)}, bf16[144,256]{1,0:T(8,128)(2,1)S(1)}, u32[]{:S(2)}, u32[]{:S(2)}) collective-permute-start(bf16[144,256]{1,0:T(8,128)(2,1)S(1)} %get-tuple-element.1000.q_ref), channel_id=1, source_target_pairs={{0,2},{1,3},{2,0},{3,1},{4,6},{5,7},{6,4},{7,5},{8,10},{9,11},{10,... | collective-permute-start | bytes 221192 | tf_op jit(solution)/shard_map/while/body/eval_jaxpr/exchange/ppermute | solution.py:308
  230.1 18.9 %collective-permute-start = (bf16[144,256]{1,0:T(8,128)(2,1)S(1)}, bf16[144,256]{1,0:T(8,128)(2,1)S(1)}, u32[]{:S(2)}, u32[]{:S(2)}) collective-permute-start(bf16[144,256]{1,0:T(8,128)(2,1)S(1)} %get-tuple-element.1000.q_ref), channel_id=1, source_target_pairs={{0,1},{1,0},{2,3},{3,2},{4,5},{5,4},{6,7},{7,6},{8,9},{9,8},{10,11... | collective-permute-start | bytes 221192 | tf_op jit(solution)/shard_map/while/body/eval_jaxpr/exchange/ppermute | solution.py:308
  245.0 10.7 %collective-permute-start.5 = (bf16[144,384]{1,0:T(8,128)(2,1)S(1)}, bf16[144,384]{1,0:T(8,128)(2,1)S(1)}, u32[]{:S(2)}, u32[]{:S(2)}) collective-permute-start(bf16[144,384]{1,0:T(8,128)(2,1)S(1)} %attend.83), channel_id=1, source_target_pairs={{0,3},{1,2},{2,1},{3,0},{4,7},{5,6},{6,5},{7,4},{8,11},{9,10},{10,... | collective-permute-start | bytes 331784 | tf_op jit(solution)/shard_map/while/body/eval_jaxpr/attend/ppermute | solution.py:328
  248.0 7.7 %collective-permute-start.3 = (bf16[144,384]{1,0:T(8,128)(2,1)S(1)}, bf16[144,384]{1,0:T(8,128)(2,1)S(1)}, u32[]{:S(2)}, u32[]{:S(2)}) collective-permute-start(bf16[144,384]{1,0:T(8,128)(2,1)S(1)} %attend.82), channel_id=1, source_target_pairs={{0,2},{1,3},{2,0},{3,1},{4,6},{5,7},{6,4},{7,5},{8,10},{9,11},{10,... | collective-permute-start | bytes 331784 | tf_op jit(solution)/shard_map/while/body/eval_jaxpr/attend/ppermute | solution.py:328
  250.6 5.0 collective-permute-start.1
  256.9 4.9 collective-permute-start.8
  270.6 4.8 collective-permute-start.11
  282.5 17.8 %all-to-all-start = ((bf16[8,144,128]{2,1,0:T(8,128)(2,1)}), bf16[8,144,128]{2,1,0:T(8,128)(2,1)S(1)}, u32[]{:S(2)}, u32[]{:S(2)}) async-start(bf16[8,144,128]{2,1,0:T(8,128)(2,1)} %get-tuple-element.1001), calls=%async_computation | async-start | bytes 589824 | tf_op jit(solution)/shard_map/while/body/eval_jaxpr/exchange/all_to_all | solution.py:309
  289.7 14.0 %collective-permute-start.2 = (bf16[144,256]{1,0:T(8,128)(2,1)S(1)}, bf16[144,256]{1,0:T(8,128)(2,1)S(1)}, u32[]{:S(2)}, u32[]{:S(2)}) collective-permute-start(bf16[144,256]{1,0:T(8,128)(2,1)S(1)} %get-tuple-element.1000.q_ref), channel_id=1, source_target_pairs={{0,2},{1,3},{2,0},{3,1},{4,6},{5,7},{6,4},{7,5},{8,10},{9,11},{10,... | collective-permute-start | bytes 221192 | tf_op jit(solution)/shard_map/while/body/eval_jaxpr/exchange/ppermute | solution.py:308
  290.5 15.6 %collective-permute-start = (bf16[144,256]{1,0:T(8,128)(2,1)S(1)}, bf16[144,256]{1,0:T(8,128)(2,1)S(1)}, u32[]{:S(2)}, u32[]{:S(2)}) collective-permute-start(bf16[144,256]{1,0:T(8,128)(2,1)S(1)} %get-tuple-element.1000.q_ref), channel_id=1, source_target_pairs={{0,1},{1,0},{2,3},{3,2},{4,5},{5,4},{6,7},{7,6},{8,9},{9,8},{10,11... | collective-permute-start | bytes 221192 | tf_op jit(solution)/shard_map/while/body/eval_jaxpr/exchange/ppermute | solution.py:308
  301.9 8.1 %collective-permute-start.5 = (bf16[144,384]{1,0:T(8,128)(2,1)S(1)}, bf16[144,384]{1,0:T(8,128)(2,1)S(1)}, u32[]{:S(2)}, u32[]{:S(2)}) collective-permute-start(bf16[144,384]{1,0:T(8,128)(2,1)S(1)} %attend.83), channel_id=1, source_target_pairs={{0,3},{1,2},{2,1},{3,0},{4,7},{5,6},{6,5},{7,4},{8,11},{9,10},{10,... | collective-permute-start | bytes 331784 | tf_op jit(solution)/shard_map/while/body/eval_jaxpr/attend/ppermute | solution.py:328
  305.3 5.2 collective-permute-start.3
  327.7 4.8 collective-permute-start.11
  348.6 16.4 %all-to-all-start.1 = ((bf16[8,144,128]{2,1,0:T(8,128)(2,1)}), bf16[8,144,128]{2,1,0:T(8,128)(2,1)S(1)}, u32[]{:S(2)}, u32[]{:S(2)}) async-start(bf16[8,144,128]{2,1,0:T(8,128)(2,1)} %get-tuple-element.1015), calls=%async_computation.1 | async-start | bytes 589824 | tf_op jit(solution)/shard_map/while/body/eval_jaxpr/exchange/all_to_all | solution.py:309
  354.4 14.5 %collective-permute-start.16 = (bf16[144,256]{1,0:T(8,128)(2,1)S(1)}, bf16[144,256]{1,0:T(8,128)(2,1)S(1)}, u32[]{:S(2)}, u32[]{:S(2)}) collective-permute-start(bf16[144,256]{1,0:T(8,128)(2,1)S(1)} %get-tuple-element.1014.q_ref), channel_id=1, source_target_pairs={{0,2},{1,3},{2,0},{3,1},{4,6},{5,7},{6,4},{7,5},{8,10},{9,11},{10,... | collective-permute-start | bytes 221192 | tf_op jit(solution)/shard_map/while/body/eval_jaxpr/exchange/ppermute | solution.py:308
  354.9 16.1 %collective-permute-start.14 = (bf16[144,256]{1,0:T(8,128)(2,1)S(1)}, bf16[144,256]{1,0:T(8,128)(2,1)S(1)}, u32[]{:S(2)}, u32[]{:S(2)}) collective-permute-start(bf16[144,256]{1,0:T(8,128)(2,1)S(1)} %get-tuple-element.1014.q_ref), channel_id=1, source_target_pairs={{0,1},{1,0},{2,3},{3,2},{4,5},{5,4},{6,7},{7,6},{8,9},{9,8},{10,11... | collective-permute-start | bytes 221192 | tf_op jit(solution)/shard_map/while/body/eval_jaxpr/exchange/ppermute | solution.py:308
  366.6 8.1 %collective-permute-start.19 = (bf16[144,384]{1,0:T(8,128)(2,1)S(1)}, bf16[144,384]{1,0:T(8,128)(2,1)S(1)}, u32[]{:S(2)}, u32[]{:S(2)}) collective-permute-start(bf16[144,384]{1,0:T(8,128)(2,1)S(1)} %attend.88), channel_id=1, source_target_pairs={{0,3},{1,2},{2,1},{3,0},{4,7},{5,6},{6,5},{7,4},{8,11},{9,10},{10,... | collective-permute-start | bytes 331784 | tf_op jit(solution)/shard_map/while/body/eval_jaxpr/attend/ppermute | solution.py:328
  370.4 5.2 collective-permute-start.17
  392.1 4.8 collective-permute-start.25
  403.9 16.4 %all-to-all-start.1 = ((bf16[8,144,128]{2,1,0:T(8,128)(2,1)}), bf16[8,144,128]{2,1,0:T(8,128)(2,1)S(1)}, u32[]{:S(2)}, u32[]{:S(2)}) async-start(bf16[8,144,128]{2,1,0:T(8,128)(2,1)} %get-tuple-element.1015), calls=%async_computation.1 | async-start | bytes 589824 | tf_op jit(solution)/shard_map/while/body/eval_jaxpr/exchange/all_to_all | solution.py:309
  409.2 14.5 %collective-permute-start.16 = (bf16[144,256]{1,0:T(8,128)(2,1)S(1)}, bf16[144,256]{1,0:T(8,128)(2,1)S(1)}, u32[]{:S(2)}, u32[]{:S(2)}) collective-permute-start(bf16[144,256]{1,0:T(8,128)(2,1)S(1)} %get-tuple-element.1014.q_ref), channel_id=1, source_target_pairs={{0,2},{1,3},{2,0},{3,1},{4,6},{5,7},{6,4},{7,5},{8,10},{9,11},{10,... | collective-permute-start | bytes 221192 | tf_op jit(solution)/shard_map/while/body/eval_jaxpr/exchange/ppermute | solution.py:308
  410.0 16.0 %collective-permute-start.14 = (bf16[144,256]{1,0:T(8,128)(2,1)S(1)}, bf16[144,256]{1,0:T(8,128)(2,1)S(1)}, u32[]{:S(2)}, u32[]{:S(2)}) collective-permute-start(bf16[144,256]{1,0:T(8,128)(2,1)S(1)} %get-tuple-element.1014.q_ref), channel_id=1, source_target_pairs={{0,1},{1,0},{2,3},{3,2},{4,5},{5,4},{6,7},{7,6},{8,9},{9,8},{10,11... | collective-permute-start | bytes 221192 | tf_op jit(solution)/shard_map/while/body/eval_jaxpr/exchange/ppermute | solution.py:308
  421.8 8.1 %collective-permute-start.19 = (bf16[144,384]{1,0:T(8,128)(2,1)S(1)}, bf16[144,384]{1,0:T(8,128)(2,1)S(1)}, u32[]{:S(2)}, u32[]{:S(2)}) collective-permute-start(bf16[144,384]{1,0:T(8,128)(2,1)S(1)} %attend.88), channel_id=1, source_target_pairs={{0,3},{1,2},{2,1},{3,0},{4,7},{5,6},{6,5},{7,4},{8,11},{9,10},{10,... | collective-permute-start | bytes 331784 | tf_op jit(solution)/shard_map/while/body/eval_jaxpr/attend/ppermute | solution.py:328
  425.2 5.2 collective-permute-start.17
  446.9 4.8 collective-permute-start.25
  458.7 16.4 %all-to-all-start.1 = ((bf16[8,144,128]{2,1,0:T(8,128)(2,1)}), bf16[8,144,128]{2,1,0:T(8,128)(2,1)S(1)}, u32[]{:S(2)}, u32[]{:S(2)}) async-start(bf16[8,144,128]{2,1,0:T(8,128)(2,1)} %get-tuple-element.1015), calls=%async_computation.1 | async-start | bytes 589824 | tf_op jit(solution)/shard_map/while/body/eval_jaxpr/exchange/all_to_all | solution.py:309
  464.5 14.5 %collective-permute-start.16 = (bf16[144,256]{1,0:T(8,128)(2,1)S(1)}, bf16[144,256]{1,0:T(8,128)(2,1)S(1)}, u32[]{:S(2)}, u32[]{:S(2)}) collective-permute-start(bf16[144,256]{1,0:T(8,128)(2,1)S(1)} %get-tuple-element.1014.q_ref), channel_id=1, source_target_pairs={{0,2},{1,3},{2,0},{3,1},{4,6},{5,7},{6,4},{7,5},{8,10},{9,11},{10,... | collective-permute-start | bytes 221192 | tf_op jit(solution)/shard_map/while/body/eval_jaxpr/exchange/ppermute | solution.py:308
  465.0 16.1 %collective-permute-start.14 = (bf16[144,256]{1,0:T(8,128)(2,1)S(1)}, bf16[144,256]{1,0:T(8,128)(2,1)S(1)}, u32[]{:S(2)}, u32[]{:S(2)}) collective-permute-start(bf16[144,256]{1,0:T(8,128)(2,1)S(1)} %get-tuple-element.1014.q_ref), channel_id=1, source_target_pairs={{0,1},{1,0},{2,3},{3,2},{4,5},{5,4},{6,7},{7,6},{8,9},{9,8},{10,11... | collective-permute-start | bytes 221192 | tf_op jit(solution)/shard_map/while/body/eval_jaxpr/exchange/ppermute | solution.py:308
  476.7 8.1 %collective-permute-start.19 = (bf16[144,384]{1,0:T(8,128)(2,1)S(1)}, bf16[144,384]{1,0:T(8,128)(2,1)S(1)}, u32[]{:S(2)}, u32[]{:S(2)}) collective-permute-start(bf16[144,384]{1,0:T(8,128)(2,1)S(1)} %attend.88), channel_id=1, source_target_pairs={{0,3},{1,2},{2,1},{3,0},{4,7},{5,6},{6,5},{7,4},{8,11},{9,10},{10,... | collective-permute-start | bytes 331784 | tf_op jit(solution)/shard_map/while/body/eval_jaxpr/attend/ppermute | solution.py:328
  480.5 5.2 collective-permute-start.17
  514.0 16.4 %all-to-all-start.1 = ((bf16[8,144,128]{2,1,0:T(8,128)(2,1)}), bf16[8,144,128]{2,1,0:T(8,128)(2,1)S(1)}, u32[]{:S(2)}, u32[]{:S(2)}) async-start(bf16[8,144,128]{2,1,0:T(8,128)(2,1)} %get-tuple-element.1015), calls=%async_computation.1 | async-start | bytes 589824 | tf_op jit(solution)/shard_map/while/body/eval_jaxpr/exchange/all_to_all | solution.py:309
  519.3 14.5 %collective-permute-start.16 = (bf16[144,256]{1,0:T(8,128)(2,1)S(1)}, bf16[144,256]{1,0:T(8,128)(2,1)S(1)}, u32[]{:S(2)}, u32[]{:S(2)}) collective-permute-start(bf16[144,256]{1,0:T(8,128)(2,1)S(1)} %get-tuple-element.1014.q_ref), channel_id=1, source_target_pairs={{0,2},{1,3},{2,0},{3,1},{4,6},{5,7},{6,4},{7,5},{8,10},{9,11},{10,... | collective-permute-start | bytes 221192 | tf_op jit(solution)/shard_map/while/body/eval_jaxpr/exchange/ppermute | solution.py:308
  520.1 16.0 %collective-permute-start.14 = (bf16[144,256]{1,0:T(8,128)(2,1)S(1)}, bf16[144,256]{1,0:T(8,128)(2,1)S(1)}, u32[]{:S(2)}, u32[]{:S(2)}) collective-permute-start(bf16[144,256]{1,0:T(8,128)(2,1)S(1)} %get-tuple-element.1014.q_ref), channel_id=1, source_target_pairs={{0,1},{1,0},{2,3},{3,2},{4,5},{5,4},{6,7},{7,6},{8,9},{9,8},{10,11... | collective-permute-start | bytes 221192 | tf_op jit(solution)/shard_map/while/body/eval_jaxpr/exchange/ppermute | solution.py:308
  531.9 8.1 %collective-permute-start.19 = (bf16[144,384]{1,0:T(8,128)(2,1)S(1)}, bf16[144,384]{1,0:T(8,128)(2,1)S(1)}, u32[]{:S(2)}, u32[]{:S(2)}) collective-permute-start(bf16[144,384]{1,0:T(8,128)(2,1)S(1)} %attend.88), channel_id=1, source_target_pairs={{0,3},{1,2},{2,1},{3,0},{4,7},{5,6},{6,5},{7,4},{8,11},{9,10},{10,... | collective-permute-start | bytes 331784 | tf_op jit(solution)/shard_map/while/body/eval_jaxpr/attend/ppermute | solution.py:328
  535.3 5.2 collective-permute-start.17
  557.0 4.8 collective-permute-start.25
  (65 other events, 270.0 us)
Sparse Core Ops, SparseCore 0:
  31.2 117.4 all-gather.4
  151.3 116.5 all-gather.6

commit v4 on v3

--- a/solution.py
+++ b/solution.py
@@ -71,56 +71,77 @@
     place(scal[0], scal[3], [p0, p1, p2, p3, p4], out_ref, sems)
 
 
-def project(me, gain_ref, piece_refs, w_of, q_ref, kv_ref):
+ORDER = (0, 2, 4, 6, 1, 3, 5, 7)
+
+
+def stream(me, slot, w_ref, first, held, sems):
+    copies = []
+    for i, mask in enumerate(ORDER):
+        owner = jnp.bitwise_xor(me, mask)
+        source = w_ref.at[pl.ds(XN * owner, XN), slot, :, first : first + held.shape[-1]]
+        copies.append(pltpu.make_async_copy(source, held.at[i], sems.at[i]))
+    for copy in copies:
+        copy.start()
+    return copies
+
+
+def streamed(copies, held):
+    def w_of(i):
+        copies[i].wait()
+        return held[i].reshape(QW, held.shape[-1])
+
+    return w_of
+
+
+def assembled(me, seq, parts, held, first):
+    x_me = jnp.bitwise_and(seq, XN - 1)
+    width = held.shape[-1]
+    for d in range(XN):
+        held[jnp.bitwise_xor(x_me, d)] = parts[d][:, :, first : first + width]
+    return lambda i: held[:, jnp.bitwise_xor(me, ORDER[i])].reshape(QW, width)
+
+
+def project(me, gain_ref, piece_refs, w_of):
     pieces = [(mask, value.astype(F32)) for mask, value in in_order(piece_refs)]
-    rows = pieces[0][1].shape[0]
     width = sum(value.shape[1] for _, value in pieces)
     squares = functools.reduce(jnp.add, [value * value for _, value in pieces])
     scale = lax.rsqrt(jnp.sum(squares, axis=-1, keepdims=True) / width + EPS)
-    q_sum = jnp.zeros((rows, QW), F32)
-    kv_sum = jnp.zeros((rows, 2 * HD), F32)
-    for mask, value in pieces:
-        owner = jnp.bitwise_xor(me, mask)
-        gain = gain_ref[0, pl.ds(owner, 1), 0, :].astype(F32)
+    total = None
+    for i, (mask, value) in enumerate(pieces):
+        gain = gain_ref[0, pl.ds(jnp.bitwise_xor(me, mask), 1), 0, :].astype(F32)
         normed = (value * scale * gain).astype(BF16)
-        wq, wkv = w_of(owner)
-        q_sum += jnp.dot(normed, wq, preferred_element_type=F32)
-        kv_sum += jnp.dot(normed, wkv, preferred_element_type=F32)
-    q_ref[...] = q_sum.astype(BF16)
-    pair = kv_sum.astype(BF16)
+        part = jnp.dot(normed, w_of(i), preferred_element_type=F32)
+        total = part if total is None else total + part
+    return total.astype(BF16)
+
+
+def write_keys(pair, kv_ref):
     for i in range(kv_ref.shape[0]):
         kv_ref[i] = pair
 
 
-def project_kernel(
-    scal, gain_ref, p0, p1, p2, p3, p4, wq_ref, wkv_ref, out_in, q_ref, kv_ref, out_ref, sems
+def keys_kernel(scal, gain_ref, p0, p1, p2, p3, p4, w_ref, kv_ref, held, sems):
+    w_of = streamed(stream(scal[0], scal[2], w_ref, QW, held, sems), held)
+    write_keys(project(scal[0], gain_ref, [p0, p1, p2, p3, p4], w_of), kv_ref)
+
+
+def queries_kernel(
+    scal, gain_ref, p0, p1, p2, p3, p4, w_ref, out_in, q_ref, out_ref, held, sems, out_sems
 ):
-    def w_of(owner):
-        wq = wq_ref[pl.ds(XN * owner, XN), 0].reshape(QW, QW)
-        wkv = wkv_ref[pl.ds(XN * owner, XN), 0].reshape(QW, 2 * HD)
-        return wq, wkv
-
     refs = [p0, p1, p2, p3, p4]
-    project(scal[0], gain_ref, refs, w_of, q_ref, kv_ref)
-    place(scal[0], scal[3], refs, out_ref, sems)
-
-
-def assemble(seq, parts, held):
-    x_me = jnp.bitwise_and(seq, XN - 1)
-    for d in range(XN):
-        held[jnp.bitwise_xor(x_me, d)] = parts[d][...]
-
-
-def first_project_kernel(
-    scal, gain_ref, p0, p1, p2, p3, p4, w0, w1, w2, w3, q_ref, kv_ref, held
-):
-    assemble(scal[1], [w0, w1, w2, w3], held)
-
-    def w_of(owner):
-        w = held[:, owner].reshape(QW, QW + 2 * HD)
-        return w[:, :QW], w[:, QW:]
-
-    project(scal[0], gain_ref, [p0, p1, p2, p3, p4], w_of, q_ref, kv_ref)
+    w_of = streamed(stream(scal[0], scal[2], w_ref, 0, held, sems), held)
+    q_ref[...] = project(scal[0], gain_ref, refs, w_of)
+    place(scal[0], scal[3], refs, out_ref, out_sems)
+
+
+def first_keys_kernel(scal, gain_ref, p0, p1, p2, p3, p4, w0, w1, w2, w3, kv_ref, held):
+    w_of = assembled(scal[0], scal[1], [w0, w1, w2, w3], held, QW)
+    write_keys(project(scal[0], gain_ref, [p0, p1, p2, p3, p4], w_of), kv_ref)
+
+
+def first_queries_kernel(scal, gain_ref, p0, p1, p2, p3, p4, w0, w1, w2, w3, q_ref, held):
+    w_of = assembled(scal[0], scal[1], [w0, w1, w2, w3], held, 0)
+    q_ref[...] = project(scal[0], gain_ref, [p0, p1, p2, p3, p4], w_of)
 
 
 def attend_kernel(scal, q_ref, k_ref, o_ref, *, d, blocks, tok):
@@ -128,11 +149,11 @@
     x_me = jnp.bitwise_and(seq, XN - 1)
     span = ZN * tok
     rows = SHARE * tok
-    row = lax.broadcasted_iota(jnp.int32, (rows, span), 0)
-    col = lax.broadcasted_iota(jnp.int32, (rows, span), 1)
-    slack = lax.rem(row, tok) - lax.div(col, tok) * (XN * tok) - lax.rem(col, tok)
+    row = lax.rem(lax.broadcasted_iota(jnp.int32, (rows, 1), 0), tok)
+    col = lax.broadcasted_iota(jnp.int32, (1, span), 1)
+    col = lax.div(col, tok) * (XN * tok) + lax.rem(col, tok)
     asker = seq - x_me + jnp.bitwise_xor(x_me, d)
-    visible = slack >= (x_me - asker) * tok
+    visible = col <= row + (asker - x_me) * tok
     factor = HD**-0.5 * LOG2E
     q_parts = []
     for b in range(blocks):
@@ -142,12 +163,13 @@
     q_rows = jnp.concatenate([q_rows, jnp.zeros((blocks * rows, HD), BF16)], axis=1)
     pairs = []
     scores = {}
+    key_lane = lax.broadcasted_iota(jnp.int32, (span, 2 * HD), 1) < HD
     for kb in range(blocks):
         pair = k_ref[:, kb * tok : (kb + 1) * tok, :].reshape(span, 2 * HD)
         s = lax.dot_general(
             q_rows[kb * rows :], pair, (((1,), (1,)), ((), ())), preferred_element_type=F32
         )
-        pairs.append(pair)
+        pairs.append(jnp.where(key_lane, jnp.ones_like(pair), pair))
         for b in range(kb, blocks):
             part = s[(b - kb) * rows : (b - kb + 1) * rows]
             scores[b, kb] = jnp.where(visible, part, NEG) if b == kb else part
@@ -155,20 +177,18 @@
     for b in range(blocks):
         peak = functools.reduce(jnp.maximum, [scores[b, kb] for kb in range(b + 1)])
         peaks.append(jnp.max(peak, axis=-1, keepdims=True) * factor)
-    totals = [jnp.zeros((rows, span), F32) for _ in range(blocks)]
     sums = [jnp.zeros((rows, 2 * HD), F32) for _ in range(blocks)]
     for kb in range(blocks):
         probs = []
         for b in range(kb, blocks):
             p = jnp.exp2(scores[b, kb] * factor - peaks[b])
-            totals[b] += p
             probs.append(p.astype(BF16))
         got = jnp.dot(jnp.concatenate(probs, axis=0), pairs[kb], preferred_element_type=F32)
         for b in range(kb, blocks):
             sums[b] += got[(b - kb) * rows : (b - kb + 1) * rows]
     lane = lax.broadcasted_iota(jnp.int32, (tok, 2 * HD), 1)
     for b in range(blocks):
-        total = jnp.sum(totals[b], axis=-1, keepdims=True)
+        total = sums[b][:, :1]
         result = (sums[b][:, HD:] / total).astype(BF16)
         weight = peaks[b] + jnp.log(total) * LOG2E
         high = weight.astype(BF16).astype(F32)
@@ -198,24 +218,22 @@
         a_ref[:, cols] = mixed.astype(BF16)
 
 
-def output(me, piece_refs, h_ref, w_of, o_ref):
+def output(piece_refs, h_ref, w_of, o_ref):
     total = h_ref[...].astype(F32)
     update = jnp.zeros(total.shape, F32)
-    for mask, value in in_order(piece_refs):
-        update += jnp.dot(value, w_of(jnp.bitwise_xor(me, mask)), preferred_element_type=F32)
+    for i, (_, value) in enumerate(in_order(piece_refs)):
+        update += jnp.dot(value, w_of(i), preferred_element_type=F32)
     o_ref[...] = (total + update).astype(BF16)
 
 
-def output_kernel(scal, a0, a1, a2, a3, a4, h_ref, w_ref, o_ref):
-    def w_of(owner):
-        return w_ref[pl.ds(XN * owner, XN), 0].reshape(QW, QW)
-
-    output(scal[0], [a0, a1, a2, a3, a4], h_ref, w_of, o_ref)
+def output_kernel(scal, a0, a1, a2, a3, a4, h_ref, w_ref, o_ref, held, sems):
+    w_of = streamed(stream(scal[0], scal[2], w_ref, QW + 2 * HD, held, sems), held)
+    output([a0, a1, a2, a3, a4], h_ref, w_of, o_ref)
 
 
 def first_output_kernel(scal, a0, a1, a2, a3, a4, h_ref, w0, w1, w2, w3, o_ref, held):
-    assemble(scal[1], [w0, w1, w2, w3], held)
-    output(scal[0], [a0, a1, a2, a3, a4], h_ref, lambda owner: held[:, owner].reshape(QW, QW), o_ref)
+    w_of = assembled(scal[0], scal[1], [w0, w1, w2, w3], held, 0)
+    output([a0, a1, a2, a3, a4], h_ref, w_of, o_ref)
 
 
 def whole(shape):
@@ -264,7 +282,7 @@
         return w[0].reshape(shard, SN, -1).transpose(1, 0, 2)
 
     gain_rows = jnp.pad(norm_gain.reshape(4, width // 4), ((0, 12), (0, all_w - width // 4)))
-    mine = jnp.concatenate([cut(w_query), cut(w_out), cut(w_key), cut(w_value)], axis=-1)
+    mine = jnp.concatenate([cut(w_query), cut(w_key), cut(w_value), cut(w_out)], axis=-1)
     mine = jnp.concatenate([mine, jnp.broadcast_to(gain_rows[None], (SN, 16, all_w))], axis=1)
     by_layer = lax.all_to_all(mine, "section", split_axis=0, concat_axis=0, tiled=True)
     gains = by_layer[:, shard : shard + 4, : width // 4].reshape(layers, SN, 1, QW)
@@ -272,14 +290,20 @@
     with jax.named_scope("weights"):
         early = lax.all_gather(by_layer[1:4, :shard], "seq", axis=0)
         late = lax.all_gather(by_layer[4:, :shard], "seq", axis=0)
-        first = jnp.broadcast_to(by_layer[None, 0, :shard], (ZN, shard, all_w))
-        first = lax.all_to_all(
-            first, "seq", split_axis=0, concat_axis=0, tiled=True, axis_index_groups=along_z()
-        )
-        first_qkv = jnp.concatenate([first[:, :, :QW], first[:, :, 2 * QW :]], axis=-1)
-        first_out = first[:, :, QW : 2 * QW]
-        first_qkv = [first_qkv] + [lax.ppermute(first_qkv, "seq", seq_pairs(d)) for d in (1, 2, 3)]
-        first_out = [first_out] + [lax.ppermute(first_out, "seq", seq_pairs(d)) for d in (1, 2, 3)]
+
+        def over_z(part):
+            part = jnp.broadcast_to(part[None], (ZN,) + part.shape)
+            return lax.all_to_all(
+                part, "seq", split_axis=0, concat_axis=0, tiled=True, axis_index_groups=along_z()
+            )
+
+        def over_x(part):
+            return [part] + [lax.ppermute(part, "seq", seq_pairs(d)) for d in (1, 2, 3)]
+
+        first_qkv = over_z(by_layer[0, :shard, :qkv_w])
+        first_qkv, first_out = lax.optimization_barrier((first_qkv, by_layer[0, :shard, qkv_w:]))
+        first_qkv, first_out = lax.optimization_barrier((over_x(first_qkv), over_z(first_out)))
+        first_out = over_x(first_out)
 
     flat = inputs.reshape(rows, width)
 
@@ -297,11 +321,14 @@
     gain_spec = pl.BlockSpec((1, SN, 1, QW), lambda i, scal: (scal[3], 0, 0, 0))
     sems = [pltpu.SemaphoreType.DMA((SN,))]
     seq_keys = ZN * XN * tok
-    project_cost = (2 * rows * width * qkv_w, 2 * (width * qkv_w + rows * width))
-    output_cost = (2 * rows * width * QW, 2 * (width * QW + rows * width))
-
-    def weight_spec(width_, index):
-        return pl.BlockSpec((ZN * XN, 1, shard, width_), lambda i, scal: (0, scal[2], 0, index))
+    keys_cost = (4 * rows * width * HD, 2 * (width * 2 * HD + rows * width))
+    full_cost = (2 * rows * width * QW, 2 * (width * QW + rows * width))
+
+    def room(width_):
+        return [pltpu.VMEM((SN, XN, shard, width_), BF16), pltpu.SemaphoreType.DMA((SN,))]
+
+    def first_room(width_):
+        return [pltpu.VMEM((XN, ZN, shard, width_), BF16)]
 
     def exchange(q, kv):
         with jax.named_scope("exchange"):
@@ -341,16 +368,11 @@
         return jnp.stack([jnp.asarray(v, jnp.int32) for v in (me, seq, slot, layer)])
 
     scal = numbers(0, 0)
+    first_specs = [gain_spec] + piece_specs + [whole((ZN, shard, qkv_w))] * XN
     with jax.named_scope("project"):
-        q, kv = call(
-            first_project_kernel,
-            scal,
-            (gains, *pieces, *first_qkv),
-            [gain_spec] + piece_specs + [whole((ZN, shard, qkv_w))] * XN,
-            [piece_shape, kv_shape],
-            *project_cost,
-            scratch=[pltpu.VMEM((XN, ZN, shard, qkv_w), BF16)],
-        )
+        args = (gains, *pieces, *first_qkv)
+        kv = call(first_keys_kernel, scal, args, first_specs, kv_shape, *keys_cost, scratch=first_room(2 * HD))
+        q = call(first_queries_kernel, scal, args, first_specs, piece_shape, *full_cost, scratch=first_room(QW))
     qs, kv = exchange(q, kv)
     kv, first_out = lax.optimization_barrier((kv, first_out))
     heads = attend(scal, qs, kv)
@@ -361,8 +383,8 @@
             (*heads, pieces[0], *first_out),
             piece_specs + [whole((rows, QW))] + [whole((ZN, shard, QW))] * XN,
             piece_shape,
-            *output_cost,
-            scratch=[pltpu.VMEM((XN, ZN, shard, QW), BF16)],
+            *full_cost,
+            scratch=first_room(QW),
         )
         pieces = spread(own)
     out = jnp.zeros((rows, width), BF16)
@@ -372,15 +394,18 @@
             pieces, out = carry
             scal = numbers(layer - first_layer, layer)
             with jax.named_scope("project"):
-                q, kv, out = call(
-                    project_kernel,
+                specs = [gain_spec] + piece_specs + [in_place()]
+                args = (gains, *pieces, group)
+                kv = call(keys_kernel, scal, args, specs, kv_shape, *keys_cost, scratch=room(2 * HD))
+                q, out = call(
+                    queries_kernel,
                     scal,
-                    (gains, *pieces, group, group, out),
-                    [gain_spec] + piece_specs + [weight_spec(QW, 0), weight_spec(2 * HD, 4), in_place()],
-                    [piece_shape, kv_shape, out_shape],
-                    *project_cost,
-                    scratch=sems,
-                    own=(8, 2),
+                    (*args, out),
+                    specs + [in_place()],
+                    [piece_shape, out_shape],
+                    *full_cost,
+                    scratch=room(QW) + sems,
+                    own=(7, 1),
                 )
             heads = attend(scal, *exchange(q, kv))
             with jax.named_scope("output"):
@@ -388,9 +413,10 @@
                     output_kernel,
                     scal,
                     (*heads, pieces[0], group),
-                    piece_specs + [whole((rows, QW)), weight_spec(QW, 1)],
+                    piece_specs + [whole((rows, QW)), in_place()],
                     piece_shape,
-                    *output_cost,
+                    *full_cost,
+                    scratch=room(QW),
                 )
                 return spread(own), out
 

time: 583 us -> 598 us (1.026)
  blocking collectives: 50 us -> 18.8 us
  Pallas kernels: 102 us -> 128 us
  starting transfers between devices: 195 us -> 221 us
  waiting for transfers between devices: 193 us -> 185 us
    all_to_all x1 -> x0, blocking collectives: 31.2 us -> none  [local(): lax.all_to_all(first, 'seq', split_axis=0, concat_axis=0, tiled=True, axi...]
    pallas_call x57 -> x65, Pallas kernels: 102 us -> 128 us  [call(): pl.pallas_call(kernel, out_shape=out_shape, grid_spec=pltpu.PrefetchScala...]
    all_to_all x0 -> x2, waiting for transfers between devices: none -> 16.1 us  [over_z(): lax.all_to_all(part, 'seq', split_axis=0, concat_axis=0, tiled=True, axis...]
    all_to_all x8, waiting for transfers between devices: 60 us -> 47.4 us  [exchange(): lax.all_to_all(kv, 'seq', split_axis=0, concat_axis=0, tiled=True, axis_i...]
    all_to_all x0 -> x2, starting transfers between devices: none -> 11.6 us  [over_z(): lax.all_to_all(part, 'seq', split_axis=0, concat_axis=0, tiled=True, axis...]
    ppermute x24, waiting for transfers between devices: 11.5 us -> 1.95 us  [exchange(): qs = [q] + [lax.ppermute(q, 'seq', seq_pairs(d)) for d in (1, 2, 3)]]
  transfers between devices with their start and end apart: 128 -> 130, of which waited for: 89 -> 79; matrix products, arithmetic and copies ran while one was open for 1% -> 1% of each run, Pallas kernels for 13% -> 17%
where the time goes in v4:
time: 598 us; the launch traced here: 588 us
  starting transfers between devices  221 us (37%)
  waiting for transfers between devices  185 us (31%)
  Pallas kernels  128 us (21%)
  blocking collectives  18.8 us (3%)
  between operations  13.8 us (2%)
  loops' own time  10.3 us (2%)
  local copies, waits for them, and re-layouts  9.02 us (2%)
    pallas_call x65, Pallas kernels, call(): pl.pallas_call(kernel, out_shape=out_shape, grid_spec=pltpu.PrefetchScala...  128 us
    ppermute x48, starting transfers between devices, spread(): lax.ppermute(piece, 'section', section_pairs(2 * d))  55.7 us
    ppermute x48, waiting for transfers between devices, spread(): lax.ppermute(piece, 'section', section_pairs(2 * d))  49.7 us
    ppermute x16, starting transfers between devices, spread(): other = lax.ppermute(jnp.stack(near), 'section', section_pairs(1))  48.8 us
    all_to_all x8, waiting for transfers between devices, exchange(): lax.all_to_all(kv, 'seq', split_axis=0, concat_axis=0, tiled=True, axis_i...  47.4 us
    ppermute x24, starting transfers between devices, attend(): parts[d] = lax.ppermute(part, 'seq', seq_pairs(d)) if d else part  34.6 us
    all_to_all x8, starting transfers between devices, exchange(): lax.all_to_all(kv, 'seq', split_axis=0, concat_axis=0, tiled=True, axis_i...  33.9 us
    ppermute x6, waiting for transfers between devices, over_x(): return [part] + [lax.ppermute(part, 'seq', seq_pairs(d)) for d in (1, 2, 3)]  30.7 us
  transfers between devices with their start and end apart: 130, of which 79 were waited for; matrix products, arithmetic and copies ran while one was open for 1% of the time, Pallas kernels for 17%

profile of v4, /device:TPU:1, one launch (start us, length us, event | category | flops | bytes accessed | tf_op | source)
XLA Modules:
  0.0 587.5 jit_solution(8326903972181930879)
XLA Ops:
  11.6 18.8 %all_to_all.32 = bf16[8,80,640]{2,1,0:T(8,128)(2,1)S(1)} all-to-all(bf16[8,80,640]{2,1,0:T(8,128)(2,1)S(1)} %copy.40), channel_id=1, replica_groups=mesh['section'=8,'seq'=32] {'section'}, dimensions={0} | all-to-all | bytes 1638400 | tf_op jit(solution)/shard_map/all_to_all | solution.py:287
  32.8 8.2 %all-to-all-start.3 = ((bf16[8,64,384]{2,1,0:T(8,128)(2,1)}), bf16[8,64,384]{2,1,0:T(8,128)(2,1)S(1)}, u32[]{:S(2)}, u32[]{:S(2)}) async-start(bf16[8,64,384]{2,1,0:T(8,128)(2,1)} %broadcast_in_dim.24), calls=%async_computation.3 | async-start | bytes 786432 | tf_op jit(solution)/shard_map/weights/all_to_all | solution.py:296
  41.0 16.1 %all-to-all-done.3.w0 = bf16[8,64,384]{2,1,0:T(8,128)(2,1)S(1)} async-done(((bf16[8,64,384]{2,1,0:T(8,128)(2,1)}), bf16[8,64,384]{2,1,0:T(8,128)(2,1)S(1)}, u32[]{:S(2)}, u32[]{:S(2)}) %all-to-all-start.3) | async-done | bytes 393248 | tf_op jit(solution)/shard_map/weights/all_to_all | solution.py:296
  57.9 3.4 all-to-all-start.4
  62.9 2.5 collective-permute-start.29
  66.5 4.1 collective-permute-done.28.w1
  70.6 10.7 %collective-permute-done.29.w2 = bf16[8,64,384]{2,1,0:T(8,128)(2,1)S(1)} collective-permute-done((bf16[8,64,384]{2,1,0:T(8,128)(2,1)S(1)}, bf16[8,64,384]{2,1,0:T(8,128)(2,1)S(1)}, u32[]{:S(2)}, u32[]{:S(2)}) %collective-permute-start.29) | collective-permute-done | bytes 393248 | tf_op jit(solution)/shard_map/weights/ppermute | solution.py:301
  83.1 6.2 %all-to-all-start.5 = ((bf16[8,144,128]{2,1,0:T(8,128)(2,1)}), bf16[8,144,128]{2,1,0:T(8,128)(2,1)S(1)}, u32[]{:S(2)}, u32[]{:S(2)}) async-start(bf16[8,144,128]{2,1,0:T(8,128)(2,1)} %project.47), calls=%async_computation.5 | async-start | bytes 589824 | tf_op jit(solution)/shard_map/exchange/all_to_all | solution.py:336
  90.6 2.6 collective-permute-start.33
  96.2 5.0 collective-permute-done.31.w1
  101.3 10.8 %collective-permute-done.32.w2 = bf16[8,64,256]{2,1,0:T(8,128)(2,1)S(1)} collective-permute-done((bf16[8,64,256]{2,1,0:T(8,128)(2,1)S(1)}, bf16[8,64,256]{2,1,0:T(8,128)(2,1)S(1)}, u32[]{:S(2)}, u32[]{:S(2)}) %collective-permute-start.32) | collective-permute-done | bytes 262176 | tf_op jit(solution)/shard_map/weights/ppermute | solution.py:301
  113.8 2.7 collective-permute-start.39
  122.2 2.5 attend.75.o0
  126.4 3.4 collective-permute-done.35.o1
  132.2 2.8 collective-permute-start.42
  137.2 8.6 %collective-permute-start.43 = (bf16[4,144,256]{2,1,0:T(8,128)(2,1)S(1)}, bf16[4,144,256]{2,1,0:T(8,128)(2,1)S(1)}, u32[]{:S(2)}, u32[]{:S(2)}) collective-permute-start(bf16[4,144,256]{2,1,0:T(8,128)(2,1)S(1)} %pad_maximum_fusion.6), channel_id=1, source_target_pairs={{0,32},{32,0},{64,96},{96,64},{128,160},{160,128},{192,224},{224,1... | collective-permute-start | bytes 884744 | tf_op jit(solution)/shard_map/attend/ppermute | solution.py:41
  148.5 3.6 collective-permute-start.45
  152.1 3.3 collective-permute-done.45
  160.0 181.7 %while.54 = (s32[]{:T(128)}, bf16[144,256]{1,0:T(8,128)(2,1)S(1)}, bf16[144,256]{1,0:T(8,128)(2,1)S(1)}, bf16[144,256]{1,0:T(8,128)(2,1)S(1)}, bf16[144,256]{1,0...) while((s32[]{:T(128)}, bf16[144,256]{1,0:T(8,128)(2,1)S(1)}, ...), condition=%wide.region_1.2_spmd, body=%wide.region_0.1_spmd.sunk | while | flops 1284710400 | bytes 15377133 | solution.py:428
  160.1 3.5 project.49
  163.6 6.9 %all-to-all-start = ((bf16[8,144,128]{2,1,0:T(8,128)(2,1)}), bf16[8,144,128]{2,1,0:T(8,128)(2,1)S(1)}, u32[]{:S(2)}, u32[]{:S(2)}) async-start(bf16[8,144,128]{2,1,0:T(8,128)(2,1)} %project.49), calls=%async_computation | async-start | bytes 589824 | tf_op jit(solution)/shard_map/while/body/eval_jaxpr/exchange/all_to_all | solution.py:336
  173.2 3.1 collective-permute-start.2
  177.0 7.8 %all-to-all-done.k_ref = bf16[8,144,128]{2,1,0:T(8,128)(2,1)S(1)} async-done(((bf16[8,144,128]{2,1,0:T(8,128)(2,1)}), bf16[8,144,128]{2,1,0:T(8,128)(2,1)S(1)}, u32[]{:S(2)}, u32[]{:S(2)}) %all-to-all-start) | async-done | bytes 294944 | tf_op jit(solution)/shard_map/while/body/eval_jaxpr/exchange/all_to_all | solution.py:336
  188.4 5.0 collective-permute-start.3
  197.0 2.9 collective-permute-done.5.o3
  201.4 3.1 collective-permute-start.6
  207.5 3.3 collective-permute-start.9
  224.5 3.5 project.49
  228.0 3.4 all-to-all-start
  231.4 2.6 project.48
  235.1 2.8 collective-permute-start.4
  239.8 7.5 %all-to-all-done.k_ref = bf16[8,144,128]{2,1,0:T(8,128)(2,1)S(1)} async-done(((bf16[8,144,128]{2,1,0:T(8,128)(2,1)}), bf16[8,144,128]{2,1,0:T(8,128)(2,1)S(1)}, u32[]{:S(2)}, u32[]{:S(2)}) %all-to-all-start) | async-done | bytes 294944 | tf_op jit(solution)/shard_map/while/body/eval_jaxpr/exchange/all_to_all | solution.py:336
  253.3 2.9 collective-permute-start.5
  260.5 3.5 collective-permute-start.8
  284.3 3.5 project.49
  287.8 3.5 all-to-all-start
  294.2 2.7 collective-permute-start.2
  297.7 6.0 %all-to-all-done.k_ref = bf16[8,144,128]{2,1,0:T(8,128)(2,1)S(1)} async-done(((bf16[8,144,128]{2,1,0:T(8,128)(2,1)}), bf16[8,144,128]{2,1,0:T(8,128)(2,1)S(1)}, u32[]{:S(2)}, u32[]{:S(2)}) %all-to-all-start) | async-done | bytes 294944 | tf_op jit(solution)/shard_map/while/body/eval_jaxpr/exchange/all_to_all | solution.py:336
  307.4 3.3 collective-permute-start.3
  314.4 2.8 collective-permute-done.5.o3
  324.6 3.7 collective-permute-start.9
  341.7 237.4 %while.55 = (s32[]{:T(128)}, bf16[144,256]{1,0:T(8,128)(2,1)S(1)}, bf16[144,256]{1,0:T(8,128)(2,1)S(1)}, bf16[144,256]{1,0:T(8,128)(2,1)S(1)}, bf16[144,256]{1,0...) while((s32[]{:T(128)}, bf16[144,256]{1,0:T(8,128)(2,1)S(1)}, ...), condition=%wide.region_3.4_spmd, body=%wide.region_2.3_spmd.sunk | while | flops 1284710400 | bytes 15377145 | solution.py:428
  351.6 3.5 project.51
  355.1 3.4 all-to-all-start.1
  358.5 2.5 project.50
  364.9 6.5 %all-to-all-done.1.k_ref = bf16[8,144,128]{2,1,0:T(8,128)(2,1)S(1)} async-done(((bf16[8,144,128]{2,1,0:T(8,128)(2,1)}), bf16[8,144,128]{2,1,0:T(8,128)(2,1)S(1)}, u32[]{:S(2)}, u32[]{:S(2)}) %all-to-all-start.1) | async-done | bytes 294944 | tf_op jit(solution)/shard_map/while/body/eval_jaxpr/exchange/all_to_all | solution.py:336
  391.1 3.7 collective-permute-start.23
  408.1 3.5 project.51
  411.5 3.4 all-to-all-start.1
  417.9 2.6 collective-permute-start.16
  421.4 6.5 %all-to-all-done.1.k_ref = bf16[8,144,128]{2,1,0:T(8,128)(2,1)S(1)} async-done(((bf16[8,144,128]{2,1,0:T(8,128)(2,1)}), bf16[8,144,128]{2,1,0:T(8,128)(2,1)S(1)}, u32[]{:S(2)}, u32[]{:S(2)}) %all-to-all-start.1) | async-done | bytes 294944 | tf_op jit(solution)/shard_map/while/body/eval_jaxpr/exchange/all_to_all | solution.py:336
  431.7 2.7 collective-permute-start.17
  448.1 3.7 collective-permute-start.23
  465.4 3.5 project.51
  468.8 3.4 all-to-all-start.1
  472.3 2.5 project.50
  478.7 6.5 %all-to-all-done.1.k_ref = bf16[8,144,128]{2,1,0:T(8,128)(2,1)S(1)} async-done(((bf16[8,144,128]{2,1,0:T(8,128)(2,1)}), bf16[8,144,128]{2,1,0:T(8,128)(2,1)S(1)}, u32[]{:S(2)}, u32[]{:S(2)}) %all-to-all-start.1) | async-done | bytes 294944 | tf_op jit(solution)/shard_map/while/body/eval_jaxpr/exchange/all_to_all | solution.py:336
  504.8 3.7 collective-permute-start.23
  521.9 3.5 project.51
  525.3 3.4 all-to-all-start.1
  531.6 2.6 collective-permute-start.16
  535.2 6.5 %all-to-all-done.1.k_ref = bf16[8,144,128]{2,1,0:T(8,128)(2,1)S(1)} async-done(((bf16[8,144,128]{2,1,0:T(8,128)(2,1)}), bf16[8,144,128]{2,1,0:T(8,128)(2,1)S(1)}, u32[]{:S(2)}, u32[]{:S(2)}) %all-to-all-start.1) | async-done | bytes 294944 | tf_op jit(solution)/shard_map/while/body/eval_jaxpr/exchange/all_to_all | solution.py:336
  545.4 2.7 collective-permute-start.17
  561.9 3.7 collective-permute-start.23
  (330 shorter events, 276.5 us)
Async XLA Ops:
  6.5 153.4 %all-gather.5.cloned.1.call-start = ((), (), s32[]{:S(2)}) async-start(), calls=%async_computation.6 | async-start | bytes 8110080 | tf_op jit(solution)/shard_map/weights/all_gather | solution.py:291
  31.2 310.5 %all-gather.7.cloned.1.call-start = ((), (), s32[]{:S(2)}) async-start(), calls=%async_computation.7 | async-start | bytes 10813440 | tf_op jit(solution)/shard_map/weights/all_gather | solution.py:292
  32.8 24.3 %all-to-all-start.3 = ((bf16[8,64,384]{2,1,0:T(8,128)(2,1)}), bf16[8,64,384]{2,1,0:T(8,128)(2,1)S(1)}, u32[]{:S(2)}, u32[]{:S(2)}) async-start(bf16[8,64,384]{2,1,0:T(8,128)(2,1)} %broadcast_in_dim.24), calls=%async_computation.3 | async-start | bytes 786432 | tf_op jit(solution)/shard_map/weights/all_to_all | solution.py:296
  57.9 23.4 %all-to-all-start.4 = ((bf16[8,64,256]{2,1,0:T(8,128)(2,1)}), bf16[8,64,256]{2,1,0:T(8,128)(2,1)S(1)}, u32[]{:S(2)}, u32[]{:S(2)}) async-start(bf16[8,64,256]{2,1,0:T(8,128)(2,1)} %broadcast_in_dim.25), calls=%async_computation.4 | async-start | bytes 524288 | tf_op jit(solution)/shard_map/weights/all_to_all | solution.py:296
  61.3 9.3 %collective-permute-start.28 = (bf16[8,64,384]{2,1,0:T(8,128)(2,1)S(1)}, bf16[8,64,384]{2,1,0:T(8,128)(2,1)S(1)}, u32[]{:S(2)}, u32[]{:S(2)}) collective-permute-start(bf16[8,64,384]{2,1,0:T(8,128)(2,1)S(1)} %all-to-all-done.3.w0), channel_id=1, source_target_pairs={{0,1},{1,0},{2,3},{3,2},{4,5},{5,4},{6,7},{7,6},{8,9},{9,8},{10,11... | collective-permute-start | bytes 1179656 | tf_op jit(solution)/shard_map/weights/ppermute | solution.py:301
  62.9 18.4 %collective-permute-start.29 = (bf16[8,64,384]{2,1,0:T(8,128)(2,1)S(1)}, bf16[8,64,384]{2,1,0:T(8,128)(2,1)S(1)}, u32[]{:S(2)}, u32[]{:S(2)}) collective-permute-start(bf16[8,64,384]{2,1,0:T(8,128)(2,1)S(1)} %all-to-all-done.3.w0), channel_id=1, source_target_pairs={{0,2},{1,3},{2,0},{3,1},{4,6},{5,7},{6,4},{7,5},{8,10},{9,11},{10,... | collective-permute-start | bytes 1179656 | tf_op jit(solution)/shard_map/weights/ppermute | solution.py:301
  65.4 15.9 %collective-permute-start.30 = (bf16[8,64,384]{2,1,0:T(8,128)(2,1)S(1)}, bf16[8,64,384]{2,1,0:T(8,128)(2,1)S(1)}, u32[]{:S(2)}, u32[]{:S(2)}) collective-permute-start(bf16[8,64,384]{2,1,0:T(8,128)(2,1)S(1)} %all-to-all-done.3.w0), channel_id=1, source_target_pairs={{0,3},{1,2},{2,1},{3,0},{4,7},{5,6},{6,5},{7,4},{8,11},{9,10},{10,... | collective-permute-start | bytes 1179656 | tf_op jit(solution)/shard_map/weights/ppermute | solution.py:301
  83.1 29.1 %all-to-all-start.5 = ((bf16[8,144,128]{2,1,0:T(8,128)(2,1)}), bf16[8,144,128]{2,1,0:T(8,128)(2,1)S(1)}, u32[]{:S(2)}, u32[]{:S(2)}) async-start(bf16[8,144,128]{2,1,0:T(8,128)(2,1)} %project.47), calls=%async_computation.5 | async-start | bytes 589824 | tf_op jit(solution)/shard_map/exchange/all_to_all | solution.py:336
  89.3 11.9 %collective-permute-start.31 = (bf16[8,64,256]{2,1,0:T(8,128)(2,1)S(1)}, bf16[8,64,256]{2,1,0:T(8,128)(2,1)S(1)}, u32[]{:S(2)}, u32[]{:S(2)}) collective-permute-start(bf16[8,64,256]{2,1,0:T(8,128)(2,1)S(1)} %all-to-all-done.4.w0), channel_id=1, source_target_pairs={{0,1},{1,0},{2,3},{3,2},{4,5},{5,4},{6,7},{7,6},{8,9},{9,8},{10,11... | collective-permute-start | bytes 786440 | tf_op jit(solution)/shard_map/weights/ppermute | solution.py:301
  89.3 22.8 %collective-permute-start.32 = (bf16[8,64,256]{2,1,0:T(8,128)(2,1)S(1)}, bf16[8,64,256]{2,1,0:T(8,128)(2,1)S(1)}, u32[]{:S(2)}, u32[]{:S(2)}) collective-permute-start(bf16[8,64,256]{2,1,0:T(8,128)(2,1)S(1)} %all-to-all-done.4.w0), channel_id=1, source_target_pairs={{0,2},{1,3},{2,0},{3,1},{4,6},{5,7},{6,4},{7,5},{8,10},{9,11},{10,... | collective-permute-start | bytes 786440 | tf_op jit(solution)/shard_map/weights/ppermute | solution.py:301
  90.6 21.6 %collective-permute-start.33 = (bf16[8,64,256]{2,1,0:T(8,128)(2,1)S(1)}, bf16[8,64,256]{2,1,0:T(8,128)(2,1)S(1)}, u32[]{:S(2)}, u32[]{:S(2)}) collective-permute-start(bf16[8,64,256]{2,1,0:T(8,128)(2,1)S(1)} %all-to-all-done.4.w0), channel_id=1, source_target_pairs={{0,3},{1,2},{2,1},{3,0},{4,7},{5,6},{6,5},{7,4},{8,11},{9,10},{10,... | collective-permute-start | bytes 786440 | tf_op jit(solution)/shard_map/weights/ppermute | solution.py:301
  95.6 16.6 %collective-permute-start.38 = (bf16[144,256]{1,0:T(8,128)(2,1)}, bf16[144,256]{1,0:T(8,128)(2,1)S(1)}, u32[]{:S(2)}, u32[]{:S(2)}) collective-permute-start(bf16[144,256]{1,0:T(8,128)(2,1)} %project.46.q_ref), channel_id=1, source_target_pairs={{0,3},{1,2},{2,1},{3,0},{4,7},{5,6},{6,5},{7,4},{8,11},{9,10},{10,... | collective-permute-start | bytes 221192 | tf_op jit(solution)/shard_map/exchange/ppermute | solution.py:335
  95.6 20.9 %collective-permute-start.36 = (bf16[144,256]{1,0:T(8,128)(2,1)}, bf16[144,256]{1,0:T(8,128)(2,1)S(1)}, u32[]{:S(2)}, u32[]{:S(2)}) collective-permute-start(bf16[144,256]{1,0:T(8,128)(2,1)} %project.46.q_ref), channel_id=1, source_target_pairs={{0,2},{1,3},{2,0},{3,1},{4,6},{5,7},{6,4},{7,5},{8,10},{9,11},{10,... | collective-permute-start | bytes 221192 | tf_op jit(solution)/shard_map/exchange/ppermute | solution.py:335
  101.3 17.7 %collective-permute-start.34 = (bf16[144,256]{1,0:T(8,128)(2,1)}, bf16[144,256]{1,0:T(8,128)(2,1)S(1)}, u32[]{:S(2)}, u32[]{:S(2)}) collective-permute-start(bf16[144,256]{1,0:T(8,128)(2,1)} %project.46.q_ref), channel_id=1, source_target_pairs={{0,1},{1,0},{2,3},{3,2},{4,5},{5,4},{6,7},{7,6},{8,9},{9,8},{10,11... | collective-permute-start | bytes 221192 | tf_op jit(solution)/shard_map/exchange/ppermute | solution.py:335
  113.8 10.9 %collective-permute-start.39 = (bf16[144,384]{1,0:T(8,128)(2,1)S(1)}, bf16[144,384]{1,0:T(8,128)(2,1)S(1)}, u32[]{:S(2)}, u32[]{:S(2)}) collective-permute-start(bf16[144,384]{1,0:T(8,128)(2,1)S(1)} %attend.78), channel_id=1, source_target_pairs={{0,3},{1,2},{2,1},{3,0},{4,7},{5,6},{6,5},{7,4},{8,11},{9,10},{10,... | collective-permute-start | bytes 331784 | tf_op jit(solution)/shard_map/attend/ppermute | solution.py:355
  118.2 8.3 %collective-permute-start.37 = (bf16[144,384]{1,0:T(8,128)(2,1)S(1)}, bf16[144,384]{1,0:T(8,128)(2,1)S(1)}, u32[]{:S(2)}, u32[]{:S(2)}) collective-permute-start(bf16[144,384]{1,0:T(8,128)(2,1)S(1)} %attend.77), channel_id=1, source_target_pairs={{0,2},{1,3},{2,0},{3,1},{4,6},{5,7},{6,4},{7,5},{8,10},{9,11},{10,... | collective-permute-start | bytes 331784 | tf_op jit(solution)/shard_map/attend/ppermute | solution.py:355
  120.6 9.2 %collective-permute-start.35 = (bf16[144,384]{1,0:T(8,128)(2,1)S(1)}, bf16[144,384]{1,0:T(8,128)(2,1)S(1)}, u32[]{:S(2)}, u32[]{:S(2)}) collective-permute-start(bf16[144,384]{1,0:T(8,128)(2,1)S(1)} %attend.76), channel_id=1, source_target_pairs={{0,1},{1,0},{2,3},{3,2},{4,5},{5,4},{6,7},{7,6},{8,9},{9,8},{10,11... | collective-permute-start | bytes 331784 | tf_op jit(solution)/shard_map/attend/ppermute | solution.py:355
  137.2 9.8 %collective-permute-start.43 = (bf16[4,144,256]{2,1,0:T(8,128)(2,1)S(1)}, bf16[4,144,256]{2,1,0:T(8,128)(2,1)S(1)}, u32[]{:S(2)}, u32[]{:S(2)}) collective-permute-start(bf16[4,144,256]{2,1,0:T(8,128)(2,1)S(1)} %pad_maximum_fusion.6), channel_id=1, source_target_pairs={{0,32},{32,0},{64,96},{96,64},{128,160},{160,128},{192,224},{224,1... | collective-permute-start | bytes 884744 | tf_op jit(solution)/shard_map/attend/ppermute | solution.py:41
  148.5 6.9 %collective-permute-start.45 = (bf16[144,256]{1,0:T(8,128)(2,1)S(1)}, bf16[144,256]{1,0:T(8,128)(2,1)S(1)}, u32[]{:S(2)}, u32[]{:S(2)}) collective-permute-start(bf16[144,256]{1,0:T(8,128)(2,1)S(1)} %output.23), channel_id=1, source_target_pairs={{0,128},{32,160},{64,192},{96,224},{128,0},{160,32},{192,64},{224,... | collective-permute-start | bytes 221192 | tf_op jit(solution)/shard_map/output/ppermute | solution.py:40
  163.6 21.2 %all-to-all-start = ((bf16[8,144,128]{2,1,0:T(8,128)(2,1)}), bf16[8,144,128]{2,1,0:T(8,128)(2,1)S(1)}, u32[]{:S(2)}, u32[]{:S(2)}) async-start(bf16[8,144,128]{2,1,0:T(8,128)(2,1)} %project.49), calls=%async_computation | async-start | bytes 589824 | tf_op jit(solution)/shard_map/while/body/eval_jaxpr/exchange/all_to_all | solution.py:336
  173.2 13.5 %collective-permute-start.2 = (bf16[144,256]{1,0:T(8,128)(2,1)S(1)}, bf16[144,256]{1,0:T(8,128)(2,1)S(1)}, u32[]{:S(2)}, u32[]{:S(2)}) collective-permute-start(bf16[144,256]{1,0:T(8,128)(2,1)S(1)} %get-tuple-element.1004.q_ref), channel_id=1, source_target_pairs={{0,2},{1,3},{2,0},{3,1},{4,6},{5,7},{6,4},{7,5},{8,10},{9,11},{10,... | collective-permute-start | bytes 221192 | tf_op jit(solution)/shard_map/while/body/eval_jaxpr/exchange/ppermute | solution.py:335
  176.3 17.1 %collective-permute-start.4 = (bf16[144,256]{1,0:T(8,128)(2,1)S(1)}, bf16[144,256]{1,0:T(8,128)(2,1)S(1)}, u32[]{:S(2)}, u32[]{:S(2)}) collective-permute-start(bf16[144,256]{1,0:T(8,128)(2,1)S(1)} %get-tuple-element.1004.q_ref), channel_id=1, source_target_pairs={{0,3},{1,2},{2,1},{3,0},{4,7},{5,6},{6,5},{7,4},{8,11},{9,10},{10,... | collective-permute-start | bytes 221192 | tf_op jit(solution)/shard_map/while/body/eval_jaxpr/exchange/ppermute | solution.py:335
  186.5 10.4 %collective-permute-start.1 = (bf16[144,384]{1,0:T(8,128)(2,1)S(1)}, bf16[144,384]{1,0:T(8,128)(2,1)S(1)}, u32[]{:S(2)}, u32[]{:S(2)}) collective-permute-start(bf16[144,384]{1,0:T(8,128)(2,1)S(1)} %attend.81), channel_id=1, source_target_pairs={{0,1},{1,0},{2,3},{3,2},{4,5},{5,4},{6,7},{7,6},{8,9},{9,8},{10,11... | collective-permute-start | bytes 331784 | tf_op jit(solution)/shard_map/while/body/eval_jaxpr/attend/ppermute | solution.py:355
  188.4 8.6 %collective-permute-start.3 = (bf16[144,384]{1,0:T(8,128)(2,1)S(1)}, bf16[144,384]{1,0:T(8,128)(2,1)S(1)}, u32[]{:S(2)}, u32[]{:S(2)}) collective-permute-start(bf16[144,384]{1,0:T(8,128)(2,1)S(1)} %attend.82), channel_id=1, source_target_pairs={{0,2},{1,3},{2,0},{3,1},{4,6},{5,7},{6,4},{7,5},{8,10},{9,11},{10,... | collective-permute-start | bytes 331784 | tf_op jit(solution)/shard_map/while/body/eval_jaxpr/attend/ppermute | solution.py:355
  201.2 5.3 collective-permute-start.8
  201.3 5.2 collective-permute-start.7
  201.4 6.1 %collective-permute-start.6 = (bf16[144,256]{1,0:T(8,128)(2,1)S(1)}, bf16[144,256]{1,0:T(8,128)(2,1)S(1)}, u32[]{:S(2)}, u32[]{:S(2)}) collective-permute-start(bf16[144,256]{1,0:T(8,128)(2,1)S(1)} %attend.84.a0), channel_id=1, source_target_pairs={{0,64},{32,96},{64,0},{96,32},{128,192},{160,224},{192,128},{224,1... | collective-permute-start | bytes 221192 | tf_op jit(solution)/shard_map/while/body/eval_jaxpr/attend/ppermute | solution.py:40
  228.0 19.2 %all-to-all-start = ((bf16[8,144,128]{2,1,0:T(8,128)(2,1)}), bf16[8,144,128]{2,1,0:T(8,128)(2,1)S(1)}, u32[]{:S(2)}, u32[]{:S(2)}) async-start(bf16[8,144,128]{2,1,0:T(8,128)(2,1)} %project.49), calls=%async_computation | async-start | bytes 589824 | tf_op jit(solution)/shard_map/while/body/eval_jaxpr/exchange/all_to_all | solution.py:336
  234.0 5.8 collective-permute-start
  234.1 14.9 %collective-permute-start.2 = (bf16[144,256]{1,0:T(8,128)(2,1)S(1)}, bf16[144,256]{1,0:T(8,128)(2,1)S(1)}, u32[]{:S(2)}, u32[]{:S(2)}) collective-permute-start(bf16[144,256]{1,0:T(8,128)(2,1)S(1)} %get-tuple-element.1004.q_ref), channel_id=1, source_target_pairs={{0,2},{1,3},{2,0},{3,1},{4,6},{5,7},{6,4},{7,5},{8,10},{9,11},{10,... | collective-permute-start | bytes 221192 | tf_op jit(solution)/shard_map/while/body/eval_jaxpr/exchange/ppermute | solution.py:335
  235.1 16.5 %collective-permute-start.4 = (bf16[144,256]{1,0:T(8,128)(2,1)S(1)}, bf16[144,256]{1,0:T(8,128)(2,1)S(1)}, u32[]{:S(2)}, u32[]{:S(2)}) collective-permute-start(bf16[144,256]{1,0:T(8,128)(2,1)S(1)} %get-tuple-element.1004.q_ref), channel_id=1, source_target_pairs={{0,3},{1,2},{2,1},{3,0},{4,7},{5,6},{6,5},{7,4},{8,11},{9,10},{10,... | collective-permute-start | bytes 221192 | tf_op jit(solution)/shard_map/while/body/eval_jaxpr/exchange/ppermute | solution.py:335
  248.9 9.0 %collective-permute-start.1 = (bf16[144,384]{1,0:T(8,128)(2,1)S(1)}, bf16[144,384]{1,0:T(8,128)(2,1)S(1)}, u32[]{:S(2)}, u32[]{:S(2)}) collective-permute-start(bf16[144,384]{1,0:T(8,128)(2,1)S(1)} %attend.81), channel_id=1, source_target_pairs={{0,1},{1,0},{2,3},{3,2},{4,5},{5,4},{6,7},{7,6},{8,9},{9,8},{10,11... | collective-permute-start | bytes 331784 | tf_op jit(solution)/shard_map/while/body/eval_jaxpr/attend/ppermute | solution.py:355
  250.6 7.3 %collective-permute-start.3 = (bf16[144,384]{1,0:T(8,128)(2,1)S(1)}, bf16[144,384]{1,0:T(8,128)(2,1)S(1)}, u32[]{:S(2)}, u32[]{:S(2)}) collective-permute-start(bf16[144,384]{1,0:T(8,128)(2,1)S(1)} %attend.82), channel_id=1, source_target_pairs={{0,2},{1,3},{2,0},{3,1},{4,6},{5,7},{6,4},{7,5},{8,10},{9,11},{10,... | collective-permute-start | bytes 331784 | tf_op jit(solution)/shard_map/while/body/eval_jaxpr/attend/ppermute | solution.py:355
  253.3 6.0 %collective-permute-start.5 = (bf16[144,384]{1,0:T(8,128)(2,1)S(1)}, bf16[144,384]{1,0:T(8,128)(2,1)S(1)}, u32[]{:S(2)}, u32[]{:S(2)}) collective-permute-start(bf16[144,384]{1,0:T(8,128)(2,1)S(1)} %attend.83), channel_id=1, source_target_pairs={{0,3},{1,2},{2,1},{3,0},{4,7},{5,6},{6,5},{7,4},{8,11},{9,10},{10,... | collective-permute-start | bytes 331784 | tf_op jit(solution)/shard_map/while/body/eval_jaxpr/attend/ppermute | solution.py:355
  260.5 5.8 collective-permute-start.8
  287.8 16.0 %all-to-all-start = ((bf16[8,144,128]{2,1,0:T(8,128)(2,1)}), bf16[8,144,128]{2,1,0:T(8,128)(2,1)S(1)}, u32[]{:S(2)}, u32[]{:S(2)}) async-start(bf16[8,144,128]{2,1,0:T(8,128)(2,1)} %project.49), calls=%async_computation | async-start | bytes 589824 | tf_op jit(solution)/shard_map/while/body/eval_jaxpr/exchange/all_to_all | solution.py:336
  294.2 11.6 %collective-permute-start.2 = (bf16[144,256]{1,0:T(8,128)(2,1)S(1)}, bf16[144,256]{1,0:T(8,128)(2,1)S(1)}, u32[]{:S(2)}, u32[]{:S(2)}) collective-permute-start(bf16[144,256]{1,0:T(8,128)(2,1)S(1)} %get-tuple-element.1004.q_ref), channel_id=1, source_target_pairs={{0,2},{1,3},{2,0},{3,1},{4,6},{5,7},{6,4},{7,5},{8,10},{9,11},{10,... | collective-permute-start | bytes 221192 | tf_op jit(solution)/shard_map/while/body/eval_jaxpr/exchange/ppermute | solution.py:335
  296.9 13.8 %collective-permute-start.4 = (bf16[144,256]{1,0:T(8,128)(2,1)S(1)}, bf16[144,256]{1,0:T(8,128)(2,1)S(1)}, u32[]{:S(2)}, u32[]{:S(2)}) collective-permute-start(bf16[144,256]{1,0:T(8,128)(2,1)S(1)} %get-tuple-element.1004.q_ref), channel_id=1, source_target_pairs={{0,3},{1,2},{2,1},{3,0},{4,7},{5,6},{6,5},{7,4},{8,11},{9,10},{10,... | collective-permute-start | bytes 221192 | tf_op jit(solution)/shard_map/while/body/eval_jaxpr/exchange/ppermute | solution.py:335
  305.4 9.0 %collective-permute-start.1 = (bf16[144,384]{1,0:T(8,128)(2,1)S(1)}, bf16[144,384]{1,0:T(8,128)(2,1)S(1)}, u32[]{:S(2)}, u32[]{:S(2)}) collective-permute-start(bf16[144,384]{1,0:T(8,128)(2,1)S(1)} %attend.81), channel_id=1, source_target_pairs={{0,1},{1,0},{2,3},{3,2},{4,5},{5,4},{6,7},{7,6},{8,9},{9,8},{10,11... | collective-permute-start | bytes 331784 | tf_op jit(solution)/shard_map/while/body/eval_jaxpr/attend/ppermute | solution.py:355
  307.4 7.0 %collective-permute-start.3 = (bf16[144,384]{1,0:T(8,128)(2,1)S(1)}, bf16[144,384]{1,0:T(8,128)(2,1)S(1)}, u32[]{:S(2)}, u32[]{:S(2)}) collective-permute-start(bf16[144,384]{1,0:T(8,128)(2,1)S(1)} %attend.82), channel_id=1, source_target_pairs={{0,2},{1,3},{2,0},{3,1},{4,6},{5,7},{6,4},{7,5},{8,10},{9,11},{10,... | collective-permute-start | bytes 331784 | tf_op jit(solution)/shard_map/while/body/eval_jaxpr/attend/ppermute | solution.py:355
  324.6 4.9 collective-permute-start.9
  355.1 16.4 %all-to-all-start.1 = ((bf16[8,144,128]{2,1,0:T(8,128)(2,1)}), bf16[8,144,128]{2,1,0:T(8,128)(2,1)S(1)}, u32[]{:S(2)}, u32[]{:S(2)}) async-start(bf16[8,144,128]{2,1,0:T(8,128)(2,1)} %project.51), calls=%async_computation.1 | async-start | bytes 589824 | tf_op jit(solution)/shard_map/while/body/eval_jaxpr/exchange/all_to_all | solution.py:336
  361.1 12.1 %collective-permute-start.16 = (bf16[144,256]{1,0:T(8,128)(2,1)S(1)}, bf16[144,256]{1,0:T(8,128)(2,1)S(1)}, u32[]{:S(2)}, u32[]{:S(2)}) collective-permute-start(bf16[144,256]{1,0:T(8,128)(2,1)S(1)} %get-tuple-element.1017.q_ref), channel_id=1, source_target_pairs={{0,2},{1,3},{2,0},{3,1},{4,6},{5,7},{6,4},{7,5},{8,10},{9,11},{10,... | collective-permute-start | bytes 221192 | tf_op jit(solution)/shard_map/while/body/eval_jaxpr/exchange/ppermute | solution.py:335
  363.2 13.8 %collective-permute-start.18 = (bf16[144,256]{1,0:T(8,128)(2,1)S(1)}, bf16[144,256]{1,0:T(8,128)(2,1)S(1)}, u32[]{:S(2)}, u32[]{:S(2)}) collective-permute-start(bf16[144,256]{1,0:T(8,128)(2,1)S(1)} %get-tuple-element.1017.q_ref), channel_id=1, source_target_pairs={{0,3},{1,2},{2,1},{3,0},{4,7},{5,6},{6,5},{7,4},{8,11},{9,10},{10,... | collective-permute-start | bytes 221192 | tf_op jit(solution)/shard_map/while/body/eval_jaxpr/exchange/ppermute | solution.py:335
  373.1 9.0 %collective-permute-start.15 = (bf16[144,384]{1,0:T(8,128)(2,1)S(1)}, bf16[144,384]{1,0:T(8,128)(2,1)S(1)}, u32[]{:S(2)}, u32[]{:S(2)}) collective-permute-start(bf16[144,384]{1,0:T(8,128)(2,1)S(1)} %attend.86), channel_id=1, source_target_pairs={{0,1},{1,0},{2,3},{3,2},{4,5},{5,4},{6,7},{7,6},{8,9},{9,8},{10,11... | collective-permute-start | bytes 331784 | tf_op jit(solution)/shard_map/while/body/eval_jaxpr/attend/ppermute | solution.py:355
  374.9 7.3 %collective-permute-start.17 = (bf16[144,384]{1,0:T(8,128)(2,1)S(1)}, bf16[144,384]{1,0:T(8,128)(2,1)S(1)}, u32[]{:S(2)}, u32[]{:S(2)}) collective-permute-start(bf16[144,384]{1,0:T(8,128)(2,1)S(1)} %attend.87), channel_id=1, source_target_pairs={{0,2},{1,3},{2,0},{3,1},{4,6},{5,7},{6,4},{7,5},{8,10},{9,11},{10,... | collective-permute-start | bytes 331784 | tf_op jit(solution)/shard_map/while/body/eval_jaxpr/attend/ppermute | solution.py:355
  391.1 4.9 collective-permute-start.23
  411.5 16.4 %all-to-all-start.1 = ((bf16[8,144,128]{2,1,0:T(8,128)(2,1)}), bf16[8,144,128]{2,1,0:T(8,128)(2,1)S(1)}, u32[]{:S(2)}, u32[]{:S(2)}) async-start(bf16[8,144,128]{2,1,0:T(8,128)(2,1)} %project.51), calls=%async_computation.1 | async-start | bytes 589824 | tf_op jit(solution)/shard_map/while/body/eval_jaxpr/exchange/all_to_all | solution.py:336
  417.9 12.1 %collective-permute-start.16 = (bf16[144,256]{1,0:T(8,128)(2,1)S(1)}, bf16[144,256]{1,0:T(8,128)(2,1)S(1)}, u32[]{:S(2)}, u32[]{:S(2)}) collective-permute-start(bf16[144,256]{1,0:T(8,128)(2,1)S(1)} %get-tuple-element.1017.q_ref), channel_id=1, source_target_pairs={{0,2},{1,3},{2,0},{3,1},{4,6},{5,7},{6,4},{7,5},{8,10},{9,11},{10,... | collective-permute-start | bytes 221192 | tf_op jit(solution)/shard_map/while/body/eval_jaxpr/exchange/ppermute | solution.py:335
  420.5 13.8 %collective-permute-start.18 = (bf16[144,256]{1,0:T(8,128)(2,1)S(1)}, bf16[144,256]{1,0:T(8,128)(2,1)S(1)}, u32[]{:S(2)}, u32[]{:S(2)}) collective-permute-start(bf16[144,256]{1,0:T(8,128)(2,1)S(1)} %get-tuple-element.1017.q_ref), channel_id=1, source_target_pairs={{0,3},{1,2},{2,1},{3,0},{4,7},{5,6},{6,5},{7,4},{8,11},{9,10},{10,... | collective-permute-start | bytes 221192 | tf_op jit(solution)/shard_map/while/body/eval_jaxpr/exchange/ppermute | solution.py:335
  429.6 9.0 %collective-permute-start.15 = (bf16[144,384]{1,0:T(8,128)(2,1)S(1)}, bf16[144,384]{1,0:T(8,128)(2,1)S(1)}, u32[]{:S(2)}, u32[]{:S(2)}) collective-permute-start(bf16[144,384]{1,0:T(8,128)(2,1)S(1)} %attend.86), channel_id=1, source_target_pairs={{0,1},{1,0},{2,3},{3,2},{4,5},{5,4},{6,7},{7,6},{8,9},{9,8},{10,11... | collective-permute-start | bytes 331784 | tf_op jit(solution)/shard_map/while/body/eval_jaxpr/attend/ppermute | solution.py:355
  431.7 7.0 %collective-permute-start.17 = (bf16[144,384]{1,0:T(8,128)(2,1)S(1)}, bf16[144,384]{1,0:T(8,128)(2,1)S(1)}, u32[]{:S(2)}, u32[]{:S(2)}) collective-permute-start(bf16[144,384]{1,0:T(8,128)(2,1)S(1)} %attend.87), channel_id=1, source_target_pairs={{0,2},{1,3},{2,0},{3,1},{4,6},{5,7},{6,4},{7,5},{8,10},{9,11},{10,... | collective-permute-start | bytes 331784 | tf_op jit(solution)/shard_map/while/body/eval_jaxpr/attend/ppermute | solution.py:355
  448.1 4.9 collective-permute-start.23
  468.8 16.4 %all-to-all-start.1 = ((bf16[8,144,128]{2,1,0:T(8,128)(2,1)}), bf16[8,144,128]{2,1,0:T(8,128)(2,1)S(1)}, u32[]{:S(2)}, u32[]{:S(2)}) async-start(bf16[8,144,128]{2,1,0:T(8,128)(2,1)} %project.51), calls=%async_computation.1 | async-start | bytes 589824 | tf_op jit(solution)/shard_map/while/body/eval_jaxpr/exchange/all_to_all | solution.py:336
  474.9 12.1 %collective-permute-start.16 = (bf16[144,256]{1,0:T(8,128)(2,1)S(1)}, bf16[144,256]{1,0:T(8,128)(2,1)S(1)}, u32[]{:S(2)}, u32[]{:S(2)}) collective-permute-start(bf16[144,256]{1,0:T(8,128)(2,1)S(1)} %get-tuple-element.1017.q_ref), channel_id=1, source_target_pairs={{0,2},{1,3},{2,0},{3,1},{4,6},{5,7},{6,4},{7,5},{8,10},{9,11},{10,... | collective-permute-start | bytes 221192 | tf_op jit(solution)/shard_map/while/body/eval_jaxpr/exchange/ppermute | solution.py:335
  477.0 13.8 %collective-permute-start.18 = (bf16[144,256]{1,0:T(8,128)(2,1)S(1)}, bf16[144,256]{1,0:T(8,128)(2,1)S(1)}, u32[]{:S(2)}, u32[]{:S(2)}) collective-permute-start(bf16[144,256]{1,0:T(8,128)(2,1)S(1)} %get-tuple-element.1017.q_ref), channel_id=1, source_target_pairs={{0,3},{1,2},{2,1},{3,0},{4,7},{5,6},{6,5},{7,4},{8,11},{9,10},{10,... | collective-permute-start | bytes 221192 | tf_op jit(solution)/shard_map/while/body/eval_jaxpr/exchange/ppermute | solution.py:335
  486.9 9.0 %collective-permute-start.15 = (bf16[144,384]{1,0:T(8,128)(2,1)S(1)}, bf16[144,384]{1,0:T(8,128)(2,1)S(1)}, u32[]{:S(2)}, u32[]{:S(2)}) collective-permute-start(bf16[144,384]{1,0:T(8,128)(2,1)S(1)} %attend.86), channel_id=1, source_target_pairs={{0,1},{1,0},{2,3},{3,2},{4,5},{5,4},{6,7},{7,6},{8,9},{9,8},{10,11... | collective-permute-start | bytes 331784 | tf_op jit(solution)/shard_map/while/body/eval_jaxpr/attend/ppermute | solution.py:355
  488.6 7.3 %collective-permute-start.17 = (bf16[144,384]{1,0:T(8,128)(2,1)S(1)}, bf16[144,384]{1,0:T(8,128)(2,1)S(1)}, u32[]{:S(2)}, u32[]{:S(2)}) collective-permute-start(bf16[144,384]{1,0:T(8,128)(2,1)S(1)} %attend.87), channel_id=1, source_target_pairs={{0,2},{1,3},{2,0},{3,1},{4,6},{5,7},{6,4},{7,5},{8,10},{9,11},{10,... | collective-permute-start | bytes 331784 | tf_op jit(solution)/shard_map/while/body/eval_jaxpr/attend/ppermute | solution.py:355
  525.3 16.4 %all-to-all-start.1 = ((bf16[8,144,128]{2,1,0:T(8,128)(2,1)}), bf16[8,144,128]{2,1,0:T(8,128)(2,1)S(1)}, u32[]{:S(2)}, u32[]{:S(2)}) async-start(bf16[8,144,128]{2,1,0:T(8,128)(2,1)} %project.51), calls=%async_computation.1 | async-start | bytes 589824 | tf_op jit(solution)/shard_map/while/body/eval_jaxpr/exchange/all_to_all | solution.py:336
  531.6 12.1 %collective-permute-start.16 = (bf16[144,256]{1,0:T(8,128)(2,1)S(1)}, bf16[144,256]{1,0:T(8,128)(2,1)S(1)}, u32[]{:S(2)}, u32[]{:S(2)}) collective-permute-start(bf16[144,256]{1,0:T(8,128)(2,1)S(1)} %get-tuple-element.1017.q_ref), channel_id=1, source_target_pairs={{0,2},{1,3},{2,0},{3,1},{4,6},{5,7},{6,4},{7,5},{8,10},{9,11},{10,... | collective-permute-start | bytes 221192 | tf_op jit(solution)/shard_map/while/body/eval_jaxpr/exchange/ppermute | solution.py:335
  534.2 13.8 %collective-permute-start.18 = (bf16[144,256]{1,0:T(8,128)(2,1)S(1)}, bf16[144,256]{1,0:T(8,128)(2,1)S(1)}, u32[]{:S(2)}, u32[]{:S(2)}) collective-permute-start(bf16[144,256]{1,0:T(8,128)(2,1)S(1)} %get-tuple-element.1017.q_ref), channel_id=1, source_target_pairs={{0,3},{1,2},{2,1},{3,0},{4,7},{5,6},{6,5},{7,4},{8,11},{9,10},{10,... | collective-permute-start | bytes 221192 | tf_op jit(solution)/shard_map/while/body/eval_jaxpr/exchange/ppermute | solution.py:335
  543.4 9.0 %collective-permute-start.15 = (bf16[144,384]{1,0:T(8,128)(2,1)S(1)}, bf16[144,384]{1,0:T(8,128)(2,1)S(1)}, u32[]{:S(2)}, u32[]{:S(2)}) collective-permute-start(bf16[144,384]{1,0:T(8,128)(2,1)S(1)} %attend.86), channel_id=1, source_target_pairs={{0,1},{1,0},{2,3},{3,2},{4,5},{5,4},{6,7},{7,6},{8,9},{9,8},{10,11... | collective-permute-start | bytes 331784 | tf_op jit(solution)/shard_map/while/body/eval_jaxpr/attend/ppermute | solution.py:355
  545.4 7.0 %collective-permute-start.17 = (bf16[144,384]{1,0:T(8,128)(2,1)S(1)}, bf16[144,384]{1,0:T(8,128)(2,1)S(1)}, u32[]{:S(2)}, u32[]{:S(2)}) collective-permute-start(bf16[144,384]{1,0:T(8,128)(2,1)S(1)} %attend.87), channel_id=1, source_target_pairs={{0,2},{1,3},{2,0},{3,1},{4,6},{5,7},{6,4},{7,5},{8,10},{9,11},{10,... | collective-permute-start | bytes 331784 | tf_op jit(solution)/shard_map/while/body/eval_jaxpr/attend/ppermute | solution.py:355
  561.9 4.9 collective-permute-start.23
  (71 other events, 383.4 us)
Sparse Core Ops, SparseCore 0:
  31.3 118.3 all-gather.4
  152.3 115.1 all-gather.6

commit v5 on v4

v5 whole, which is shorter than its diff:
```python
import functools

import jax
import jax.numpy as jnp
from jax import lax
from jax.experimental import pallas as pl
from jax.experimental.pallas import tpu as pltpu
from jax.sharding import PartitionSpec as P

HEADS = 32
KVH = 8
HD = 64
SHARE = HEADS // KVH
QW = SHARE * HD
EPS = 1e-05
NEG = -1e30
LOG2E = 1.4426950408889634
SHARD = 64
Q_ROWS = QW // 128 * SHARD
QKV_ROWS = Q_ROWS + SHARD
ALL_ROWS = QKV_ROWS + Q_ROWS

ZN = 8
XN = 4
SN = 8
F32 = jnp.float32
BF16 = jnp.bfloat16


def seq_pairs(mask):
    return [(i, i ^ mask) for i in range(ZN * XN)]


def section_pairs(mask):
    return [(i, i ^ mask) for i in range(SN)]


def along_z():
    return [[z * XN + x for z in range(ZN)] for x in range(XN)]


def spread(piece):
    near = [piece] + [lax.ppermute(piece, "section", section_pairs(2 * d)) for d in (1, 2, 3)]
    other = lax.ppermute(jnp.stack(near), "section", section_pairs(1))
    return near + [other]


def in_order(refs):
    out = [(2 * d, refs[d][...]) for d in range(4)]
    out += [(2 * d + 1, refs[4][d]) for d in range(4)]
    return out


def place(me, layer, piece_refs, out_ref, sems):
    def copies():
        for i, (mask, source) in enumerate(sources(piece_refs)):
            first = pl.multiple_of(jnp.bitwise_xor(me, mask) * QW, QW)
            yield pltpu.make_async_copy(source, out_ref.at[:, pl.ds(first, QW)], sems.at[i])

    @pl.when(me == layer - 1)
    def _():
        for copy in copies():
            copy.start()
        for copy in copies():
            copy.wait()


def sources(refs):
    out = [(2 * d, refs[d]) for d in range(4)]
    return out + [(2 * d + 1, refs[4].at[d]) for d in range(4)]


def place_kernel(scal, p0, p1, p2, p3, p4, out_in, out_ref, sems):
    place(scal[0], scal[3], [p0, p1, p2, p3, p4], out_ref, sems)


ORDER = (0, 2, 4, 6, 1, 3, 5, 7)


def lanes(block):
    panels = block.shape[1] // SHARD
    parts = [block[:, p * SHARD : (p + 1) * SHARD, :].reshape(XN * SHARD, 128) for p in range(panels)]
    return parts[0] if panels == 1 else jnp.concatenate(parts, axis=1)


def stream(me, slot, w_ref, held, sems):
    copies = []
    for i, mask in enumerate(ORDER):
        owner = jnp.bitwise_xor(me, mask)
        source = w_ref.at[pl.ds(XN * owner, XN), slot, 0:Q_ROWS, :]
        copies.append(pltpu.make_async_copy(source, held.at[i], sems.at[i]))
    for copy in copies:
        copy.start()

    def w_of(i):
        copies[i].wait()
        return lanes(held[i])

    return w_of


def resident(me, w_ref):
    return lambda i: lanes(w_ref[pl.ds(XN * jnp.bitwise_xor(me, ORDER[i]), XN)])


def assembled(me, seq, parts, held, first):
    x_me = jnp.bitwise_and(seq, XN - 1)
    count = held.shape[2]
    for d in range(XN):
        held[jnp.bitwise_xor(x_me, d)] = parts[d][:, first : first + count, :]
    return lambda i: lanes(held[:, jnp.bitwise_xor(me, ORDER[i])])


def project(me, gain_ref, layer, piece_refs, w_of):
    pieces = [(mask, value.astype(F32)) for mask, value in in_order(piece_refs)]
    width = sum(value.shape[1] for _, value in pieces)
    squares = functools.reduce(jnp.add, [value * value for _, value in pieces])
    scale = lax.rsqrt(jnp.sum(squares, axis=-1, keepdims=True) / width + EPS)
    total = None
    for i, (mask, value) in enumerate(pieces):
        owner = jnp.bitwise_xor(me, mask)
        gain = gain_ref[layer, pl.ds(owner, 1), 0, :].astype(F32)
        normed = (value * scale * gain).astype(BF16)
        part = jnp.dot(normed, w_of(i), preferred_element_type=F32)
        total = part if total is None else total + part
    return total.astype(BF16)


def write_keys(pair, kv_ref):
    for i in range(kv_ref.shape[0]):
        kv_ref[i] = pair


def keys_kernel(scal, gain_ref, p0, p1, p2, p3, p4, wkv_ref, kv_ref):
    w_of = resident(scal[0], wkv_ref)
    write_keys(project(scal[0], gain_ref, scal[3], [p0, p1, p2, p3, p4], w_of), kv_ref)


def queries_kernel(
    scal, gain_ref, p0, p1, p2, p3, p4, w_ref, out_in, q_ref, out_ref, wout_ref, wkv_ref, held, sems, out_sems
):
    refs = [p0, p1, p2, p3, p4]
    slot = scal[2]
    w_of = stream(scal[0], slot, w_ref, held, sems)
    later = jnp.minimum(slot + 1, w_ref.shape[1] - 1)
    ahead = [
        pltpu.make_async_copy(w_ref.at[:, slot, QKV_ROWS:ALL_ROWS, :], wout_ref, sems.at[SN]),
        pltpu.make_async_copy(w_ref.at[:, later, Q_ROWS:QKV_ROWS, :], wkv_ref, sems.at[SN + 1]),
    ]
    for copy in ahead:
        copy.start()
    q_ref[...] = project(scal[0], gain_ref, scal[3], refs, w_of)
    place(scal[0], scal[3], refs, out_ref, out_sems)
    for copy in ahead:
        copy.wait()


def first_keys_kernel(scal, gain_ref, p0, p1, p2, p3, p4, w0, w1, w2, w3, kv_ref, held):
    w_of = assembled(scal[0], scal[1], [w0, w1, w2, w3], held, Q_ROWS)
    write_keys(project(scal[0], gain_ref, scal[3], [p0, p1, p2, p3, p4], w_of), kv_ref)


def first_queries_kernel(scal, gain_ref, p0, p1, p2, p3, p4, w0, w1, w2, w3, q_ref, held):
    w_of = assembled(scal[0], scal[1], [w0, w1, w2, w3], held, 0)
    q_ref[...] = project(scal[0], gain_ref, scal[3], [p0, p1, p2, p3, p4], w_of)


def attend_kernel(scal, q_ref, k_ref, o_ref, *, d, blocks, tok):
    seq = scal[1]
    x_me = jnp.bitwise_and(seq, XN - 1)
    span = ZN * tok
    rows = SHARE * tok
    row = lax.rem(lax.broadcasted_iota(jnp.int32, (rows, 1), 0), tok)
    col = lax.broadcasted_iota(jnp.int32, (1, span), 1)
    col = lax.div(col, tok) * (XN * tok) + lax.rem(col, tok)
    asker = seq - x_me + jnp.bitwise_xor(x_me, d)
    visible = col <= row + (asker - x_me) * tok
    factor = HD**-0.5 * LOG2E
    q_parts = []
    for b in range(blocks):
        q_rows = q_ref[b * tok : (b + 1) * tok, :]
        q_parts += [q_rows[:, h * HD : (h + 1) * HD] for h in range(SHARE)]
    q_rows = jnp.concatenate(q_parts, axis=0)
    q_rows = jnp.concatenate([q_rows, jnp.zeros((blocks * rows, HD), BF16)], axis=1)
    pairs = []
    scores = {}
    for kb in range(blocks):
        pair = k_ref[:, kb * tok : (kb + 1) * tok, :].reshape(span, 2 * HD)
        s = lax.dot_general(
            q_rows[kb * rows :], pair, (((1,), (1,)), ((), ())), preferred_element_type=F32
        )
        pairs.append(pair)
        for b in range(kb, blocks):
            part = s[(b - kb) * rows : (b - kb + 1) * rows]
            scores[b, kb] = jnp.where(visible, part, NEG) if b == kb else part
    peaks = []
    for b in range(blocks):
        peak = functools.reduce(jnp.maximum, [scores[b, kb] for kb in range(b + 1)])
        peaks.append(jnp.max(peak, axis=-1, keepdims=True) * factor)
    totals = [jnp.zeros((rows, span), F32) for _ in range(blocks)]
    sums = [jnp.zeros((rows, 2 * HD), F32) for _ in range(blocks)]
    for kb in range(blocks):
        probs = []
        for b in range(kb, blocks):
            p = jnp.exp2(scores[b, kb] * factor - peaks[b])
            totals[b] += p
            probs.append(p.astype(BF16))
        got = jnp.dot(jnp.concatenate(probs, axis=0), pairs[kb], preferred_element_type=F32)
        for b in range(kb, blocks):
            sums[b] += got[(b - kb) * rows : (b - kb + 1) * rows]
    lane = lax.broadcasted_iota(jnp.int32, (tok, 2 * HD), 1)
    for b in range(blocks):
        total = jnp.sum(totals[b], axis=-1, keepdims=True)
        result = (sums[b][:, HD:] / total).astype(BF16)
        weight = peaks[b] + jnp.log(total) * LOG2E
        high = weight.astype(BF16).astype(F32)
        low = weight - high
        notes = jnp.zeros((tok, 2 * HD), F32)
        for h in range(SHARE):
            part = slice(h * tok, (h + 1) * tok)
            notes = jnp.where(lane == h, high[part], notes)
            notes = jnp.where(lane == SHARE + h, low[part], notes)
        o_ref[b * tok : (b + 1) * tok, :] = jnp.concatenate(
            [result[h * tok : (h + 1) * tok] for h in range(SHARE)] + [notes.astype(BF16)], axis=1
        )


def combine_kernel(scal, o0, o1, o2, o3, a_ref):
    parts = [o0[...], o1[...], o2[...], o3[...]]
    notes = [part[:, QW:].astype(F32) for part in parts]
    for h in range(SHARE):
        weights = [n[:, h : h + 1] + n[:, SHARE + h : SHARE + h + 1] for n in notes]
        peak = functools.reduce(jnp.maximum, weights)
        weights = [jnp.exp2(w - peak) for w in weights]
        total = functools.reduce(jnp.add, weights)
        cols = slice(h * HD, (h + 1) * HD)
        mixed = functools.reduce(
            jnp.add, [w / total * part[:, cols].astype(F32) for w, part in zip(weights, parts)]
        )
        a_ref[:, cols] = mixed.astype(BF16)


def output(piece_refs, h_ref, w_of, o_ref):
    total = h_ref[...].astype(F32)
    update = jnp.zeros(total.shape, F32)
    for i, (_, value) in enumerate(in_order(piece_refs)):
        update += jnp.dot(value, w_of(i), preferred_element_type=F32)
    o_ref[...] = (total + update).astype(BF16)


def output_kernel(scal, a0, a1, a2, a3, a4, h_ref, wout_ref, o_ref):
    output([a0, a1, a2, a3, a4], h_ref, resident(scal[0], wout_ref), o_ref)


def first_output_kernel(scal, a0, a1, a2, a3, a4, h_ref, w0, w1, w2, w3, o_ref, held):
    w_of = assembled(scal[0], scal[1], [w0, w1, w2, w3], held, 0)
    output([a0, a1, a2, a3, a4], h_ref, w_of, o_ref)


VMEM = pl.BlockSpec(memory_space=pltpu.VMEM)
SMEM = pl.BlockSpec(memory_space=pltpu.SMEM)
ANY = pl.BlockSpec(memory_space=pl.ANY)


def call(kernel, scal, args, out_shape, flops, bytes_accessed, exps=0, scratch=(), big=(), own=None):
    outs = out_shape if isinstance(out_shape, list) else [out_shape]
    in_specs = [SMEM] + [ANY if i in big else VMEM for i in range(len(args))]
    out_specs = [VMEM] * len(outs)
    aliases = {}
    if own is not None:
        out_specs[own[1]] = ANY
        aliases = {own[0] + 1: own[1]}
    single = not isinstance(out_shape, list)
    return pl.pallas_call(
        kernel,
        out_shape=out_shape,
        in_specs=in_specs,
        out_specs=out_specs[0] if single else out_specs,
        scratch_shapes=list(scratch),
        input_output_aliases=aliases,
        compiler_params=pltpu.CompilerParams(vmem_limit_bytes=24 * 1024 * 1024),
        cost_estimate=pl.CostEstimate(flops=flops, bytes_accessed=bytes_accessed, transcendentals=exps),
    )(scal, *args)


def local(inputs, norm_gain, w_query, w_key, w_value, w_out):
    blocks, tok, width = inputs.shape
    rows = blocks * tok
    me = lax.axis_index("section")
    seq = lax.axis_index("seq")
    layers = lax.axis_size("section")
    shard = w_query.shape[1]
    assert shard == SHARD

    def panels(w):
        w = w.reshape(shard, SN, -1, 128)
        return w.transpose(1, 2, 0, 3).reshape(SN, -1, 128)

    pair = jnp.concatenate([w_key[0].reshape(shard, SN, HD), w_value[0].reshape(shard, SN, HD)], axis=-1)
    gain_rows = jnp.broadcast_to(norm_gain.reshape(1, width // 128, 128), (SN, width // 128, 128))
    mine = jnp.concatenate([panels(w_query[0]), panels(pair), panels(w_out[0]), gain_rows], axis=1)
    by_layer = lax.all_to_all(mine, "section", split_axis=0, concat_axis=0, tiled=True)
    gains = by_layer[:, ALL_ROWS:].reshape(layers, SN, 1, QW)
    by_layer = by_layer[:, :ALL_ROWS]

    with jax.named_scope("weights"):
        early = lax.all_gather(by_layer[1:4], "seq", axis=0)
        late = lax.all_gather(by_layer[4:], "seq", axis=0)

        def over_z(part):
            part = jnp.broadcast_to(part[None], (ZN,) + part.shape)
            return lax.all_to_all(
                part, "seq", split_axis=0, concat_axis=0, tiled=True, axis_index_groups=along_z()
            )

        def over_x(part):
            return [part] + [lax.ppermute(part, "seq", seq_pairs(d)) for d in (1, 2, 3)]

        first_qkv = over_z(by_layer[0, :QKV_ROWS])
        first_qkv, first_out = lax.optimization_barrier((first_qkv, by_layer[0, QKV_ROWS:]))
        first_qkv, first_out = lax.optimization_barrier((over_x(first_qkv), over_z(first_out)))
        first_out = over_x(first_out)

    flat = inputs.reshape(rows, width)

    def input_piece(mask):
        return lax.dynamic_slice_in_dim(flat, jnp.bitwise_xor(me, mask) * QW, QW, 1)

    pieces = [input_piece(2 * d) for d in range(4)]
    pieces.append(jnp.stack([input_piece(2 * d + 1) for d in range(4)]))

    piece_shape = jax.ShapeDtypeStruct((rows, QW), BF16)
    kv_shape = jax.ShapeDtypeStruct((ZN, rows, 2 * HD), BF16)
    part_shape = jax.ShapeDtypeStruct((rows, QW + 2 * HD), BF16)
    out_shape = jax.ShapeDtypeStruct((rows, width), BF16)
    seq_keys = ZN * XN * tok
    keys_cost = (4 * rows * width * HD, 2 * (width * 2 * HD + rows * width))
    full_cost = (2 * rows * width * QW, 2 * (width * QW + rows * width))

    def first_room(count):
        return [pltpu.VMEM((XN, ZN, count, 128), BF16)]

    def exchange(q, kv):
        with jax.named_scope("exchange"):
            qs = [q] + [lax.ppermute(q, "seq", seq_pairs(d)) for d in (1, 2, 3)]
            kv = lax.all_to_all(
                kv, "seq", split_axis=0, concat_axis=0, tiled=True, axis_index_groups=along_z()
            )
        return qs, kv

    def attend(scal, qs, kv):
        parts = [None] * XN
        with jax.named_scope("attend"):
            for d in (2, 1, 3, 0):
                part = call(
                    functools.partial(attend_kernel, d=d, blocks=blocks, tok=tok),
                    scal,
                    (qs[d], kv),
                    part_shape,
                    SHARE * tok * seq_keys * 128 * 6,
                    2 * (ZN * rows * 128 + 3 * rows * QW),
                    SHARE * tok * seq_keys * 6 // 4,
                )
                parts[d] = lax.ppermute(part, "seq", seq_pairs(d)) if d else part
            attended = call(
                combine_kernel,
                scal,
                parts,
                piece_shape,
                10 * rows * QW,
                10 * rows * QW,
            )
            return spread(attended)

    def numbers(slot, layer):
        return jnp.stack([jnp.asarray(v, jnp.int32) for v in (me, seq, slot, layer)])

    scal = numbers(0, 0)
    with jax.named_scope("project"):
        args = (gains, *pieces, *first_qkv)
        kv = call(first_keys_kernel, scal, args, kv_shape, *keys_cost, scratch=first_room(SHARD))
        q = call(first_queries_kernel, scal, args, piece_shape, *full_cost, scratch=first_room(Q_ROWS))
    qs, kv = exchange(q, kv)
    kv, first_out = lax.optimization_barrier((kv, first_out))
    heads = attend(scal, qs, kv)
    with jax.named_scope("output"):
        args = (*heads, pieces[0], *first_out)
        own = call(first_output_kernel, scal, args, piece_shape, *full_cost, scratch=first_room(Q_ROWS))
        pieces = spread(own)
    out = jnp.zeros((rows, width), BF16)

    wkv_shape = jax.ShapeDtypeStruct((ZN * XN, SHARD, 128), BF16)
    wout_shape = jax.ShapeDtypeStruct((ZN * XN, Q_ROWS, 128), BF16)
    query_room = [
        pltpu.VMEM((SN, XN, Q_ROWS, 128), BF16),
        pltpu.SemaphoreType.DMA((SN + 2,)),
        pltpu.SemaphoreType.DMA((SN,)),
    ]

    def step(group, first_layer):
        def body(layer, carry):
            pieces, out, wkv = carry
            scal = numbers(layer - first_layer, layer)
            with jax.named_scope("project"):
                kv = call(keys_kernel, scal, (gains, *pieces, wkv), kv_shape, *keys_cost)
                q, out, wout, wkv = call(
                    queries_kernel,
                    scal,
                    (gains, *pieces, group, out),
                    [piece_shape, out_shape, wout_shape, wkv_shape],
                    *full_cost,
                    scratch=query_room,
                    big=(6, 7),
                    own=(7, 1),
                )
            heads = attend(scal, *exchange(q, kv))
            with jax.named_scope("output"):
                own = call(output_kernel, scal, (*heads, pieces[0], wout), piece_shape, *full_cost)
                return spread(own), out, wkv

        return body

    for group, begin, end in ((early, 1, 4), (late, 4, layers)):
        carry = (pieces, out, group[:, 0, Q_ROWS:QKV_ROWS])
        pieces, out, _ = lax.fori_loop(begin, end, step(group, begin), carry)
    out = call(
        place_kernel,
        numbers(0, layers),
        (*pieces, out),
        out_shape,
        0,
        4 * rows * width,
        scratch=[pltpu.SemaphoreType.DMA((SN,))],
        big=(5,),
        own=(5, 0),
    )
    return out.reshape(1, blocks, tok, width)


def solution(mesh):
    in_specs = (
        P(None, "seq", None),
        P("section", None),
        P("section", "seq", None),
        P("section", "seq", None),
        P("section", "seq", None),
        P("section", "seq", None),
    )
    out_specs = P("section", None, "seq", None)
    return jax.shard_map(local, mesh=mesh, in_specs=in_specs, out_specs=out_specs, check_vma=False)
```

time: 598 us -> 655 us (1.095)
  waiting for transfers between devices: 185 us -> 274 us
  Pallas kernels: 128 us -> 105 us
    all_gather x2, waiting for transfers between devices: 0.01 us -> 98.7 us  [the longest x1 98.7 us: local(): late = lax.all_gather(by_layer[4:], 'seq', axis=0)]
    pallas_call x65, Pallas kernels: 128 us -> 105 us  [call(): pl.pallas_call(kernel, out_shape=out_shape, in_specs=in_specs, out_specs=...]
    all_to_all x8, waiting for transfers between devices: 47.4 us -> 40.7 us  [exchange(): lax.all_to_all(kv, 'seq', split_axis=0, concat_axis=0, tiled=True, axis_i...]
  transfers between devices with their start and end apart: 130 -> 130, of which waited for: 79 -> 79; matrix products, arithmetic and copies ran while one was open for 1% -> 1% of each run, Pallas kernels for 17% -> 12%
where the time goes in v5:
time: 655 us; the launch traced here: 649 us
  waiting for transfers between devices  274 us (42%)
  starting transfers between devices  218 us (33%)
  Pallas kernels  105 us (16%)
  blocking collectives  17 us (3%)
  between operations  13.8 us (2%)
  loops' own time  9.94 us (2%)
  local copies, waits for them, and re-layouts  9.71 us (1%)
    pallas_call x65, Pallas kernels, call(): pl.pallas_call(kernel, out_shape=out_shape, in_specs=in_specs, out_specs=...  105 us
    all_gather x1, waiting for transfers between devices, local(): late = lax.all_gather(by_layer[4:], 'seq', axis=0)  98.7 us
    ppermute x48, starting transfers between devices, spread(): lax.ppermute(piece, 'section', section_pairs(2 * d))  54.9 us
    ppermute x16, starting transfers between devices, spread(): other = lax.ppermute(jnp.stack(near), 'section', section_pairs(1))  52.7 us
    ppermute x48, waiting for transfers between devices, spread(): lax.ppermute(piece, 'section', section_pairs(2 * d))  50.7 us
    all_to_all x8, waiting for transfers between devices, exchange(): lax.all_to_all(kv, 'seq', split_axis=0, concat_axis=0, tiled=True, axis_i...  40.7 us
    ppermute x24, starting transfers between devices, attend(): parts[d] = lax.ppermute(part, 'seq', seq_pairs(d)) if d else part  31.6 us
    all_to_all x8, starting transfers between devices, exchange(): lax.all_to_all(kv, 'seq', split_axis=0, concat_axis=0, tiled=True, axis_i...  30.5 us
  transfers between devices with their start and end apart: 130, of which 79 were waited for; matrix products, arithmetic and copies ran while one was open for 1% of the time, Pallas kernels for 12%

profile of v5, /device:TPU:1, one launch (start us, length us, event | category | flops | bytes accessed | tf_op | source)
XLA Modules:
  0.0 649.1 jit_solution(8307678437051878822)
XLA Ops:
  9.5 17.0 %all_to_all.32 = bf16[8,336,128]{2,1,0:T(8,128)(2,1)S(1)} all-to-all(bf16[8,336,128]{2,1,0:T(8,128)(2,1)S(1)} %pad_maximum_fusion.4), channel_id=1, replica_groups=mesh['section'=8,'seq'=32] {'section'}, dimensions={0} | all-to-all | bytes 1376256 | tf_op jit(solution)/shard_map/all_to_all | solution.py:302
  28.9 8.2 %all-to-all-start.3 = ((bf16[8,192,128]{2,1,0:T(8,128)(2,1)}), bf16[8,192,128]{2,1,0:T(8,128)(2,1)S(1)}, u32[]{:S(2)}, u32[]{:S(2)}) async-start(bf16[8,192,128]{2,1,0:T(8,128)(2,1)} %broadcast_in_dim.26), calls=%async_computation.3 | async-start | bytes 786432 | tf_op jit(solution)/shard_map/weights/all_to_all | solution.py:312
  37.1 15.0 %all-to-all-done.3.w0 = bf16[8,192,128]{2,1,0:T(8,128)(2,1)S(1)} async-done(((bf16[8,192,128]{2,1,0:T(8,128)(2,1)}), bf16[8,192,128]{2,1,0:T(8,128)(2,1)S(1)}, u32[]{:S(2)}, u32[]{:S(2)}) %all-to-all-start.3) | async-done | bytes 393248 | tf_op jit(solution)/shard_map/weights/all_to_all | solution.py:312
  52.9 3.4 all-to-all-start.4
  57.5 2.4 collective-permute-start.29
  60.5 4.1 collective-permute-done.28.w1
  64.5 9.5 %collective-permute-done.29.w2 = bf16[8,192,128]{2,1,0:T(8,128)(2,1)S(1)} collective-permute-done((bf16[8,192,128]{2,1,0:T(8,128)(2,1)S(1)}, bf16[8,192,128]{2,1,0:T(8,128)(2,1)S(1)}, u32[]{:S(2)}, u32[]{:S(2)}) %collective-permute-start.29) | collective-permute-done | bytes 393248 | tf_op jit(solution)/shard_map/weights/ppermute | solution.py:317
  75.8 5.9 all-to-all-start.5
  81.7 2.4 collective-permute-start.32
  88.8 4.0 collective-permute-done.31.w1
  92.8 12.1 %collective-permute-done.32.w2 = bf16[8,128,128]{2,1,0:T(8,128)(2,1)S(1)} collective-permute-done((bf16[8,128,128]{2,1,0:T(8,128)(2,1)S(1)}, bf16[8,128,128]{2,1,0:T(8,128)(2,1)S(1)}, u32[]{:S(2)}, u32[]{:S(2)}) %collective-permute-start.32) | collective-permute-done | bytes 262176 | tf_op jit(solution)/shard_map/weights/ppermute | solution.py:317
  115.4 2.2 collective-permute-done.39.o3
  118.2 3.8 collective-permute-done.35.o1
  123.4 3.7 collective-permute-start.42
  129.4 10.7 %collective-permute-start.43 = (bf16[4,144,256]{2,1,0:T(8,128)(2,1)S(1)}, bf16[4,144,256]{2,1,0:T(8,128)(2,1)S(1)}, u32[]{:S(2)}, u32[]{:S(2)}) collective-permute-start(bf16[4,144,256]{2,1,0:T(8,128)(2,1)S(1)} %pad_maximum_fusion.6), channel_id=1, source_target_pairs={{0,32},{32,0},{64,96},{96,64},{128,160},{160,128},{192,224},{224,1... | collective-permute-start | bytes 884744 | tf_op jit(solution)/shard_map/attend/ppermute | solution.py:44
  142.9 3.6 collective-permute-start.45
  146.6 3.2 collective-permute-done.45
  155.0 98.7 %all-gather.7.cloned.1.call-done = bf16[128,320,128]{2,1,0:T(8,128)(2,1)} async-done(((bf16[4,320,128]{2,1,0:T(8,128)(2,1)}), bf16[128,320,128]{2,1,0:T(8,128)(2,1)}) %all-gather.7.cloned.1.call-update) | async-done | bytes 10485776 | tf_op jit(solution)/shard_map/weights/all_gather | solution.py:308
  254.9 162.8 %while.58 = (s32[]{:T(128)}, bf16[144,256]{1,0:T(8,128)(2,1)S(1)}, bf16[144,256]{1,0:T(8,128)(2,1)S(1)}, bf16[144,256]{1,0:T(8,128)(2,1)S(1)}, bf16[144,256]{1,0...) while((s32[]{:T(128)}, bf16[144,256]{1,0:T(8,128)(2,1)S(1)}, ...), condition=%wide.region_1.0_spmd, body=%wide.region_0.0_spmd.sunk | while | flops 1284710400 | bytes 15377141 | solution.py:425
  255.0 2.2 project.49
  257.2 4.1 all-to-all-start
  261.3 3.3 project.48
  268.5 3.4 all-to-all-done.k_ref
  278.5 2.2 collective-permute-start.5
  282.3 2.3 collective-permute-done.5.o3
  285.8 2.6 collective-permute-start.8
  290.3 2.8 collective-permute-done.7.a2
  293.1 4.9 collective-permute-start.9
  309.8 2.2 project.49
  312.0 3.4 all-to-all-start
  315.5 3.4 project.48
  318.9 3.3 collective-permute-start.2
  322.8 5.6 all-to-all-done.k_ref
  331.7 3.3 collective-permute-start.3
  338.8 2.6 collective-permute-done.5.o3
  349.0 3.7 collective-permute-start.9
  364.5 2.2 project.49
  366.8 3.4 all-to-all-start
  370.2 3.3 project.48
  377.5 5.7 all-to-all-done.k_ref
  402.3 3.7 collective-permute-start.9
  417.7 223.0 %while.59 = (s32[]{:T(128)}, bf16[144,256]{1,0:T(8,128)(2,1)S(1)}, bf16[144,256]{1,0:T(8,128)(2,1)S(1)}, bf16[144,256]{1,0:T(8,128)(2,1)S(1)}, bf16[144,256]{1,0...) while((s32[]{:T(128)}, bf16[144,256]{1,0:T(8,128)(2,1)S(1)}, ...), condition=%wide.region_3.0_spmd, body=%wide.region_2.0_spmd.sunk | while | flops 1284710400 | bytes 15377153 | solution.py:425
  428.9 3.4 all-to-all-start.1
  432.3 2.5 project.50
  435.7 2.5 collective-permute-start.16
  438.8 6.5 all-to-all-done.1.k_ref
  449.2 2.6 collective-permute-start.17
  455.6 2.6 collective-permute-done.19.o3
  465.9 3.7 collective-permute-start.23
  483.1 3.4 all-to-all-start.1
  486.5 2.5 project.50
  493.0 6.5 all-to-all-done.1.k_ref
  518.5 3.7 collective-permute-start.23
  535.7 3.4 all-to-all-start.1
  539.2 2.5 project.50
  542.5 2.5 collective-permute-start.16
  545.6 6.5 all-to-all-done.1.k_ref
  556.1 2.6 collective-permute-start.17
  562.5 2.6 collective-permute-done.19.o3
  572.6 3.7 collective-permute-start.23
  589.9 3.4 all-to-all-start.1
  593.3 2.5 project.50
  599.8 6.5 all-to-all-done.1.k_ref
  625.2 3.7 collective-permute-start.23
  (337 shorter events, 261.9 us)
Async XLA Ops:
  6.5 146.6 %all-gather.5.cloned.1.call-start = ((), (), s32[]{:S(2)}) async-start(), calls=%async_computation.6 | async-start | bytes 8110080 | tf_op jit(solution)/shard_map/weights/all_gather | solution.py:307
  27.3 226.4 %all-gather.7.cloned.1.call-start = ((), (), s32[]{:S(2)}) async-start(), calls=%async_computation.7 | async-start | bytes 10813440 | tf_op jit(solution)/shard_map/weights/all_gather | solution.py:308
  28.9 23.2 %all-to-all-start.3 = ((bf16[8,192,128]{2,1,0:T(8,128)(2,1)}), bf16[8,192,128]{2,1,0:T(8,128)(2,1)S(1)}, u32[]{:S(2)}, u32[]{:S(2)}) async-start(bf16[8,192,128]{2,1,0:T(8,128)(2,1)} %broadcast_in_dim.26), calls=%async_computation.3 | async-start | bytes 786432 | tf_op jit(solution)/shard_map/weights/all_to_all | solution.py:312
  52.9 21.2 %all-to-all-start.4 = ((bf16[8,128,128]{2,1,0:T(8,128)(2,1)}), bf16[8,128,128]{2,1,0:T(8,128)(2,1)S(1)}, u32[]{:S(2)}, u32[]{:S(2)}) async-start(bf16[8,128,128]{2,1,0:T(8,128)(2,1)} %broadcast_in_dim.27), calls=%async_computation.4 | async-start | bytes 524288 | tf_op jit(solution)/shard_map/weights/all_to_all | solution.py:312
  56.3 8.3 %collective-permute-start.28 = (bf16[8,192,128]{2,1,0:T(8,128)(2,1)S(1)}, bf16[8,192,128]{2,1,0:T(8,128)(2,1)S(1)}, u32[]{:S(2)}, u32[]{:S(2)}) collective-permute-start(bf16[8,192,128]{2,1,0:T(8,128)(2,1)S(1)} %all-to-all-done.3.w0), channel_id=1, source_target_pairs={{0,1},{1,0},{2,3},{3,2},{4,5},{5,4},{6,7},{7,6},{8,9},{9,8},{10,11... | collective-permute-start | bytes 1179656 | tf_op jit(solution)/shard_map/weights/ppermute | solution.py:317
  57.5 16.6 %collective-permute-start.29 = (bf16[8,192,128]{2,1,0:T(8,128)(2,1)S(1)}, bf16[8,192,128]{2,1,0:T(8,128)(2,1)S(1)}, u32[]{:S(2)}, u32[]{:S(2)}) collective-permute-start(bf16[8,192,128]{2,1,0:T(8,128)(2,1)S(1)} %all-to-all-done.3.w0), channel_id=1, source_target_pairs={{0,2},{1,3},{2,0},{3,1},{4,6},{5,7},{6,4},{7,5},{8,10},{9,11},{10,... | collective-permute-start | bytes 1179656 | tf_op jit(solution)/shard_map/weights/ppermute | solution.py:317
  59.9 14.2 %collective-permute-start.30 = (bf16[8,192,128]{2,1,0:T(8,128)(2,1)S(1)}, bf16[8,192,128]{2,1,0:T(8,128)(2,1)S(1)}, u32[]{:S(2)}, u32[]{:S(2)}) collective-permute-start(bf16[8,192,128]{2,1,0:T(8,128)(2,1)S(1)} %all-to-all-done.3.w0), channel_id=1, source_target_pairs={{0,3},{1,2},{2,1},{3,0},{4,7},{5,6},{6,5},{7,4},{8,11},{9,10},{10,... | collective-permute-start | bytes 1179656 | tf_op jit(solution)/shard_map/weights/ppermute | solution.py:317
  75.8 29.0 %all-to-all-start.5 = ((bf16[8,144,128]{2,1,0:T(8,128)(2,1)}), bf16[8,144,128]{2,1,0:T(8,128)(2,1)S(1)}, u32[]{:S(2)}, u32[]{:S(2)}) async-start(bf16[8,144,128]{2,1,0:T(8,128)(2,1)} %project.47), calls=%async_computation.5 | async-start | bytes 589824 | tf_op jit(solution)/shard_map/exchange/all_to_all | solution.py:346
  81.7 11.0 %collective-permute-start.31 = (bf16[8,128,128]{2,1,0:T(8,128)(2,1)S(1)}, bf16[8,128,128]{2,1,0:T(8,128)(2,1)S(1)}, u32[]{:S(2)}, u32[]{:S(2)}) collective-permute-start(bf16[8,128,128]{2,1,0:T(8,128)(2,1)S(1)} %all-to-all-done.4.w0), channel_id=1, source_target_pairs={{0,1},{1,0},{2,3},{3,2},{4,5},{5,4},{6,7},{7,6},{8,9},{9,8},{10,11... | collective-permute-start | bytes 786440 | tf_op jit(solution)/shard_map/weights/ppermute | solution.py:317
  81.7 23.1 %collective-permute-start.32 = (bf16[8,128,128]{2,1,0:T(8,128)(2,1)S(1)}, bf16[8,128,128]{2,1,0:T(8,128)(2,1)S(1)}, u32[]{:S(2)}, u32[]{:S(2)}) collective-permute-start(bf16[8,128,128]{2,1,0:T(8,128)(2,1)S(1)} %all-to-all-done.4.w0), channel_id=1, source_target_pairs={{0,2},{1,3},{2,0},{3,1},{4,6},{5,7},{6,4},{7,5},{8,10},{9,11},{10,... | collective-permute-start | bytes 786440 | tf_op jit(solution)/shard_map/weights/ppermute | solution.py:317
  84.1 20.7 %collective-permute-start.33 = (bf16[8,128,128]{2,1,0:T(8,128)(2,1)S(1)}, bf16[8,128,128]{2,1,0:T(8,128)(2,1)S(1)}, u32[]{:S(2)}, u32[]{:S(2)}) collective-permute-start(bf16[8,128,128]{2,1,0:T(8,128)(2,1)S(1)} %all-to-all-done.4.w0), channel_id=1, source_target_pairs={{0,3},{1,2},{2,1},{3,0},{4,7},{5,6},{6,5},{7,4},{8,11},{9,10},{10,... | collective-permute-start | bytes 786440 | tf_op jit(solution)/shard_map/weights/ppermute | solution.py:317
  87.6 17.3 %collective-permute-start.38 = (bf16[144,256]{1,0:T(8,128)(2,1)}, bf16[144,256]{1,0:T(8,128)(2,1)S(1)}, u32[]{:S(2)}, u32[]{:S(2)}) collective-permute-start(bf16[144,256]{1,0:T(8,128)(2,1)} %project.46.q_ref), channel_id=1, source_target_pairs={{0,3},{1,2},{2,1},{3,0},{4,7},{5,6},{6,5},{7,4},{8,11},{9,10},{10,... | collective-permute-start | bytes 221192 | tf_op jit(solution)/shard_map/exchange/ppermute | solution.py:345
  88.8 19.2 %collective-permute-start.36 = (bf16[144,256]{1,0:T(8,128)(2,1)}, bf16[144,256]{1,0:T(8,128)(2,1)S(1)}, u32[]{:S(2)}, u32[]{:S(2)}) collective-permute-start(bf16[144,256]{1,0:T(8,128)(2,1)} %project.46.q_ref), channel_id=1, source_target_pairs={{0,2},{1,3},{2,0},{3,1},{4,6},{5,7},{6,4},{7,5},{8,10},{9,11},{10,... | collective-permute-start | bytes 221192 | tf_op jit(solution)/shard_map/exchange/ppermute | solution.py:345
  92.8 17.5 %collective-permute-start.34 = (bf16[144,256]{1,0:T(8,128)(2,1)}, bf16[144,256]{1,0:T(8,128)(2,1)S(1)}, u32[]{:S(2)}, u32[]{:S(2)}) collective-permute-start(bf16[144,256]{1,0:T(8,128)(2,1)} %project.46.q_ref), channel_id=1, source_target_pairs={{0,1},{1,0},{2,3},{3,2},{4,5},{5,4},{6,7},{7,6},{8,9},{9,8},{10,11... | collective-permute-start | bytes 221192 | tf_op jit(solution)/shard_map/exchange/ppermute | solution.py:345
  106.4 11.3 %collective-permute-start.39 = (bf16[144,384]{1,0:T(8,128)(2,1)S(1)}, bf16[144,384]{1,0:T(8,128)(2,1)S(1)}, u32[]{:S(2)}, u32[]{:S(2)}) collective-permute-start(bf16[144,384]{1,0:T(8,128)(2,1)S(1)} %attend.78), channel_id=1, source_target_pairs={{0,3},{1,2},{2,1},{3,0},{4,7},{5,6},{6,5},{7,4},{8,11},{9,10},{10,... | collective-permute-start | bytes 331784 | tf_op jit(solution)/shard_map/attend/ppermute | solution.py:364
  109.5 8.7 %collective-permute-start.37 = (bf16[144,384]{1,0:T(8,128)(2,1)S(1)}, bf16[144,384]{1,0:T(8,128)(2,1)S(1)}, u32[]{:S(2)}, u32[]{:S(2)}) collective-permute-start(bf16[144,384]{1,0:T(8,128)(2,1)S(1)} %attend.77), channel_id=1, source_target_pairs={{0,2},{1,3},{2,0},{3,1},{4,6},{5,7},{6,4},{7,5},{8,10},{9,11},{10,... | collective-permute-start | bytes 331784 | tf_op jit(solution)/shard_map/attend/ppermute | solution.py:364
  111.9 10.1 %collective-permute-start.35 = (bf16[144,384]{1,0:T(8,128)(2,1)S(1)}, bf16[144,384]{1,0:T(8,128)(2,1)S(1)}, u32[]{:S(2)}, u32[]{:S(2)}) collective-permute-start(bf16[144,384]{1,0:T(8,128)(2,1)S(1)} %attend.76), channel_id=1, source_target_pairs={{0,1},{1,0},{2,3},{3,2},{4,5},{5,4},{6,7},{7,6},{8,9},{9,8},{10,11... | collective-permute-start | bytes 331784 | tf_op jit(solution)/shard_map/attend/ppermute | solution.py:364
  123.3 5.1 collective-permute-start.41
  123.4 5.9 collective-permute-start.42
  129.4 12.0 %collective-permute-start.43 = (bf16[4,144,256]{2,1,0:T(8,128)(2,1)S(1)}, bf16[4,144,256]{2,1,0:T(8,128)(2,1)S(1)}, u32[]{:S(2)}, u32[]{:S(2)}) collective-permute-start(bf16[4,144,256]{2,1,0:T(8,128)(2,1)S(1)} %pad_maximum_fusion.6), channel_id=1, source_target_pairs={{0,32},{32,0},{64,96},{96,64},{128,160},{160,128},{192,224},{224,1... | collective-permute-start | bytes 884744 | tf_op jit(solution)/shard_map/attend/ppermute | solution.py:44
  142.9 6.9 %collective-permute-start.45 = (bf16[144,256]{1,0:T(8,128)(2,1)S(1)}, bf16[144,256]{1,0:T(8,128)(2,1)S(1)}, u32[]{:S(2)}, u32[]{:S(2)}) collective-permute-start(bf16[144,256]{1,0:T(8,128)(2,1)S(1)} %output.23), channel_id=1, source_target_pairs={{0,128},{32,160},{64,192},{96,224},{128,0},{160,32},{192,64},{224,... | collective-permute-start | bytes 221192 | tf_op jit(solution)/shard_map/output/ppermute | solution.py:43
  151.5 103.3 %collective-permute-start.47 = (bf16[4,144,256]{2,1,0:T(8,128)(2,1)S(1)}, bf16[4,144,256]{2,1,0:T(8,128)(2,1)S(1)}, u32[]{:S(2)}, u32[]{:S(2)}) collective-permute-start(bf16[4,144,256]{2,1,0:T(8,128)(2,1)S(1)} %pad_maximum_fusion.7), channel_id=1, source_target_pairs={{0,32},{32,0},{64,96},{96,64},{128,160},{160,128},{192,224},{224,1... | collective-permute-start | bytes 884744 | tf_op jit(solution)/shard_map/output/ppermute | solution.py:44
  257.2 14.8 %all-to-all-start = ((bf16[8,144,128]{2,1,0:T(8,128)(2,1)}), bf16[8,144,128]{2,1,0:T(8,128)(2,1)S(1)}, u32[]{:S(2)}, u32[]{:S(2)}) async-start(bf16[8,144,128]{2,1,0:T(8,128)(2,1)} %project.49), calls=%async_computation | async-start | bytes 589824 | tf_op jit(solution)/shard_map/while/body/eval_jaxpr/exchange/all_to_all | solution.py:346
  264.7 8.9 %collective-permute-start.2 = (bf16[144,256]{1,0:T(8,128)(2,1)S(1)}, bf16[144,256]{1,0:T(8,128)(2,1)S(1)}, u32[]{:S(2)}, u32[]{:S(2)}) collective-permute-start(bf16[144,256]{1,0:T(8,128)(2,1)S(1)} %get-tuple-element.1057.q_ref), channel_id=1, source_target_pairs={{0,2},{1,3},{2,0},{3,1},{4,6},{5,7},{6,4},{7,5},{8,10},{9,11},{10,... | collective-permute-start | bytes 221192 | tf_op jit(solution)/shard_map/while/body/eval_jaxpr/exchange/ppermute | solution.py:345
  266.4 10.6 %collective-permute-start.4 = (bf16[144,256]{1,0:T(8,128)(2,1)S(1)}, bf16[144,256]{1,0:T(8,128)(2,1)S(1)}, u32[]{:S(2)}, u32[]{:S(2)}) collective-permute-start(bf16[144,256]{1,0:T(8,128)(2,1)S(1)} %get-tuple-element.1057.q_ref), channel_id=1, source_target_pairs={{0,3},{1,2},{2,1},{3,0},{4,7},{5,6},{6,5},{7,4},{8,11},{9,10},{10,... | collective-permute-start | bytes 221192 | tf_op jit(solution)/shard_map/while/body/eval_jaxpr/exchange/ppermute | solution.py:345
  273.5 8.8 %collective-permute-start.1 = (bf16[144,384]{1,0:T(8,128)(2,1)S(1)}, bf16[144,384]{1,0:T(8,128)(2,1)S(1)}, u32[]{:S(2)}, u32[]{:S(2)}) collective-permute-start(bf16[144,384]{1,0:T(8,128)(2,1)S(1)} %attend.81), channel_id=1, source_target_pairs={{0,1},{1,0},{2,3},{3,2},{4,5},{5,4},{6,7},{7,6},{8,9},{9,8},{10,11... | collective-permute-start | bytes 331784 | tf_op jit(solution)/shard_map/while/body/eval_jaxpr/attend/ppermute | solution.py:364
  275.2 7.1 %collective-permute-start.3 = (bf16[144,384]{1,0:T(8,128)(2,1)S(1)}, bf16[144,384]{1,0:T(8,128)(2,1)S(1)}, u32[]{:S(2)}, u32[]{:S(2)}) collective-permute-start(bf16[144,384]{1,0:T(8,128)(2,1)S(1)} %attend.82), channel_id=1, source_target_pairs={{0,2},{1,3},{2,0},{3,1},{4,6},{5,7},{6,4},{7,5},{8,10},{9,11},{10,... | collective-permute-start | bytes 331784 | tf_op jit(solution)/shard_map/while/body/eval_jaxpr/attend/ppermute | solution.py:364
  278.5 6.1 collective-permute-start.5
  293.1 6.1 collective-permute-start.9
  312.0 16.4 %all-to-all-start = ((bf16[8,144,128]{2,1,0:T(8,128)(2,1)}), bf16[8,144,128]{2,1,0:T(8,128)(2,1)S(1)}, u32[]{:S(2)}, u32[]{:S(2)}) async-start(bf16[8,144,128]{2,1,0:T(8,128)(2,1)} %project.49), calls=%async_computation | async-start | bytes 589824 | tf_op jit(solution)/shard_map/while/body/eval_jaxpr/exchange/all_to_all | solution.py:346
  318.9 11.1 %collective-permute-start.2 = (bf16[144,256]{1,0:T(8,128)(2,1)S(1)}, bf16[144,256]{1,0:T(8,128)(2,1)S(1)}, u32[]{:S(2)}, u32[]{:S(2)}) collective-permute-start(bf16[144,256]{1,0:T(8,128)(2,1)S(1)} %get-tuple-element.1057.q_ref), channel_id=1, source_target_pairs={{0,2},{1,3},{2,0},{3,1},{4,6},{5,7},{6,4},{7,5},{8,10},{9,11},{10,... | collective-permute-start | bytes 221192 | tf_op jit(solution)/shard_map/while/body/eval_jaxpr/exchange/ppermute | solution.py:345
  322.2 12.8 %collective-permute-start.4 = (bf16[144,256]{1,0:T(8,128)(2,1)S(1)}, bf16[144,256]{1,0:T(8,128)(2,1)S(1)}, u32[]{:S(2)}, u32[]{:S(2)}) collective-permute-start(bf16[144,256]{1,0:T(8,128)(2,1)S(1)} %get-tuple-element.1057.q_ref), channel_id=1, source_target_pairs={{0,3},{1,2},{2,1},{3,0},{4,7},{5,6},{6,5},{7,4},{8,11},{9,10},{10,... | collective-permute-start | bytes 221192 | tf_op jit(solution)/shard_map/while/body/eval_jaxpr/exchange/ppermute | solution.py:345
  330.0 8.8 %collective-permute-start.1 = (bf16[144,384]{1,0:T(8,128)(2,1)S(1)}, bf16[144,384]{1,0:T(8,128)(2,1)S(1)}, u32[]{:S(2)}, u32[]{:S(2)}) collective-permute-start(bf16[144,384]{1,0:T(8,128)(2,1)S(1)} %attend.81), channel_id=1, source_target_pairs={{0,1},{1,0},{2,3},{3,2},{4,5},{5,4},{6,7},{7,6},{8,9},{9,8},{10,11... | collective-permute-start | bytes 331784 | tf_op jit(solution)/shard_map/while/body/eval_jaxpr/attend/ppermute | solution.py:364
  331.7 7.1 %collective-permute-start.3 = (bf16[144,384]{1,0:T(8,128)(2,1)S(1)}, bf16[144,384]{1,0:T(8,128)(2,1)S(1)}, u32[]{:S(2)}, u32[]{:S(2)}) collective-permute-start(bf16[144,384]{1,0:T(8,128)(2,1)S(1)} %attend.82), channel_id=1, source_target_pairs={{0,2},{1,3},{2,0},{3,1},{4,6},{5,7},{6,4},{7,5},{8,10},{9,11},{10,... | collective-permute-start | bytes 331784 | tf_op jit(solution)/shard_map/while/body/eval_jaxpr/attend/ppermute | solution.py:364
  349.0 4.9 collective-permute-start.9
  366.8 16.4 %all-to-all-start = ((bf16[8,144,128]{2,1,0:T(8,128)(2,1)}), bf16[8,144,128]{2,1,0:T(8,128)(2,1)S(1)}, u32[]{:S(2)}, u32[]{:S(2)}) async-start(bf16[8,144,128]{2,1,0:T(8,128)(2,1)} %project.49), calls=%async_computation | async-start | bytes 589824 | tf_op jit(solution)/shard_map/while/body/eval_jaxpr/exchange/all_to_all | solution.py:346
  373.6 11.2 %collective-permute-start.2 = (bf16[144,256]{1,0:T(8,128)(2,1)S(1)}, bf16[144,256]{1,0:T(8,128)(2,1)S(1)}, u32[]{:S(2)}, u32[]{:S(2)}) collective-permute-start(bf16[144,256]{1,0:T(8,128)(2,1)S(1)} %get-tuple-element.1057.q_ref), channel_id=1, source_target_pairs={{0,2},{1,3},{2,0},{3,1},{4,6},{5,7},{6,4},{7,5},{8,10},{9,11},{10,... | collective-permute-start | bytes 221192 | tf_op jit(solution)/shard_map/while/body/eval_jaxpr/exchange/ppermute | solution.py:345
  375.4 12.8 %collective-permute-start.4 = (bf16[144,256]{1,0:T(8,128)(2,1)S(1)}, bf16[144,256]{1,0:T(8,128)(2,1)S(1)}, u32[]{:S(2)}, u32[]{:S(2)}) collective-permute-start(bf16[144,256]{1,0:T(8,128)(2,1)S(1)} %get-tuple-element.1057.q_ref), channel_id=1, source_target_pairs={{0,3},{1,2},{2,1},{3,0},{4,7},{5,6},{6,5},{7,4},{8,11},{9,10},{10,... | collective-permute-start | bytes 221192 | tf_op jit(solution)/shard_map/while/body/eval_jaxpr/exchange/ppermute | solution.py:345
  384.7 8.8 %collective-permute-start.1 = (bf16[144,384]{1,0:T(8,128)(2,1)S(1)}, bf16[144,384]{1,0:T(8,128)(2,1)S(1)}, u32[]{:S(2)}, u32[]{:S(2)}) collective-permute-start(bf16[144,384]{1,0:T(8,128)(2,1)S(1)} %attend.81), channel_id=1, source_target_pairs={{0,1},{1,0},{2,3},{3,2},{4,5},{5,4},{6,7},{7,6},{8,9},{9,8},{10,11... | collective-permute-start | bytes 331784 | tf_op jit(solution)/shard_map/while/body/eval_jaxpr/attend/ppermute | solution.py:364
  386.4 7.1 %collective-permute-start.3 = (bf16[144,384]{1,0:T(8,128)(2,1)S(1)}, bf16[144,384]{1,0:T(8,128)(2,1)S(1)}, u32[]{:S(2)}, u32[]{:S(2)}) collective-permute-start(bf16[144,384]{1,0:T(8,128)(2,1)S(1)} %attend.82), channel_id=1, source_target_pairs={{0,2},{1,3},{2,0},{3,1},{4,6},{5,7},{6,4},{7,5},{8,10},{9,11},{10,... | collective-permute-start | bytes 331784 | tf_op jit(solution)/shard_map/while/body/eval_jaxpr/attend/ppermute | solution.py:364
  428.9 16.4 %all-to-all-start.1 = ((bf16[8,144,128]{2,1,0:T(8,128)(2,1)}), bf16[8,144,128]{2,1,0:T(8,128)(2,1)S(1)}, u32[]{:S(2)}, u32[]{:S(2)}) async-start(bf16[8,144,128]{2,1,0:T(8,128)(2,1)} %project.51), calls=%async_computation.1 | async-start | bytes 589824 | tf_op jit(solution)/shard_map/while/body/eval_jaxpr/exchange/all_to_all | solution.py:346
  435.7 12.0 %collective-permute-start.16 = (bf16[144,256]{1,0:T(8,128)(2,1)S(1)}, bf16[144,256]{1,0:T(8,128)(2,1)S(1)}, u32[]{:S(2)}, u32[]{:S(2)}) collective-permute-start(bf16[144,256]{1,0:T(8,128)(2,1)S(1)} %get-tuple-element.1073.q_ref), channel_id=1, source_target_pairs={{0,2},{1,3},{2,0},{3,1},{4,6},{5,7},{6,4},{7,5},{8,10},{9,11},{10,... | collective-permute-start | bytes 221192 | tf_op jit(solution)/shard_map/while/body/eval_jaxpr/exchange/ppermute | solution.py:345
  438.2 13.6 %collective-permute-start.18 = (bf16[144,256]{1,0:T(8,128)(2,1)S(1)}, bf16[144,256]{1,0:T(8,128)(2,1)S(1)}, u32[]{:S(2)}, u32[]{:S(2)}) collective-permute-start(bf16[144,256]{1,0:T(8,128)(2,1)S(1)} %get-tuple-element.1073.q_ref), channel_id=1, source_target_pairs={{0,3},{1,2},{2,1},{3,0},{4,7},{5,6},{6,5},{7,4},{8,11},{9,10},{10,... | collective-permute-start | bytes 221192 | tf_op jit(solution)/shard_map/while/body/eval_jaxpr/exchange/ppermute | solution.py:345
  446.8 8.8 %collective-permute-start.15 = (bf16[144,384]{1,0:T(8,128)(2,1)S(1)}, bf16[144,384]{1,0:T(8,128)(2,1)S(1)}, u32[]{:S(2)}, u32[]{:S(2)}) collective-permute-start(bf16[144,384]{1,0:T(8,128)(2,1)S(1)} %attend.86), channel_id=1, source_target_pairs={{0,1},{1,0},{2,3},{3,2},{4,5},{5,4},{6,7},{7,6},{8,9},{9,8},{10,11... | collective-permute-start | bytes 331784 | tf_op jit(solution)/shard_map/while/body/eval_jaxpr/attend/ppermute | solution.py:364
  449.2 6.4 collective-permute-start.17
  465.9 4.9 collective-permute-start.23
  483.1 16.4 %all-to-all-start.1 = ((bf16[8,144,128]{2,1,0:T(8,128)(2,1)}), bf16[8,144,128]{2,1,0:T(8,128)(2,1)S(1)}, u32[]{:S(2)}, u32[]{:S(2)}) async-start(bf16[8,144,128]{2,1,0:T(8,128)(2,1)} %project.51), calls=%async_computation.1 | async-start | bytes 589824 | tf_op jit(solution)/shard_map/while/body/eval_jaxpr/exchange/all_to_all | solution.py:346
  489.2 12.0 %collective-permute-start.16 = (bf16[144,256]{1,0:T(8,128)(2,1)S(1)}, bf16[144,256]{1,0:T(8,128)(2,1)S(1)}, u32[]{:S(2)}, u32[]{:S(2)}) collective-permute-start(bf16[144,256]{1,0:T(8,128)(2,1)S(1)} %get-tuple-element.1073.q_ref), channel_id=1, source_target_pairs={{0,2},{1,3},{2,0},{3,1},{4,6},{5,7},{6,4},{7,5},{8,10},{9,11},{10,... | collective-permute-start | bytes 221192 | tf_op jit(solution)/shard_map/while/body/eval_jaxpr/exchange/ppermute | solution.py:345
  490.9 13.6 %collective-permute-start.18 = (bf16[144,256]{1,0:T(8,128)(2,1)S(1)}, bf16[144,256]{1,0:T(8,128)(2,1)S(1)}, u32[]{:S(2)}, u32[]{:S(2)}) collective-permute-start(bf16[144,256]{1,0:T(8,128)(2,1)S(1)} %get-tuple-element.1073.q_ref), channel_id=1, source_target_pairs={{0,3},{1,2},{2,1},{3,0},{4,7},{5,6},{6,5},{7,4},{8,11},{9,10},{10,... | collective-permute-start | bytes 221192 | tf_op jit(solution)/shard_map/while/body/eval_jaxpr/exchange/ppermute | solution.py:345
  501.1 8.8 %collective-permute-start.15 = (bf16[144,384]{1,0:T(8,128)(2,1)S(1)}, bf16[144,384]{1,0:T(8,128)(2,1)S(1)}, u32[]{:S(2)}, u32[]{:S(2)}) collective-permute-start(bf16[144,384]{1,0:T(8,128)(2,1)S(1)} %attend.86), channel_id=1, source_target_pairs={{0,1},{1,0},{2,3},{3,2},{4,5},{5,4},{6,7},{7,6},{8,9},{9,8},{10,11... | collective-permute-start | bytes 331784 | tf_op jit(solution)/shard_map/while/body/eval_jaxpr/attend/ppermute | solution.py:364
  502.7 7.1 %collective-permute-start.17 = (bf16[144,384]{1,0:T(8,128)(2,1)S(1)}, bf16[144,384]{1,0:T(8,128)(2,1)S(1)}, u32[]{:S(2)}, u32[]{:S(2)}) collective-permute-start(bf16[144,384]{1,0:T(8,128)(2,1)S(1)} %attend.87), channel_id=1, source_target_pairs={{0,2},{1,3},{2,0},{3,1},{4,6},{5,7},{6,4},{7,5},{8,10},{9,11},{10,... | collective-permute-start | bytes 331784 | tf_op jit(solution)/shard_map/while/body/eval_jaxpr/attend/ppermute | solution.py:364
  518.5 4.9 collective-permute-start.23
  535.7 16.4 %all-to-all-start.1 = ((bf16[8,144,128]{2,1,0:T(8,128)(2,1)}), bf16[8,144,128]{2,1,0:T(8,128)(2,1)S(1)}, u32[]{:S(2)}, u32[]{:S(2)}) async-start(bf16[8,144,128]{2,1,0:T(8,128)(2,1)} %project.51), calls=%async_computation.1 | async-start | bytes 589824 | tf_op jit(solution)/shard_map/while/body/eval_jaxpr/exchange/all_to_all | solution.py:346
  542.5 12.0 %collective-permute-start.16 = (bf16[144,256]{1,0:T(8,128)(2,1)S(1)}, bf16[144,256]{1,0:T(8,128)(2,1)S(1)}, u32[]{:S(2)}, u32[]{:S(2)}) collective-permute-start(bf16[144,256]{1,0:T(8,128)(2,1)S(1)} %get-tuple-element.1073.q_ref), channel_id=1, source_target_pairs={{0,2},{1,3},{2,0},{3,1},{4,6},{5,7},{6,4},{7,5},{8,10},{9,11},{10,... | collective-permute-start | bytes 221192 | tf_op jit(solution)/shard_map/while/body/eval_jaxpr/exchange/ppermute | solution.py:345
  545.0 13.6 %collective-permute-start.18 = (bf16[144,256]{1,0:T(8,128)(2,1)S(1)}, bf16[144,256]{1,0:T(8,128)(2,1)S(1)}, u32[]{:S(2)}, u32[]{:S(2)}) collective-permute-start(bf16[144,256]{1,0:T(8,128)(2,1)S(1)} %get-tuple-element.1073.q_ref), channel_id=1, source_target_pairs={{0,3},{1,2},{2,1},{3,0},{4,7},{5,6},{6,5},{7,4},{8,11},{9,10},{10,... | collective-permute-start | bytes 221192 | tf_op jit(solution)/shard_map/while/body/eval_jaxpr/exchange/ppermute | solution.py:345
  553.7 8.8 %collective-permute-start.15 = (bf16[144,384]{1,0:T(8,128)(2,1)S(1)}, bf16[144,384]{1,0:T(8,128)(2,1)S(1)}, u32[]{:S(2)}, u32[]{:S(2)}) collective-permute-start(bf16[144,384]{1,0:T(8,128)(2,1)S(1)} %attend.86), channel_id=1, source_target_pairs={{0,1},{1,0},{2,3},{3,2},{4,5},{5,4},{6,7},{7,6},{8,9},{9,8},{10,11... | collective-permute-start | bytes 331784 | tf_op jit(solution)/shard_map/while/body/eval_jaxpr/attend/ppermute | solution.py:364
  556.1 6.4 collective-permute-start.17
  572.6 4.9 collective-permute-start.23
  589.9 16.4 %all-to-all-start.1 = ((bf16[8,144,128]{2,1,0:T(8,128)(2,1)}), bf16[8,144,128]{2,1,0:T(8,128)(2,1)S(1)}, u32[]{:S(2)}, u32[]{:S(2)}) async-start(bf16[8,144,128]{2,1,0:T(8,128)(2,1)} %project.51), calls=%async_computation.1 | async-start | bytes 589824 | tf_op jit(solution)/shard_map/while/body/eval_jaxpr/exchange/all_to_all | solution.py:346
  595.9 12.0 %collective-permute-start.16 = (bf16[144,256]{1,0:T(8,128)(2,1)S(1)}, bf16[144,256]{1,0:T(8,128)(2,1)S(1)}, u32[]{:S(2)}, u32[]{:S(2)}) collective-permute-start(bf16[144,256]{1,0:T(8,128)(2,1)S(1)} %get-tuple-element.1073.q_ref), channel_id=1, source_target_pairs={{0,2},{1,3},{2,0},{3,1},{4,6},{5,7},{6,4},{7,5},{8,10},{9,11},{10,... | collective-permute-start | bytes 221192 | tf_op jit(solution)/shard_map/while/body/eval_jaxpr/exchange/ppermute | solution.py:345
  597.7 13.6 %collective-permute-start.18 = (bf16[144,256]{1,0:T(8,128)(2,1)S(1)}, bf16[144,256]{1,0:T(8,128)(2,1)S(1)}, u32[]{:S(2)}, u32[]{:S(2)}) collective-permute-start(bf16[144,256]{1,0:T(8,128)(2,1)S(1)} %get-tuple-element.1073.q_ref), channel_id=1, source_target_pairs={{0,3},{1,2},{2,1},{3,0},{4,7},{5,6},{6,5},{7,4},{8,11},{9,10},{10,... | collective-permute-start | bytes 221192 | tf_op jit(solution)/shard_map/while/body/eval_jaxpr/exchange/ppermute | solution.py:345
  607.8 8.8 %collective-permute-start.15 = (bf16[144,384]{1,0:T(8,128)(2,1)S(1)}, bf16[144,384]{1,0:T(8,128)(2,1)S(1)}, u32[]{:S(2)}, u32[]{:S(2)}) collective-permute-start(bf16[144,384]{1,0:T(8,128)(2,1)S(1)} %attend.86), channel_id=1, source_target_pairs={{0,1},{1,0},{2,3},{3,2},{4,5},{5,4},{6,7},{7,6},{8,9},{9,8},{10,11... | collective-permute-start | bytes 331784 | tf_op jit(solution)/shard_map/while/body/eval_jaxpr/attend/ppermute | solution.py:364
  609.5 7.1 %collective-permute-start.17 = (bf16[144,384]{1,0:T(8,128)(2,1)S(1)}, bf16[144,384]{1,0:T(8,128)(2,1)S(1)}, u32[]{:S(2)}, u32[]{:S(2)}) collective-permute-start(bf16[144,384]{1,0:T(8,128)(2,1)S(1)} %attend.87), channel_id=1, source_target_pairs={{0,2},{1,3},{2,0},{3,1},{4,6},{5,7},{6,4},{7,5},{8,10},{9,11},{10,... | collective-permute-start | bytes 331784 | tf_op jit(solution)/shard_map/while/body/eval_jaxpr/attend/ppermute | solution.py:364
  625.2 4.9 collective-permute-start.23
  (73 other events, 440.6 us)
Sparse Core Ops, SparseCore 0:
  27.4 118.3 all-gather.4
  148.4 105.2 all-gather.6

commit v6 on v5

--- a/solution.py
+++ b/solution.py
@@ -226,17 +226,22 @@
 
 
 def combine_kernel(scal, o0, o1, o2, o3, a_ref):
-    parts = [o0[...], o1[...], o2[...], o3[...]]
-    notes = [part[:, QW:].astype(F32) for part in parts]
-    for h in range(SHARE):
-        weights = [n[:, h : h + 1] + n[:, SHARE + h : SHARE + h + 1] for n in notes]
-        peak = functools.reduce(jnp.maximum, weights)
-        weights = [jnp.exp2(w - peak) for w in weights]
-        total = functools.reduce(jnp.add, weights)
-        cols = slice(h * HD, (h + 1) * HD)
-        mixed = functools.reduce(
-            jnp.add, [w / total * part[:, cols].astype(F32) for w, part in zip(weights, parts)]
-        )
+    refs = [o0, o1, o2, o3]
+    tile = 2 * HD
+    notes = [o_ref[:, QW:].astype(F32) for o_ref in refs]
+    weights = [n + pltpu.roll(n, tile - SHARE, 1) for n in notes]
+    peak = functools.reduce(jnp.maximum, weights)
+    weights = [jnp.exp2(w - peak) for w in weights]
+    total = functools.reduce(jnp.add, weights)
+    weights = [w / total for w in weights]
+    left = lax.broadcasted_iota(jnp.int32, notes[0].shape, 1) < HD
+    for j in range(SHARE // 2):
+        cols = slice(j * tile, (j + 1) * tile)
+        mixed = None
+        for w, o_ref in zip(weights, refs):
+            share = jnp.where(left, w[:, 2 * j : 2 * j + 1], w[:, 2 * j + 1 : 2 * j + 2])
+            term = share * o_ref[:, cols].astype(F32)
+            mixed = term if mixed is None else mixed + term
         a_ref[:, cols] = mixed.astype(BF16)
 
 
@@ -342,7 +347,10 @@
 
     def exchange(q, kv):
         with jax.named_scope("exchange"):
-            qs = [q] + [lax.ppermute(q, "seq", seq_pairs(d)) for d in (1, 2, 3)]
+            qs = [lax.ppermute(q, "seq", seq_pairs(d)) for d in (3, 2, 1)]
+            qs[0], qs[1] = lax.optimization_barrier((qs[0], qs[1]))
+            qs[1], qs[2] = lax.optimization_barrier((qs[1], qs[2]))
+            qs = [q] + qs[::-1]
             kv = lax.all_to_all(
                 kv, "seq", split_axis=0, concat_axis=0, tiled=True, axis_index_groups=along_z()
             )
@@ -351,7 +359,7 @@
     def attend(scal, qs, kv):
         parts = [None] * XN
         with jax.named_scope("attend"):
-            for d in (2, 1, 3, 0):
+            for d in (3, 2, 1, 0):
                 part = call(
                     functools.partial(attend_kernel, d=d, blocks=blocks, tok=tok),
                     scal,
@@ -421,6 +429,7 @@
         return body
 
     for group, begin, end in ((early, 1, 4), (late, 4, layers)):
+        group, pieces = lax.optimization_barrier((group, pieces))
         carry = (pieces, out, group[:, 0, Q_ROWS:QKV_ROWS])
         pieces, out, _ = lax.fori_loop(begin, end, step(group, begin), carry)
     out = call(

time: 655 us -> 571 us (0.87)
  waiting for transfers between devices: 274 us -> 192 us
    all_gather x1, waiting for transfers between devices: 98.7 us -> 0.01 us  [local(): late = lax.all_gather(by_layer[4:], 'seq', axis=0)]
    ppermute x24, waiting for transfers between devices: 0.75 us -> 50.5 us  [exchange(): qs = [lax.ppermute(q, 'seq', seq_pairs(d)) for d in (3, 2, 1)]]
    all_to_all x8, waiting for transfers between devices: 40.7 us -> 21.2 us  [exchange(): lax.all_to_all(kv, 'seq', split_axis=0, concat_axis=0, tiled=True, axis_i...]
    ppermute x6, waiting for transfers between devices: 29.6 us -> 13.6 us  [over_x(): return [part] + [lax.ppermute(part, 'seq', seq_pairs(d)) for d in (1, 2, 3)]]
    all_to_all x8, starting transfers between devices: 30.5 us -> 39.8 us  [exchange(): lax.all_to_all(kv, 'seq', split_axis=0, concat_axis=0, tiled=True, axis_i...]
    ppermute x24, starting transfers between devices: 31.6 us -> 25.1 us  [attend(): parts[d] = lax.ppermute(part, 'seq', seq_pairs(d)) if d else part]
  transfers between devices with their start and end apart: 130 -> 130, of which waited for: 79 -> 102; matrix products, arithmetic and copies ran while one was open for 1% -> 1% of each run, Pallas kernels for 12% -> 14%
where the time goes in v6:
time: 571 us; the launch traced here: 562 us
  starting transfers between devices  218 us (38%)
  waiting for transfers between devices  192 us (34%)
  Pallas kernels  99.4 us (17%)
  blocking collectives  17 us (3%)
  between operations  13.9 us (2%)
  loops' own time  9.97 us (2%)
  local copies, waits for them, and re-layouts  9.53 us (2%)
    pallas_call x65, Pallas kernels, call(): pl.pallas_call(kernel, out_shape=out_shape, in_specs=in_specs, out_specs=...  99.4 us
    ppermute x48, starting transfers between devices, spread(): lax.ppermute(piece, 'section', section_pairs(2 * d))  54.9 us
    ppermute x16, starting transfers between devices, spread(): other = lax.ppermute(jnp.stack(near), 'section', section_pairs(1))  54.5 us
    ppermute x24, waiting for transfers between devices, exchange(): qs = [lax.ppermute(q, 'seq', seq_pairs(d)) for d in (3, 2, 1)]  50.5 us
    ppermute x48, waiting for transfers between devices, spread(): lax.ppermute(piece, 'section', section_pairs(2 * d))  48.2 us
    all_to_all x8, starting transfers between devices, exchange(): lax.all_to_all(kv, 'seq', split_axis=0, concat_axis=0, tiled=True, axis_i...  39.8 us
    ppermute x24, starting transfers between devices, attend(): parts[d] = lax.ppermute(part, 'seq', seq_pairs(d)) if d else part  25.1 us
    ppermute x24, starting transfers between devices, exchange(): qs = [lax.ppermute(q, 'seq', seq_pairs(d)) for d in (3, 2, 1)]  24.7 us
  transfers between devices with their start and end apart: 130, of which 102 were waited for; matrix products, arithmetic and copies ran while one was open for 1% of the time, Pallas kernels for 14%

profile of v6, /device:TPU:1, one launch (start us, length us, event | category | flops | bytes accessed | tf_op | source)
XLA Modules:
  0.0 561.6 jit_solution(13736593902421647122)
XLA Ops:
  9.5 17.0 %all_to_all.32 = bf16[8,336,128]{2,1,0:T(8,128)(2,1)S(1)} all-to-all(bf16[8,336,128]{2,1,0:T(8,128)(2,1)S(1)} %pad_maximum_fusion.4), channel_id=1, replica_groups=mesh['section'=8,'seq'=32] {'section'}, dimensions={0} | all-to-all | bytes 1376256 | tf_op jit(solution)/shard_map/all_to_all | solution.py:307
  28.9 8.2 %all-to-all-start.3 = ((bf16[8,192,128]{2,1,0:T(8,128)(2,1)}), bf16[8,192,128]{2,1,0:T(8,128)(2,1)S(1)}, u32[]{:S(2)}, u32[]{:S(2)}) async-start(bf16[8,192,128]{2,1,0:T(8,128)(2,1)} %broadcast_in_dim.26), calls=%async_computation.3 | async-start | bytes 786432 | tf_op jit(solution)/shard_map/weights/all_to_all | solution.py:317
  37.1 15.0 %all-to-all-done.3.w0 = bf16[8,192,128]{2,1,0:T(8,128)(2,1)S(1)} async-done(((bf16[8,192,128]{2,1,0:T(8,128)(2,1)}), bf16[8,192,128]{2,1,0:T(8,128)(2,1)S(1)}, u32[]{:S(2)}, u32[]{:S(2)}) %all-to-all-start.3) | async-done | bytes 393248 | tf_op jit(solution)/shard_map/weights/all_to_all | solution.py:317
  52.8 3.4 all-to-all-start.4
  57.5 2.4 collective-permute-start.29
  60.5 4.1 collective-permute-done.28.w1
  64.5 9.5 %collective-permute-done.29.w2 = bf16[8,192,128]{2,1,0:T(8,128)(2,1)S(1)} collective-permute-done((bf16[8,192,128]{2,1,0:T(8,128)(2,1)S(1)}, bf16[8,192,128]{2,1,0:T(8,128)(2,1)S(1)}, u32[]{:S(2)}, u32[]{:S(2)}) %collective-permute-start.29) | collective-permute-done | bytes 393248 | tf_op jit(solution)/shard_map/weights/ppermute | solution.py:322
  75.8 5.9 %all-to-all-start.5 = ((bf16[8,144,128]{2,1,0:T(8,128)(2,1)}), bf16[8,144,128]{2,1,0:T(8,128)(2,1)S(1)}, u32[]{:S(2)}, u32[]{:S(2)}) async-start(bf16[8,144,128]{2,1,0:T(8,128)(2,1)} %project.47), calls=%async_computation.5 | async-start | bytes 589824 | tf_op jit(solution)/shard_map/exchange/all_to_all | solution.py:354
  81.7 2.4 collective-permute-start.32
  88.2 14.0 %collective-permute-done.34.q_ref = bf16[144,256]{1,0:T(8,128)(2,1)S(1)} collective-permute-done((bf16[144,256]{1,0:T(8,128)(2,1)S(1)}, bf16[144,256]{1,0:T(8,128)(2,1)S(1)}, u32[]{:S(2)}, u32[]{:S(2)}) %collective-permute-start.34) | collective-permute-done | bytes 73760 | tf_op jit(solution)/shard_map/exchange/ppermute | solution.py:350
  102.9 4.7 collective-permute-done.35.q_ref
  107.6 2.6 collective-permute-done.36.q_ref
  116.5 2.1 collective-permute-start.37
  120.2 2.4 collective-permute-done.38.o2
  122.6 3.0 collective-permute-done.37.o1
  127.1 3.6 collective-permute-start.42
  132.9 10.9 %collective-permute-start.43 = (bf16[4,144,256]{2,1,0:T(8,128)(2,1)S(1)}, bf16[4,144,256]{2,1,0:T(8,128)(2,1)S(1)}, u32[]{:S(2)}, u32[]{:S(2)}) collective-permute-start(bf16[4,144,256]{2,1,0:T(8,128)(2,1)S(1)} %pad_maximum_fusion.6), channel_id=1, source_target_pairs={{0,32},{32,0},{64,96},{96,64},{128,160},{160,128},{192,224},{224,1... | collective-permute-start | bytes 884744 | tf_op jit(solution)/shard_map/attend/ppermute | solution.py:44
  146.5 3.6 collective-permute-start.45
  150.0 3.3 collective-permute-done.45
  159.0 170.2 %while.58 = (s32[]{:T(128)}, bf16[144,256]{1,0:T(8,128)(2,1)S(1)}, bf16[144,256]{1,0:T(8,128)(2,1)S(1)}, bf16[144,256]{1,0:T(8,128)(2,1)S(1)}, bf16[144,256]{1,0...) while((s32[]{:T(128)}, bf16[144,256]{1,0:T(8,128)(2,1)S(1)}, ...), condition=%wide.region_1.0_spmd, body=%wide.region_0.0_spmd.sunk | while | flops 1284710400 | bytes 15377141 | solution.py:434
  160.8 6.8 %all-to-all-start = ((bf16[8,144,128]{2,1,0:T(8,128)(2,1)}), bf16[8,144,128]{2,1,0:T(8,128)(2,1)S(1)}, u32[]{:S(2)}, u32[]{:S(2)}) async-start(bf16[8,144,128]{2,1,0:T(8,128)(2,1)} %project.49), calls=%async_computation | async-start | bytes 589824 | tf_op jit(solution)/shard_map/while/body/eval_jaxpr/exchange/all_to_all | solution.py:354
  167.6 2.5 project.48
  177.1 4.2 all-to-all-done.k_ref
  182.8 3.5 collective-permute-start.4
  196.0 2.4 collective-permute-start.6
  201.0 4.4 collective-permute-start.9
  219.5 3.4 all-to-all-start
  222.9 2.6 project.48
  228.9 4.8 collective-permute-done.q_ref
  233.8 2.4 collective-permute-done.2.q_ref
  236.2 2.5 all-to-all-done.k_ref
  248.7 4.3 collective-permute-done.5.o3
  260.5 2.4 collective-permute-start.9
  276.6 5.2 all-to-all-start
  281.9 2.5 project.48
  289.2 2.2 collective-permute-done.1.q_ref
  291.4 2.9 all-to-all-done.k_ref
  313.0 4.1 collective-permute-start.9
  325.8 2.1 collective-permute-start.13
  330.2 222.8 %while.59 = (s32[]{:T(128)}, bf16[144,256]{1,0:T(8,128)(2,1)S(1)}, bf16[144,256]{1,0:T(8,128)(2,1)S(1)}, bf16[144,256]{1,0:T(8,128)(2,1)S(1)}, bf16[144,256]{1,0...) while((s32[]{:T(128)}, bf16[144,256]{1,0:T(8,128)(2,1)S(1)}, ...), condition=%wide.region_3.0_spmd, body=%wide.region_2.0_spmd.sunk | while | flops 1284710400 | bytes 15377153 | solution.py:434
  341.6 4.4 all-to-all-start.1
  346.0 2.5 project.50
  353.3 2.2 collective-permute-done.15.q_ref
  355.5 2.9 all-to-all-done.1.k_ref
  376.8 4.1 collective-permute-start.23
  389.5 2.2 collective-permute-start.27
  394.7 4.7 all-to-all-start.1
  399.4 2.5 project.50
  406.7 2.2 collective-permute-done.15.q_ref
  408.9 2.9 all-to-all-done.1.k_ref
  430.3 4.1 collective-permute-start.23
  442.8 2.3 collective-permute-start.27
  448.1 4.7 all-to-all-start.1
  452.8 2.5 project.50
  460.1 2.2 collective-permute-done.15.q_ref
  462.3 2.9 all-to-all-done.1.k_ref
  483.7 4.1 collective-permute-start.23
  496.2 2.3 collective-permute-start.27
  501.5 4.7 all-to-all-start.1
  506.2 2.5 project.50
  513.5 2.2 collective-permute-done.15.q_ref
  515.7 2.9 all-to-all-done.1.k_ref
  537.1 4.1 collective-permute-start.23
  549.6 2.3 collective-permute-start.27
  (341 shorter events, 280.3 us)
Async XLA Ops:
  6.5 151.3 %all-gather.7.cloned.1.call-start = ((), (), s32[]{:S(2)}) async-start(), calls=%async_computation.7 | async-start | bytes 8110080 | tf_op jit(solution)/shard_map/weights/all_gather | solution.py:312
  27.3 301.9 %all-gather.5.cloned.1.call-start = ((), (), s32[]{:S(2)}) async-start(), calls=%async_computation.6 | async-start | bytes 10813440 | tf_op jit(solution)/shard_map/weights/all_gather | solution.py:313
  28.9 23.2 %all-to-all-start.3 = ((bf16[8,192,128]{2,1,0:T(8,128)(2,1)}), bf16[8,192,128]{2,1,0:T(8,128)(2,1)S(1)}, u32[]{:S(2)}, u32[]{:S(2)}) async-start(bf16[8,192,128]{2,1,0:T(8,128)(2,1)} %broadcast_in_dim.26), calls=%async_computation.3 | async-start | bytes 786432 | tf_op jit(solution)/shard_map/weights/all_to_all | solution.py:317
  52.8 21.2 %all-to-all-start.4 = ((bf16[8,128,128]{2,1,0:T(8,128)(2,1)}), bf16[8,128,128]{2,1,0:T(8,128)(2,1)S(1)}, u32[]{:S(2)}, u32[]{:S(2)}) async-start(bf16[8,128,128]{2,1,0:T(8,128)(2,1)} %broadcast_in_dim.27), calls=%async_computation.4 | async-start | bytes 524288 | tf_op jit(solution)/shard_map/weights/all_to_all | solution.py:317
  56.3 8.3 %collective-permute-start.28 = (bf16[8,192,128]{2,1,0:T(8,128)(2,1)S(1)}, bf16[8,192,128]{2,1,0:T(8,128)(2,1)S(1)}, u32[]{:S(2)}, u32[]{:S(2)}) collective-permute-start(bf16[8,192,128]{2,1,0:T(8,128)(2,1)S(1)} %all-to-all-done.3.w0), channel_id=1, source_target_pairs={{0,1},{1,0},{2,3},{3,2},{4,5},{5,4},{6,7},{7,6},{8,9},{9,8},{10,11... | collective-permute-start | bytes 1179656 | tf_op jit(solution)/shard_map/weights/ppermute | solution.py:322
  57.5 16.6 %collective-permute-start.29 = (bf16[8,192,128]{2,1,0:T(8,128)(2,1)S(1)}, bf16[8,192,128]{2,1,0:T(8,128)(2,1)S(1)}, u32[]{:S(2)}, u32[]{:S(2)}) collective-permute-start(bf16[8,192,128]{2,1,0:T(8,128)(2,1)S(1)} %all-to-all-done.3.w0), channel_id=1, source_target_pairs={{0,2},{1,3},{2,0},{3,1},{4,6},{5,7},{6,4},{7,5},{8,10},{9,11},{10,... | collective-permute-start | bytes 1179656 | tf_op jit(solution)/shard_map/weights/ppermute | solution.py:322
  59.9 14.2 %collective-permute-start.30 = (bf16[8,192,128]{2,1,0:T(8,128)(2,1)S(1)}, bf16[8,192,128]{2,1,0:T(8,128)(2,1)S(1)}, u32[]{:S(2)}, u32[]{:S(2)}) collective-permute-start(bf16[8,192,128]{2,1,0:T(8,128)(2,1)S(1)} %all-to-all-done.3.w0), channel_id=1, source_target_pairs={{0,3},{1,2},{2,1},{3,0},{4,7},{5,6},{6,5},{7,4},{8,11},{9,10},{10,... | collective-permute-start | bytes 1179656 | tf_op jit(solution)/shard_map/weights/ppermute | solution.py:322
  75.8 34.5 %all-to-all-start.5 = ((bf16[8,144,128]{2,1,0:T(8,128)(2,1)}), bf16[8,144,128]{2,1,0:T(8,128)(2,1)S(1)}, u32[]{:S(2)}, u32[]{:S(2)}) async-start(bf16[8,144,128]{2,1,0:T(8,128)(2,1)} %project.47), calls=%async_computation.5 | async-start | bytes 589824 | tf_op jit(solution)/shard_map/exchange/all_to_all | solution.py:354
  81.7 28.5 %collective-permute-start.31 = (bf16[8,128,128]{2,1,0:T(8,128)(2,1)S(1)}, bf16[8,128,128]{2,1,0:T(8,128)(2,1)S(1)}, u32[]{:S(2)}, u32[]{:S(2)}) collective-permute-start(bf16[8,128,128]{2,1,0:T(8,128)(2,1)S(1)} %all-to-all-done.4.w0), channel_id=1, source_target_pairs={{0,1},{1,0},{2,3},{3,2},{4,5},{5,4},{6,7},{7,6},{8,9},{9,8},{10,11... | collective-permute-start | bytes 786440 | tf_op jit(solution)/shard_map/weights/ppermute | solution.py:322
  81.7 28.5 %collective-permute-start.32 = (bf16[8,128,128]{2,1,0:T(8,128)(2,1)S(1)}, bf16[8,128,128]{2,1,0:T(8,128)(2,1)S(1)}, u32[]{:S(2)}, u32[]{:S(2)}) collective-permute-start(bf16[8,128,128]{2,1,0:T(8,128)(2,1)S(1)} %all-to-all-done.4.w0), channel_id=1, source_target_pairs={{0,2},{1,3},{2,0},{3,1},{4,6},{5,7},{6,4},{7,5},{8,10},{9,11},{10,... | collective-permute-start | bytes 786440 | tf_op jit(solution)/shard_map/weights/ppermute | solution.py:322
  84.1 26.1 %collective-permute-start.33 = (bf16[8,128,128]{2,1,0:T(8,128)(2,1)S(1)}, bf16[8,128,128]{2,1,0:T(8,128)(2,1)S(1)}, u32[]{:S(2)}, u32[]{:S(2)}) collective-permute-start(bf16[8,128,128]{2,1,0:T(8,128)(2,1)S(1)} %all-to-all-done.4.w0), channel_id=1, source_target_pairs={{0,3},{1,2},{2,1},{3,0},{4,7},{5,6},{6,5},{7,4},{8,11},{9,10},{10,... | collective-permute-start | bytes 786440 | tf_op jit(solution)/shard_map/weights/ppermute | solution.py:322
  86.9 15.4 %collective-permute-start.34 = (bf16[144,256]{1,0:T(8,128)(2,1)S(1)}, bf16[144,256]{1,0:T(8,128)(2,1)S(1)}, u32[]{:S(2)}, u32[]{:S(2)}) collective-permute-start(bf16[144,256]{1,0:T(8,128)(2,1)S(1)} %project.46.q_ref), channel_id=1, source_target_pairs={{0,3},{1,2},{2,1},{3,0},{4,7},{5,6},{6,5},{7,4},{8,11},{9,10},{10,... | collective-permute-start | bytes 221192 | tf_op jit(solution)/shard_map/exchange/ppermute | solution.py:350
  88.2 19.4 %collective-permute-start.35 = (bf16[144,256]{1,0:T(8,128)(2,1)S(1)}, bf16[144,256]{1,0:T(8,128)(2,1)S(1)}, u32[]{:S(2)}, u32[]{:S(2)}) collective-permute-start(bf16[144,256]{1,0:T(8,128)(2,1)S(1)} %project.46.q_ref), channel_id=1, source_target_pairs={{0,2},{1,3},{2,0},{3,1},{4,6},{5,7},{6,4},{7,5},{8,10},{9,11},{10,... | collective-permute-start | bytes 221192 | tf_op jit(solution)/shard_map/exchange/ppermute | solution.py:350
  102.3 8.0 %collective-permute-start.36 = (bf16[144,256]{1,0:T(8,128)(2,1)S(1)}, bf16[144,256]{1,0:T(8,128)(2,1)S(1)}, u32[]{:S(2)}, u32[]{:S(2)}) collective-permute-start(bf16[144,256]{1,0:T(8,128)(2,1)S(1)} %project.46.q_ref), channel_id=1, source_target_pairs={{0,1},{1,0},{2,3},{3,2},{4,5},{5,4},{6,7},{7,6},{8,9},{9,8},{10,11... | collective-permute-start | bytes 221192 | tf_op jit(solution)/shard_map/exchange/ppermute | solution.py:350
  111.8 8.4 %collective-permute-start.39 = (bf16[144,384]{1,0:T(8,128)(2,1)S(1)}, bf16[144,384]{1,0:T(8,128)(2,1)S(1)}, u32[]{:S(2)}, u32[]{:S(2)}) collective-permute-start(bf16[144,384]{1,0:T(8,128)(2,1)S(1)} %attend.78), channel_id=1, source_target_pairs={{0,3},{1,2},{2,1},{3,0},{4,7},{5,6},{6,5},{7,4},{8,11},{9,10},{10,... | collective-permute-start | bytes 331784 | tf_op jit(solution)/shard_map/attend/ppermute | solution.py:372
  114.4 8.2 %collective-permute-start.38 = (bf16[144,384]{1,0:T(8,128)(2,1)S(1)}, bf16[144,384]{1,0:T(8,128)(2,1)S(1)}, u32[]{:S(2)}, u32[]{:S(2)}) collective-permute-start(bf16[144,384]{1,0:T(8,128)(2,1)S(1)} %attend.77), channel_id=1, source_target_pairs={{0,2},{1,3},{2,0},{3,1},{4,6},{5,7},{6,4},{7,5},{8,10},{9,11},{10,... | collective-permute-start | bytes 331784 | tf_op jit(solution)/shard_map/attend/ppermute | solution.py:372
  116.5 9.1 %collective-permute-start.37 = (bf16[144,384]{1,0:T(8,128)(2,1)S(1)}, bf16[144,384]{1,0:T(8,128)(2,1)S(1)}, u32[]{:S(2)}, u32[]{:S(2)}) collective-permute-start(bf16[144,384]{1,0:T(8,128)(2,1)S(1)} %attend.76), channel_id=1, source_target_pairs={{0,1},{1,0},{2,3},{3,2},{4,5},{5,4},{6,7},{7,6},{8,9},{9,8},{10,11... | collective-permute-start | bytes 331784 | tf_op jit(solution)/shard_map/attend/ppermute | solution.py:372
  126.8 5.1 collective-permute-start.41
  127.1 5.7 %collective-permute-start.42 = (bf16[144,256]{1,0:T(8,128)(2,1)S(1)}, bf16[144,256]{1,0:T(8,128)(2,1)S(1)}, u32[]{:S(2)}, u32[]{:S(2)}) collective-permute-start(bf16[144,256]{1,0:T(8,128)(2,1)S(1)} %attend.79.a0), channel_id=1, source_target_pairs={{0,192},{32,224},{64,128},{96,160},{128,64},{160,96},{192,0},{224,... | collective-permute-start | bytes 221192 | tf_op jit(solution)/shard_map/attend/ppermute | solution.py:43
  132.9 12.1 %collective-permute-start.43 = (bf16[4,144,256]{2,1,0:T(8,128)(2,1)S(1)}, bf16[4,144,256]{2,1,0:T(8,128)(2,1)S(1)}, u32[]{:S(2)}, u32[]{:S(2)}) collective-permute-start(bf16[4,144,256]{2,1,0:T(8,128)(2,1)S(1)} %pad_maximum_fusion.6), channel_id=1, source_target_pairs={{0,32},{32,0},{64,96},{96,64},{128,160},{160,128},{192,224},{224,1... | collective-permute-start | bytes 884744 | tf_op jit(solution)/shard_map/attend/ppermute | solution.py:44
  146.5 6.9 %collective-permute-start.45 = (bf16[144,256]{1,0:T(8,128)(2,1)S(1)}, bf16[144,256]{1,0:T(8,128)(2,1)S(1)}, u32[]{:S(2)}, u32[]{:S(2)}) collective-permute-start(bf16[144,256]{1,0:T(8,128)(2,1)S(1)} %output.23), channel_id=1, source_target_pairs={{0,128},{32,160},{64,192},{96,224},{128,0},{160,32},{192,64},{224,... | collective-permute-start | bytes 221192 | tf_op jit(solution)/shard_map/output/ppermute | solution.py:43
  150.0 4.9 collective-permute-start.46
  160.8 20.4 %all-to-all-start = ((bf16[8,144,128]{2,1,0:T(8,128)(2,1)}), bf16[8,144,128]{2,1,0:T(8,128)(2,1)S(1)}, u32[]{:S(2)}, u32[]{:S(2)}) async-start(bf16[8,144,128]{2,1,0:T(8,128)(2,1)} %project.49), calls=%async_computation | async-start | bytes 589824 | tf_op jit(solution)/shard_map/while/body/eval_jaxpr/exchange/all_to_all | solution.py:354
  170.1 4.9 collective-permute-start
  171.6 5.1 collective-permute-start.1
  182.8 8.8 %collective-permute-start.4 = (bf16[144,384]{1,0:T(8,128)(2,1)S(1)}, bf16[144,384]{1,0:T(8,128)(2,1)S(1)}, u32[]{:S(2)}, u32[]{:S(2)}) collective-permute-start(bf16[144,384]{1,0:T(8,128)(2,1)S(1)} %attend.82), channel_id=1, source_target_pairs={{0,2},{1,3},{2,0},{3,1},{4,6},{5,7},{6,4},{7,5},{8,10},{9,11},{10,... | collective-permute-start | bytes 331784 | tf_op jit(solution)/shard_map/while/body/eval_jaxpr/attend/ppermute | solution.py:372
  196.0 4.9 collective-permute-start.6
  201.0 5.7 %collective-permute-start.9 = (bf16[4,144,256]{2,1,0:T(8,128)(2,1)S(1)}, bf16[4,144,256]{2,1,0:T(8,128)(2,1)S(1)}, u32[]{:S(2)}, u32[]{:S(2)}) collective-permute-start(bf16[4,144,256]{2,1,0:T(8,128)(2,1)S(1)} %pad_maximum_fusion.12), channel_id=1, source_target_pairs={{0,32},{32,0},{64,96},{96,64},{128,160},{160,128},{192,224},{224,1... | collective-permute-start | bytes 884744 | tf_op jit(solution)/shard_map/while/body/eval_jaxpr/attend/ppermute | solution.py:44
  208.4 5.1 collective-permute-start.10
  219.5 19.2 %all-to-all-start = ((bf16[8,144,128]{2,1,0:T(8,128)(2,1)}), bf16[8,144,128]{2,1,0:T(8,128)(2,1)S(1)}, u32[]{:S(2)}, u32[]{:S(2)}) async-start(bf16[8,144,128]{2,1,0:T(8,128)(2,1)} %project.49), calls=%async_computation | async-start | bytes 589824 | tf_op jit(solution)/shard_map/while/body/eval_jaxpr/exchange/all_to_all | solution.py:354
  225.5 8.1 %collective-permute-start = (bf16[144,256]{1,0:T(8,128)(2,1)S(1)}, bf16[144,256]{1,0:T(8,128)(2,1)S(1)}, u32[]{:S(2)}, u32[]{:S(2)}) collective-permute-start(bf16[144,256]{1,0:T(8,128)(2,1)S(1)} %get-tuple-element.1105.q_ref), channel_id=1, source_target_pairs={{0,3},{1,2},{2,1},{3,0},{4,7},{5,6},{6,5},{7,4},{8,11},{9,10},{10,... | collective-permute-start | bytes 221192 | tf_op jit(solution)/shard_map/while/body/eval_jaxpr/exchange/ppermute | solution.py:350
  226.8 7.0 %collective-permute-start.1 = (bf16[144,256]{1,0:T(8,128)(2,1)S(1)}, bf16[144,256]{1,0:T(8,128)(2,1)S(1)}, u32[]{:S(2)}, u32[]{:S(2)}) collective-permute-start(bf16[144,256]{1,0:T(8,128)(2,1)S(1)} %get-tuple-element.1105.q_ref), channel_id=1, source_target_pairs={{0,2},{1,3},{2,0},{3,1},{4,6},{5,7},{6,4},{7,5},{8,10},{9,11},{10,... | collective-permute-start | bytes 221192 | tf_op jit(solution)/shard_map/while/body/eval_jaxpr/exchange/ppermute | solution.py:350
  227.2 9.0 %collective-permute-start.2 = (bf16[144,256]{1,0:T(8,128)(2,1)S(1)}, bf16[144,256]{1,0:T(8,128)(2,1)S(1)}, u32[]{:S(2)}, u32[]{:S(2)}) collective-permute-start(bf16[144,256]{1,0:T(8,128)(2,1)S(1)} %get-tuple-element.1105.q_ref), channel_id=1, source_target_pairs={{0,1},{1,0},{2,3},{3,2},{4,5},{5,4},{6,7},{7,6},{8,9},{9,8},{10,11... | collective-permute-start | bytes 221192 | tf_op jit(solution)/shard_map/while/body/eval_jaxpr/exchange/ppermute | solution.py:350
  240.3 8.5 %collective-permute-start.4 = (bf16[144,384]{1,0:T(8,128)(2,1)S(1)}, bf16[144,384]{1,0:T(8,128)(2,1)S(1)}, u32[]{:S(2)}, u32[]{:S(2)}) collective-permute-start(bf16[144,384]{1,0:T(8,128)(2,1)S(1)} %attend.82), channel_id=1, source_target_pairs={{0,2},{1,3},{2,0},{3,1},{4,6},{5,7},{6,4},{7,5},{8,10},{9,11},{10,... | collective-permute-start | bytes 331784 | tf_op jit(solution)/shard_map/while/body/eval_jaxpr/attend/ppermute | solution.py:372
  243.4 9.7 %collective-permute-start.5 = (bf16[144,384]{1,0:T(8,128)(2,1)S(1)}, bf16[144,384]{1,0:T(8,128)(2,1)S(1)}, u32[]{:S(2)}, u32[]{:S(2)}) collective-permute-start(bf16[144,384]{1,0:T(8,128)(2,1)S(1)} %attend.83), channel_id=1, source_target_pairs={{0,3},{1,2},{2,1},{3,0},{4,7},{5,6},{6,5},{7,4},{8,11},{9,10},{10,... | collective-permute-start | bytes 331784 | tf_op jit(solution)/shard_map/while/body/eval_jaxpr/attend/ppermute | solution.py:372
  245.7 7.4 %collective-permute-start.3 = (bf16[144,384]{1,0:T(8,128)(2,1)S(1)}, bf16[144,384]{1,0:T(8,128)(2,1)S(1)}, u32[]{:S(2)}, u32[]{:S(2)}) collective-permute-start(bf16[144,384]{1,0:T(8,128)(2,1)S(1)} %attend.81), channel_id=1, source_target_pairs={{0,1},{1,0},{2,3},{3,2},{4,5},{5,4},{6,7},{7,6},{8,9},{9,8},{10,11... | collective-permute-start | bytes 331784 | tf_op jit(solution)/shard_map/while/body/eval_jaxpr/attend/ppermute | solution.py:372
  276.6 17.6 %all-to-all-start = ((bf16[8,144,128]{2,1,0:T(8,128)(2,1)}), bf16[8,144,128]{2,1,0:T(8,128)(2,1)S(1)}, u32[]{:S(2)}, u32[]{:S(2)}) async-start(bf16[8,144,128]{2,1,0:T(8,128)(2,1)} %project.49), calls=%async_computation | async-start | bytes 589824 | tf_op jit(solution)/shard_map/while/body/eval_jaxpr/exchange/all_to_all | solution.py:354
  286.4 5.0 collective-permute-start.1
  295.8 7.7 %collective-permute-start.4 = (bf16[144,384]{1,0:T(8,128)(2,1)S(1)}, bf16[144,384]{1,0:T(8,128)(2,1)S(1)}, u32[]{:S(2)}, u32[]{:S(2)}) collective-permute-start(bf16[144,384]{1,0:T(8,128)(2,1)S(1)} %attend.82), channel_id=1, source_target_pairs={{0,2},{1,3},{2,0},{3,1},{4,6},{5,7},{6,4},{7,5},{8,10},{9,11},{10,... | collective-permute-start | bytes 331784 | tf_op jit(solution)/shard_map/while/body/eval_jaxpr/attend/ppermute | solution.py:372
  313.0 5.3 collective-permute-start.9
  341.6 16.8 %all-to-all-start.1 = ((bf16[8,144,128]{2,1,0:T(8,128)(2,1)}), bf16[8,144,128]{2,1,0:T(8,128)(2,1)S(1)}, u32[]{:S(2)}, u32[]{:S(2)}) async-start(bf16[8,144,128]{2,1,0:T(8,128)(2,1)} %project.51), calls=%async_computation.1 | async-start | bytes 589824 | tf_op jit(solution)/shard_map/while/body/eval_jaxpr/exchange/all_to_all | solution.py:354
  350.5 5.0 collective-permute-start.15
  350.5 5.0 collective-permute-start.16
  360.0 7.5 %collective-permute-start.18 = (bf16[144,384]{1,0:T(8,128)(2,1)S(1)}, bf16[144,384]{1,0:T(8,128)(2,1)S(1)}, u32[]{:S(2)}, u32[]{:S(2)}) collective-permute-start(bf16[144,384]{1,0:T(8,128)(2,1)S(1)} %attend.87), channel_id=1, source_target_pairs={{0,2},{1,3},{2,0},{3,1},{4,6},{5,7},{6,4},{7,5},{8,10},{9,11},{10,... | collective-permute-start | bytes 331784 | tf_op jit(solution)/shard_map/while/body/eval_jaxpr/attend/ppermute | solution.py:372
  363.0 5.0 collective-permute-start.19
  376.8 5.3 collective-permute-start.23
  394.7 17.1 %all-to-all-start.1 = ((bf16[8,144,128]{2,1,0:T(8,128)(2,1)}), bf16[8,144,128]{2,1,0:T(8,128)(2,1)S(1)}, u32[]{:S(2)}, u32[]{:S(2)}) async-start(bf16[8,144,128]{2,1,0:T(8,128)(2,1)} %project.51), calls=%async_computation.1 | async-start | bytes 589824 | tf_op jit(solution)/shard_map/while/body/eval_jaxpr/exchange/all_to_all | solution.py:354
  403.9 5.0 collective-permute-start.15
  403.9 5.0 collective-permute-start.16
  413.4 7.5 %collective-permute-start.18 = (bf16[144,384]{1,0:T(8,128)(2,1)S(1)}, bf16[144,384]{1,0:T(8,128)(2,1)S(1)}, u32[]{:S(2)}, u32[]{:S(2)}) collective-permute-start(bf16[144,384]{1,0:T(8,128)(2,1)S(1)} %attend.87), channel_id=1, source_target_pairs={{0,2},{1,3},{2,0},{3,1},{4,6},{5,7},{6,4},{7,5},{8,10},{9,11},{10,... | collective-permute-start | bytes 331784 | tf_op jit(solution)/shard_map/while/body/eval_jaxpr/attend/ppermute | solution.py:372
  416.3 5.0 collective-permute-start.19
  430.3 5.3 collective-permute-start.23
  448.1 17.1 %all-to-all-start.1 = ((bf16[8,144,128]{2,1,0:T(8,128)(2,1)}), bf16[8,144,128]{2,1,0:T(8,128)(2,1)S(1)}, u32[]{:S(2)}, u32[]{:S(2)}) async-start(bf16[8,144,128]{2,1,0:T(8,128)(2,1)} %project.51), calls=%async_computation.1 | async-start | bytes 589824 | tf_op jit(solution)/shard_map/while/body/eval_jaxpr/exchange/all_to_all | solution.py:354
  457.3 5.0 collective-permute-start.15
  457.3 5.0 collective-permute-start.16
  466.8 7.5 %collective-permute-start.18 = (bf16[144,384]{1,0:T(8,128)(2,1)S(1)}, bf16[144,384]{1,0:T(8,128)(2,1)S(1)}, u32[]{:S(2)}, u32[]{:S(2)}) collective-permute-start(bf16[144,384]{1,0:T(8,128)(2,1)S(1)} %attend.87), channel_id=1, source_target_pairs={{0,2},{1,3},{2,0},{3,1},{4,6},{5,7},{6,4},{7,5},{8,10},{9,11},{10,... | collective-permute-start | bytes 331784 | tf_op jit(solution)/shard_map/while/body/eval_jaxpr/attend/ppermute | solution.py:372
  469.7 5.0 collective-permute-start.19
  483.7 5.3 collective-permute-start.23
  501.5 17.1 %all-to-all-start.1 = ((bf16[8,144,128]{2,1,0:T(8,128)(2,1)}), bf16[8,144,128]{2,1,0:T(8,128)(2,1)S(1)}, u32[]{:S(2)}, u32[]{:S(2)}) async-start(bf16[8,144,128]{2,1,0:T(8,128)(2,1)} %project.51), calls=%async_computation.1 | async-start | bytes 589824 | tf_op jit(solution)/shard_map/while/body/eval_jaxpr/exchange/all_to_all | solution.py:354
  510.7 5.0 collective-permute-start.15
  510.7 5.0 collective-permute-start.16
  520.2 7.5 %collective-permute-start.18 = (bf16[144,384]{1,0:T(8,128)(2,1)S(1)}, bf16[144,384]{1,0:T(8,128)(2,1)S(1)}, u32[]{:S(2)}, u32[]{:S(2)}) collective-permute-start(bf16[144,384]{1,0:T(8,128)(2,1)S(1)} %attend.87), channel_id=1, source_target_pairs={{0,2},{1,3},{2,0},{3,1},{4,6},{5,7},{6,4},{7,5},{8,10},{9,11},{10,... | collective-permute-start | bytes 331784 | tf_op jit(solution)/shard_map/while/body/eval_jaxpr/attend/ppermute | solution.py:372
  523.1 5.0 collective-permute-start.19
  537.1 5.3 collective-permute-start.23
  (75 other events, 360.8 us)
Sparse Core Ops, SparseCore 0:
  27.4 118.4 all-gather.6
  148.4 116.7 all-gather.4

commit v7 on v6

--- a/solution.py
+++ b/solution.py
@@ -356,7 +356,7 @@
             )
         return qs, kv
 
-    def attend(scal, qs, kv):
+    def attend(scal, qs, kv, held_up=None):
         parts = [None] * XN
         with jax.named_scope("attend"):
             for d in (3, 2, 1, 0):
@@ -370,6 +370,8 @@
                     SHARE * tok * seq_keys * 6 // 4,
                 )
                 parts[d] = lax.ppermute(part, "seq", seq_pairs(d)) if d else part
+            if held_up:
+                parts[0], held_up[3] = lax.optimization_barrier((parts[0], held_up[3]))
             attended = call(
                 combine_kernel,
                 scal,
@@ -378,6 +380,8 @@
                 10 * rows * QW,
                 10 * rows * QW,
             )
+            if held_up:
+                attended, held_up[2] = lax.optimization_barrier((attended, held_up[2]))
             return spread(attended)
 
     def numbers(slot, layer):
@@ -389,8 +393,8 @@
         kv = call(first_keys_kernel, scal, args, kv_shape, *keys_cost, scratch=first_room(SHARD))
         q = call(first_queries_kernel, scal, args, piece_shape, *full_cost, scratch=first_room(Q_ROWS))
     qs, kv = exchange(q, kv)
-    kv, first_out = lax.optimization_barrier((kv, first_out))
-    heads = attend(scal, qs, kv)
+    kv, first_out[1] = lax.optimization_barrier((kv, first_out[1]))
+    heads = attend(scal, qs, kv, first_out)
     with jax.named_scope("output"):
         args = (*heads, pieces[0], *first_out)
         own = call(first_output_kernel, scal, args, piece_shape, *full_cost, scratch=first_room(Q_ROWS))

time: 571 us -> 578 us (1.012)
  Pallas kernels: 99.4 us -> 108 us
  waiting for transfers between devices: 192 us -> 184 us
  starting transfers between devices: 218 us -> 224 us
    pallas_call x65, Pallas kernels: 99.4 us -> 108 us  [call(): pl.pallas_call(kernel, out_shape=out_shape, in_specs=in_specs, out_specs=...]
  transfers between devices with their start and end apart: 130 -> 130, of which waited for: 102 -> 104; matrix products, arithmetic and copies ran while one was open for 1% -> 1% of each run, Pallas kernels for 14% -> 15%
where the time goes in v7:
time: 578 us; the launch traced here: 568 us
  starting transfers between devices  224 us (39%)
  waiting for transfers between devices  184 us (32%)
  Pallas kernels  108 us (19%)
  blocking collectives  17 us (3%)
  between operations  13.8 us (2%)
  local copies, waits for them, and re-layouts  10.6 us (2%)
  loops' own time  9.7 us (2%)
    pallas_call x65, Pallas kernels, call(): pl.pallas_call(kernel, out_shape=out_shape, in_specs=in_specs, out_specs=...  108 us
    ppermute x48, starting transfers between devices, spread(): lax.ppermute(piece, 'section', section_pairs(2 * d))  55 us
    ppermute x16, starting transfers between devices, spread(): other = lax.ppermute(jnp.stack(near), 'section', section_pairs(1))  53.9 us
    ppermute x48, waiting for transfers between devices, spread(): lax.ppermute(piece, 'section', section_pairs(2 * d))  51.2 us
    ppermute x24, waiting for transfers between devices, exchange(): qs = [lax.ppermute(q, 'seq', seq_pairs(d)) for d in (3, 2, 1)]  46.5 us
    all_to_all x8, starting transfers between devices, exchange(): lax.all_to_all(kv, 'seq', split_axis=0, concat_axis=0, tiled=True, axis_i...  45.6 us
    ppermute x24, starting transfers between devices, exchange(): qs = [lax.ppermute(q, 'seq', seq_pairs(d)) for d in (3, 2, 1)]  26.5 us
    ppermute x24, starting transfers between devices, attend(): parts[d] = lax.ppermute(part, 'seq', seq_pairs(d)) if d else part  24.1 us
  transfers between devices with their start and end apart: 130, of which 104 were waited for; matrix products, arithmetic and copies ran while one was open for 1% of the time, Pallas kernels for 15%

profile of v7, /device:TPU:1, one launch (start us, length us, event | category | flops | bytes accessed | tf_op | source)
XLA Modules:
  0.0 568.4 jit_solution(10665354473101880152)
XLA Ops:
  9.5 17.0 %all_to_all.32 = bf16[8,336,128]{2,1,0:T(8,128)(2,1)S(1)} all-to-all(bf16[8,336,128]{2,1,0:T(8,128)(2,1)S(1)} %pad_maximum_fusion.4), channel_id=1, replica_groups=mesh['section'=8,'seq'=32] {'section'}, dimensions={0} | all-to-all | bytes 1376256 | tf_op jit(solution)/shard_map/all_to_all | solution.py:307
  29.0 8.2 %all-to-all-start.3 = ((bf16[8,192,128]{2,1,0:T(8,128)(2,1)}), bf16[8,192,128]{2,1,0:T(8,128)(2,1)S(1)}, u32[]{:S(2)}, u32[]{:S(2)}) async-start(bf16[8,192,128]{2,1,0:T(8,128)(2,1)} %broadcast_in_dim.26), calls=%async_computation.3 | async-start | bytes 786432 | tf_op jit(solution)/shard_map/weights/all_to_all | solution.py:317
  37.2 15.0 %all-to-all-done.3.w0 = bf16[8,192,128]{2,1,0:T(8,128)(2,1)S(1)} async-done(((bf16[8,192,128]{2,1,0:T(8,128)(2,1)}), bf16[8,192,128]{2,1,0:T(8,128)(2,1)S(1)}, u32[]{:S(2)}, u32[]{:S(2)}) %all-to-all-start.3) | async-done | bytes 393248 | tf_op jit(solution)/shard_map/weights/all_to_all | solution.py:317
  52.9 3.4 all-to-all-start.4
  57.5 2.4 collective-permute-start.29
  60.5 4.1 collective-permute-done.28.w1
  64.5 9.5 %collective-permute-done.29.w2 = bf16[8,192,128]{2,1,0:T(8,128)(2,1)S(1)} collective-permute-done((bf16[8,192,128]{2,1,0:T(8,128)(2,1)S(1)}, bf16[8,192,128]{2,1,0:T(8,128)(2,1)S(1)}, u32[]{:S(2)}, u32[]{:S(2)}) %collective-permute-start.29) | collective-permute-done | bytes 393248 | tf_op jit(solution)/shard_map/weights/ppermute | solution.py:322
  75.8 5.9 %all-to-all-start.5 = ((bf16[8,144,128]{2,1,0:T(8,128)(2,1)}), bf16[8,144,128]{2,1,0:T(8,128)(2,1)S(1)}, u32[]{:S(2)}, u32[]{:S(2)}) async-start(bf16[8,144,128]{2,1,0:T(8,128)(2,1)} %project.47), calls=%async_computation.5 | async-start | bytes 589824 | tf_op jit(solution)/shard_map/exchange/all_to_all | solution.py:354
  86.7 2.1 collective-permute-start.34
  89.3 18.2 %collective-permute-done.34.q_ref = bf16[144,256]{1,0:T(8,128)(2,1)S(1)} collective-permute-done((bf16[144,256]{1,0:T(8,128)(2,1)S(1)}, bf16[144,256]{1,0:T(8,128)(2,1)S(1)}, u32[]{:S(2)}, u32[]{:S(2)}) %collective-permute-start.34) | collective-permute-done | bytes 73760 | tf_op jit(solution)/shard_map/exchange/ppermute | solution.py:350
  107.6 2.6 collective-permute-done.35.q_ref
  121.9 3.4 collective-permute-done.36.o1
  126.7 3.7 collective-permute-start.42
  132.6 11.0 %collective-permute-start.43 = (bf16[4,144,256]{2,1,0:T(8,128)(2,1)S(1)}, bf16[4,144,256]{2,1,0:T(8,128)(2,1)S(1)}, u32[]{:S(2)}, u32[]{:S(2)}) collective-permute-start(bf16[4,144,256]{2,1,0:T(8,128)(2,1)S(1)} %pad_maximum_fusion.6), channel_id=1, source_target_pairs={{0,32},{32,0},{64,96},{96,64},{128,160},{160,128},{192,224},{224,1... | collective-permute-start | bytes 884744 | tf_op jit(solution)/shard_map/attend/ppermute | solution.py:44
  146.5 3.6 collective-permute-start.45
  150.0 3.3 collective-permute-done.45
  157.8 1.9 slice_bitcast_fusion.1
  159.8 170.0 %while.58 = (s32[]{:T(128)}, bf16[144,256]{1,0:T(8,128)(2,1)S(1)}, bf16[144,256]{1,0:T(8,128)(2,1)S(1)}, bf16[144,256]{1,0:T(8,128)(2,1)S(1)}, bf16[144,256]{1,0...) while((s32[]{:T(128)}, bf16[144,256]{1,0:T(8,128)(2,1)S(1)}, ...), condition=%wide.region_1.0_spmd, body=%wide.region_0.0_spmd.sunk | while | flops 1284710400 | bytes 15377141 | solution.py:438
  159.9 2.2 project.49
  162.2 6.7 %all-to-all-start = ((bf16[8,144,128]{2,1,0:T(8,128)(2,1)}), bf16[8,144,128]{2,1,0:T(8,128)(2,1)S(1)}, u32[]{:S(2)}, u32[]{:S(2)}) async-start(bf16[8,144,128]{2,1,0:T(8,128)(2,1)} %project.49), calls=%async_computation | async-start | bytes 589824 | tf_op jit(solution)/shard_map/while/body/eval_jaxpr/exchange/all_to_all | solution.py:354
  168.9 3.3 project.48
  178.6 4.1 all-to-all-done.k_ref
  184.2 1.9 collective-permute-start.4
  202.0 5.0 collective-permute-start.9
  219.3 2.2 project.49
  221.5 3.4 all-to-all-start
  225.0 3.4 project.48
  231.7 5.0 collective-permute-done.q_ref
  236.7 2.3 collective-permute-done.2.q_ref
  244.3 2.1 collective-permute-start.5
  249.9 2.4 collective-permute-done.5.o3
  253.4 2.6 collective-permute-start.8
  258.3 2.5 collective-permute-done.7.a2
  260.8 2.2 collective-permute-start.9
  271.8 2.1 collective-permute-start.13
  275.2 2.2 project.49
  277.5 5.9 %all-to-all-start = ((bf16[8,144,128]{2,1,0:T(8,128)(2,1)}), bf16[8,144,128]{2,1,0:T(8,128)(2,1)S(1)}, u32[]{:S(2)}, u32[]{:S(2)}) async-start(bf16[8,144,128]{2,1,0:T(8,128)(2,1)} %project.49), calls=%async_computation | async-start | bytes 589824 | tf_op jit(solution)/shard_map/while/body/eval_jaxpr/exchange/all_to_all | solution.py:354
  283.3 3.3 project.48
  292.9 2.8 all-to-all-done.k_ref
  314.1 4.0 collective-permute-start.9
  331.7 228.2 %while.59 = (s32[]{:T(128)}, bf16[144,256]{1,0:T(8,128)(2,1)S(1)}, bf16[144,256]{1,0:T(8,128)(2,1)S(1)}, bf16[144,256]{1,0:T(8,128)(2,1)S(1)}, bf16[144,256]{1,0...) while((s32[]{:T(128)}, bf16[144,256]{1,0:T(8,128)(2,1)S(1)}, ...), condition=%wide.region_3.0_spmd, body=%wide.region_2.0_spmd.sunk | while | flops 1284710400 | bytes 15377153 | solution.py:438
  341.1 2.2 project.51
  343.3 6.0 %all-to-all-start.1 = ((bf16[8,144,128]{2,1,0:T(8,128)(2,1)}), bf16[8,144,128]{2,1,0:T(8,128)(2,1)S(1)}, u32[]{:S(2)}, u32[]{:S(2)}) async-start(bf16[8,144,128]{2,1,0:T(8,128)(2,1)} %project.51), calls=%async_computation.1 | async-start | bytes 589824 | tf_op jit(solution)/shard_map/while/body/eval_jaxpr/exchange/all_to_all | solution.py:354
  349.3 3.3 project.50
  358.9 2.8 all-to-all-done.1.k_ref
  380.1 4.1 collective-permute-start.23
  396.0 2.2 project.51
  398.2 5.9 %all-to-all-start.1 = ((bf16[8,144,128]{2,1,0:T(8,128)(2,1)}), bf16[8,144,128]{2,1,0:T(8,128)(2,1)S(1)}, u32[]{:S(2)}, u32[]{:S(2)}) async-start(bf16[8,144,128]{2,1,0:T(8,128)(2,1)} %project.51), calls=%async_computation.1 | async-start | bytes 589824 | tf_op jit(solution)/shard_map/while/body/eval_jaxpr/exchange/all_to_all | solution.py:354
  404.1 3.3 project.50
  413.7 2.8 all-to-all-done.1.k_ref
  434.8 4.0 collective-permute-start.23
  447.3 2.1 collective-permute-start.27
  450.7 2.2 project.51
  452.9 5.9 %all-to-all-start.1 = ((bf16[8,144,128]{2,1,0:T(8,128)(2,1)}), bf16[8,144,128]{2,1,0:T(8,128)(2,1)S(1)}, u32[]{:S(2)}, u32[]{:S(2)}) async-start(bf16[8,144,128]{2,1,0:T(8,128)(2,1)} %project.51), calls=%async_computation.1 | async-start | bytes 589824 | tf_op jit(solution)/shard_map/while/body/eval_jaxpr/exchange/all_to_all | solution.py:354
  458.8 3.3 project.50
  468.4 2.8 all-to-all-done.1.k_ref
  489.5 4.1 collective-permute-start.23
  502.0 2.1 collective-permute-start.27
  505.4 2.2 project.51
  507.6 5.9 %all-to-all-start.1 = ((bf16[8,144,128]{2,1,0:T(8,128)(2,1)}), bf16[8,144,128]{2,1,0:T(8,128)(2,1)S(1)}, u32[]{:S(2)}, u32[]{:S(2)}) async-start(bf16[8,144,128]{2,1,0:T(8,128)(2,1)} %project.51), calls=%async_computation.1 | async-start | bytes 589824 | tf_op jit(solution)/shard_map/while/body/eval_jaxpr/exchange/all_to_all | solution.py:354
  513.5 3.3 project.50
  523.1 2.8 all-to-all-done.1.k_ref
  544.1 4.1 collective-permute-start.23
  556.7 2.1 collective-permute-start.27
  (336 shorter events, 278.3 us)
Async XLA Ops:
  6.5 151.3 %all-gather.7.cloned.1.call-start = ((), (), s32[]{:S(2)}) async-start(), calls=%async_computation.7 | async-start | bytes 8110080 | tf_op jit(solution)/shard_map/weights/all_gather | solution.py:312
  27.3 302.5 %all-gather.5.cloned.1.call-start = ((), (), s32[]{:S(2)}) async-start(), calls=%async_computation.6 | async-start | bytes 10813440 | tf_op jit(solution)/shard_map/weights/all_gather | solution.py:313
  29.0 23.2 %all-to-all-start.3 = ((bf16[8,192,128]{2,1,0:T(8,128)(2,1)}), bf16[8,192,128]{2,1,0:T(8,128)(2,1)S(1)}, u32[]{:S(2)}, u32[]{:S(2)}) async-start(bf16[8,192,128]{2,1,0:T(8,128)(2,1)} %broadcast_in_dim.26), calls=%async_computation.3 | async-start | bytes 786432 | tf_op jit(solution)/shard_map/weights/all_to_all | solution.py:317
  52.9 21.2 %all-to-all-start.4 = ((bf16[8,128,128]{2,1,0:T(8,128)(2,1)}), bf16[8,128,128]{2,1,0:T(8,128)(2,1)S(1)}, u32[]{:S(2)}, u32[]{:S(2)}) async-start(bf16[8,128,128]{2,1,0:T(8,128)(2,1)} %broadcast_in_dim.27), calls=%async_computation.4 | async-start | bytes 524288 | tf_op jit(solution)/shard_map/weights/all_to_all | solution.py:317
  56.3 8.3 %collective-permute-start.28 = (bf16[8,192,128]{2,1,0:T(8,128)(2,1)S(1)}, bf16[8,192,128]{2,1,0:T(8,128)(2,1)S(1)}, u32[]{:S(2)}, u32[]{:S(2)}) collective-permute-start(bf16[8,192,128]{2,1,0:T(8,128)(2,1)S(1)} %all-to-all-done.3.w0), channel_id=1, source_target_pairs={{0,1},{1,0},{2,3},{3,2},{4,5},{5,4},{6,7},{7,6},{8,9},{9,8},{10,11... | collective-permute-start | bytes 1179656 | tf_op jit(solution)/shard_map/weights/ppermute | solution.py:322
  57.5 16.5 %collective-permute-start.29 = (bf16[8,192,128]{2,1,0:T(8,128)(2,1)S(1)}, bf16[8,192,128]{2,1,0:T(8,128)(2,1)S(1)}, u32[]{:S(2)}, u32[]{:S(2)}) collective-permute-start(bf16[8,192,128]{2,1,0:T(8,128)(2,1)S(1)} %all-to-all-done.3.w0), channel_id=1, source_target_pairs={{0,2},{1,3},{2,0},{3,1},{4,6},{5,7},{6,4},{7,5},{8,10},{9,11},{10,... | collective-permute-start | bytes 1179656 | tf_op jit(solution)/shard_map/weights/ppermute | solution.py:322
  59.9 14.1 %collective-permute-start.30 = (bf16[8,192,128]{2,1,0:T(8,128)(2,1)S(1)}, bf16[8,192,128]{2,1,0:T(8,128)(2,1)S(1)}, u32[]{:S(2)}, u32[]{:S(2)}) collective-permute-start(bf16[8,192,128]{2,1,0:T(8,128)(2,1)S(1)} %all-to-all-done.3.w0), channel_id=1, source_target_pairs={{0,3},{1,2},{2,1},{3,0},{4,7},{5,6},{6,5},{7,4},{8,11},{9,10},{10,... | collective-permute-start | bytes 1179656 | tf_op jit(solution)/shard_map/weights/ppermute | solution.py:322
  75.8 34.4 %all-to-all-start.5 = ((bf16[8,144,128]{2,1,0:T(8,128)(2,1)}), bf16[8,144,128]{2,1,0:T(8,128)(2,1)S(1)}, u32[]{:S(2)}, u32[]{:S(2)}) async-start(bf16[8,144,128]{2,1,0:T(8,128)(2,1)} %project.47), calls=%async_computation.5 | async-start | bytes 589824 | tf_op jit(solution)/shard_map/exchange/all_to_all | solution.py:354
  81.7 28.5 %collective-permute-start.31 = (bf16[8,128,128]{2,1,0:T(8,128)(2,1)S(1)}, bf16[8,128,128]{2,1,0:T(8,128)(2,1)S(1)}, u32[]{:S(2)}, u32[]{:S(2)}) collective-permute-start(bf16[8,128,128]{2,1,0:T(8,128)(2,1)S(1)} %all-to-all-done.4.w0), channel_id=1, source_target_pairs={{0,1},{1,0},{2,3},{3,2},{4,5},{5,4},{6,7},{7,6},{8,9},{9,8},{10,11... | collective-permute-start | bytes 786440 | tf_op jit(solution)/shard_map/weights/ppermute | solution.py:322
  83.0 6.3 %collective-permute-start.33 = (bf16[144,256]{1,0:T(8,128)(2,1)S(1)}, bf16[144,256]{1,0:T(8,128)(2,1)S(1)}, u32[]{:S(2)}, u32[]{:S(2)}) collective-permute-start(bf16[144,256]{1,0:T(8,128)(2,1)S(1)} %project.46.q_ref), channel_id=1, source_target_pairs={{0,3},{1,2},{2,1},{3,0},{4,7},{5,6},{6,5},{7,4},{8,11},{9,10},{10,... | collective-permute-start | bytes 221192 | tf_op jit(solution)/shard_map/exchange/ppermute | solution.py:350
  84.0 36.1 %collective-permute-start.32 = (bf16[8,128,128]{2,1,0:T(8,128)(2,1)S(1)}, bf16[8,128,128]{2,1,0:T(8,128)(2,1)S(1)}, u32[]{:S(2)}, u32[]{:S(2)}) collective-permute-start(bf16[8,128,128]{2,1,0:T(8,128)(2,1)S(1)} %all-to-all-done.4.w0), channel_id=1, source_target_pairs={{0,3},{1,2},{2,1},{3,0},{4,7},{5,6},{6,5},{7,4},{8,11},{9,10},{10,... | collective-permute-start | bytes 786440 | tf_op jit(solution)/shard_map/weights/ppermute | solution.py:322
  85.8 40.7 %collective-permute-start.39 = (bf16[8,128,128]{2,1,0:T(8,128)(2,1)S(1)}, bf16[8,128,128]{2,1,0:T(8,128)(2,1)S(1)}, u32[]{:S(2)}, u32[]{:S(2)}) collective-permute-start(bf16[8,128,128]{2,1,0:T(8,128)(2,1)S(1)} %all-to-all-done.4.w0), channel_id=1, source_target_pairs={{0,2},{1,3},{2,0},{3,1},{4,6},{5,7},{6,4},{7,5},{8,10},{9,11},{10,... | collective-permute-start | bytes 786440 | tf_op jit(solution)/shard_map/weights/ppermute | solution.py:322
  86.7 20.9 %collective-permute-start.34 = (bf16[144,256]{1,0:T(8,128)(2,1)S(1)}, bf16[144,256]{1,0:T(8,128)(2,1)S(1)}, u32[]{:S(2)}, u32[]{:S(2)}) collective-permute-start(bf16[144,256]{1,0:T(8,128)(2,1)S(1)} %project.46.q_ref), channel_id=1, source_target_pairs={{0,2},{1,3},{2,0},{3,1},{4,6},{5,7},{6,4},{7,5},{8,10},{9,11},{10,... | collective-permute-start | bytes 221192 | tf_op jit(solution)/shard_map/exchange/ppermute | solution.py:350
  89.3 20.8 %collective-permute-start.35 = (bf16[144,256]{1,0:T(8,128)(2,1)S(1)}, bf16[144,256]{1,0:T(8,128)(2,1)S(1)}, u32[]{:S(2)}, u32[]{:S(2)}) collective-permute-start(bf16[144,256]{1,0:T(8,128)(2,1)S(1)} %project.46.q_ref), channel_id=1, source_target_pairs={{0,1},{1,0},{2,3},{3,2},{4,5},{5,4},{6,7},{7,6},{8,9},{9,8},{10,11... | collective-permute-start | bytes 221192 | tf_op jit(solution)/shard_map/exchange/ppermute | solution.py:350
  111.8 8.4 %collective-permute-start.38 = (bf16[144,384]{1,0:T(8,128)(2,1)S(1)}, bf16[144,384]{1,0:T(8,128)(2,1)S(1)}, u32[]{:S(2)}, u32[]{:S(2)}) collective-permute-start(bf16[144,384]{1,0:T(8,128)(2,1)S(1)} %attend.78), channel_id=1, source_target_pairs={{0,3},{1,2},{2,1},{3,0},{4,7},{5,6},{6,5},{7,4},{8,11},{9,10},{10,... | collective-permute-start | bytes 331784 | tf_op jit(solution)/shard_map/attend/ppermute | solution.py:372
  114.3 7.6 %collective-permute-start.37 = (bf16[144,384]{1,0:T(8,128)(2,1)S(1)}, bf16[144,384]{1,0:T(8,128)(2,1)S(1)}, u32[]{:S(2)}, u32[]{:S(2)}) collective-permute-start(bf16[144,384]{1,0:T(8,128)(2,1)S(1)} %attend.77), channel_id=1, source_target_pairs={{0,2},{1,3},{2,0},{3,1},{4,6},{5,7},{6,4},{7,5},{8,10},{9,11},{10,... | collective-permute-start | bytes 331784 | tf_op jit(solution)/shard_map/attend/ppermute | solution.py:372
  117.1 8.3 %collective-permute-start.36 = (bf16[144,384]{1,0:T(8,128)(2,1)S(1)}, bf16[144,384]{1,0:T(8,128)(2,1)S(1)}, u32[]{:S(2)}, u32[]{:S(2)}) collective-permute-start(bf16[144,384]{1,0:T(8,128)(2,1)S(1)} %attend.76), channel_id=1, source_target_pairs={{0,1},{1,0},{2,3},{3,2},{4,5},{5,4},{6,7},{7,6},{8,9},{9,8},{10,11... | collective-permute-start | bytes 331784 | tf_op jit(solution)/shard_map/attend/ppermute | solution.py:372
  126.6 4.8 collective-permute-start.41
  126.7 5.9 %collective-permute-start.42 = (bf16[144,256]{1,0:T(8,128)(2,1)S(1)}, bf16[144,256]{1,0:T(8,128)(2,1)S(1)}, u32[]{:S(2)}, u32[]{:S(2)}) collective-permute-start(bf16[144,256]{1,0:T(8,128)(2,1)S(1)} %attend.79.a0), channel_id=1, source_target_pairs={{0,192},{32,224},{64,128},{96,160},{128,64},{160,96},{192,0},{224,... | collective-permute-start | bytes 221192 | tf_op jit(solution)/shard_map/attend/ppermute | solution.py:43
  132.6 12.2 %collective-permute-start.43 = (bf16[4,144,256]{2,1,0:T(8,128)(2,1)S(1)}, bf16[4,144,256]{2,1,0:T(8,128)(2,1)S(1)}, u32[]{:S(2)}, u32[]{:S(2)}) collective-permute-start(bf16[4,144,256]{2,1,0:T(8,128)(2,1)S(1)} %pad_maximum_fusion.6), channel_id=1, source_target_pairs={{0,32},{32,0},{64,96},{96,64},{128,160},{160,128},{192,224},{224,1... | collective-permute-start | bytes 884744 | tf_op jit(solution)/shard_map/attend/ppermute | solution.py:44
  146.5 6.9 %collective-permute-start.45 = (bf16[144,256]{1,0:T(8,128)(2,1)S(1)}, bf16[144,256]{1,0:T(8,128)(2,1)S(1)}, u32[]{:S(2)}, u32[]{:S(2)}) collective-permute-start(bf16[144,256]{1,0:T(8,128)(2,1)S(1)} %output.23), channel_id=1, source_target_pairs={{0,128},{32,160},{64,192},{96,224},{128,0},{160,32},{192,64},{224,... | collective-permute-start | bytes 221192 | tf_op jit(solution)/shard_map/output/ppermute | solution.py:43
  150.0 4.9 collective-permute-start.46
  162.2 20.5 %all-to-all-start = ((bf16[8,144,128]{2,1,0:T(8,128)(2,1)}), bf16[8,144,128]{2,1,0:T(8,128)(2,1)S(1)}, u32[]{:S(2)}, u32[]{:S(2)}) async-start(bf16[8,144,128]{2,1,0:T(8,128)(2,1)} %project.49), calls=%async_computation | async-start | bytes 589824 | tf_op jit(solution)/shard_map/while/body/eval_jaxpr/exchange/all_to_all | solution.py:354
  172.2 4.9 collective-permute-start
  172.8 5.0 collective-permute-start.1
  184.2 8.0 %collective-permute-start.4 = (bf16[144,384]{1,0:T(8,128)(2,1)S(1)}, bf16[144,384]{1,0:T(8,128)(2,1)S(1)}, u32[]{:S(2)}, u32[]{:S(2)}) collective-permute-start(bf16[144,384]{1,0:T(8,128)(2,1)S(1)} %attend.82), channel_id=1, source_target_pairs={{0,2},{1,3},{2,0},{3,1},{4,6},{5,7},{6,4},{7,5},{8,10},{9,11},{10,... | collective-permute-start | bytes 331784 | tf_op jit(solution)/shard_map/while/body/eval_jaxpr/attend/ppermute | solution.py:372
  187.7 6.1 %collective-permute-start.5 = (bf16[144,384]{1,0:T(8,128)(2,1)S(1)}, bf16[144,384]{1,0:T(8,128)(2,1)S(1)}, u32[]{:S(2)}, u32[]{:S(2)}) collective-permute-start(bf16[144,384]{1,0:T(8,128)(2,1)S(1)} %attend.83), channel_id=1, source_target_pairs={{0,3},{1,2},{2,1},{3,0},{4,7},{5,6},{6,5},{7,4},{8,11},{9,10},{10,... | collective-permute-start | bytes 331784 | tf_op jit(solution)/shard_map/while/body/eval_jaxpr/attend/ppermute | solution.py:372
  202.0 6.2 %collective-permute-start.9 = (bf16[4,144,256]{2,1,0:T(8,128)(2,1)S(1)}, bf16[4,144,256]{2,1,0:T(8,128)(2,1)S(1)}, u32[]{:S(2)}, u32[]{:S(2)}) collective-permute-start(bf16[4,144,256]{2,1,0:T(8,128)(2,1)S(1)} %pad_maximum_fusion.12), channel_id=1, source_target_pairs={{0,32},{32,0},{64,96},{96,64},{128,160},{160,128},{192,224},{224,1... | collective-permute-start | bytes 884744 | tf_op jit(solution)/shard_map/while/body/eval_jaxpr/attend/ppermute | solution.py:44
  209.1 4.8 collective-permute-start.11
  209.8 5.2 collective-permute-start.10
  221.5 19.3 %all-to-all-start = ((bf16[8,144,128]{2,1,0:T(8,128)(2,1)}), bf16[8,144,128]{2,1,0:T(8,128)(2,1)S(1)}, u32[]{:S(2)}, u32[]{:S(2)}) async-start(bf16[8,144,128]{2,1,0:T(8,128)(2,1)} %project.49), calls=%async_computation | async-start | bytes 589824 | tf_op jit(solution)/shard_map/while/body/eval_jaxpr/exchange/all_to_all | solution.py:354
  228.4 8.3 %collective-permute-start = (bf16[144,256]{1,0:T(8,128)(2,1)S(1)}, bf16[144,256]{1,0:T(8,128)(2,1)S(1)}, u32[]{:S(2)}, u32[]{:S(2)}) collective-permute-start(bf16[144,256]{1,0:T(8,128)(2,1)S(1)} %get-tuple-element.1107.q_ref), channel_id=1, source_target_pairs={{0,3},{1,2},{2,1},{3,0},{4,7},{5,6},{6,5},{7,4},{8,11},{9,10},{10,... | collective-permute-start | bytes 221192 | tf_op jit(solution)/shard_map/while/body/eval_jaxpr/exchange/ppermute | solution.py:350
  229.0 7.7 %collective-permute-start.1 = (bf16[144,256]{1,0:T(8,128)(2,1)S(1)}, bf16[144,256]{1,0:T(8,128)(2,1)S(1)}, u32[]{:S(2)}, u32[]{:S(2)}) collective-permute-start(bf16[144,256]{1,0:T(8,128)(2,1)S(1)} %get-tuple-element.1107.q_ref), channel_id=1, source_target_pairs={{0,2},{1,3},{2,0},{3,1},{4,6},{5,7},{6,4},{7,5},{8,10},{9,11},{10,... | collective-permute-start | bytes 221192 | tf_op jit(solution)/shard_map/while/body/eval_jaxpr/exchange/ppermute | solution.py:350
  230.2 8.8 %collective-permute-start.2 = (bf16[144,256]{1,0:T(8,128)(2,1)S(1)}, bf16[144,256]{1,0:T(8,128)(2,1)S(1)}, u32[]{:S(2)}, u32[]{:S(2)}) collective-permute-start(bf16[144,256]{1,0:T(8,128)(2,1)S(1)} %get-tuple-element.1107.q_ref), channel_id=1, source_target_pairs={{0,1},{1,0},{2,3},{3,2},{4,5},{5,4},{6,7},{7,6},{8,9},{9,8},{10,11... | collective-permute-start | bytes 221192 | tf_op jit(solution)/shard_map/while/body/eval_jaxpr/exchange/ppermute | solution.py:350
  242.4 7.6 %collective-permute-start.4 = (bf16[144,384]{1,0:T(8,128)(2,1)S(1)}, bf16[144,384]{1,0:T(8,128)(2,1)S(1)}, u32[]{:S(2)}, u32[]{:S(2)}) collective-permute-start(bf16[144,384]{1,0:T(8,128)(2,1)S(1)} %attend.82), channel_id=1, source_target_pairs={{0,2},{1,3},{2,0},{3,1},{4,6},{5,7},{6,4},{7,5},{8,10},{9,11},{10,... | collective-permute-start | bytes 331784 | tf_op jit(solution)/shard_map/while/body/eval_jaxpr/attend/ppermute | solution.py:372
  244.3 8.0 %collective-permute-start.5 = (bf16[144,384]{1,0:T(8,128)(2,1)S(1)}, bf16[144,384]{1,0:T(8,128)(2,1)S(1)}, u32[]{:S(2)}, u32[]{:S(2)}) collective-permute-start(bf16[144,384]{1,0:T(8,128)(2,1)S(1)} %attend.83), channel_id=1, source_target_pairs={{0,3},{1,2},{2,1},{3,0},{4,7},{5,6},{6,5},{7,4},{8,11},{9,10},{10,... | collective-permute-start | bytes 331784 | tf_op jit(solution)/shard_map/while/body/eval_jaxpr/attend/ppermute | solution.py:372
  253.4 4.9 collective-permute-start.8
  256.0 4.8 collective-permute-start.7
  277.5 18.3 %all-to-all-start = ((bf16[8,144,128]{2,1,0:T(8,128)(2,1)}), bf16[8,144,128]{2,1,0:T(8,128)(2,1)S(1)}, u32[]{:S(2)}, u32[]{:S(2)}) async-start(bf16[8,144,128]{2,1,0:T(8,128)(2,1)} %project.49), calls=%async_computation | async-start | bytes 589824 | tf_op jit(solution)/shard_map/while/body/eval_jaxpr/exchange/all_to_all | solution.py:354
  287.6 5.0 collective-permute-start.1
  297.3 7.5 %collective-permute-start.4 = (bf16[144,384]{1,0:T(8,128)(2,1)S(1)}, bf16[144,384]{1,0:T(8,128)(2,1)S(1)}, u32[]{:S(2)}, u32[]{:S(2)}) collective-permute-start(bf16[144,384]{1,0:T(8,128)(2,1)S(1)} %attend.82), channel_id=1, source_target_pairs={{0,2},{1,3},{2,0},{3,1},{4,6},{5,7},{6,4},{7,5},{8,10},{9,11},{10,... | collective-permute-start | bytes 331784 | tf_op jit(solution)/shard_map/while/body/eval_jaxpr/attend/ppermute | solution.py:372
  300.4 4.9 collective-permute-start.5
  314.1 5.3 collective-permute-start.9
  343.3 18.4 %all-to-all-start.1 = ((bf16[8,144,128]{2,1,0:T(8,128)(2,1)}), bf16[8,144,128]{2,1,0:T(8,128)(2,1)S(1)}, u32[]{:S(2)}, u32[]{:S(2)}) async-start(bf16[8,144,128]{2,1,0:T(8,128)(2,1)} %project.51), calls=%async_computation.1 | async-start | bytes 589824 | tf_op jit(solution)/shard_map/while/body/eval_jaxpr/exchange/all_to_all | solution.py:354
  353.5 5.0 collective-permute-start.15
  363.3 7.5 %collective-permute-start.18 = (bf16[144,384]{1,0:T(8,128)(2,1)S(1)}, bf16[144,384]{1,0:T(8,128)(2,1)S(1)}, u32[]{:S(2)}, u32[]{:S(2)}) collective-permute-start(bf16[144,384]{1,0:T(8,128)(2,1)S(1)} %attend.87), channel_id=1, source_target_pairs={{0,2},{1,3},{2,0},{3,1},{4,6},{5,7},{6,4},{7,5},{8,10},{9,11},{10,... | collective-permute-start | bytes 331784 | tf_op jit(solution)/shard_map/while/body/eval_jaxpr/attend/ppermute | solution.py:372
  365.5 6.0 %collective-permute-start.19 = (bf16[144,384]{1,0:T(8,128)(2,1)S(1)}, bf16[144,384]{1,0:T(8,128)(2,1)S(1)}, u32[]{:S(2)}, u32[]{:S(2)}) collective-permute-start(bf16[144,384]{1,0:T(8,128)(2,1)S(1)} %attend.88), channel_id=1, source_target_pairs={{0,3},{1,2},{2,1},{3,0},{4,7},{5,6},{6,5},{7,4},{8,11},{9,10},{10,... | collective-permute-start | bytes 331784 | tf_op jit(solution)/shard_map/while/body/eval_jaxpr/attend/ppermute | solution.py:372
  380.1 5.3 collective-permute-start.23
  387.5 4.8 collective-permute-start.25
  398.2 18.3 %all-to-all-start.1 = ((bf16[8,144,128]{2,1,0:T(8,128)(2,1)}), bf16[8,144,128]{2,1,0:T(8,128)(2,1)S(1)}, u32[]{:S(2)}, u32[]{:S(2)}) async-start(bf16[8,144,128]{2,1,0:T(8,128)(2,1)} %project.51), calls=%async_computation.1 | async-start | bytes 589824 | tf_op jit(solution)/shard_map/while/body/eval_jaxpr/exchange/all_to_all | solution.py:354
  408.3 5.0 collective-permute-start.15
  418.1 7.5 %collective-permute-start.18 = (bf16[144,384]{1,0:T(8,128)(2,1)S(1)}, bf16[144,384]{1,0:T(8,128)(2,1)S(1)}, u32[]{:S(2)}, u32[]{:S(2)}) collective-permute-start(bf16[144,384]{1,0:T(8,128)(2,1)S(1)} %attend.87), channel_id=1, source_target_pairs={{0,2},{1,3},{2,0},{3,1},{4,6},{5,7},{6,4},{7,5},{8,10},{9,11},{10,... | collective-permute-start | bytes 331784 | tf_op jit(solution)/shard_map/while/body/eval_jaxpr/attend/ppermute | solution.py:372
  420.4 6.0 %collective-permute-start.19 = (bf16[144,384]{1,0:T(8,128)(2,1)S(1)}, bf16[144,384]{1,0:T(8,128)(2,1)S(1)}, u32[]{:S(2)}, u32[]{:S(2)}) collective-permute-start(bf16[144,384]{1,0:T(8,128)(2,1)S(1)} %attend.88), channel_id=1, source_target_pairs={{0,3},{1,2},{2,1},{3,0},{4,7},{5,6},{6,5},{7,4},{8,11},{9,10},{10,... | collective-permute-start | bytes 331784 | tf_op jit(solution)/shard_map/while/body/eval_jaxpr/attend/ppermute | solution.py:372
  434.8 5.3 collective-permute-start.23
  452.9 18.3 %all-to-all-start.1 = ((bf16[8,144,128]{2,1,0:T(8,128)(2,1)}), bf16[8,144,128]{2,1,0:T(8,128)(2,1)S(1)}, u32[]{:S(2)}, u32[]{:S(2)}) async-start(bf16[8,144,128]{2,1,0:T(8,128)(2,1)} %project.51), calls=%async_computation.1 | async-start | bytes 589824 | tf_op jit(solution)/shard_map/while/body/eval_jaxpr/exchange/all_to_all | solution.py:354
  463.0 5.0 collective-permute-start.15
  472.8 7.5 %collective-permute-start.18 = (bf16[144,384]{1,0:T(8,128)(2,1)S(1)}, bf16[144,384]{1,0:T(8,128)(2,1)S(1)}, u32[]{:S(2)}, u32[]{:S(2)}) collective-permute-start(bf16[144,384]{1,0:T(8,128)(2,1)S(1)} %attend.87), channel_id=1, source_target_pairs={{0,2},{1,3},{2,0},{3,1},{4,6},{5,7},{6,4},{7,5},{8,10},{9,11},{10,... | collective-permute-start | bytes 331784 | tf_op jit(solution)/shard_map/while/body/eval_jaxpr/attend/ppermute | solution.py:372
  475.0 6.1 %collective-permute-start.19 = (bf16[144,384]{1,0:T(8,128)(2,1)S(1)}, bf16[144,384]{1,0:T(8,128)(2,1)S(1)}, u32[]{:S(2)}, u32[]{:S(2)}) collective-permute-start(bf16[144,384]{1,0:T(8,128)(2,1)S(1)} %attend.88), channel_id=1, source_target_pairs={{0,3},{1,2},{2,1},{3,0},{4,7},{5,6},{6,5},{7,4},{8,11},{9,10},{10,... | collective-permute-start | bytes 331784 | tf_op jit(solution)/shard_map/while/body/eval_jaxpr/attend/ppermute | solution.py:372
  489.5 5.3 collective-permute-start.23
  507.6 18.3 %all-to-all-start.1 = ((bf16[8,144,128]{2,1,0:T(8,128)(2,1)}), bf16[8,144,128]{2,1,0:T(8,128)(2,1)S(1)}, u32[]{:S(2)}, u32[]{:S(2)}) async-start(bf16[8,144,128]{2,1,0:T(8,128)(2,1)} %project.51), calls=%async_computation.1 | async-start | bytes 589824 | tf_op jit(solution)/shard_map/while/body/eval_jaxpr/exchange/all_to_all | solution.py:354
  517.6 5.0 collective-permute-start.15
  527.4 7.5 %collective-permute-start.18 = (bf16[144,384]{1,0:T(8,128)(2,1)S(1)}, bf16[144,384]{1,0:T(8,128)(2,1)S(1)}, u32[]{:S(2)}, u32[]{:S(2)}) collective-permute-start(bf16[144,384]{1,0:T(8,128)(2,1)S(1)} %attend.87), channel_id=1, source_target_pairs={{0,2},{1,3},{2,0},{3,1},{4,6},{5,7},{6,4},{7,5},{8,10},{9,11},{10,... | collective-permute-start | bytes 331784 | tf_op jit(solution)/shard_map/while/body/eval_jaxpr/attend/ppermute | solution.py:372
  529.7 6.0 %collective-permute-start.19 = (bf16[144,384]{1,0:T(8,128)(2,1)S(1)}, bf16[144,384]{1,0:T(8,128)(2,1)S(1)}, u32[]{:S(2)}, u32[]{:S(2)}) collective-permute-start(bf16[144,384]{1,0:T(8,128)(2,1)S(1)} %attend.88), channel_id=1, source_target_pairs={{0,3},{1,2},{2,1},{3,0},{4,7},{5,6},{6,5},{7,4},{8,11},{9,10},{10,... | collective-permute-start | bytes 331784 | tf_op jit(solution)/shard_map/while/body/eval_jaxpr/attend/ppermute | solution.py:372
  544.1 5.3 collective-permute-start.23
  (73 other events, 353.3 us)
Sparse Core Ops, SparseCore 0:
  27.4 118.4 all-gather.6
  148.5 114.2 all-gather.4

commit v8 on v6

--- a/solution.py
+++ b/solution.py
@@ -83,11 +83,11 @@
     return parts[0] if panels == 1 else jnp.concatenate(parts, axis=1)
 
 
-def stream(me, slot, w_ref, held, sems):
+def stream(me, row, w_ref, held, sems):
     copies = []
     for i, mask in enumerate(ORDER):
         owner = jnp.bitwise_xor(me, mask)
-        source = w_ref.at[pl.ds(XN * owner, XN), slot, 0:Q_ROWS, :]
+        source = w_ref.at[pl.ds(XN * owner, XN), pl.ds(row, Q_ROWS), :]
         copies.append(pltpu.make_async_copy(source, held.at[i], sems.at[i]))
     for copy in copies:
         copy.start()
@@ -140,12 +140,12 @@
     scal, gain_ref, p0, p1, p2, p3, p4, w_ref, out_in, q_ref, out_ref, wout_ref, wkv_ref, held, sems, out_sems
 ):
     refs = [p0, p1, p2, p3, p4]
-    slot = scal[2]
-    w_of = stream(scal[0], slot, w_ref, held, sems)
-    later = jnp.minimum(slot + 1, w_ref.shape[1] - 1)
+    row = pl.multiple_of(scal[2], SHARD)
+    w_of = stream(scal[0], row, w_ref, held, sems)
+    later = pl.multiple_of(jnp.minimum(row + ALL_ROWS, w_ref.shape[1] - ALL_ROWS), SHARD)
     ahead = [
-        pltpu.make_async_copy(w_ref.at[:, slot, QKV_ROWS:ALL_ROWS, :], wout_ref, sems.at[SN]),
-        pltpu.make_async_copy(w_ref.at[:, later, Q_ROWS:QKV_ROWS, :], wkv_ref, sems.at[SN + 1]),
+        pltpu.make_async_copy(w_ref.at[:, pl.ds(row + QKV_ROWS, Q_ROWS), :], wout_ref, sems.at[SN]),
+        pltpu.make_async_copy(w_ref.at[:, pl.ds(later + Q_ROWS, SHARD), :], wkv_ref, sems.at[SN + 1]),
     ]
     for copy in ahead:
         copy.start()
@@ -257,9 +257,15 @@
     output([a0, a1, a2, a3, a4], h_ref, resident(scal[0], wout_ref), o_ref)
 
 
-def first_output_kernel(scal, a0, a1, a2, a3, a4, h_ref, w0, w1, w2, w3, o_ref, held):
-    w_of = assembled(scal[0], scal[1], [w0, w1, w2, w3], held, 0)
-    output([a0, a1, a2, a3, a4], h_ref, w_of, o_ref)
+def first_output_kernel(scal, a0, a1, a2, a3, a4, h_ref, w_ref, o_ref, wkv_ref, held, sems):
+    own = pltpu.make_async_copy(w_ref.at[:, 0:Q_ROWS, :], held, sems.at[0])
+    ahead = w_ref.at[:, 2 * Q_ROWS : 2 * Q_ROWS + SHARD, :]
+    ahead = pltpu.make_async_copy(ahead, wkv_ref, sems.at[1])
+    own.start()
+    ahead.start()
+    own.wait()
+    output([a0, a1, a2, a3, a4], h_ref, resident(scal[0], held), o_ref)
+    ahead.wait()
 
 
 VMEM = pl.BlockSpec(memory_space=pltpu.VMEM)
@@ -309,8 +315,9 @@
     by_layer = by_layer[:, :ALL_ROWS]
 
     with jax.named_scope("weights"):
-        early = lax.all_gather(by_layer[1:4], "seq", axis=0)
-        late = lax.all_gather(by_layer[4:], "seq", axis=0)
+        early = jnp.concatenate([by_layer[0, QKV_ROWS:], by_layer[1:4].reshape(-1, 128)])
+        early = lax.all_gather(early, "seq", axis=0)
+        late = lax.all_gather(by_layer[4:].reshape(-1, 128), "seq", axis=0)
 
         def over_z(part):
             part = jnp.broadcast_to(part[None], (ZN,) + part.shape)
@@ -321,10 +328,7 @@
         def over_x(part):
             return [part] + [lax.ppermute(part, "seq", seq_pairs(d)) for d in (1, 2, 3)]
 
-        first_qkv = over_z(by_layer[0, :QKV_ROWS])
-        first_qkv, first_out = lax.optimization_barrier((first_qkv, by_layer[0, QKV_ROWS:]))
-        first_qkv, first_out = lax.optimization_barrier((over_x(first_qkv), over_z(first_out)))
-        first_out = over_x(first_out)
+        first_qkv = over_x(over_z(by_layer[0, :QKV_ROWS]))
 
     flat = inputs.reshape(rows, width)
 
@@ -380,35 +384,41 @@
             )
             return spread(attended)
 
-    def numbers(slot, layer):
-        return jnp.stack([jnp.asarray(v, jnp.int32) for v in (me, seq, slot, layer)])
-
+    def numbers(row, layer):
+        return jnp.stack([jnp.asarray(v, jnp.int32) for v in (me, seq, row, layer)])
+
+    wkv_shape = jax.ShapeDtypeStruct((ZN * XN, SHARD, 128), BF16)
+    wout_shape = jax.ShapeDtypeStruct((ZN * XN, Q_ROWS, 128), BF16)
     scal = numbers(0, 0)
     with jax.named_scope("project"):
         args = (gains, *pieces, *first_qkv)
         kv = call(first_keys_kernel, scal, args, kv_shape, *keys_cost, scratch=first_room(SHARD))
         q = call(first_queries_kernel, scal, args, piece_shape, *full_cost, scratch=first_room(Q_ROWS))
     qs, kv = exchange(q, kv)
-    kv, first_out = lax.optimization_barrier((kv, first_out))
     heads = attend(scal, qs, kv)
     with jax.named_scope("output"):
-        args = (*heads, pieces[0], *first_out)
-        own = call(first_output_kernel, scal, args, piece_shape, *full_cost, scratch=first_room(Q_ROWS))
+        own, wkv = call(
+            first_output_kernel,
+            scal,
+            (*heads, pieces[0], early),
+            [piece_shape, wkv_shape],
+            *full_cost,
+            scratch=[pltpu.VMEM(wout_shape.shape, BF16), pltpu.SemaphoreType.DMA((2,))],
+            big=(6,),
+        )
         pieces = spread(own)
     out = jnp.zeros((rows, width), BF16)
 
-    wkv_shape = jax.ShapeDtypeStruct((ZN * XN, SHARD, 128), BF16)
-    wout_shape = jax.ShapeDtypeStruct((ZN * XN, Q_ROWS, 128), BF16)
     query_room = [
         pltpu.VMEM((SN, XN, Q_ROWS, 128), BF16),
         pltpu.SemaphoreType.DMA((SN + 2,)),
         pltpu.SemaphoreType.DMA((SN,)),
     ]
 
-    def step(group, first_layer):
+    def step(group, first_row, first_layer):
         def body(layer, carry):
             pieces, out, wkv = carry
-            scal = numbers(layer - first_layer, layer)
+            scal = numbers(first_row + (layer - first_layer) * ALL_ROWS, layer)
             with jax.named_scope("project"):
                 kv = call(keys_kernel, scal, (gains, *pieces, wkv), kv_shape, *keys_cost)
                 q, out, wout, wkv = call(
@@ -428,10 +438,10 @@
 
         return body
 
-    for group, begin, end in ((early, 1, 4), (late, 4, layers)):
-        group, pieces = lax.optimization_barrier((group, pieces))
-        carry = (pieces, out, group[:, 0, Q_ROWS:QKV_ROWS])
-        pieces, out, _ = lax.fori_loop(begin, end, step(group, begin), carry)
+    pieces, out, wkv = lax.fori_loop(1, 4, step(early, Q_ROWS, 1), (pieces, out, wkv))
+    late, pieces = lax.optimization_barrier((late, pieces))
+    wkv = late[:, Q_ROWS:QKV_ROWS]
+    pieces, out, wkv = lax.fori_loop(4, layers, step(late, 0, 4), (pieces, out, wkv))
     out = call(
         place_kernel,
         numbers(0, layers),

time: 571 us -> 557 us (0.975)
  blocking collectives: 17 us -> 38.7 us
  starting transfers between devices: 218 us -> 200 us
  waiting for transfers between devices: 192 us -> 180 us
    all_to_all x0 -> x1, blocking collectives: none -> 21.7 us  [over_z(): lax.all_to_all(part, 'seq', split_axis=0, concat_axis=0, tiled=True, axis...]
    ppermute x24, waiting for transfers between devices: 50.5 us -> 31.9 us  [exchange(): qs = [lax.ppermute(q, 'seq', seq_pairs(d)) for d in (3, 2, 1)]]
    all_to_all x2 -> x0, waiting for transfers between devices: 15 us -> none  [over_z(): lax.all_to_all(part, 'seq', split_axis=0, concat_axis=0, tiled=True, axis...]
    all_gather x2, waiting for transfers between devices: 0.01 us -> 13.7 us  [the longest x1 13.7 us: local(): early = lax.all_gather(early, 'seq', axis=0)]
    all_to_all x2 -> x0, starting transfers between devices: 11.6 us -> none  [over_z(): lax.all_to_all(part, 'seq', split_axis=0, concat_axis=0, tiled=True, axis...]
    all_to_all x8, waiting for transfers between devices: 21.2 us -> 30.4 us  [exchange(): lax.all_to_all(kv, 'seq', split_axis=0, concat_axis=0, tiled=True, axis_i...]
    ppermute x6 -> x3, waiting for transfers between devices: 13.6 us -> 15.9 us  [over_x(): return [part] + [lax.ppermute(part, 'seq', seq_pairs(d)) for d in (1, 2, 3)]]
  transfers between devices with their start and end apart: 130 -> 125, of which waited for: 102 -> 106; matrix products, arithmetic and copies ran while one was open for 1% -> 0% of each run, Pallas kernels for 14% -> 14%
where the time goes in v8:
time: 557 us; the launch traced here: 552 us
  starting transfers between devices  200 us (36%)
  waiting for transfers between devices  180 us (32%)
  Pallas kernels  100 us (18%)
  blocking collectives  38.7 us (7%)
  between operations  13.8 us (2%)
  loops' own time  9.99 us (2%)
  local copies, waits for them, and re-layouts  6.39 us (1%)
    pallas_call x65, Pallas kernels, call(): pl.pallas_call(kernel, out_shape=out_shape, in_specs=in_specs, out_specs=...  100 us
    ppermute x48, starting transfers between devices, spread(): lax.ppermute(piece, 'section', section_pairs(2 * d))  54.9 us
    ppermute x16, starting transfers between devices, spread(): other = lax.ppermute(jnp.stack(near), 'section', section_pairs(1))  49.3 us
    ppermute x48, waiting for transfers between devices, spread(): lax.ppermute(piece, 'section', section_pairs(2 * d))  48.3 us
    all_to_all x8, starting transfers between devices, exchange(): lax.all_to_all(kv, 'seq', split_axis=0, concat_axis=0, tiled=True, axis_i...  40.1 us
    ppermute x24, waiting for transfers between devices, exchange(): qs = [lax.ppermute(q, 'seq', seq_pairs(d)) for d in (3, 2, 1)]  31.9 us
    all_to_all x8, waiting for transfers between devices, exchange(): lax.all_to_all(kv, 'seq', split_axis=0, concat_axis=0, tiled=True, axis_i...  30.4 us
    ppermute x24, starting transfers between devices, exchange(): qs = [lax.ppermute(q, 'seq', seq_pairs(d)) for d in (3, 2, 1)]  26.9 us
  transfers between devices with their start and end apart: 125, of which 106 were waited for; matrix products, arithmetic and copies ran while one was open for 0% of the time, Pallas kernels for 14%

profile of v8, /device:TPU:1, one launch (start us, length us, event | category | flops | bytes accessed | tf_op | source)
XLA Modules:
  0.0 552.2 jit_solution(14867890682770531390)
XLA Ops:
  10.3 17.0 %all_to_all.27 = bf16[8,336,128]{2,1,0:T(8,128)(2,1)S(1)} all-to-all(bf16[8,336,128]{2,1,0:T(8,128)(2,1)S(1)} %pad_maximum_fusion.4), channel_id=1, replica_groups=mesh['section'=8,'seq'=32] {'section'}, dimensions={0} | all-to-all | bytes 1376256 | tf_op jit(solution)/shard_map/all_to_all | solution.py:313
  29.0 21.7 %all_to_all.28.w0 = bf16[8,192,128]{2,1,0:T(8,128)(2,1)S(1)} all-to-all(bf16[8,192,128]{2,1,0:T(8,128)(2,1)S(1)} %broadcast_in_dim.20), channel_id=1, replica_groups={{0,4,8,12,16,20,24,28},{1,5,9,13,17,21,25,29},{2,6,10,14,18,22,26,30},{..., dimensions={0} | all-to-all | bytes 786432 | tf_op jit(solution)/shard_map/weights/all_to_all | solution.py:324
  51.9 2.5 collective-permute-start.29
  54.8 5.1 collective-permute-done.28.w1
  59.9 10.7 %collective-permute-done.29.w2 = bf16[8,192,128]{2,1,0:T(8,128)(2,1)S(1)} collective-permute-done((bf16[8,192,128]{2,1,0:T(8,128)(2,1)S(1)}, bf16[8,192,128]{2,1,0:T(8,128)(2,1)S(1)}, u32[]{:S(2)}, u32[]{:S(2)}) %collective-permute-start.29) | collective-permute-done | bytes 393248 | tf_op jit(solution)/shard_map/weights/ppermute | solution.py:329
  72.4 7.2 %all-to-all-start.4 = ((bf16[8,144,128]{2,1,0:T(8,128)(2,1)}), bf16[8,144,128]{2,1,0:T(8,128)(2,1)S(1)}, u32[]{:S(2)}, u32[]{:S(2)}) async-start(bf16[8,144,128]{2,1,0:T(8,128)(2,1)} %project.47), calls=%async_computation.4 | async-start | bytes 589824 | tf_op jit(solution)/shard_map/exchange/all_to_all | solution.py:358
  81.5 2.5 collective-permute-start.33
  84.0 3.4 collective-permute-done.31.q_ref
  87.7 2.9 collective-permute-done.33.q_ref
  90.6 3.6 all-to-all-done.4.k_ref
  99.1 3.3 collective-permute-start.34
  105.0 5.2 collective-permute-done.34.o1
  111.7 3.7 collective-permute-start.39
  117.8 5.3 collective-permute-start.40
  124.3 13.7 %all-gather.6.cloned.1.call-done = bf16[34816,128]{1,0:T(8,128)(2,1)} async-done(((bf16[1088,128]{1,0:T(8,128)(2,1)}), bf16[34816,128]{1,0:T(8,128)(2,1)}) %all-gather.6.cloned.1.call-update) | async-done | bytes 8912912 | tf_op jit(solution)/shard_map/weights/all_gather | solution.py:319
  138.0 2.1 output.23
  144.1 2.4 collective-permute-done.42
  147.8 1.8 collective-permute-start.44
  150.9 168.6 %while.58 = (s32[]{:T(128)}, bf16[144,256]{1,0:T(8,128)(2,1)S(1)}, bf16[144,256]{1,0:T(8,128)(2,1)S(1)}, bf16[144,256]{1,0:T(8,128)(2,1)S(1)}, bf16[144,256]{1,0...) while((s32[]{:T(128)}, bf16[144,256]{1,0:T(8,128)(2,1)S(1)}, ...), condition=%wide.region_1.0_spmd, body=%wide.region_0.0_spmd.sunk | while | flops 1284710400 | bytes 15377181 | solution.py:441
  152.7 4.1 all-to-all-start
  156.8 2.5 project.48
  166.1 6.4 %all-to-all-done.k_ref = bf16[8,144,128]{2,1,0:T(8,128)(2,1)S(1)} async-done(((bf16[8,144,128]{2,1,0:T(8,128)(2,1)}), bf16[8,144,128]{2,1,0:T(8,128)(2,1)S(1)}, u32[]{:S(2)}, u32[]{:S(2)}) %all-to-all-start) | async-done | bytes 294944 | tf_op jit(solution)/shard_map/while/body/eval_jaxpr/exchange/all_to_all | solution.py:358
  177.4 3.3 collective-permute-start.5
  183.9 2.0 collective-permute-start.8
  188.4 2.2 collective-permute-done.7.a2
  190.6 3.9 collective-permute-start.9
  208.1 3.6 all-to-all-start
  211.7 2.6 project.48
  214.3 2.9 collective-permute-start
  217.8 3.7 collective-permute-done.q_ref
  221.5 2.7 collective-permute-done.1.q_ref
  225.1 2.4 all-to-all-done.k_ref
  231.5 2.6 collective-permute-start.3
  237.4 5.4 collective-permute-done.3.o1
  251.2 3.8 collective-permute-start.9
  268.6 4.3 all-to-all-start
  272.9 2.5 project.48
  276.2 2.6 collective-permute-start.2
  281.7 3.6 all-to-all-done.k_ref
  291.2 2.3 collective-permute-start.5
  303.4 4.3 collective-permute-start.9
  316.3 2.1 collective-permute-start.13
  320.6 223.1 %while.59 = (s32[]{:T(128)}, bf16[144,256]{1,0:T(8,128)(2,1)S(1)}, bf16[144,256]{1,0:T(8,128)(2,1)S(1)}, bf16[144,256]{1,0:T(8,128)(2,1)S(1)}, bf16[144,256]{1,0...) while((s32[]{:T(128)}, bf16[144,256]{1,0:T(8,128)(2,1)S(1)}, ...), condition=%wide.region_3.0_spmd, body=%wide.region_2.0_spmd.sunk | while | flops 1284710400 | bytes 15377173 | solution.py:444
  332.0 5.0 all-to-all-start.1
  337.0 2.5 project.50
  340.9 2.0 collective-permute-start.16
  345.8 3.6 all-to-all-done.1.k_ref
  367.2 4.1 collective-permute-start.23
  379.7 2.1 collective-permute-start.27
  384.8 5.6 %all-to-all-start.1 = ((bf16[8,144,128]{2,1,0:T(8,128)(2,1)}), bf16[8,144,128]{2,1,0:T(8,128)(2,1)S(1)}, u32[]{:S(2)}, u32[]{:S(2)}) async-start(bf16[8,144,128]{2,1,0:T(8,128)(2,1)} %project.51), calls=%async_computation.1 | async-start | bytes 589824 | tf_op jit(solution)/shard_map/while/body/eval_jaxpr/exchange/all_to_all | solution.py:358
  390.4 2.5 project.50
  399.2 3.6 all-to-all-done.1.k_ref
  421.1 4.1 collective-permute-start.23
  433.6 2.1 collective-permute-start.27
  438.7 5.1 all-to-all-start.1
  443.8 2.5 project.50
  452.6 3.6 all-to-all-done.1.k_ref
  474.5 4.1 collective-permute-start.23
  487.0 2.1 collective-permute-start.27
  492.1 5.1 all-to-all-start.1
  497.2 2.5 project.50
  506.0 3.6 all-to-all-done.1.k_ref
  527.9 4.1 collective-permute-start.23
  540.4 2.1 collective-permute-start.27
  (322 shorter events, 266.6 us)
Async XLA Ops:
  6.5 131.5 %all-gather.6.cloned.1.call-start = ((), (), s32[]{:S(2)}) async-start(), calls=%async_computation.6 | async-start | bytes 9191424 | tf_op jit(solution)/shard_map/weights/all_gather | solution.py:319
  28.1 291.4 %all-gather.4.cloned.1.call-start = ((), (), s32[]{:S(2)}) async-start(), calls=%async_computation.5 | async-start | bytes 10813440 | tf_op jit(solution)/shard_map/weights/all_gather | solution.py:320
  50.7 9.2 %collective-permute-start.28 = (bf16[8,192,128]{2,1,0:T(8,128)(2,1)S(1)}, bf16[8,192,128]{2,1,0:T(8,128)(2,1)S(1)}, u32[]{:S(2)}, u32[]{:S(2)}) collective-permute-start(bf16[8,192,128]{2,1,0:T(8,128)(2,1)S(1)} %all_to_all.28.w0), channel_id=1, source_target_pairs={{0,1},{1,0},{2,3},{3,2},{4,5},{5,4},{6,7},{7,6},{8,9},{9,8},{10,11... | collective-permute-start | bytes 1179656 | tf_op jit(solution)/shard_map/weights/ppermute | solution.py:329
  51.9 18.7 %collective-permute-start.29 = (bf16[8,192,128]{2,1,0:T(8,128)(2,1)S(1)}, bf16[8,192,128]{2,1,0:T(8,128)(2,1)S(1)}, u32[]{:S(2)}, u32[]{:S(2)}) collective-permute-start(bf16[8,192,128]{2,1,0:T(8,128)(2,1)S(1)} %all_to_all.28.w0), channel_id=1, source_target_pairs={{0,2},{1,3},{2,0},{3,1},{4,6},{5,7},{6,4},{7,5},{8,10},{9,11},{10,... | collective-permute-start | bytes 1179656 | tf_op jit(solution)/shard_map/weights/ppermute | solution.py:329
  54.4 16.3 %collective-permute-start.30 = (bf16[8,192,128]{2,1,0:T(8,128)(2,1)S(1)}, bf16[8,192,128]{2,1,0:T(8,128)(2,1)S(1)}, u32[]{:S(2)}, u32[]{:S(2)}) collective-permute-start(bf16[8,192,128]{2,1,0:T(8,128)(2,1)S(1)} %all_to_all.28.w0), channel_id=1, source_target_pairs={{0,3},{1,2},{2,1},{3,0},{4,7},{5,6},{6,5},{7,4},{8,11},{9,10},{10,... | collective-permute-start | bytes 1179656 | tf_op jit(solution)/shard_map/weights/ppermute | solution.py:329
  72.4 21.8 %all-to-all-start.4 = ((bf16[8,144,128]{2,1,0:T(8,128)(2,1)}), bf16[8,144,128]{2,1,0:T(8,128)(2,1)S(1)}, u32[]{:S(2)}, u32[]{:S(2)}) async-start(bf16[8,144,128]{2,1,0:T(8,128)(2,1)} %project.47), calls=%async_computation.4 | async-start | bytes 589824 | tf_op jit(solution)/shard_map/exchange/all_to_all | solution.py:358
  80.7 6.7 %collective-permute-start.31 = (bf16[144,256]{1,0:T(8,128)(2,1)S(1)}, bf16[144,256]{1,0:T(8,128)(2,1)S(1)}, u32[]{:S(2)}, u32[]{:S(2)}) collective-permute-start(bf16[144,256]{1,0:T(8,128)(2,1)S(1)} %project.46.q_ref), channel_id=1, source_target_pairs={{0,3},{1,2},{2,1},{3,0},{4,7},{5,6},{6,5},{7,4},{8,11},{9,10},{10,... | collective-permute-start | bytes 221192 | tf_op jit(solution)/shard_map/exchange/ppermute | solution.py:354
  81.5 6.2 %collective-permute-start.32 = (bf16[144,256]{1,0:T(8,128)(2,1)S(1)}, bf16[144,256]{1,0:T(8,128)(2,1)S(1)}, u32[]{:S(2)}, u32[]{:S(2)}) collective-permute-start(bf16[144,256]{1,0:T(8,128)(2,1)S(1)} %project.46.q_ref), channel_id=1, source_target_pairs={{0,2},{1,3},{2,0},{3,1},{4,6},{5,7},{6,4},{7,5},{8,10},{9,11},{10,... | collective-permute-start | bytes 221192 | tf_op jit(solution)/shard_map/exchange/ppermute | solution.py:354
  81.5 9.1 %collective-permute-start.33 = (bf16[144,256]{1,0:T(8,128)(2,1)S(1)}, bf16[144,256]{1,0:T(8,128)(2,1)S(1)}, u32[]{:S(2)}, u32[]{:S(2)}) collective-permute-start(bf16[144,256]{1,0:T(8,128)(2,1)S(1)} %project.46.q_ref), channel_id=1, source_target_pairs={{0,1},{1,0},{2,3},{3,2},{4,5},{5,4},{6,7},{7,6},{8,9},{9,8},{10,11... | collective-permute-start | bytes 221192 | tf_op jit(solution)/shard_map/exchange/ppermute | solution.py:354
  95.8 8.6 %collective-permute-start.36 = (bf16[144,384]{1,0:T(8,128)(2,1)S(1)}, bf16[144,384]{1,0:T(8,128)(2,1)S(1)}, u32[]{:S(2)}, u32[]{:S(2)}) collective-permute-start(bf16[144,384]{1,0:T(8,128)(2,1)S(1)} %attend.78), channel_id=1, source_target_pairs={{0,3},{1,2},{2,1},{3,0},{4,7},{5,6},{6,5},{7,4},{8,11},{9,10},{10,... | collective-permute-start | bytes 331784 | tf_op jit(solution)/shard_map/attend/ppermute | solution.py:376
  97.4 7.6 %collective-permute-start.35 = (bf16[144,384]{1,0:T(8,128)(2,1)S(1)}, bf16[144,384]{1,0:T(8,128)(2,1)S(1)}, u32[]{:S(2)}, u32[]{:S(2)}) collective-permute-start(bf16[144,384]{1,0:T(8,128)(2,1)S(1)} %attend.77), channel_id=1, source_target_pairs={{0,2},{1,3},{2,0},{3,1},{4,6},{5,7},{6,4},{7,5},{8,10},{9,11},{10,... | collective-permute-start | bytes 331784 | tf_op jit(solution)/shard_map/attend/ppermute | solution.py:376
  99.1 11.1 %collective-permute-start.34 = (bf16[144,384]{1,0:T(8,128)(2,1)S(1)}, bf16[144,384]{1,0:T(8,128)(2,1)S(1)}, u32[]{:S(2)}, u32[]{:S(2)}) collective-permute-start(bf16[144,384]{1,0:T(8,128)(2,1)S(1)} %attend.76), channel_id=1, source_target_pairs={{0,1},{1,0},{2,3},{3,2},{4,5},{5,4},{6,7},{7,6},{8,9},{9,8},{10,11... | collective-permute-start | bytes 331784 | tf_op jit(solution)/shard_map/attend/ppermute | solution.py:376
  111.6 5.1 collective-permute-start.38
  111.7 6.0 %collective-permute-start.39 = (bf16[144,256]{1,0:T(8,128)(2,1)S(1)}, bf16[144,256]{1,0:T(8,128)(2,1)S(1)}, u32[]{:S(2)}, u32[]{:S(2)}) collective-permute-start(bf16[144,256]{1,0:T(8,128)(2,1)S(1)} %attend.79.a0), channel_id=1, source_target_pairs={{0,192},{32,224},{64,128},{96,160},{128,64},{160,96},{192,0},{224,... | collective-permute-start | bytes 221192 | tf_op jit(solution)/shard_map/attend/ppermute | solution.py:43
  117.8 6.5 %collective-permute-start.40 = (bf16[4,144,256]{2,1,0:T(8,128)(2,1)S(1)}, bf16[4,144,256]{2,1,0:T(8,128)(2,1)S(1)}, u32[]{:S(2)}, u32[]{:S(2)}) collective-permute-start(bf16[4,144,256]{2,1,0:T(8,128)(2,1)S(1)} %pad_maximum_fusion.6), channel_id=1, source_target_pairs={{0,32},{32,0},{64,96},{96,64},{128,160},{160,128},{192,224},{224,1... | collective-permute-start | bytes 884744 | tf_op jit(solution)/shard_map/attend/ppermute | solution.py:44
  141.0 5.5 collective-permute-start.42
  142.3 5.5 collective-permute-start.43
  152.7 19.8 %all-to-all-start = ((bf16[8,144,128]{2,1,0:T(8,128)(2,1)}), bf16[8,144,128]{2,1,0:T(8,128)(2,1)S(1)}, u32[]{:S(2)}, u32[]{:S(2)}) async-start(bf16[8,144,128]{2,1,0:T(8,128)(2,1)} %project.49), calls=%async_computation | async-start | bytes 589824 | tf_op jit(solution)/shard_map/while/body/eval_jaxpr/exchange/all_to_all | solution.py:358
  159.3 4.9 collective-permute-start
  160.2 5.3 collective-permute-start.1
  161.0 5.1 collective-permute-start.2
  174.1 8.1 %collective-permute-start.4 = (bf16[144,384]{1,0:T(8,128)(2,1)S(1)}, bf16[144,384]{1,0:T(8,128)(2,1)S(1)}, u32[]{:S(2)}, u32[]{:S(2)}) collective-permute-start(bf16[144,384]{1,0:T(8,128)(2,1)S(1)} %attend.82), channel_id=1, source_target_pairs={{0,2},{1,3},{2,0},{3,1},{4,6},{5,7},{6,4},{7,5},{8,10},{9,11},{10,... | collective-permute-start | bytes 331784 | tf_op jit(solution)/shard_map/while/body/eval_jaxpr/attend/ppermute | solution.py:376
  175.7 6.5 %collective-permute-start.3 = (bf16[144,384]{1,0:T(8,128)(2,1)S(1)}, bf16[144,384]{1,0:T(8,128)(2,1)S(1)}, u32[]{:S(2)}, u32[]{:S(2)}) collective-permute-start(bf16[144,384]{1,0:T(8,128)(2,1)S(1)} %attend.81), channel_id=1, source_target_pairs={{0,1},{1,0},{2,3},{3,2},{4,5},{5,4},{6,7},{7,6},{8,9},{9,8},{10,11... | collective-permute-start | bytes 331784 | tf_op jit(solution)/shard_map/while/body/eval_jaxpr/attend/ppermute | solution.py:376
  177.4 5.4 collective-permute-start.5
  190.6 5.1 collective-permute-start.9
  196.6 4.9 collective-permute-start.12
  197.8 4.8 collective-permute-start.11
  208.1 19.3 %all-to-all-start = ((bf16[8,144,128]{2,1,0:T(8,128)(2,1)}), bf16[8,144,128]{2,1,0:T(8,128)(2,1)S(1)}, u32[]{:S(2)}, u32[]{:S(2)}) async-start(bf16[8,144,128]{2,1,0:T(8,128)(2,1)} %project.49), calls=%async_computation | async-start | bytes 589824 | tf_op jit(solution)/shard_map/while/body/eval_jaxpr/exchange/all_to_all | solution.py:358
  214.3 7.2 %collective-permute-start = (bf16[144,256]{1,0:T(8,128)(2,1)S(1)}, bf16[144,256]{1,0:T(8,128)(2,1)S(1)}, u32[]{:S(2)}, u32[]{:S(2)}) collective-permute-start(bf16[144,256]{1,0:T(8,128)(2,1)S(1)} %get-tuple-element.1049.q_ref), channel_id=1, source_target_pairs={{0,3},{1,2},{2,1},{3,0},{4,7},{5,6},{6,5},{7,4},{8,11},{9,10},{10,... | collective-permute-start | bytes 221192 | tf_op jit(solution)/shard_map/while/body/eval_jaxpr/exchange/ppermute | solution.py:354
  217.1 7.0 %collective-permute-start.1 = (bf16[144,256]{1,0:T(8,128)(2,1)S(1)}, bf16[144,256]{1,0:T(8,128)(2,1)S(1)}, u32[]{:S(2)}, u32[]{:S(2)}) collective-permute-start(bf16[144,256]{1,0:T(8,128)(2,1)S(1)} %get-tuple-element.1049.q_ref), channel_id=1, source_target_pairs={{0,2},{1,3},{2,0},{3,1},{4,6},{5,7},{6,4},{7,5},{8,10},{9,11},{10,... | collective-permute-start | bytes 221192 | tf_op jit(solution)/shard_map/while/body/eval_jaxpr/exchange/ppermute | solution.py:354
  217.1 7.9 %collective-permute-start.2 = (bf16[144,256]{1,0:T(8,128)(2,1)S(1)}, bf16[144,256]{1,0:T(8,128)(2,1)S(1)}, u32[]{:S(2)}, u32[]{:S(2)}) collective-permute-start(bf16[144,256]{1,0:T(8,128)(2,1)S(1)} %get-tuple-element.1049.q_ref), channel_id=1, source_target_pairs={{0,1},{1,0},{2,3},{3,2},{4,5},{5,4},{6,7},{7,6},{8,9},{9,8},{10,11... | collective-permute-start | bytes 221192 | tf_op jit(solution)/shard_map/while/body/eval_jaxpr/exchange/ppermute | solution.py:354
  229.0 8.4 %collective-permute-start.4 = (bf16[144,384]{1,0:T(8,128)(2,1)S(1)}, bf16[144,384]{1,0:T(8,128)(2,1)S(1)}, u32[]{:S(2)}, u32[]{:S(2)}) collective-permute-start(bf16[144,384]{1,0:T(8,128)(2,1)S(1)} %attend.82), channel_id=1, source_target_pairs={{0,2},{1,3},{2,0},{3,1},{4,6},{5,7},{6,4},{7,5},{8,10},{9,11},{10,... | collective-permute-start | bytes 331784 | tf_op jit(solution)/shard_map/while/body/eval_jaxpr/attend/ppermute | solution.py:376
  231.5 11.2 %collective-permute-start.3 = (bf16[144,384]{1,0:T(8,128)(2,1)S(1)}, bf16[144,384]{1,0:T(8,128)(2,1)S(1)}, u32[]{:S(2)}, u32[]{:S(2)}) collective-permute-start(bf16[144,384]{1,0:T(8,128)(2,1)S(1)} %attend.81), channel_id=1, source_target_pairs={{0,1},{1,0},{2,3},{3,2},{4,5},{5,4},{6,7},{7,6},{8,9},{9,8},{10,11... | collective-permute-start | bytes 331784 | tf_op jit(solution)/shard_map/while/body/eval_jaxpr/attend/ppermute | solution.py:376
  235.7 8.1 %collective-permute-start.5 = (bf16[144,384]{1,0:T(8,128)(2,1)S(1)}, bf16[144,384]{1,0:T(8,128)(2,1)S(1)}, u32[]{:S(2)}, u32[]{:S(2)}) collective-permute-start(bf16[144,384]{1,0:T(8,128)(2,1)S(1)} %attend.83), channel_id=1, source_target_pairs={{0,3},{1,2},{2,1},{3,0},{4,7},{5,6},{6,5},{7,4},{8,11},{9,10},{10,... | collective-permute-start | bytes 331784 | tf_op jit(solution)/shard_map/while/body/eval_jaxpr/attend/ppermute | solution.py:376
  251.2 5.1 collective-permute-start.9
  258.3 4.8 collective-permute-start.11
  268.6 16.7 %all-to-all-start = ((bf16[8,144,128]{2,1,0:T(8,128)(2,1)}), bf16[8,144,128]{2,1,0:T(8,128)(2,1)S(1)}, u32[]{:S(2)}, u32[]{:S(2)}) async-start(bf16[8,144,128]{2,1,0:T(8,128)(2,1)} %project.49), calls=%async_computation | async-start | bytes 589824 | tf_op jit(solution)/shard_map/while/body/eval_jaxpr/exchange/all_to_all | solution.py:358
  276.0 5.0 collective-permute-start.1
  276.2 5.6 %collective-permute-start.2 = (bf16[144,256]{1,0:T(8,128)(2,1)S(1)}, bf16[144,256]{1,0:T(8,128)(2,1)S(1)}, u32[]{:S(2)}, u32[]{:S(2)}) collective-permute-start(bf16[144,256]{1,0:T(8,128)(2,1)S(1)} %get-tuple-element.1049.q_ref), channel_id=1, source_target_pairs={{0,1},{1,0},{2,3},{3,2},{4,5},{5,4},{6,7},{7,6},{8,9},{9,8},{10,11... | collective-permute-start | bytes 221192 | tf_op jit(solution)/shard_map/while/body/eval_jaxpr/exchange/ppermute | solution.py:354
  286.9 8.1 %collective-permute-start.4 = (bf16[144,384]{1,0:T(8,128)(2,1)S(1)}, bf16[144,384]{1,0:T(8,128)(2,1)S(1)}, u32[]{:S(2)}, u32[]{:S(2)}) collective-permute-start(bf16[144,384]{1,0:T(8,128)(2,1)S(1)} %attend.82), channel_id=1, source_target_pairs={{0,2},{1,3},{2,0},{3,1},{4,6},{5,7},{6,4},{7,5},{8,10},{9,11},{10,... | collective-permute-start | bytes 331784 | tf_op jit(solution)/shard_map/while/body/eval_jaxpr/attend/ppermute | solution.py:376
  288.5 6.5 %collective-permute-start.3 = (bf16[144,384]{1,0:T(8,128)(2,1)S(1)}, bf16[144,384]{1,0:T(8,128)(2,1)S(1)}, u32[]{:S(2)}, u32[]{:S(2)}) collective-permute-start(bf16[144,384]{1,0:T(8,128)(2,1)S(1)} %attend.81), channel_id=1, source_target_pairs={{0,1},{1,0},{2,3},{3,2},{4,5},{5,4},{6,7},{7,6},{8,9},{9,8},{10,11... | collective-permute-start | bytes 331784 | tf_op jit(solution)/shard_map/while/body/eval_jaxpr/attend/ppermute | solution.py:376
  291.2 4.9 collective-permute-start.5
  303.4 5.6 %collective-permute-start.9 = (bf16[4,144,256]{2,1,0:T(8,128)(2,1)S(1)}, bf16[4,144,256]{2,1,0:T(8,128)(2,1)S(1)}, u32[]{:S(2)}, u32[]{:S(2)}) collective-permute-start(bf16[4,144,256]{2,1,0:T(8,128)(2,1)S(1)} %pad_maximum_fusion.13), channel_id=1, source_target_pairs={{0,32},{32,0},{64,96},{96,64},{128,160},{160,128},{192,224},{224,1... | collective-permute-start | bytes 884744 | tf_op jit(solution)/shard_map/while/body/eval_jaxpr/attend/ppermute | solution.py:44
  332.0 17.4 %all-to-all-start.1 = ((bf16[8,144,128]{2,1,0:T(8,128)(2,1)}), bf16[8,144,128]{2,1,0:T(8,128)(2,1)S(1)}, u32[]{:S(2)}, u32[]{:S(2)}) async-start(bf16[8,144,128]{2,1,0:T(8,128)(2,1)} %project.51), calls=%async_computation.1 | async-start | bytes 589824 | tf_op jit(solution)/shard_map/while/body/eval_jaxpr/exchange/all_to_all | solution.py:358
  340.7 5.0 collective-permute-start.15
  340.9 5.0 collective-permute-start.16
  351.0 7.5 %collective-permute-start.18 = (bf16[144,384]{1,0:T(8,128)(2,1)S(1)}, bf16[144,384]{1,0:T(8,128)(2,1)S(1)}, u32[]{:S(2)}, u32[]{:S(2)}) collective-permute-start(bf16[144,384]{1,0:T(8,128)(2,1)S(1)} %attend.87), channel_id=1, source_target_pairs={{0,2},{1,3},{2,0},{3,1},{4,6},{5,7},{6,4},{7,5},{8,10},{9,11},{10,... | collective-permute-start | bytes 331784 | tf_op jit(solution)/shard_map/while/body/eval_jaxpr/attend/ppermute | solution.py:376
  353.8 5.2 collective-permute-start.19
  367.2 5.3 collective-permute-start.23
  384.8 18.0 %all-to-all-start.1 = ((bf16[8,144,128]{2,1,0:T(8,128)(2,1)}), bf16[8,144,128]{2,1,0:T(8,128)(2,1)S(1)}, u32[]{:S(2)}, u32[]{:S(2)}) async-start(bf16[8,144,128]{2,1,0:T(8,128)(2,1)} %project.51), calls=%async_computation.1 | async-start | bytes 589824 | tf_op jit(solution)/shard_map/while/body/eval_jaxpr/exchange/all_to_all | solution.py:358
  394.1 5.0 collective-permute-start.15
  404.4 7.5 %collective-permute-start.18 = (bf16[144,384]{1,0:T(8,128)(2,1)S(1)}, bf16[144,384]{1,0:T(8,128)(2,1)S(1)}, u32[]{:S(2)}, u32[]{:S(2)}) collective-permute-start(bf16[144,384]{1,0:T(8,128)(2,1)S(1)} %attend.87), channel_id=1, source_target_pairs={{0,2},{1,3},{2,0},{3,1},{4,6},{5,7},{6,4},{7,5},{8,10},{9,11},{10,... | collective-permute-start | bytes 331784 | tf_op jit(solution)/shard_map/while/body/eval_jaxpr/attend/ppermute | solution.py:376
  406.6 6.1 %collective-permute-start.19 = (bf16[144,384]{1,0:T(8,128)(2,1)S(1)}, bf16[144,384]{1,0:T(8,128)(2,1)S(1)}, u32[]{:S(2)}, u32[]{:S(2)}) collective-permute-start(bf16[144,384]{1,0:T(8,128)(2,1)S(1)} %attend.88), channel_id=1, source_target_pairs={{0,3},{1,2},{2,1},{3,0},{4,7},{5,6},{6,5},{7,4},{8,11},{9,10},{10,... | collective-permute-start | bytes 331784 | tf_op jit(solution)/shard_map/while/body/eval_jaxpr/attend/ppermute | solution.py:376
  421.1 5.3 collective-permute-start.23
  438.7 17.5 %all-to-all-start.1 = ((bf16[8,144,128]{2,1,0:T(8,128)(2,1)}), bf16[8,144,128]{2,1,0:T(8,128)(2,1)S(1)}, u32[]{:S(2)}, u32[]{:S(2)}) async-start(bf16[8,144,128]{2,1,0:T(8,128)(2,1)} %project.51), calls=%async_computation.1 | async-start | bytes 589824 | tf_op jit(solution)/shard_map/while/body/eval_jaxpr/exchange/all_to_all | solution.py:358
  447.5 5.0 collective-permute-start.15
  457.8 7.5 %collective-permute-start.18 = (bf16[144,384]{1,0:T(8,128)(2,1)S(1)}, bf16[144,384]{1,0:T(8,128)(2,1)S(1)}, u32[]{:S(2)}, u32[]{:S(2)}) collective-permute-start(bf16[144,384]{1,0:T(8,128)(2,1)S(1)} %attend.87), channel_id=1, source_target_pairs={{0,2},{1,3},{2,0},{3,1},{4,6},{5,7},{6,4},{7,5},{8,10},{9,11},{10,... | collective-permute-start | bytes 331784 | tf_op jit(solution)/shard_map/while/body/eval_jaxpr/attend/ppermute | solution.py:376
  460.0 6.0 %collective-permute-start.19 = (bf16[144,384]{1,0:T(8,128)(2,1)S(1)}, bf16[144,384]{1,0:T(8,128)(2,1)S(1)}, u32[]{:S(2)}, u32[]{:S(2)}) collective-permute-start(bf16[144,384]{1,0:T(8,128)(2,1)S(1)} %attend.88), channel_id=1, source_target_pairs={{0,3},{1,2},{2,1},{3,0},{4,7},{5,6},{6,5},{7,4},{8,11},{9,10},{10,... | collective-permute-start | bytes 331784 | tf_op jit(solution)/shard_map/while/body/eval_jaxpr/attend/ppermute | solution.py:376
  474.5 5.3 collective-permute-start.23
  492.1 17.5 %all-to-all-start.1 = ((bf16[8,144,128]{2,1,0:T(8,128)(2,1)}), bf16[8,144,128]{2,1,0:T(8,128)(2,1)S(1)}, u32[]{:S(2)}, u32[]{:S(2)}) async-start(bf16[8,144,128]{2,1,0:T(8,128)(2,1)} %project.51), calls=%async_computation.1 | async-start | bytes 589824 | tf_op jit(solution)/shard_map/while/body/eval_jaxpr/exchange/all_to_all | solution.py:358
  500.9 5.0 collective-permute-start.15
  511.2 7.5 %collective-permute-start.18 = (bf16[144,384]{1,0:T(8,128)(2,1)S(1)}, bf16[144,384]{1,0:T(8,128)(2,1)S(1)}, u32[]{:S(2)}, u32[]{:S(2)}) collective-permute-start(bf16[144,384]{1,0:T(8,128)(2,1)S(1)} %attend.87), channel_id=1, source_target_pairs={{0,2},{1,3},{2,0},{3,1},{4,6},{5,7},{6,4},{7,5},{8,10},{9,11},{10,... | collective-permute-start | bytes 331784 | tf_op jit(solution)/shard_map/while/body/eval_jaxpr/attend/ppermute | solution.py:376
  513.4 6.0 %collective-permute-start.19 = (bf16[144,384]{1,0:T(8,128)(2,1)S(1)}, bf16[144,384]{1,0:T(8,128)(2,1)S(1)}, u32[]{:S(2)}, u32[]{:S(2)}) collective-permute-start(bf16[144,384]{1,0:T(8,128)(2,1)S(1)} %attend.88), channel_id=1, source_target_pairs={{0,3},{1,2},{2,1},{3,0},{4,7},{5,6},{6,5},{7,4},{8,11},{9,10},{10,... | collective-permute-start | bytes 331784 | tf_op jit(solution)/shard_map/while/body/eval_jaxpr/attend/ppermute | solution.py:376
  527.9 5.3 collective-permute-start.23
  (65 other events, 292.0 us)
Sparse Core Ops, SparseCore 0:
  28.2 109.7 all-gather.5
  140.6 115.9 all-gather.3

commit v9 on v8

--- a/solution.py
+++ b/solution.py
@@ -16,6 +16,7 @@
 NEG = -1e30
 LOG2E = 1.4426950408889634
 SHARD = 64
+SPLIT = 3
 Q_ROWS = QW // 128 * SHARD
 QKV_ROWS = Q_ROWS + SHARD
 ALL_ROWS = QKV_ROWS + Q_ROWS
@@ -315,9 +316,9 @@
     by_layer = by_layer[:, :ALL_ROWS]
 
     with jax.named_scope("weights"):
-        early = jnp.concatenate([by_layer[0, QKV_ROWS:], by_layer[1:4].reshape(-1, 128)])
+        early = jnp.concatenate([by_layer[0, QKV_ROWS:], by_layer[1:SPLIT].reshape(-1, 128)])
         early = lax.all_gather(early, "seq", axis=0)
-        late = lax.all_gather(by_layer[4:].reshape(-1, 128), "seq", axis=0)
+        late = lax.all_gather(by_layer[SPLIT:].reshape(-1, 128), "seq", axis=0)
 
         def over_z(part):
             part = jnp.broadcast_to(part[None], (ZN,) + part.shape)
@@ -438,10 +439,10 @@
 
         return body
 
-    pieces, out, wkv = lax.fori_loop(1, 4, step(early, Q_ROWS, 1), (pieces, out, wkv))
+    pieces, out, wkv = lax.fori_loop(1, SPLIT, step(early, Q_ROWS, 1), (pieces, out, wkv))
     late, pieces = lax.optimization_barrier((late, pieces))
     wkv = late[:, Q_ROWS:QKV_ROWS]
-    pieces, out, wkv = lax.fori_loop(4, layers, step(late, 0, 4), (pieces, out, wkv))
+    pieces, out, wkv = lax.fori_loop(SPLIT, layers, step(late, 0, SPLIT), (pieces, out, wkv))
     out = call(
         place_kernel,
         numbers(0, layers),

time: 557 us -> 552 us (level)
  waiting for transfers between devices: 180 us -> 169 us
    all_gather x1, waiting for transfers between devices: 13.7 us -> 2.76 us  [local(): early = lax.all_gather(early, 'seq', axis=0)]
    all_to_all x8, waiting for transfers between devices: 30.4 us -> 23.9 us  [exchange(): lax.all_to_all(kv, 'seq', split_axis=0, concat_axis=0, tiled=True, axis_i...]
  transfers between devices with their start and end apart: 125 -> 125, of which waited for: 106 -> 106; matrix products, arithmetic and copies ran while one was open for 0% -> 0% of each run, Pallas kernels for 14% -> 13%
where the time goes in v9:
time: 552 us; the launch traced here: 544 us
  starting transfers between devices  204 us (37%)
  waiting for transfers between devices  169 us (31%)
  Pallas kernels  100 us (18%)
  blocking collectives  38.8 us (7%)
  between operations  13.8 us (2%)
  loops' own time  9.99 us (2%)
  local copies, waits for them, and re-layouts  6.42 us (1%)
    pallas_call x65, Pallas kernels, call(): pl.pallas_call(kernel, out_shape=out_shape, in_specs=in_specs, out_specs=...  100 us
    ppermute x48, starting transfers between devices, spread(): lax.ppermute(piece, 'section', section_pairs(2 * d))  56.3 us
    ppermute x16, starting transfers between devices, spread(): other = lax.ppermute(jnp.stack(near), 'section', section_pairs(1))  53.6 us
    ppermute x48, waiting for transfers between devices, spread(): lax.ppermute(piece, 'section', section_pairs(2 * d))  50.7 us
    all_to_all x8, starting transfers between devices, exchange(): lax.all_to_all(kv, 'seq', split_axis=0, concat_axis=0, tiled=True, axis_i...  37.1 us
    ppermute x24, waiting for transfers between devices, exchange(): qs = [lax.ppermute(q, 'seq', seq_pairs(d)) for d in (3, 2, 1)]  31.2 us
    ppermute x24, starting transfers between devices, exchange(): qs = [lax.ppermute(q, 'seq', seq_pairs(d)) for d in (3, 2, 1)]  27.2 us
    ppermute x24, starting transfers between devices, attend(): parts[d] = lax.ppermute(part, 'seq', seq_pairs(d)) if d else part  25.4 us
  transfers between devices with their start and end apart: 125, of which 106 were waited for; matrix products, arithmetic and copies ran while one was open for 0% of the time, Pallas kernels for 13%

profile of v9, /device:TPU:1, one launch (start us, length us, event | category | flops | bytes accessed | tf_op | source)
XLA Modules:
  0.0 544.3 jit_solution(14047048383681910053)
XLA Ops:
  10.3 17.0 %all_to_all.27 = bf16[8,336,128]{2,1,0:T(8,128)(2,1)S(1)} all-to-all(bf16[8,336,128]{2,1,0:T(8,128)(2,1)S(1)} %pad_maximum_fusion.4), channel_id=1, replica_groups=mesh['section'=8,'seq'=32] {'section'}, dimensions={0} | all-to-all | bytes 1376256 | tf_op jit(solution)/shard_map/all_to_all | solution.py:314
  29.0 21.8 %all_to_all.28.w0 = bf16[8,192,128]{2,1,0:T(8,128)(2,1)S(1)} all-to-all(bf16[8,192,128]{2,1,0:T(8,128)(2,1)S(1)} %broadcast_in_dim.20), channel_id=1, replica_groups={{0,4,8,12,16,20,24,28},{1,5,9,13,17,21,25,29},{2,6,10,14,18,22,26,30},{..., dimensions={0} | all-to-all | bytes 786432 | tf_op jit(solution)/shard_map/weights/all_to_all | solution.py:325
  52.0 2.5 collective-permute-start.29
  54.9 5.1 collective-permute-done.28.w1
  60.0 10.5 %collective-permute-done.29.w2 = bf16[8,192,128]{2,1,0:T(8,128)(2,1)S(1)} collective-permute-done((bf16[8,192,128]{2,1,0:T(8,128)(2,1)S(1)}, bf16[8,192,128]{2,1,0:T(8,128)(2,1)S(1)}, u32[]{:S(2)}, u32[]{:S(2)}) %collective-permute-start.29) | collective-permute-done | bytes 393248 | tf_op jit(solution)/shard_map/weights/ppermute | solution.py:330
  72.2 4.9 all-to-all-start.4
  78.2 2.0 collective-permute-start.31
  82.8 3.5 collective-permute-done.32.q_ref
  89.0 2.3 collective-permute-start.36
  97.1 3.3 collective-permute-done.35.o2
  100.4 1.9 collective-permute-done.34.o1
  103.5 3.1 collective-permute-start.37
  106.6 2.5 collective-permute-start.39
  109.1 2.3 collective-permute-done.38.a2
  112.2 8.4 %collective-permute-start.40 = (bf16[4,144,256]{2,1,0:T(8,128)(2,1)S(1)}, bf16[4,144,256]{2,1,0:T(8,128)(2,1)S(1)}, u32[]{:S(2)}, u32[]{:S(2)}) collective-permute-start(bf16[4,144,256]{2,1,0:T(8,128)(2,1)S(1)} %pad_maximum_fusion.6), channel_id=1, source_target_pairs={{0,32},{32,0},{64,96},{96,64},{128,160},{160,128},{192,224},{224,1... | collective-permute-start | bytes 884744 | tf_op jit(solution)/shard_map/attend/ppermute | solution.py:45
  121.9 2.8 all-gather.6.cloned.1.call-done
  124.6 2.1 output.23
  130.7 2.2 collective-permute-done.42
  132.9 2.0 collective-permute-done.43
  134.9 2.1 collective-permute-start.44
  138.3 115.2 %while.58 = (s32[]{:T(128)}, bf16[144,256]{1,0:T(8,128)(2,1)S(1)}, bf16[144,256]{1,0:T(8,128)(2,1)S(1)}, bf16[144,256]{1,0:T(8,128)(2,1)S(1)}, bf16[144,256]{1,0...) while((s32[]{:T(128)}, bf16[144,256]{1,0:T(8,128)(2,1)S(1)}, ...), condition=%wide.region_1.0_spmd, body=%wide.region_0.0_spmd.sunk | while | flops 1284710400 | bytes 15377181 | solution.py:442
  140.2 4.0 all-to-all-start
  144.1 2.5 project.48
  150.0 2.7 collective-permute-done.q_ref
  153.4 6.2 %all-to-all-done.k_ref = bf16[8,144,128]{2,1,0:T(8,128)(2,1)S(1)} async-done(((bf16[8,144,128]{2,1,0:T(8,128)(2,1)}), bf16[8,144,128]{2,1,0:T(8,128)(2,1)S(1)}, u32[]{:S(2)}, u32[]{:S(2)}) %all-to-all-start) | async-done | bytes 294944 | tf_op jit(solution)/shard_map/while/body/eval_jaxpr/exchange/all_to_all | solution.py:359
  164.8 3.0 collective-permute-start.5
  177.7 3.9 collective-permute-start.9
  195.2 3.4 all-to-all-start
  198.6 2.6 project.48
  201.2 3.2 collective-permute-start
  205.1 3.7 collective-permute-done.q_ref
  208.8 2.6 collective-permute-done.1.q_ref
  218.3 2.6 collective-permute-start.3
  224.2 5.5 %collective-permute-done.3.o1 = bf16[144,384]{1,0:T(8,128)(2,1)S(1)} collective-permute-done((bf16[144,384]{1,0:T(8,128)(2,1)S(1)}, bf16[144,384]{1,0:T(8,128)(2,1)S(1)}, u32[]{:S(2)}, u32[]{:S(2)}) %collective-permute-start.3) | collective-permute-done | bytes 110624 | tf_op jit(solution)/shard_map/while/body/eval_jaxpr/attend/ppermute | solution.py:377
  238.1 3.4 collective-permute-start.9
  248.1 1.9 collective-permute-done.11
  253.6 4.1 all-gather.4.cloned.1.call-done
  258.8 277.1 %while.59 = (s32[]{:T(128)}, bf16[144,256]{1,0:T(8,128)(2,1)S(1)}, bf16[144,256]{1,0:T(8,128)(2,1)S(1)}, bf16[144,256]{1,0:T(8,128)(2,1)S(1)}, bf16[144,256]{1,0...) while((s32[]{:T(128)}, bf16[144,256]{1,0:T(8,128)(2,1)S(1)}, ...), condition=%wide.region_3.0_spmd, body=%wide.region_2.0_spmd.sunk | while | flops 1284710400 | bytes 15377173 | solution.py:445
  270.2 3.9 all-to-all-start.1
  274.1 2.5 project.50
  282.8 2.0 all-to-all-done.1.k_ref
  296.8 2.5 collective-permute-start.22
  301.3 2.8 collective-permute-done.21.a2
  304.1 6.1 %collective-permute-start.23 = (bf16[4,144,256]{2,1,0:T(8,128)(2,1)S(1)}, bf16[4,144,256]{2,1,0:T(8,128)(2,1)S(1)}, u32[]{:S(2)}, u32[]{:S(2)}) collective-permute-start(bf16[4,144,256]{2,1,0:T(8,128)(2,1)S(1)} %pad_maximum_fusion.15), channel_id=1, source_target_pairs={{0,32},{32,0},{64,96},{96,64},{128,160},{160,128},{192,224},{224,1... | collective-permute-start | bytes 884744 | tf_op jit(solution)/shard_map/while/body/eval_jaxpr/attend/ppermute | solution.py:45
  323.7 5.5 %all-to-all-start.1 = ((bf16[8,144,128]{2,1,0:T(8,128)(2,1)}), bf16[8,144,128]{2,1,0:T(8,128)(2,1)S(1)}, u32[]{:S(2)}, u32[]{:S(2)}) async-start(bf16[8,144,128]{2,1,0:T(8,128)(2,1)} %project.51), calls=%async_computation.1 | async-start | bytes 589824 | tf_op jit(solution)/shard_map/while/body/eval_jaxpr/exchange/all_to_all | solution.py:359
  329.2 2.5 project.50
  338.0 3.6 all-to-all-done.1.k_ref
  359.9 4.1 collective-permute-start.23
  372.4 2.1 collective-permute-start.27
  377.5 5.1 all-to-all-start.1
  382.6 2.5 project.50
  391.4 3.6 all-to-all-done.1.k_ref
  413.3 4.1 collective-permute-start.23
  425.8 2.1 collective-permute-start.27
  430.9 5.1 all-to-all-start.1
  436.0 2.5 project.50
  444.8 3.6 all-to-all-done.1.k_ref
  466.7 4.1 collective-permute-start.23
  479.2 2.1 collective-permute-start.27
  484.3 5.1 all-to-all-start.1
  489.4 2.5 project.50
  498.2 3.6 all-to-all-done.1.k_ref
  520.1 4.1 collective-permute-start.23
  532.6 2.1 collective-permute-start.27
  (322 shorter events, 273.3 us)
Async XLA Ops:
  6.5 118.1 %all-gather.6.cloned.1.call-start = ((), (), s32[]{:S(2)}) async-start(), calls=%async_computation.6 | async-start | bytes 6488064 | tf_op jit(solution)/shard_map/weights/all_gather | solution.py:320
  28.1 229.6 %all-gather.4.cloned.1.call-start = ((), (), s32[]{:S(2)}) async-start(), calls=%async_computation.5 | async-start | bytes 13516800 | tf_op jit(solution)/shard_map/weights/all_gather | solution.py:321
  50.8 9.2 %collective-permute-start.28 = (bf16[8,192,128]{2,1,0:T(8,128)(2,1)S(1)}, bf16[8,192,128]{2,1,0:T(8,128)(2,1)S(1)}, u32[]{:S(2)}, u32[]{:S(2)}) collective-permute-start(bf16[8,192,128]{2,1,0:T(8,128)(2,1)S(1)} %all_to_all.28.w0), channel_id=1, source_target_pairs={{0,1},{1,0},{2,3},{3,2},{4,5},{5,4},{6,7},{7,6},{8,9},{9,8},{10,11... | collective-permute-start | bytes 1179656 | tf_op jit(solution)/shard_map/weights/ppermute | solution.py:330
  52.0 18.4 %collective-permute-start.29 = (bf16[8,192,128]{2,1,0:T(8,128)(2,1)S(1)}, bf16[8,192,128]{2,1,0:T(8,128)(2,1)S(1)}, u32[]{:S(2)}, u32[]{:S(2)}) collective-permute-start(bf16[8,192,128]{2,1,0:T(8,128)(2,1)S(1)} %all_to_all.28.w0), channel_id=1, source_target_pairs={{0,2},{1,3},{2,0},{3,1},{4,6},{5,7},{6,4},{7,5},{8,10},{9,11},{10,... | collective-permute-start | bytes 1179656 | tf_op jit(solution)/shard_map/weights/ppermute | solution.py:330
  54.5 16.0 %collective-permute-start.30 = (bf16[8,192,128]{2,1,0:T(8,128)(2,1)S(1)}, bf16[8,192,128]{2,1,0:T(8,128)(2,1)S(1)}, u32[]{:S(2)}, u32[]{:S(2)}) collective-permute-start(bf16[8,192,128]{2,1,0:T(8,128)(2,1)S(1)} %all_to_all.28.w0), channel_id=1, source_target_pairs={{0,3},{1,2},{2,1},{3,0},{4,7},{5,6},{6,5},{7,4},{8,11},{9,10},{10,... | collective-permute-start | bytes 1179656 | tf_op jit(solution)/shard_map/weights/ppermute | solution.py:330
  72.2 15.3 %all-to-all-start.4 = ((bf16[8,144,128]{2,1,0:T(8,128)(2,1)}), bf16[8,144,128]{2,1,0:T(8,128)(2,1)S(1)}, u32[]{:S(2)}, u32[]{:S(2)}) async-start(bf16[8,144,128]{2,1,0:T(8,128)(2,1)} %project.47), calls=%async_computation.4 | async-start | bytes 589824 | tf_op jit(solution)/shard_map/exchange/all_to_all | solution.py:359
  80.2 6.1 %collective-permute-start.32 = (bf16[144,256]{1,0:T(8,128)(2,1)S(1)}, bf16[144,256]{1,0:T(8,128)(2,1)S(1)}, u32[]{:S(2)}, u32[]{:S(2)}) collective-permute-start(bf16[144,256]{1,0:T(8,128)(2,1)S(1)} %project.46.q_ref), channel_id=1, source_target_pairs={{0,2},{1,3},{2,0},{3,1},{4,6},{5,7},{6,4},{7,5},{8,10},{9,11},{10,... | collective-permute-start | bytes 221192 | tf_op jit(solution)/shard_map/exchange/ppermute | solution.py:355
  80.2 7.1 %collective-permute-start.33 = (bf16[144,256]{1,0:T(8,128)(2,1)S(1)}, bf16[144,256]{1,0:T(8,128)(2,1)S(1)}, u32[]{:S(2)}, u32[]{:S(2)}) collective-permute-start(bf16[144,256]{1,0:T(8,128)(2,1)S(1)} %project.46.q_ref), channel_id=1, source_target_pairs={{0,1},{1,0},{2,3},{3,2},{4,5},{5,4},{6,7},{7,6},{8,9},{9,8},{10,11... | collective-permute-start | bytes 221192 | tf_op jit(solution)/shard_map/exchange/ppermute | solution.py:355
  89.0 8.1 %collective-permute-start.36 = (bf16[144,384]{1,0:T(8,128)(2,1)S(1)}, bf16[144,384]{1,0:T(8,128)(2,1)S(1)}, u32[]{:S(2)}, u32[]{:S(2)}) collective-permute-start(bf16[144,384]{1,0:T(8,128)(2,1)S(1)} %attend.78), channel_id=1, source_target_pairs={{0,3},{1,2},{2,1},{3,0},{4,7},{5,6},{6,5},{7,4},{8,11},{9,10},{10,... | collective-permute-start | bytes 331784 | tf_op jit(solution)/shard_map/attend/ppermute | solution.py:377
  92.9 7.6 %collective-permute-start.35 = (bf16[144,384]{1,0:T(8,128)(2,1)S(1)}, bf16[144,384]{1,0:T(8,128)(2,1)S(1)}, u32[]{:S(2)}, u32[]{:S(2)}) collective-permute-start(bf16[144,384]{1,0:T(8,128)(2,1)S(1)} %attend.77), channel_id=1, source_target_pairs={{0,2},{1,3},{2,0},{3,1},{4,6},{5,7},{6,4},{7,5},{8,10},{9,11},{10,... | collective-permute-start | bytes 331784 | tf_op jit(solution)/shard_map/attend/ppermute | solution.py:377
  94.5 7.8 %collective-permute-start.34 = (bf16[144,384]{1,0:T(8,128)(2,1)S(1)}, bf16[144,384]{1,0:T(8,128)(2,1)S(1)}, u32[]{:S(2)}, u32[]{:S(2)}) collective-permute-start(bf16[144,384]{1,0:T(8,128)(2,1)S(1)} %attend.76), channel_id=1, source_target_pairs={{0,1},{1,0},{2,3},{3,2},{4,5},{5,4},{6,7},{7,6},{8,9},{9,8},{10,11... | collective-permute-start | bytes 331784 | tf_op jit(solution)/shard_map/attend/ppermute | solution.py:377
  103.5 5.6 %collective-permute-start.37 = (bf16[144,256]{1,0:T(8,128)(2,1)S(1)}, bf16[144,256]{1,0:T(8,128)(2,1)S(1)}, u32[]{:S(2)}, u32[]{:S(2)}) collective-permute-start(bf16[144,256]{1,0:T(8,128)(2,1)S(1)} %attend.79.a0), channel_id=1, source_target_pairs={{0,64},{32,96},{64,0},{96,32},{128,192},{160,224},{192,128},{224,1... | collective-permute-start | bytes 221192 | tf_op jit(solution)/shard_map/attend/ppermute | solution.py:44
  106.6 4.8 collective-permute-start.38
  106.6 5.6 %collective-permute-start.39 = (bf16[144,256]{1,0:T(8,128)(2,1)S(1)}, bf16[144,256]{1,0:T(8,128)(2,1)S(1)}, u32[]{:S(2)}, u32[]{:S(2)}) collective-permute-start(bf16[144,256]{1,0:T(8,128)(2,1)S(1)} %attend.79.a0), channel_id=1, source_target_pairs={{0,192},{32,224},{64,128},{96,160},{128,64},{160,96},{192,0},{224,... | collective-permute-start | bytes 221192 | tf_op jit(solution)/shard_map/attend/ppermute | solution.py:44
  112.2 9.6 %collective-permute-start.40 = (bf16[4,144,256]{2,1,0:T(8,128)(2,1)S(1)}, bf16[4,144,256]{2,1,0:T(8,128)(2,1)S(1)}, u32[]{:S(2)}, u32[]{:S(2)}) collective-permute-start(bf16[4,144,256]{2,1,0:T(8,128)(2,1)S(1)} %pad_maximum_fusion.6), channel_id=1, source_target_pairs={{0,32},{32,0},{64,96},{96,64},{128,160},{160,128},{192,224},{224,1... | collective-permute-start | bytes 884744 | tf_op jit(solution)/shard_map/attend/ppermute | solution.py:45
  127.8 5.1 collective-permute-start.42
  129.7 5.2 collective-permute-start.43
  140.2 19.5 %all-to-all-start = ((bf16[8,144,128]{2,1,0:T(8,128)(2,1)}), bf16[8,144,128]{2,1,0:T(8,128)(2,1)S(1)}, u32[]{:S(2)}, u32[]{:S(2)}) async-start(bf16[8,144,128]{2,1,0:T(8,128)(2,1)} %project.49), calls=%async_computation | async-start | bytes 589824 | tf_op jit(solution)/shard_map/while/body/eval_jaxpr/exchange/all_to_all | solution.py:359
  146.7 6.1 %collective-permute-start = (bf16[144,256]{1,0:T(8,128)(2,1)S(1)}, bf16[144,256]{1,0:T(8,128)(2,1)S(1)}, u32[]{:S(2)}, u32[]{:S(2)}) collective-permute-start(bf16[144,256]{1,0:T(8,128)(2,1)S(1)} %get-tuple-element.1049.q_ref), channel_id=1, source_target_pairs={{0,3},{1,2},{2,1},{3,0},{4,7},{5,6},{6,5},{7,4},{8,11},{9,10},{10,... | collective-permute-start | bytes 221192 | tf_op jit(solution)/shard_map/while/body/eval_jaxpr/exchange/ppermute | solution.py:355
  147.3 5.4 collective-permute-start.1
  148.5 4.9 collective-permute-start.2
  161.2 8.2 %collective-permute-start.4 = (bf16[144,384]{1,0:T(8,128)(2,1)S(1)}, bf16[144,384]{1,0:T(8,128)(2,1)S(1)}, u32[]{:S(2)}, u32[]{:S(2)}) collective-permute-start(bf16[144,384]{1,0:T(8,128)(2,1)S(1)} %attend.82), channel_id=1, source_target_pairs={{0,2},{1,3},{2,0},{3,1},{4,6},{5,7},{6,4},{7,5},{8,10},{9,11},{10,... | collective-permute-start | bytes 331784 | tf_op jit(solution)/shard_map/while/body/eval_jaxpr/attend/ppermute | solution.py:377
  163.1 6.2 %collective-permute-start.3 = (bf16[144,384]{1,0:T(8,128)(2,1)S(1)}, bf16[144,384]{1,0:T(8,128)(2,1)S(1)}, u32[]{:S(2)}, u32[]{:S(2)}) collective-permute-start(bf16[144,384]{1,0:T(8,128)(2,1)S(1)} %attend.81), channel_id=1, source_target_pairs={{0,1},{1,0},{2,3},{3,2},{4,5},{5,4},{6,7},{7,6},{8,9},{9,8},{10,11... | collective-permute-start | bytes 331784 | tf_op jit(solution)/shard_map/while/body/eval_jaxpr/attend/ppermute | solution.py:377
  164.8 5.8 %collective-permute-start.5 = (bf16[144,384]{1,0:T(8,128)(2,1)S(1)}, bf16[144,384]{1,0:T(8,128)(2,1)S(1)}, u32[]{:S(2)}, u32[]{:S(2)}) collective-permute-start(bf16[144,384]{1,0:T(8,128)(2,1)S(1)} %attend.83), channel_id=1, source_target_pairs={{0,3},{1,2},{2,1},{3,0},{4,7},{5,6},{6,5},{7,4},{8,11},{9,10},{10,... | collective-permute-start | bytes 331784 | tf_op jit(solution)/shard_map/while/body/eval_jaxpr/attend/ppermute | solution.py:377
  177.7 5.1 collective-permute-start.9
  183.7 4.9 collective-permute-start.12
  185.0 4.8 collective-permute-start.11
  195.2 18.5 %all-to-all-start = ((bf16[8,144,128]{2,1,0:T(8,128)(2,1)}), bf16[8,144,128]{2,1,0:T(8,128)(2,1)S(1)}, u32[]{:S(2)}, u32[]{:S(2)}) async-start(bf16[8,144,128]{2,1,0:T(8,128)(2,1)} %project.49), calls=%async_computation | async-start | bytes 589824 | tf_op jit(solution)/shard_map/while/body/eval_jaxpr/exchange/all_to_all | solution.py:359
  201.2 7.6 %collective-permute-start = (bf16[144,256]{1,0:T(8,128)(2,1)S(1)}, bf16[144,256]{1,0:T(8,128)(2,1)S(1)}, u32[]{:S(2)}, u32[]{:S(2)}) collective-permute-start(bf16[144,256]{1,0:T(8,128)(2,1)S(1)} %get-tuple-element.1049.q_ref), channel_id=1, source_target_pairs={{0,3},{1,2},{2,1},{3,0},{4,7},{5,6},{6,5},{7,4},{8,11},{9,10},{10,... | collective-permute-start | bytes 221192 | tf_op jit(solution)/shard_map/while/body/eval_jaxpr/exchange/ppermute | solution.py:355
  204.4 7.0 %collective-permute-start.1 = (bf16[144,256]{1,0:T(8,128)(2,1)S(1)}, bf16[144,256]{1,0:T(8,128)(2,1)S(1)}, u32[]{:S(2)}, u32[]{:S(2)}) collective-permute-start(bf16[144,256]{1,0:T(8,128)(2,1)S(1)} %get-tuple-element.1049.q_ref), channel_id=1, source_target_pairs={{0,2},{1,3},{2,0},{3,1},{4,6},{5,7},{6,4},{7,5},{8,10},{9,11},{10,... | collective-permute-start | bytes 221192 | tf_op jit(solution)/shard_map/while/body/eval_jaxpr/exchange/ppermute | solution.py:355
  204.4 8.1 %collective-permute-start.2 = (bf16[144,256]{1,0:T(8,128)(2,1)S(1)}, bf16[144,256]{1,0:T(8,128)(2,1)S(1)}, u32[]{:S(2)}, u32[]{:S(2)}) collective-permute-start(bf16[144,256]{1,0:T(8,128)(2,1)S(1)} %get-tuple-element.1049.q_ref), channel_id=1, source_target_pairs={{0,1},{1,0},{2,3},{3,2},{4,5},{5,4},{6,7},{7,6},{8,9},{9,8},{10,11... | collective-permute-start | bytes 221192 | tf_op jit(solution)/shard_map/while/body/eval_jaxpr/exchange/ppermute | solution.py:355
  215.2 9.0 %collective-permute-start.4 = (bf16[144,384]{1,0:T(8,128)(2,1)S(1)}, bf16[144,384]{1,0:T(8,128)(2,1)S(1)}, u32[]{:S(2)}, u32[]{:S(2)}) collective-permute-start(bf16[144,384]{1,0:T(8,128)(2,1)S(1)} %attend.82), channel_id=1, source_target_pairs={{0,2},{1,3},{2,0},{3,1},{4,6},{5,7},{6,4},{7,5},{8,10},{9,11},{10,... | collective-permute-start | bytes 331784 | tf_op jit(solution)/shard_map/while/body/eval_jaxpr/attend/ppermute | solution.py:377
  218.3 11.3 %collective-permute-start.3 = (bf16[144,384]{1,0:T(8,128)(2,1)S(1)}, bf16[144,384]{1,0:T(8,128)(2,1)S(1)}, u32[]{:S(2)}, u32[]{:S(2)}) collective-permute-start(bf16[144,384]{1,0:T(8,128)(2,1)S(1)} %attend.81), channel_id=1, source_target_pairs={{0,1},{1,0},{2,3},{3,2},{4,5},{5,4},{6,7},{7,6},{8,9},{9,8},{10,11... | collective-permute-start | bytes 331784 | tf_op jit(solution)/shard_map/while/body/eval_jaxpr/attend/ppermute | solution.py:377
  222.5 8.1 %collective-permute-start.5 = (bf16[144,384]{1,0:T(8,128)(2,1)S(1)}, bf16[144,384]{1,0:T(8,128)(2,1)S(1)}, u32[]{:S(2)}, u32[]{:S(2)}) collective-permute-start(bf16[144,384]{1,0:T(8,128)(2,1)S(1)} %attend.83), channel_id=1, source_target_pairs={{0,3},{1,2},{2,1},{3,0},{4,7},{5,6},{6,5},{7,4},{8,11},{9,10},{10,... | collective-permute-start | bytes 331784 | tf_op jit(solution)/shard_map/while/body/eval_jaxpr/attend/ppermute | solution.py:377
  231.8 4.9 collective-permute-start.8
  270.2 14.6 %all-to-all-start.1 = ((bf16[8,144,128]{2,1,0:T(8,128)(2,1)}), bf16[8,144,128]{2,1,0:T(8,128)(2,1)S(1)}, u32[]{:S(2)}, u32[]{:S(2)}) async-start(bf16[8,144,128]{2,1,0:T(8,128)(2,1)} %project.51), calls=%async_computation.1 | async-start | bytes 589824 | tf_op jit(solution)/shard_map/while/body/eval_jaxpr/exchange/all_to_all | solution.py:359
  277.3 5.0 collective-permute-start.15
  286.4 7.5 %collective-permute-start.18 = (bf16[144,384]{1,0:T(8,128)(2,1)S(1)}, bf16[144,384]{1,0:T(8,128)(2,1)S(1)}, u32[]{:S(2)}, u32[]{:S(2)}) collective-permute-start(bf16[144,384]{1,0:T(8,128)(2,1)S(1)} %attend.87), channel_id=1, source_target_pairs={{0,2},{1,3},{2,0},{3,1},{4,6},{5,7},{6,4},{7,5},{8,10},{9,11},{10,... | collective-permute-start | bytes 331784 | tf_op jit(solution)/shard_map/while/body/eval_jaxpr/attend/ppermute | solution.py:377
  289.2 6.1 %collective-permute-start.19 = (bf16[144,384]{1,0:T(8,128)(2,1)S(1)}, bf16[144,384]{1,0:T(8,128)(2,1)S(1)}, u32[]{:S(2)}, u32[]{:S(2)}) collective-permute-start(bf16[144,384]{1,0:T(8,128)(2,1)S(1)} %attend.88), channel_id=1, source_target_pairs={{0,3},{1,2},{2,1},{3,0},{4,7},{5,6},{6,5},{7,4},{8,11},{9,10},{10,... | collective-permute-start | bytes 331784 | tf_op jit(solution)/shard_map/while/body/eval_jaxpr/attend/ppermute | solution.py:377
  304.1 7.3 %collective-permute-start.23 = (bf16[4,144,256]{2,1,0:T(8,128)(2,1)S(1)}, bf16[4,144,256]{2,1,0:T(8,128)(2,1)S(1)}, u32[]{:S(2)}, u32[]{:S(2)}) collective-permute-start(bf16[4,144,256]{2,1,0:T(8,128)(2,1)S(1)} %pad_maximum_fusion.15), channel_id=1, source_target_pairs={{0,32},{32,0},{64,96},{96,64},{128,160},{160,128},{192,224},{224,1... | collective-permute-start | bytes 884744 | tf_op jit(solution)/shard_map/while/body/eval_jaxpr/attend/ppermute | solution.py:45
  313.4 4.8 collective-permute-start.25
  323.7 17.9 %all-to-all-start.1 = ((bf16[8,144,128]{2,1,0:T(8,128)(2,1)}), bf16[8,144,128]{2,1,0:T(8,128)(2,1)S(1)}, u32[]{:S(2)}, u32[]{:S(2)}) async-start(bf16[8,144,128]{2,1,0:T(8,128)(2,1)} %project.51), calls=%async_computation.1 | async-start | bytes 589824 | tf_op jit(solution)/shard_map/while/body/eval_jaxpr/exchange/all_to_all | solution.py:359
  331.7 4.8 collective-permute-start.14
  332.4 5.0 collective-permute-start.15
  343.2 7.5 %collective-permute-start.18 = (bf16[144,384]{1,0:T(8,128)(2,1)S(1)}, bf16[144,384]{1,0:T(8,128)(2,1)S(1)}, u32[]{:S(2)}, u32[]{:S(2)}) collective-permute-start(bf16[144,384]{1,0:T(8,128)(2,1)S(1)} %attend.87), channel_id=1, source_target_pairs={{0,2},{1,3},{2,0},{3,1},{4,6},{5,7},{6,4},{7,5},{8,10},{9,11},{10,... | collective-permute-start | bytes 331784 | tf_op jit(solution)/shard_map/while/body/eval_jaxpr/attend/ppermute | solution.py:377
  345.4 6.0 %collective-permute-start.19 = (bf16[144,384]{1,0:T(8,128)(2,1)S(1)}, bf16[144,384]{1,0:T(8,128)(2,1)S(1)}, u32[]{:S(2)}, u32[]{:S(2)}) collective-permute-start(bf16[144,384]{1,0:T(8,128)(2,1)S(1)} %attend.88), channel_id=1, source_target_pairs={{0,3},{1,2},{2,1},{3,0},{4,7},{5,6},{6,5},{7,4},{8,11},{9,10},{10,... | collective-permute-start | bytes 331784 | tf_op jit(solution)/shard_map/while/body/eval_jaxpr/attend/ppermute | solution.py:377
  359.9 5.3 collective-permute-start.23
  367.4 4.8 collective-permute-start.25
  377.5 17.5 %all-to-all-start.1 = ((bf16[8,144,128]{2,1,0:T(8,128)(2,1)}), bf16[8,144,128]{2,1,0:T(8,128)(2,1)S(1)}, u32[]{:S(2)}, u32[]{:S(2)}) async-start(bf16[8,144,128]{2,1,0:T(8,128)(2,1)} %project.51), calls=%async_computation.1 | async-start | bytes 589824 | tf_op jit(solution)/shard_map/while/body/eval_jaxpr/exchange/all_to_all | solution.py:359
  385.8 5.0 collective-permute-start.15
  396.6 7.5 %collective-permute-start.18 = (bf16[144,384]{1,0:T(8,128)(2,1)S(1)}, bf16[144,384]{1,0:T(8,128)(2,1)S(1)}, u32[]{:S(2)}, u32[]{:S(2)}) collective-permute-start(bf16[144,384]{1,0:T(8,128)(2,1)S(1)} %attend.87), channel_id=1, source_target_pairs={{0,2},{1,3},{2,0},{3,1},{4,6},{5,7},{6,4},{7,5},{8,10},{9,11},{10,... | collective-permute-start | bytes 331784 | tf_op jit(solution)/shard_map/while/body/eval_jaxpr/attend/ppermute | solution.py:377
  398.8 6.0 %collective-permute-start.19 = (bf16[144,384]{1,0:T(8,128)(2,1)S(1)}, bf16[144,384]{1,0:T(8,128)(2,1)S(1)}, u32[]{:S(2)}, u32[]{:S(2)}) collective-permute-start(bf16[144,384]{1,0:T(8,128)(2,1)S(1)} %attend.88), channel_id=1, source_target_pairs={{0,3},{1,2},{2,1},{3,0},{4,7},{5,6},{6,5},{7,4},{8,11},{9,10},{10,... | collective-permute-start | bytes 331784 | tf_op jit(solution)/shard_map/while/body/eval_jaxpr/attend/ppermute | solution.py:377
  413.3 5.3 collective-permute-start.23
  430.9 17.5 %all-to-all-start.1 = ((bf16[8,144,128]{2,1,0:T(8,128)(2,1)}), bf16[8,144,128]{2,1,0:T(8,128)(2,1)S(1)}, u32[]{:S(2)}, u32[]{:S(2)}) async-start(bf16[8,144,128]{2,1,0:T(8,128)(2,1)} %project.51), calls=%async_computation.1 | async-start | bytes 589824 | tf_op jit(solution)/shard_map/while/body/eval_jaxpr/exchange/all_to_all | solution.py:359
  439.2 5.0 collective-permute-start.15
  450.0 7.5 %collective-permute-start.18 = (bf16[144,384]{1,0:T(8,128)(2,1)S(1)}, bf16[144,384]{1,0:T(8,128)(2,1)S(1)}, u32[]{:S(2)}, u32[]{:S(2)}) collective-permute-start(bf16[144,384]{1,0:T(8,128)(2,1)S(1)} %attend.87), channel_id=1, source_target_pairs={{0,2},{1,3},{2,0},{3,1},{4,6},{5,7},{6,4},{7,5},{8,10},{9,11},{10,... | collective-permute-start | bytes 331784 | tf_op jit(solution)/shard_map/while/body/eval_jaxpr/attend/ppermute | solution.py:377
  452.2 6.0 %collective-permute-start.19 = (bf16[144,384]{1,0:T(8,128)(2,1)S(1)}, bf16[144,384]{1,0:T(8,128)(2,1)S(1)}, u32[]{:S(2)}, u32[]{:S(2)}) collective-permute-start(bf16[144,384]{1,0:T(8,128)(2,1)S(1)} %attend.88), channel_id=1, source_target_pairs={{0,3},{1,2},{2,1},{3,0},{4,7},{5,6},{6,5},{7,4},{8,11},{9,10},{10,... | collective-permute-start | bytes 331784 | tf_op jit(solution)/shard_map/while/body/eval_jaxpr/attend/ppermute | solution.py:377
  466.7 5.3 collective-permute-start.23
  474.2 4.8 collective-permute-start.25
  484.3 17.5 %all-to-all-start.1 = ((bf16[8,144,128]{2,1,0:T(8,128)(2,1)}), bf16[8,144,128]{2,1,0:T(8,128)(2,1)S(1)}, u32[]{:S(2)}, u32[]{:S(2)}) async-start(bf16[8,144,128]{2,1,0:T(8,128)(2,1)} %project.51), calls=%async_computation.1 | async-start | bytes 589824 | tf_op jit(solution)/shard_map/while/body/eval_jaxpr/exchange/all_to_all | solution.py:359
  492.6 5.0 collective-permute-start.15
  503.3 7.5 %collective-permute-start.18 = (bf16[144,384]{1,0:T(8,128)(2,1)S(1)}, bf16[144,384]{1,0:T(8,128)(2,1)S(1)}, u32[]{:S(2)}, u32[]{:S(2)}) collective-permute-start(bf16[144,384]{1,0:T(8,128)(2,1)S(1)} %attend.87), channel_id=1, source_target_pairs={{0,2},{1,3},{2,0},{3,1},{4,6},{5,7},{6,4},{7,5},{8,10},{9,11},{10,... | collective-permute-start | bytes 331784 | tf_op jit(solution)/shard_map/while/body/eval_jaxpr/attend/ppermute | solution.py:377
  505.6 6.0 %collective-permute-start.19 = (bf16[144,384]{1,0:T(8,128)(2,1)S(1)}, bf16[144,384]{1,0:T(8,128)(2,1)S(1)}, u32[]{:S(2)}, u32[]{:S(2)}) collective-permute-start(bf16[144,384]{1,0:T(8,128)(2,1)S(1)} %attend.88), channel_id=1, source_target_pairs={{0,3},{1,2},{2,1},{3,0},{4,7},{5,6},{6,5},{7,4},{8,11},{9,10},{10,... | collective-permute-start | bytes 331784 | tf_op jit(solution)/shard_map/while/body/eval_jaxpr/attend/ppermute | solution.py:377
  520.1 5.3 collective-permute-start.23
  (65 other events, 290.2 us)
Sparse Core Ops, SparseCore 0:
  28.2 96.3 all-gather.5
  127.2 130.4 all-gather.3
